TPU v7x, 512 devices: a whole 4x4x16 slice. The times are simulated.
512 devices in a mesh: dp: 8 (over y, core), place: 64 (over x, z).
Axes of the slice: x: 4, y: 4, z: 16, core: 2. Of those that a mesh axis runs over, the one named last changes fastest.
Arguments:
- tokens: bfloat16 [8, 64, 256, 2048], P('dp', 'place'), may hold values from -6 to 6
- hidden_grad: bfloat16 [8, 64, 256, 256], P('dp', 'place'), may hold values from -6 to 6
- routing: int32 [8, 64, 4, 64], P('dp', 'place'), may hold values from 0 to 63, each once within a row
- row_count: int32 [8, 64], replicated, may hold values from 1 to 256, as said below
- old_slots: int32 [64], replicated, may hold values from 0 to 15, as said below
- new_slots: int32 [64], replicated, may hold values from 0 to 15, as said below
- master: float32 [16, 2048, 512], P(None, ('dp', 'place')), may hold values from -0.125 to 0.125
- first_moment: float32 [16, 2048, 512], P(None, ('dp', 'place')), may hold values from -0.018 to 0.018
- second_moment: float32 [16, 2048, 512], P(None, ('dp', 'place')), may hold values from 1e-06 to 0.0001
Outputs:
- new_weights: bfloat16 [64, 2048, 512], P('place')
- new_master: float32 [16, 2048, 512], P(None, ('dp', 'place'))
- new_first: float32 [16, 2048, 512], P(None, ('dp', 'place'))
- new_second: float32 [16, 2048, 512], P(None, ('dp', 'place'))
Inputs may be any that keep to these rules, and one draw needn't show every extreme that they name: `old_slots`: every expert 0 .. 15 holds at least one slot. `new_slots`: every expert 0 .. 15 holds at least one slot. The first row_count[d, p] of a device's 256 row slots are live; some device is full in every draw.
All inputs are finite; a program needn't handle non-finite values.
Results may differ from a plain program's by a relative error of at most 0.001.
The roundings to bfloat16 on the way count: a program that leaves them out, or rounds other values in their place, can miss the bound.
Values may be sent and summed in bfloat16 or wider, within the bound.
No kernel may reach another device: no remote copies, remote signals or barrier semaphores. Data moves between devices by JAX's collectives and lax.ppermute only.
A program may use at most 64 MiB of HBM per device.

v0:
```python
import jax
import jax.numpy as jnp
from jax import lax
from jax.sharding import PartitionSpec as P

decay_first = 0.9
decay_second = 0.95
learn_rate = 0.001
weight_decay = 0.1
epsilon = 1e-08
step_number = 20.0


def from_everyone(x, axis):
    copies = jnp.broadcast_to(x, (lax.axis_size(axis), *x.shape))
    return lax.all_to_all(copies, axis, split_axis=0, concat_axis=0, tiled=True)


def joined_along(parts, dim):
    lengths = list(parts.shape[1:])
    lengths[dim] *= parts.shape[0]
    return jnp.moveaxis(parts, 0, dim).reshape(lengths)


def gathered_copies(x, axis, dim):
    parts = from_everyone(x, axis)
    return joined_along(parts, dim)


def in_blocks(x, dim, peers):
    before, after = (x.shape[:dim], x.shape[dim + 1 :])
    return jnp.moveaxis(x.reshape(*before, peers, -1, *after), dim, 0)


def sent_and_summed(x, axis, dim):
    peers = lax.axis_size(axis)
    parts = lax.all_to_all(in_blocks(x, dim, peers), axis, 0, 0, tiled=True)
    return jnp.sum(parts, axis=0)


def spread(shard, slots):
    experts, rows_shard, width = shard.shape
    places = lax.axis_size("place")
    select = (slots[:, None] == jnp.arange(experts, dtype=jnp.int32)[None, :]).astype(jnp.bfloat16)
    picked = jnp.dot(
        select, shard.reshape(experts, rows_shard * width), preferred_element_type=jnp.float32
    ).astype(jnp.bfloat16)
    landed = lax.all_to_all(
        picked.reshape(places, rows_shard, width), "place", split_axis=0, concat_axis=0, tiled=True
    )
    whole = gathered_copies(landed.reshape(places * rows_shard, width), "dp", 0)
    return whole


def batch_grad(total, rows_in, grads_in, order, count, weights, start):
    rows = order.shape[0]
    half = weights.shape[1] // 2
    picked = jnp.take(rows_in, start + order, axis=0)
    both = jnp.dot(picked, weights, preferred_element_type=jnp.float32)
    gate = both[:, :half]
    upward = both[:, half:]
    sigma = jax.nn.sigmoid(gate)
    active = gate * sigma
    slope = sigma * (1.0 + gate * (1.0 - sigma))
    live = start + jnp.arange(rows, dtype=jnp.int32) < count
    incoming = jnp.where(live[:, None], grads_in[start : start + rows].astype(jnp.float32), 0.0)
    local = jnp.concatenate([incoming * upward * slope, incoming * active], axis=1).astype(
        jnp.bfloat16
    )
    return total + lax.dot_general(
        picked, local, (((0,), (0,)), ((), ())), preferred_element_type=jnp.float32
    )


def shards(
    tokens,
    hidden_grad,
    routing,
    row_count,
    old_slots,
    new_slots,
    master,
    first_moment,
    second_moment,
):
    places = lax.axis_size("place")
    groups = lax.axis_size("dp")
    experts, rows_shard, width = master.shape
    place_here = lax.axis_index("place")
    group_here = lax.axis_index("dp")
    weights = spread(master.astype(jnp.bfloat16), old_slots)
    rows_in = tokens[0, 0]
    grads_in = hidden_grad[0, 0]
    order = routing[0, 0]
    count = row_count[group_here, place_here]
    batch_rows = order.shape[1]
    summed = jnp.zeros((rows_in.shape[1], width), jnp.float32)
    for batch_index in range(order.shape[0]):
        start = batch_index * batch_rows
        summed = batch_grad(summed, rows_in, grads_in, order[batch_index], count, weights, start)
    select = (old_slots[:, None] == jnp.arange(experts, dtype=jnp.int32)[None, :]).astype(
        jnp.float32
    )
    blocks = summed.reshape(groups, places, rows_shard, width)
    partial_sum = sent_and_summed(blocks, "dp", 0)
    landed = lax.all_to_all(partial_sum, "place", split_axis=1, concat_axis=1, tiled=True)
    grad_sum = jnp.dot(
        select.T, landed.reshape(places, rows_shard * width), precision=lax.Precision.HIGHEST
    ).reshape(experts, rows_shard, width)
    per_slot = jnp.sum(row_count.astype(jnp.float32), axis=0)
    total = jnp.dot(per_slot, select, precision=lax.Precision.HIGHEST)
    grad = grad_sum / total[:, None, None]
    new_first = decay_first * first_moment + (1.0 - decay_first) * grad
    new_second = decay_second * second_moment + (1.0 - decay_second) * grad * grad
    first_hat = new_first / (1.0 - decay_first**step_number)
    second_hat = new_second / (1.0 - decay_second**step_number)
    new_master = master - learn_rate * (
        first_hat / (jnp.sqrt(second_hat) + epsilon) + weight_decay * master
    )
    new_weights = spread(new_master.astype(jnp.bfloat16), new_slots)
    return (new_weights[None], new_master, new_first, new_second)


def solution(mesh):
    placed = (
        P("dp", "place", None, None),
        P("dp", "place", None, None),
        P("dp", "place", None, None),
        P(),
        P(),
        P(),
        P(None, ("dp", "place"), None),
        P(None, ("dp", "place"), None),
        P(None, ("dp", "place"), None),
    )
    return jax.shard_map(
        shards,
        mesh=mesh,
        in_specs=placed,
        out_specs=(
            P("place", None, None),
            P(None, ("dp", "place"), None),
            P(None, ("dp", "place"), None),
            P(None, ("dp", "place"), None),
        ),
        check_vma=False,
    )
```

profile of v0, /device:TPU:1, one launch (start us, length us, event | category | flops | bytes accessed | tf_op | source)
XLA Modules:
  0.0 247.8 jit_solution(2621490347751096984)
XLA Ops:
  0.6 1.0 convert_element_type.48
  1.7 0.9 convolution_convert_fusion.1
  2.8 38.0 %all_to_all.30 = bf16[64,4,512]{2,1,0:T(4,128)(2,1)S(1)} all-to-all(bf16[64,4,512]{2,1,0:T(4,128)(2,1)S(1)} %reshape.89), channel_id=1, replica_groups=mesh['dp'=8,'place'=64] {'place'}, dimensions={0} | all-to-all | bytes 524288 | tf_op jit(solution)/shard_map/all_to_all | solution.py:48
  40.9 1.5 broadcast_in_dim.58
  42.4 7.5 %all-to-all-start.1 = ((bf16[8,256,512]{2,1,0:T(8,128)(2,1)}), bf16[8,256,512]{2,1,0:T(8,128)(2,1)S(1)}, u32[]{:S(2)}, u32[]{:S(2)}) async-start(bf16[8,256,512]{2,1,0:T(8,128)(2,1)} %broadcast_in_dim.58), calls=%async_computation.1 | async-start | bytes 4194304 | tf_op jit(solution)/shard_map/all_to_all | solution.py:16
  49.9 1.4 gather_fusion
  51.3 1.4 gather_fusion.1
  52.8 0.7 gather_fusion.3
  53.5 1.4 gather_fusion.2
  55.0 0.6 dynamic_slice.3
  55.6 0.7 add_compare_fusion
  56.2 0.7 add_compare_fusion.2
  56.9 19.2 %all-to-all-done.1 = bf16[8,256,512]{2,1,0:T(8,128)(2,1)S(1)} async-done(((bf16[8,256,512]{2,1,0:T(8,128)(2,1)}), bf16[8,256,512]{2,1,0:T(8,128)(2,1)S(1)}, u32[]{:S(2)}, u32[]{:S(2)}) %all-to-all-start.1) | async-done | bytes 2097184 | tf_op jit(solution)/shard_map/all_to_all | solution.py:16
  76.0 1.5 fusion.5
  78.8 0.8 fusion.6
  79.7 0.8 fusion.4
  81.3 0.8 fusion.8
  82.1 2.8 %add_add_fusion = f32[2048,512]{1,0:T(8,128)} fusion(f32[2048,512]{1,0:T(8,128)S(1)} %fusion.8, f32[2048,512]{1,0:T(8,128)S(1)} %fusion.4, f32[2048,512]{1,0:T(8,128)S(1)} %fusion.6, bf16[64,2048]{1,0:T(8,128)(2,1)S(1)} %gather_fusion.3, pred[64]{0:T(512)(128)(4,1)S(1)} %get-tuple-element.21, bf16[64,256]{1,0:T(8,128)(2,1)S(1)} %get-tuple-element.30, ...), kind=kOutput, calls=%fused_computation.4 | convolution fusion | flops 137625600 | bytes 17104960 | tf_op jit(solution)/shard_map/dot_general | solution.py:70
  84.9 5.2 %reshape_reshape.3 = f32[8,1,64,4,512]{4,3,2,0,1:T(4,128)} reshape(f32[2048,512]{1,0:T(8,128)} %add_add_fusion) | data formatting | bytes 8388608 | tf_op jit(solution)/shard_map/reshape;reshape | solution.py:32
  90.1 54.1 %all_to_all.31 = f32[8,1,64,4,512]{4,3,2,1,0:T(4,128)} all-to-all(f32[8,1,64,4,512]{4,3,2,1,0:T(4,128)} %bitcast.78), channel_id=1, replica_groups=mesh['dp'=8,'place'=64] {'dp'}, dimensions={0} | all-to-all | bytes 8388608 | tf_op jit(solution)/shard_map/all_to_all | solution.py:37
  144.2 3.9 %reduce_sum.20 = f32[64,4,512]{2,1,0:T(4,128)} reduce(f32[8,1,64,4,512]{4,3,2,1,0:T(4,128)} %all_to_all.31, f32[]{:T(128)} %constant.16.clone.1), dimensions={0,1}, to_apply=%region_0.0 | reduce | flops 917504 | bytes 4718596 | tf_op jit(solution)/shard_map/reduce_sum | solution.py:38
  148.1 6.3 %all-to-all-start.3 = ((f32[1,64,4,512]{3,2,0,1:T(4,128)}), f32[1,64,4,512]{3,2,0,1:T(4,128)S(1)}, u32[]{:S(2)}, u32[]{:S(2)}) async-start(f32[1,64,4,512]{3,2,0,1:T(4,128)} %bitcast.13), calls=%async_computation.3 | async-start | bytes 1048576 | tf_op jit(solution)/shard_map/all_to_all | solution.py:106
  154.5 29.2 %all-to-all-done.3 = f32[1,64,4,512]{3,2,0,1:T(4,128)S(1)} async-done(((f32[1,64,4,512]{3,2,0,1:T(4,128)}), f32[1,64,4,512]{3,2,0,1:T(4,128)S(1)}, u32[]{:S(2)}, u32[]{:S(2)}) %all-to-all-start.3) | async-done | bytes 524320 | tf_op jit(solution)/shard_map/all_to_all | solution.py:106
  183.7 0.6 convert_bitcast_fusion
  184.8 27.1 %all_to_all.32 = bf16[64,4,512]{2,1,0:T(4,128)(2,1)S(1)} all-to-all(bf16[64,4,512]{2,1,0:T(4,128)(2,1)S(1)} %reshape.94), channel_id=1, replica_groups=mesh['dp'=8,'place'=64] {'place'}, dimensions={0} | all-to-all | bytes 524288 | tf_op jit(solution)/shard_map/all_to_all | solution.py:48
  212.0 1.5 broadcast_in_dim.62
  213.5 6.7 %all-to-all-start.5 = ((bf16[8,256,512]{2,1,0:T(8,128)(2,1)}), bf16[8,256,512]{2,1,0:T(8,128)(2,1)S(1)}, u32[]{:S(2)}, u32[]{:S(2)}) async-start(bf16[8,256,512]{2,1,0:T(8,128)(2,1)} %broadcast_in_dim.62), calls=%async_computation.5 | async-start | bytes 4194304 | tf_op jit(solution)/shard_map/all_to_all | solution.py:16
  220.2 0.7 copy.36
  221.0 0.7 copy.37
  221.7 0.7 copy.38
  222.5 24.0 %all-to-all-done.5 = bf16[8,256,512]{2,1,0:T(8,128)(2,1)S(1)} async-done(((bf16[8,256,512]{2,1,0:T(8,128)(2,1)}), bf16[8,256,512]{2,1,0:T(8,128)(2,1)S(1)}, u32[]{:S(2)}, u32[]{:S(2)}) %all-to-all-start.5) | async-done | bytes 2097184 | tf_op jit(solution)/shard_map/all_to_all | solution.py:16
  246.5 1.3 copy.63
  (41 shorter events, 3.0 us)
Async XLA Ops:
  0.6 49.2 %copy-start = (bf16[1,1,256,2048]{3,2,1,0:T(8,128)(2,1)S(1)}, bf16[1,1,256,2048]{3,2,1,0:T(8,128)(2,1)}, u32[]{:S(2)}) copy-start(bf16[1,1,256,2048]{3,2,1,0:T(8,128)(2,1)} %param.11) | copy-start | bytes 3145732
  42.4 7.5 %copy-start.7 = (s32[1,1,4,64]{3,2,1,0:T(4,128)S(1)}, s32[1,1,4,64]{3,2,1,0:T(4,128)}, u32[]{:S(2)}) copy-start(s32[1,1,4,64]{3,2,1,0:T(4,128)} %param.13) | copy-start | bytes 3076
  42.4 33.7 %all-to-all-start.1 = ((bf16[8,256,512]{2,1,0:T(8,128)(2,1)}), bf16[8,256,512]{2,1,0:T(8,128)(2,1)S(1)}, u32[]{:S(2)}, u32[]{:S(2)}) async-start(bf16[8,256,512]{2,1,0:T(8,128)(2,1)} %broadcast_in_dim.58), calls=%async_computation.1 | async-start | bytes 4194304 | tf_op jit(solution)/shard_map/all_to_all | solution.py:16
  52.8 2.2 copy-start.6
  76.0 1.5 copy-start.2
  77.6 1.1 copy-start.4
  78.8 1.0 copy-start.1
  79.7 0.9 copy-start.3
  144.2 10.2 %copy-start.8 = (s32[64]{0:T(128)S(1)}, s32[64]{0:T(128)}, u32[]{:S(2)}) copy-start(s32[64]{0:T(128)} %param.15) | copy-start | bytes 772
  144.2 39.5 %copy-start.5 = (f32[16,4,512]{2,1,0:T(4,128)S(1)}, f32[16,4,512]{2,1,0:T(4,128)}, u32[]{:S(2)}) copy-start(f32[16,4,512]{2,1,0:T(4,128)} %param.17) | copy-start | bytes 393220
  144.2 39.5 %copy-start.10 = (f32[16,4,512]{2,1,0:T(4,128)S(1)}, f32[16,4,512]{2,1,0:T(4,128)}, u32[]{:S(2)}) copy-start(f32[16,4,512]{2,1,0:T(4,128)} %param.18) | copy-start | bytes 393220
  144.2 39.5 %copy-start.11 = (f32[16,4,512]{2,1,0:T(4,128)S(1)}, f32[16,4,512]{2,1,0:T(4,128)}, u32[]{:S(2)}) copy-start(f32[16,4,512]{2,1,0:T(4,128)} %param.19) | copy-start | bytes 393220
  148.1 36.2 %copy-start.9 = (s32[64]{0:T(128)S(1)}, s32[64]{0:T(128)}, u32[]{:S(2)}) copy-start(s32[64]{0:T(128)} %param.16) | copy-start | bytes 772
  148.1 35.6 %all-to-all-start.3 = ((f32[1,64,4,512]{3,2,0,1:T(4,128)}), f32[1,64,4,512]{3,2,0,1:T(4,128)S(1)}, u32[]{:S(2)}, u32[]{:S(2)}) async-start(f32[1,64,4,512]{3,2,0,1:T(4,128)} %bitcast.13), calls=%async_computation.3 | async-start | bytes 1048576 | tf_op jit(solution)/shard_map/all_to_all | solution.py:106
  213.5 33.0 %all-to-all-start.5 = ((bf16[8,256,512]{2,1,0:T(8,128)(2,1)}), bf16[8,256,512]{2,1,0:T(8,128)(2,1)S(1)}, u32[]{:S(2)}, u32[]{:S(2)}) async-start(bf16[8,256,512]{2,1,0:T(8,128)(2,1)} %broadcast_in_dim.62), calls=%async_computation.5 | async-start | bytes 4194304 | tf_op jit(solution)/shard_map/all_to_all | solution.py:16
where the time goes:
time: 248 us
  blocking collectives  119 us (48%)
  waiting for transfers between devices  72.4 us (29%)
  starting transfers between devices  20.5 us (8%)
  local copies, waits for them, and re-layouts  18.2 us (7%)
  matrix products  10.2 us (4%)
  other arithmetic  6.47 us (3%)
    all_to_all x2, blocking collectives, spread(): lax.all_to_all(picked.reshape(places, rows_shard, width), 'place', split_...  65.1 us
    all_to_all x1, blocking collectives, sent_and_summed(): parts = lax.all_to_all(in_blocks(x, dim, peers), axis, 0, 0, tiled=True)  54.1 us
    all_to_all x2, waiting for transfers between devices, from_everyone(): return lax.all_to_all(copies, axis, split_axis=0, concat_axis=0, tiled=True)  43.2 us
    all_to_all x1, waiting for transfers between devices, shards(): lax.all_to_all(partial_sum, 'place', split_axis=1, concat_axis=1, tiled=T...  29.2 us
    all_to_all x2, starting transfers between devices, from_everyone(): return lax.all_to_all(copies, axis, split_axis=0, concat_axis=0, tiled=True)  14.2 us
    all_to_all x1, starting transfers between devices, shards(): lax.all_to_all(partial_sum, 'place', split_axis=1, concat_axis=1, tiled=T...  6.27 us
    dot_general x4, matrix products, batch_grad(): lax.dot_general(picked, local, (((0,), (0,)), ((), ())), preferred_elemen...  5.23 us
    another operation x1, local copies, waits for them, and re-layouts, in_blocks(): return jnp.moveaxis(x.reshape(*before, peers, -1, *after), dim, 0)  5.18 us
  transfers between devices with their start and end apart: 3, of which 3 were waited for; matrix products, arithmetic and copies ran while one was open for 4% of the time, Pallas kernels for 0%

commit v1 on v0

v1 whole, which is shorter than its diff:
```python
import jax
import jax.numpy as jnp
from jax import lax
from jax.experimental import pallas as pl
from jax.experimental.pallas import tpu as pltpu
from jax.sharding import Mesh
from jax.sharding import PartitionSpec as P


decay_first = 0.9
decay_second = 0.95
learn_rate = 0.001
weight_decay = 0.1
epsilon = 1e-08
step_number = 20.0

Y, C, X, Z = 4, 2, 4, 16
UP = [(i, (i + 1) % Y) for i in range(Y)]
DOWN = [(i, (i - 1) % Y) for i in range(Y)]
ACROSS = [(i, (i + 2) % Y) for i in range(Y)]
SWAP = [(0, 1), (1, 0)]


def group_grad(core_ref, w_ref, h0_ref, h1_ref, *refs):
    chunks, (out_ref, local_ref) = refs[:-2], refs[-2:]
    half = w_ref.shape[1] // 2
    row = 0
    starts = []
    for k, chunk in enumerate(chunks):
        rows = chunk.shape[0]
        h_ref = h0_ref if k < len(chunks) // 2 else h1_ref
        first = row % h_ref.shape[0]
        both = jnp.dot(chunk[...], w_ref[...], preferred_element_type=jnp.float32)
        other = pltpu.roll(both, half, 1)
        lane = lax.broadcasted_iota(jnp.int32, both.shape, 1)
        gate = jnp.where(lane < half, both, other)
        sigma = jax.nn.sigmoid(gate)
        active = gate * sigma
        slope = sigma * (1.0 + gate * (1.0 - sigma))
        incoming = h_ref[first : first + rows, :].astype(jnp.float32)
        local = jnp.where(lane < half, incoming * other * slope, incoming * active)
        local_ref[:, row : row + rows] = local.T.astype(jnp.bfloat16)
        starts.append(row)
        row += rows
    core = core_ref[0]
    wide = out_ref.shape[0] // Y
    for y in range(Y):
        at = pl.multiple_of((2 * y + core) * wide, wide)
        total = jnp.zeros((2 * half, wide), jnp.float32)
        for start, chunk in zip(starts, chunks):
            total = total + jnp.dot(
                local_ref[:, start : start + chunk.shape[0]],
                chunk[:, pl.ds(at, wide)],
                preferred_element_type=jnp.float32,
            )
        out_ref[y * wide : (y + 1) * wide, :] = total.T


def call_group_grad(core, w, h0, h1, chunks):
    vmem = pl.BlockSpec(memory_space=pltpu.VMEM)
    rows = sum(c.shape[0] for c in chunks)
    deep, cols = w.shape
    return pl.pallas_call(
        group_grad,
        out_shape=jax.ShapeDtypeStruct((deep // C, cols), jnp.float32),
        in_specs=[pl.BlockSpec(memory_space=pltpu.SMEM)] + [vmem] * (3 + len(chunks)),
        out_specs=vmem,
        scratch_shapes=[pltpu.VMEM((cols, rows), jnp.bfloat16)],
        name="group_grad",
    )(core, w, h0, h1, *chunks)


def one_hot(slots, experts, dtype):
    return (slots[:, None] == jnp.arange(experts, dtype=jnp.int32)[None, :]).astype(dtype)


def shards(
    tokens, hidden_grad, routing, row_count, old_slots, new_slots, master, first_moment, second_moment
):
    y, core = lax.axis_index("y"), lax.axis_index("core")
    group_here = y * C + core
    place_here = lax.axis_index("x") * Z + lax.axis_index("z")
    experts, rows_shard, width = master.shape
    hid = width // 2
    part = hid // Y

    own = tokens[0, 0]
    rows = own.shape[0]
    low = lax.ppermute(own, "y", UP)
    high = lax.ppermute(own, "y", DOWN)
    own_c = lax.ppermute(own, "core", SWAP)

    picked = jnp.dot(
        one_hot(old_slots, experts, jnp.bfloat16),
        master.astype(jnp.bfloat16).reshape(experts, rows_shard * width),
        preferred_element_type=jnp.float32,
    ).astype(jnp.bfloat16)
    landed = lax.all_to_all(
        picked.reshape(X * Z, rows_shard, width), ("x", "z"), 0, 0, tiled=True
    ).reshape(X * Z * rows_shard, width)

    order = routing[0, 0]
    batches, batch_rows = order.shape
    count = row_count[group_here, place_here]
    live = jnp.arange(rows, dtype=jnp.int32) < count
    masked = jnp.where(live[:, None], hidden_grad[0, 0], jnp.zeros((), jnp.bfloat16))
    slot_of = (
        order[:, None, :] == jnp.arange(batch_rows, dtype=jnp.int32)[None, :, None]
    ).astype(jnp.bfloat16)
    moved = lax.dot_general(
        slot_of,
        masked.reshape(batches, batch_rows, hid),
        (((2,), (1,)), ((0,), (0,))),
        preferred_element_type=jnp.float32,
    ).astype(jnp.bfloat16).reshape(rows, hid)
    slices = [moved[:, k * part : (k + 1) * part] for k in range(Y)]
    by_chip = jnp.stack([jnp.concatenate([s, s], axis=1) for s in slices])

    def for_chip(step):
        return lax.dynamic_index_in_dim(by_chip, (y + step) % Y, keepdims=False)

    h_low = lax.ppermute(for_chip(1), "y", UP)
    h_high = lax.ppermute(for_chip(3), "y", DOWN)
    h_far = lax.ppermute(for_chip(2), "y", ACROSS)
    h_own = jnp.concatenate([for_chip(0), h_low, h_high, h_far], axis=0)
    h_own_c = lax.ppermute(h_own, "core", SWAP)

    half_rows = rows // 2
    far_a = lax.ppermute(low[:half_rows], "y", UP)
    far_b = lax.ppermute(high[half_rows:], "y", DOWN)
    low_c = lax.ppermute(low, "core", SWAP)
    high_c = lax.ppermute(high, "core", SWAP)
    far_a_c = lax.ppermute(far_a, "core", SWAP)
    far_b_c = lax.ppermute(far_b, "core", SWAP)

    columns = jnp.stack(
        [
            jnp.concatenate(
                [landed[:, k * part : (k + 1) * part], landed[:, hid + k * part : hid + (k + 1) * part]],
                axis=1,
            )
            for k in range(Y)
        ]
    )
    columns = jnp.broadcast_to(columns[:, None], (Y, C, *columns.shape[1:]))
    weights = lax.all_to_all(
        columns.reshape(Y * C, *columns.shape[2:]), ("y", "core"), 0, 0, tiled=True
    )
    weights = weights.reshape(-1, 2 * part)

    summed = call_group_grad(
        core.astype(jnp.int32).reshape(1),
        weights,
        h_own,
        h_own_c,
        [own, low, high, far_a, far_b, own_c, low_c, high_c, far_a_c, far_b_c],
    )

    got = lax.all_to_all(
        summed.reshape(Y * X, Z * rows_shard, 2 * part), ("y", "x"), 0, 0, tiled=True
    )
    got = got.reshape(Y, X, Z, rows_shard, 2 * part).transpose(2, 1, 0, 3, 4)
    got = lax.all_to_all(
        got.reshape(Z, X * Y * rows_shard, 2 * part), "z", 0, 0, tiled=True
    )
    old_zx = old_slots.reshape(X, Z).T.reshape(-1)
    select = one_hot(old_zx, experts, jnp.float32)
    grad_sum = jnp.dot(
        select.T, got.reshape(Z * X, Y * rows_shard * 2 * part), precision=lax.Precision.HIGHEST
    )
    grad_sum = (
        grad_sum.reshape(experts, Y, rows_shard, 2, part)
        .transpose(0, 2, 3, 1, 4)
        .reshape(experts, rows_shard, width)
    )
    per_slot = jnp.sum(row_count.astype(jnp.float32), axis=0)
    total = jnp.dot(
        per_slot, one_hot(old_slots, experts, jnp.float32), precision=lax.Precision.HIGHEST
    )
    grad = grad_sum / total[:, None, None]
    new_first = decay_first * first_moment + (1.0 - decay_first) * grad
    new_second = decay_second * second_moment + (1.0 - decay_second) * grad * grad
    first_hat = new_first / (1.0 - decay_first**step_number)
    second_hat = new_second / (1.0 - decay_second**step_number)
    new_master = master - learn_rate * (
        first_hat / (jnp.sqrt(second_hat) + epsilon) + weight_decay * master
    )

    new_zx = new_slots.reshape(X, Z).T.reshape(-1)
    picked = jnp.dot(
        one_hot(new_zx, experts, jnp.bfloat16),
        new_master.astype(jnp.bfloat16).reshape(experts, rows_shard * width),
        preferred_element_type=jnp.float32,
    ).astype(jnp.bfloat16)
    landed = lax.all_to_all(
        picked.reshape(Z, X * rows_shard, width), "z", 0, 0, tiled=True
    )
    landed = (
        landed.reshape(Z, X, rows_shard, width).transpose(1, 0, 2, 3).reshape(X, Z * rows_shard, width)
    )
    landed = jnp.broadcast_to(landed[None], (Y, *landed.shape))
    mine = lax.all_to_all(
        landed.reshape(Y * X, Z * rows_shard, width), ("y", "x"), 0, 0, tiled=True
    ).reshape(Y, X * Z * rows_shard, width)
    theirs = lax.ppermute(mine, "core", SWAP)
    even = jnp.where(core == 0, mine, theirs)
    odd = jnp.where(core == 0, theirs, mine)
    new_weights = jnp.stack([even, odd], axis=1).reshape(1, -1, width)
    return (new_weights, new_master, new_first, new_second)


def solution(mesh):
    fine = Mesh(mesh.devices.reshape(Y, C, X, Z), ("y", "core", "x", "z"))
    dp, place = ("y", "core"), ("x", "z")
    placed = (
        P(dp, place, None, None),
        P(dp, place, None, None),
        P(dp, place, None, None),
        P(),
        P(),
        P(),
        P(None, dp + place, None),
        P(None, dp + place, None),
        P(None, dp + place, None),
    )

    return jax.shard_map(
        shards,
        mesh=fine,
        in_specs=placed,
        out_specs=(
            P(place, None, None),
            P(None, dp + place, None),
            P(None, dp + place, None),
            P(None, dp + place, None),
        ),
        check_vma=False,
    )
```

time: 248 us -> 208 us (0.84); the launches traced: 248 us -> 205 us
  blocking collectives: 119 us -> 55.7 us
  starting transfers between devices: 20.5 us -> 83.7 us
  waiting for transfers between devices: 72.4 us -> 37.5 us
  Pallas kernels: 0 us -> 7.76 us
  local copies, waits for them, and re-layouts: 18.2 us -> 11.2 us
  matrix products: 10.2 us -> 3.88 us
    all_to_all x3, blocking collectives: 119 us -> 55.7 us  [the longest x1 25.2 us: shards(): lax.all_to_all(picked.reshape(Z, X * rows_shard, width), 'z', 0, 0, tiled...]
    ppermute x0 -> x14, starting transfers between devices: none -> 49 us  [the longest x1 9.77 us: shards(): theirs = lax.ppermute(mine, 'core', SWAP)]
    all_to_all x3, waiting for transfers between devices: 72.4 us -> 31 us  [the longest x1 21.7 us: shards(): lax.all_to_all(got.reshape(Z, X * Y * rows_shard, 2 * part), 'z', 0, 0, t...]
    all_to_all x3, starting transfers between devices: 20.5 us -> 34.7 us  [the longest x1 18.3 us: shards(): lax.all_to_all(picked.reshape(X * Z, rows_shard, width), ('x', 'z'), 0, 0...]
    pallas_call x0 -> x1, Pallas kernels: none -> 7.76 us  [call_group_grad(): pl.pallas_call(group_grad, out_shape=jax.ShapeDtypeStruct((deep // C, col...]
    ppermute x0 -> x14, waiting for transfers between devices: none -> 6.52 us  [the longest x1 4.45 us: shards(): h_far = lax.ppermute(for_chip(2), 'y', ACROSS)]
    dot_general x12 -> x5, matrix products: 10.2 us -> 3.88 us  [the longest x1 1.34 us: shards(): jnp.dot(select.T, got.reshape(Z * X, Y * rows_shard * 2 * part), precisio...]
    another operation x1 -> x0, local copies, waits for them, and re-layouts: 5.18 us -> none  [in_blocks(): return jnp.moveaxis(x.reshape(*before, peers, -1, *after), dim, 0)]
  transfers between devices with their start and end apart: 3 -> 17, of which waited for: 3 -> 4; matrix products, arithmetic and copies ran while one was open for 4% -> 6% of each run, Pallas kernels for 0% -> 0%
where the time goes in v1:
time: 208 us; the launch traced here: 205 us
  starting transfers between devices  83.7 us (40%)
  blocking collectives  55.7 us (27%)
  waiting for transfers between devices  37.5 us (18%)
  local copies, waits for them, and re-layouts  11.2 us (5%)
  Pallas kernels  7.76 us (4%)
  other arithmetic  4.01 us (2%)
  matrix products  3.88 us (2%)
    all_to_all x1, blocking collectives, shards(): lax.all_to_all(picked.reshape(Z, X * rows_shard, width), 'z', 0, 0, tiled...  25.2 us
    all_to_all x1, waiting for transfers between devices, shards(): lax.all_to_all(got.reshape(Z, X * Y * rows_shard, 2 * part), 'z', 0, 0, t...  21.7 us
    all_to_all x1, starting transfers between devices, shards(): lax.all_to_all(picked.reshape(X * Z, rows_shard, width), ('x', 'z'), 0, 0...  18.3 us
    all_to_all x1, blocking collectives, shards(): lax.all_to_all(summed.reshape(Y * X, Z * rows_shard, 2 * part), ('y', 'x'...  15.5 us
    all_to_all x1, blocking collectives, shards(): lax.all_to_all(landed.reshape(Y * X, Z * rows_shard, width), ('y', 'x'),...  15 us
    all_to_all x1, starting transfers between devices, shards(): lax.all_to_all(got.reshape(Z, X * Y * rows_shard, 2 * part), 'z', 0, 0, t...  11.3 us
    ppermute x1, starting transfers between devices, shards(): theirs = lax.ppermute(mine, 'core', SWAP)  9.77 us
    all_to_all x1, waiting for transfers between devices, shards(): lax.all_to_all(columns.reshape(Y * C, *columns.shape[2:]), ('y', 'core'),...  9.35 us
  transfers between devices with their start and end apart: 17, of which 4 were waited for; matrix products, arithmetic and copies ran while one was open for 6% of the time, Pallas kernels for 0%

profile of v1, /device:TPU:1, one launch (start us, length us, event | category | flops | bytes accessed | tf_op | source)
XLA Modules:
  0.0 205.1 jit_solution(4529092819233806400)
XLA Ops:
  0.6 4.0 %collective-permute-start.4 = (bf16[256,2048]{1,0:T(8,128)(2,1)}, bf16[256,2048]{1,0:T(8,128)(2,1)S(1)}, u32[]{:S(2)}, u32[]{:S(2)}) collective-permute-start(bf16[256,2048]{1,0:T(8,128)(2,1)} %bitcast.23.refs_0_), channel_id=1, source_target_pairs={{0,128},{128,256},{256,384},{384,0},{1,129},{129,257},{257,385},{3... | collective-permute-start | bytes 3145736 | tf_op jit(solution)/shard_map/ppermute | solution.py:89
  4.7 3.4 %collective-permute-start.5 = (bf16[256,2048]{1,0:T(8,128)(2,1)}, bf16[256,2048]{1,0:T(8,128)(2,1)S(1)}, u32[]{:S(2)}, u32[]{:S(2)}) collective-permute-start(bf16[256,2048]{1,0:T(8,128)(2,1)} %bitcast.23.refs_0_), channel_id=1, source_target_pairs={{0,384},{128,0},{256,128},{384,256},{1,385},{129,1},{257,129},{385... | collective-permute-start | bytes 3145736 | tf_op jit(solution)/shard_map/ppermute | solution.py:90
  8.0 0.9 convert_element_type.23
  10.8 18.3 %all-to-all-start = ((bf16[64,4,512]{2,1,0:T(4,128)(2,1)}), bf16[64,4,512]{2,1,0:T(4,128)(2,1)S(1)}, u32[]{:S(2)}, u32[]{:S(2)}) async-start(bf16[64,4,512]{2,1,0:T(4,128)(2,1)} %reshape.92), calls=%async_computation | async-start | bytes 524288 | tf_op jit(solution)/shard_map/all_to_all | solution.py:98
  29.1 1.3 dynamic_slice.16
  31.1 1.2 convolution_convert_fusion.2
  32.7 1.9 collective-permute-start
  34.6 4.6 %collective-permute-start.1 = (bf16[256,128]{1,0:T(8,128)(2,1)S(1)}, bf16[256,128]{1,0:T(8,128)(2,1)S(1)}, u32[]{:S(2)}, u32[]{:S(2)}) collective-permute-start(bf16[256,128]{1,0:T(8,128)(2,1)S(1)} %get-tuple-element.24), channel_id=1, source_target_pairs={{0,384},{128,0},{256,128},{384,256},{1,385},{129,1},{257,129},{385... | collective-permute-start | bytes 196616 | tf_op jit(solution)/shard_map/ppermute | solution.py:123
  39.2 2.3 %collective-permute-start.2 = (bf16[256,128]{1,0:T(8,128)(2,1)S(1)}, bf16[256,128]{1,0:T(8,128)(2,1)S(1)}, u32[]{:S(2)}, u32[]{:S(2)}) collective-permute-start(bf16[256,128]{1,0:T(8,128)(2,1)S(1)} %get-tuple-element.23), channel_id=1, source_target_pairs={{0,256},{128,384},{256,0},{384,128},{1,257},{129,385},{257,1},{385... | collective-permute-start | bytes 196616 | tf_op jit(solution)/shard_map/ppermute | solution.py:124
  41.6 4.4 %collective-permute-done.2 = bf16[256,128]{1,0:T(8,128)(2,1)S(1)} collective-permute-done((bf16[256,128]{1,0:T(8,128)(2,1)S(1)}, bf16[256,128]{1,0:T(8,128)(2,1)S(1)}, u32[]{:S(2)}, u32[]{:S(2)}) %collective-permute-start.2) | collective-permute-done | bytes 65568 | tf_op jit(solution)/shard_map/ppermute | solution.py:124
  46.1 4.8 %collective-permute-start.3 = (bf16[1024,128]{1,0:T(8,128)(2,1)S(1)}, bf16[1024,128]{1,0:T(8,128)(2,1)S(1)}, u32[]{:S(2)}, u32[]{:S(2)}) collective-permute-start(bf16[1024,128]{1,0:T(8,128)(2,1)S(1)} %pad_maximum_fusion.3.h0_ref), channel_id=1, source_target_pairs={{0,64},{64,0},{1,65},{65,1},{2,66},{66,2},{3,67},{67,3},{4,68},{68... | collective-permute-start | bytes 786440 | tf_op jit(solution)/shard_map/ppermute | solution.py:126
  50.9 0.9 slice.68
  51.8 1.9 collective-permute-start.6
  54.6 4.6 %collective-permute-start.7 = (bf16[128,2048]{1,0:T(8,128)(2,1)}, bf16[128,2048]{1,0:T(8,128)(2,1)}, u32[]{:S(2)}, u32[]{:S(2)}) collective-permute-start(bf16[128,2048]{1,0:T(8,128)(2,1)} %slice.69), channel_id=1, source_target_pairs={{0,384},{128,0},{256,128},{384,256},{1,385},{129,1},{257,129},{385... | collective-permute-start | bytes 1572872 | tf_op jit(solution)/shard_map/ppermute | solution.py:130
  59.2 2.5 %collective-permute-start.8 = (bf16[256,2048]{1,0:T(8,128)(2,1)}, bf16[256,2048]{1,0:T(8,128)(2,1)}, u32[]{:S(2)}, u32[]{:S(2)}) collective-permute-start(bf16[256,2048]{1,0:T(8,128)(2,1)} %bitcast.23.refs_0_), channel_id=1, source_target_pairs={{0,64},{64,0},{1,65},{65,1},{2,66},{66,2},{3,67},{67,3},{4,68},{68... | collective-permute-start | bytes 3145736 | tf_op jit(solution)/shard_map/ppermute | solution.py:91
  61.7 1.9 collective-permute-start.10
  63.7 2.4 %collective-permute-start.9 = (bf16[256,2048]{1,0:T(8,128)(2,1)S(1)}, bf16[256,2048]{1,0:T(8,128)(2,1)}, u32[]{:S(2)}, u32[]{:S(2)}) collective-permute-start(bf16[256,2048]{1,0:T(8,128)(2,1)S(1)} %collective-permute-done.4.refs_1_), channel_id=1, source_target_pairs={{0,64},{64,0},{1,65},{65,1},{2,66},{66,2},{3,67},{67,3},{4,68},{68... | collective-permute-start | bytes 3145736 | tf_op jit(solution)/shard_map/ppermute | solution.py:131
  66.6 2.0 collective-permute-done.6.refs_3_
  68.6 2.8 %collective-permute-start.11 = (bf16[128,2048]{1,0:T(8,128)(2,1)S(1)}, bf16[128,2048]{1,0:T(8,128)(2,1)}, u32[]{:S(2)}, u32[]{:S(2)}) collective-permute-start(bf16[128,2048]{1,0:T(8,128)(2,1)S(1)} %collective-permute-done.6.refs_3_), channel_id=1, source_target_pairs={{0,64},{64,0},{1,65},{65,1},{2,66},{66,2},{3,67},{67,3},{4,68},{68... | collective-permute-start | bytes 1572872 | tf_op jit(solution)/shard_map/ppermute | solution.py:133
  71.4 2.2 %collective-permute-start.12 = (bf16[128,2048]{1,0:T(8,128)(2,1)}, bf16[128,2048]{1,0:T(8,128)(2,1)}, u32[]{:S(2)}, u32[]{:S(2)}) collective-permute-start(bf16[128,2048]{1,0:T(8,128)(2,1)} %collective-permute-done.7.refs_4_), channel_id=1, source_target_pairs={{0,64},{64,0},{1,65},{65,1},{2,66},{66,2},{3,67},{67,3},{4,68},{68... | collective-permute-start | bytes 1572872 | tf_op jit(solution)/shard_map/ppermute | solution.py:134
  74.5 5.1 %all-to-all-start.1 = ((bf16[8,256,128]{2,1,0:T(8,128)(2,1)}), bf16[8,256,128]{2,1,0:T(8,128)(2,1)S(1)}, u32[]{:S(2)}, u32[]{:S(2)}) async-start(bf16[8,256,128]{2,1,0:T(8,128)(2,1)} %bitcast.9), calls=%async_computation.1 | async-start | bytes 1048576 | tf_op jit(solution)/shard_map/all_to_all | solution.py:146
  79.6 9.3 %all-to-all-done.1 = bf16[8,256,128]{2,1,0:T(8,128)(2,1)S(1)} async-done(((bf16[8,256,128]{2,1,0:T(8,128)(2,1)}), bf16[8,256,128]{2,1,0:T(8,128)(2,1)S(1)}, u32[]{:S(2)}, u32[]{:S(2)}) %all-to-all-start.1) | async-done | bytes 524320 | tf_op jit(solution)/shard_map/all_to_all | solution.py:146
  89.7 7.8 %group_grad.1 = f32[1024,128]{1,0:T(8,128)} custom-call(s32[1]{0:T(128)} %bitcast.4.core_ref, bf16[2048,128]{1,0:T(8,128)(2,1)} %bitcast.83, bf16[1024,128]{1,0:T(8,128)(2,1)} %copy-done.3, bf16[1024,128]{1,0:T(8,128)(2,1)} %copy-done.6, bf16[256,2048]{1,0:T(8,128)(2,1)} %bitcast.23.refs_0_, bf16[256,2048]{1,0:T(8,128)(2,1)} %copy-done, ...), custom_call_target="tpu_custom_call" | custom-call | tf_op jit(solution)/shard_map/group_grad/pallas_call | solution.py:63
  97.5 15.5 %all_to_all.30 = f32[16,64,128]{2,1,0:T(8,128)S(1)} all-to-all(f32[16,64,128]{2,1,0:T(8,128)} %bitcast.84), channel_id=1, replica_groups=mesh['y'=4,'core'=2,'x'=4,'z'=16] {'y','x'}, dimensions={0} | all-to-all | bytes 1048576 | tf_op jit(solution)/shard_map/all_to_all | solution.py:159
  113.0 1.0 copy.52
  114.0 11.3 %all-to-all-start.3 = ((f32[16,64,128]{2,1,0:T(8,128)}), f32[16,64,128]{2,1,0:T(8,128)S(1)}, u32[]{:S(2)}, u32[]{:S(2)}) async-start(f32[16,64,128]{2,1,0:T(8,128)} %copy.52), calls=%async_computation.3 | async-start | bytes 1048576 | tf_op jit(solution)/shard_map/all_to_all | solution.py:163
  126.1 21.7 %all-to-all-done.3 = f32[16,64,128]{2,1,0:T(8,128)S(1)} async-done(((f32[16,64,128]{2,1,0:T(8,128)}), f32[16,64,128]{2,1,0:T(8,128)S(1)}, u32[]{:S(2)}, u32[]{:S(2)}) %all-to-all-start.3) | async-done | bytes 524320 | tf_op jit(solution)/shard_map/all_to_all | solution.py:163
  148.2 1.3 convolution_bitcast_fusion
  150.6 25.2 %all_to_all.31 = bf16[16,16,512]{2,1,0:T(8,128)(2,1)S(1)} all-to-all(bf16[16,16,512]{2,1,0:T(8,128)(2,1)S(1)} %reshape.103), channel_id=1, replica_groups=mesh['y'=4,'core'=2,'x'=4,'z'=16] {'z'}, dimensions={0} | all-to-all | bytes 524288 | tf_op jit(solution)/shard_map/all_to_all | solution.py:195
  176.4 15.0 %all_to_all.32 = bf16[16,64,512]{2,1,0:T(8,128)(2,1)S(1)} all-to-all(bf16[16,64,512]{2,1,0:T(8,128)(2,1)S(1)} %bitcast.82), channel_id=1, replica_groups=mesh['y'=4,'core'=2,'x'=4,'z'=16] {'y','x'}, dimensions={0} | all-to-all | bytes 2097152 | tf_op jit(solution)/shard_map/all_to_all | solution.py:202
  191.4 9.8 %collective-permute-start.13 = (bf16[4,256,512]{2,1,0:T(8,128)(2,1)S(1)}, bf16[4,256,512]{2,1,0:T(8,128)(2,1)S(1)}, u32[]{:S(2)}, u32[]{:S(2)}) collective-permute-start(bf16[4,256,512]{2,1,0:T(8,128)(2,1)S(1)} %bitcast.79), channel_id=1, source_target_pairs={{0,64},{64,0},{1,65},{65,1},{2,66},{66,2},{3,67},{67,3},{4,68},{68... | collective-permute-start | bytes 3145736 | tf_op jit(solution)/shard_map/ppermute | solution.py:205
  203.6 1.5 pad_maximum_fusion
  (79 shorter events, 11.1 us)
Async XLA Ops:
  0.6 50.2 %collective-permute-start.4 = (bf16[256,2048]{1,0:T(8,128)(2,1)}, bf16[256,2048]{1,0:T(8,128)(2,1)S(1)}, u32[]{:S(2)}, u32[]{:S(2)}) collective-permute-start(bf16[256,2048]{1,0:T(8,128)(2,1)} %bitcast.23.refs_0_), channel_id=1, source_target_pairs={{0,128},{128,256},{256,384},{384,0},{1,129},{129,257},{257,385},{3... | collective-permute-start | bytes 3145736 | tf_op jit(solution)/shard_map/ppermute | solution.py:89
  4.7 49.0 %collective-permute-start.5 = (bf16[256,2048]{1,0:T(8,128)(2,1)}, bf16[256,2048]{1,0:T(8,128)(2,1)S(1)}, u32[]{:S(2)}, u32[]{:S(2)}) collective-permute-start(bf16[256,2048]{1,0:T(8,128)(2,1)} %bitcast.23.refs_0_), channel_id=1, source_target_pairs={{0,384},{128,0},{256,128},{384,256},{1,385},{129,1},{257,129},{385... | collective-permute-start | bytes 3145736 | tf_op jit(solution)/shard_map/ppermute | solution.py:90
  10.8 55.3 %all-to-all-start = ((bf16[64,4,512]{2,1,0:T(4,128)(2,1)}), bf16[64,4,512]{2,1,0:T(4,128)(2,1)S(1)}, u32[]{:S(2)}, u32[]{:S(2)}) async-start(bf16[64,4,512]{2,1,0:T(4,128)(2,1)} %reshape.92), calls=%async_computation | async-start | bytes 524288 | tf_op jit(solution)/shard_map/all_to_all | solution.py:98
  32.7 8.9 %collective-permute-start = (bf16[256,128]{1,0:T(8,128)(2,1)S(1)}, bf16[256,128]{1,0:T(8,128)(2,1)S(1)}, u32[]{:S(2)}, u32[]{:S(2)}) collective-permute-start(bf16[256,128]{1,0:T(8,128)(2,1)S(1)} %get-tuple-element.25), channel_id=1, source_target_pairs={{0,128},{128,256},{256,384},{384,0},{1,129},{129,257},{257,385},{3... | collective-permute-start | bytes 196616 | tf_op jit(solution)/shard_map/ppermute | solution.py:122
  34.6 6.9 %collective-permute-start.1 = (bf16[256,128]{1,0:T(8,128)(2,1)S(1)}, bf16[256,128]{1,0:T(8,128)(2,1)S(1)}, u32[]{:S(2)}, u32[]{:S(2)}) collective-permute-start(bf16[256,128]{1,0:T(8,128)(2,1)S(1)} %get-tuple-element.24), channel_id=1, source_target_pairs={{0,384},{128,0},{256,128},{384,256},{1,385},{129,1},{257,129},{385... | collective-permute-start | bytes 196616 | tf_op jit(solution)/shard_map/ppermute | solution.py:123
  39.2 6.8 %collective-permute-start.2 = (bf16[256,128]{1,0:T(8,128)(2,1)S(1)}, bf16[256,128]{1,0:T(8,128)(2,1)S(1)}, u32[]{:S(2)}, u32[]{:S(2)}) collective-permute-start(bf16[256,128]{1,0:T(8,128)(2,1)S(1)} %get-tuple-element.23), channel_id=1, source_target_pairs={{0,256},{128,384},{256,0},{384,128},{1,257},{129,385},{257,1},{385... | collective-permute-start | bytes 196616 | tf_op jit(solution)/shard_map/ppermute | solution.py:124
  46.0 20.5 %copy-start.3 = (bf16[1024,128]{1,0:T(8,128)(2,1)}, bf16[1024,128]{1,0:T(8,128)(2,1)S(1)}, u32[]{:S(2)}) copy-start(bf16[1024,128]{1,0:T(8,128)(2,1)S(1)} %pad_maximum_fusion.3.h0_ref) | copy-start | bytes 786436
  46.1 17.6 %collective-permute-start.3 = (bf16[1024,128]{1,0:T(8,128)(2,1)S(1)}, bf16[1024,128]{1,0:T(8,128)(2,1)S(1)}, u32[]{:S(2)}, u32[]{:S(2)}) collective-permute-start(bf16[1024,128]{1,0:T(8,128)(2,1)S(1)} %pad_maximum_fusion.3.h0_ref), channel_id=1, source_target_pairs={{0,64},{64,0},{1,65},{65,1},{2,66},{66,2},{3,67},{67,3},{4,68},{68... | collective-permute-start | bytes 786440 | tf_op jit(solution)/shard_map/ppermute | solution.py:126
  50.8 15.7 %copy-start = (bf16[256,2048]{1,0:T(8,128)(2,1)}, bf16[256,2048]{1,0:T(8,128)(2,1)S(1)}, u32[]{:S(2)}) copy-start(bf16[256,2048]{1,0:T(8,128)(2,1)S(1)} %collective-permute-done.4.refs_1_) | copy-start | bytes 3145732
  51.8 16.8 %collective-permute-start.6 = (bf16[128,2048]{1,0:T(8,128)(2,1)}, bf16[128,2048]{1,0:T(8,128)(2,1)S(1)}, u32[]{:S(2)}, u32[]{:S(2)}) collective-permute-start(bf16[128,2048]{1,0:T(8,128)(2,1)} %slice.68), channel_id=1, source_target_pairs={{0,128},{128,256},{256,384},{384,0},{1,129},{129,257},{257,385},{3... | collective-permute-start | bytes 1572872 | tf_op jit(solution)/shard_map/ppermute | solution.py:129
  53.7 20.8 %copy-start.1 = (bf16[256,2048]{1,0:T(8,128)(2,1)}, bf16[256,2048]{1,0:T(8,128)(2,1)S(1)}, u32[]{:S(2)}) copy-start(bf16[256,2048]{1,0:T(8,128)(2,1)S(1)} %collective-permute-done.5.refs_2_) | copy-start | bytes 3145732
  54.6 16.7 %collective-permute-start.7 = (bf16[128,2048]{1,0:T(8,128)(2,1)}, bf16[128,2048]{1,0:T(8,128)(2,1)}, u32[]{:S(2)}, u32[]{:S(2)}) collective-permute-start(bf16[128,2048]{1,0:T(8,128)(2,1)} %slice.69), channel_id=1, source_target_pairs={{0,384},{128,0},{256,128},{384,256},{1,385},{129,1},{257,129},{385... | collective-permute-start | bytes 1572872 | tf_op jit(solution)/shard_map/ppermute | solution.py:130
  59.2 20.3 %collective-permute-start.8 = (bf16[256,2048]{1,0:T(8,128)(2,1)}, bf16[256,2048]{1,0:T(8,128)(2,1)}, u32[]{:S(2)}, u32[]{:S(2)}) collective-permute-start(bf16[256,2048]{1,0:T(8,128)(2,1)} %bitcast.23.refs_0_), channel_id=1, source_target_pairs={{0,64},{64,0},{1,65},{65,1},{2,66},{66,2},{3,67},{67,3},{4,68},{68... | collective-permute-start | bytes 3145736 | tf_op jit(solution)/shard_map/ppermute | solution.py:91
  61.7 27.2 %collective-permute-start.10 = (bf16[256,2048]{1,0:T(8,128)(2,1)S(1)}, bf16[256,2048]{1,0:T(8,128)(2,1)}, u32[]{:S(2)}, u32[]{:S(2)}) collective-permute-start(bf16[256,2048]{1,0:T(8,128)(2,1)S(1)} %collective-permute-done.5.refs_2_), channel_id=1, source_target_pairs={{0,64},{64,0},{1,65},{65,1},{2,66},{66,2},{3,67},{67,3},{4,68},{68... | collective-permute-start | bytes 3145736 | tf_op jit(solution)/shard_map/ppermute | solution.py:132
  63.6 2.4 %copy-start.6 = (bf16[1024,128]{1,0:T(8,128)(2,1)}, bf16[1024,128]{1,0:T(8,128)(2,1)S(1)}, u32[]{:S(2)}) copy-start(bf16[1024,128]{1,0:T(8,128)(2,1)S(1)} %collective-permute-done.3.h1_ref) | copy-start | bytes 786436
  63.7 25.3 %collective-permute-start.9 = (bf16[256,2048]{1,0:T(8,128)(2,1)S(1)}, bf16[256,2048]{1,0:T(8,128)(2,1)}, u32[]{:S(2)}, u32[]{:S(2)}) collective-permute-start(bf16[256,2048]{1,0:T(8,128)(2,1)S(1)} %collective-permute-done.4.refs_1_), channel_id=1, source_target_pairs={{0,64},{64,0},{1,65},{65,1},{2,66},{66,2},{3,67},{67,3},{4,68},{68... | collective-permute-start | bytes 3145736 | tf_op jit(solution)/shard_map/ppermute | solution.py:131
  68.6 20.4 %copy-start.4 = (bf16[128,2048]{1,0:T(8,128)(2,1)}, bf16[128,2048]{1,0:T(8,128)(2,1)S(1)}, u32[]{:S(2)}) copy-start(bf16[128,2048]{1,0:T(8,128)(2,1)S(1)} %collective-permute-done.6.refs_3_) | copy-start | bytes 1572868
  68.6 20.3 %collective-permute-start.11 = (bf16[128,2048]{1,0:T(8,128)(2,1)S(1)}, bf16[128,2048]{1,0:T(8,128)(2,1)}, u32[]{:S(2)}, u32[]{:S(2)}) collective-permute-start(bf16[128,2048]{1,0:T(8,128)(2,1)S(1)} %collective-permute-done.6.refs_3_), channel_id=1, source_target_pairs={{0,64},{64,0},{1,65},{65,1},{2,66},{66,2},{3,67},{67,3},{4,68},{68... | collective-permute-start | bytes 1572872 | tf_op jit(solution)/shard_map/ppermute | solution.py:133
  71.4 17.6 %collective-permute-start.12 = (bf16[128,2048]{1,0:T(8,128)(2,1)}, bf16[128,2048]{1,0:T(8,128)(2,1)}, u32[]{:S(2)}, u32[]{:S(2)}) collective-permute-start(bf16[128,2048]{1,0:T(8,128)(2,1)} %collective-permute-done.7.refs_4_), channel_id=1, source_target_pairs={{0,64},{64,0},{1,65},{65,1},{2,66},{66,2},{3,67},{67,3},{4,68},{68... | collective-permute-start | bytes 1572872 | tf_op jit(solution)/shard_map/ppermute | solution.py:134
  74.5 14.4 %all-to-all-start.1 = ((bf16[8,256,128]{2,1,0:T(8,128)(2,1)}), bf16[8,256,128]{2,1,0:T(8,128)(2,1)S(1)}, u32[]{:S(2)}, u32[]{:S(2)}) async-start(bf16[8,256,128]{2,1,0:T(8,128)(2,1)} %bitcast.9), calls=%async_computation.1 | async-start | bytes 1048576 | tf_op jit(solution)/shard_map/all_to_all | solution.py:146
  88.9 0.8 copy-start.2
  97.5 27.8 %copy-start.10 = (s32[64]{0:T(128)S(1)}, s32[64]{0:T(128)}, u32[]{:S(2)}) copy-start(s32[64]{0:T(128)} %param.13) | copy-start | bytes 772
  97.5 28.1 %copy-start.11 = (s32[64]{0:T(128)S(1)}, s32[64]{0:T(128)}, u32[]{:S(2)}) copy-start(s32[64]{0:T(128)} %param.14) | copy-start | bytes 772
  97.5 28.4 %copy-start.9 = (s32[8,64]{1,0:T(8,128)S(1)}, s32[8,64]{1,0:T(8,128)}, u32[]{:S(2)}) copy-start(s32[8,64]{1,0:T(8,128)} %param.12) | copy-start | bytes 6148
  114.0 33.8 %all-to-all-start.3 = ((f32[16,64,128]{2,1,0:T(8,128)}), f32[16,64,128]{2,1,0:T(8,128)S(1)}, u32[]{:S(2)}, u32[]{:S(2)}) async-start(f32[16,64,128]{2,1,0:T(8,128)} %copy.52), calls=%async_computation.3 | async-start | bytes 1048576 | tf_op jit(solution)/shard_map/all_to_all | solution.py:163
  147.8 2.1 %copy-start.5 = (f32[16,4,512]{2,1,0:T(4,128)S(1)}, f32[16,4,512]{2,1,0:T(4,128)}, u32[]{:S(2)}) copy-start(f32[16,4,512]{2,1,0:T(4,128)} %param.15) | copy-start | bytes 393220
  147.9 2.1 %copy-start.7 = (f32[16,4,512]{2,1,0:T(4,128)S(1)}, f32[16,4,512]{2,1,0:T(4,128)}, u32[]{:S(2)}) copy-start(f32[16,4,512]{2,1,0:T(4,128)} %param.16) | copy-start | bytes 393220
  147.9 2.1 %copy-start.8 = (f32[16,4,512]{2,1,0:T(4,128)S(1)}, f32[16,4,512]{2,1,0:T(4,128)}, u32[]{:S(2)}) copy-start(f32[16,4,512]{2,1,0:T(4,128)} %param.17) | copy-start | bytes 393220
  191.4 12.0 %collective-permute-start.13 = (bf16[4,256,512]{2,1,0:T(8,128)(2,1)S(1)}, bf16[4,256,512]{2,1,0:T(8,128)(2,1)S(1)}, u32[]{:S(2)}, u32[]{:S(2)}) collective-permute-start(bf16[4,256,512]{2,1,0:T(8,128)(2,1)S(1)} %bitcast.79), channel_id=1, source_target_pairs={{0,64},{64,0},{1,65},{65,1},{2,66},{66,2},{3,67},{67,3},{4,68},{68... | collective-permute-start | bytes 3145736 | tf_op jit(solution)/shard_map/ppermute | solution.py:205

commit v2 on v1

v2 whole, which is shorter than its diff:
```python
import jax
import jax.numpy as jnp
from jax import lax
from jax.experimental import pallas as pl
from jax.experimental.pallas import tpu as pltpu
from jax.sharding import Mesh
from jax.sharding import PartitionSpec as P


decay_first = 0.9
decay_second = 0.95
learn_rate = 0.001
weight_decay = 0.1
epsilon = 1e-08
step_number = 20.0

Y, C, X, Z = 4, 2, 4, 16
PLACES = X * Z
UP = [(i, (i + 1) % Y) for i in range(Y)]
DOWN = [(i, (i - 1) % Y) for i in range(Y)]
ACROSS = [(i, (i + 2) % Y) for i in range(Y)]
SWAP = [(0, 1), (1, 0)]
VMEM = pl.BlockSpec(memory_space=pltpu.VMEM)
SMEM = pl.BlockSpec(memory_space=pltpu.SMEM)
ANY = pl.BlockSpec(memory_space=pl.ANY)


def grant(mib):
    return pltpu.CompilerParams(vmem_limit_bytes=mib << 20)


def lower_half(x):
    return lax.broadcasted_iota(jnp.int32, x.shape, x.ndim - 1) < x.shape[-1] // 2


def swapped(x):
    return pltpu.roll(x, x.shape[-1] // 2, x.ndim - 1)


def split_cols(*refs):
    ins, out = refs[:-1], refs[-1]
    lanes = out.shape[-1]
    half = ins[0].shape[-1] // 2
    for n, x in enumerate(ins):
        for pair in range(Y // 2):
            gate = x[:, :, pair * lanes : (pair + 1) * lanes]
            up = x[:, :, half + pair * lanes : half + (pair + 1) * lanes]
            low = lower_half(gate)
            out[2 * pair, n] = jnp.where(low, gate, swapped(up))
            out[2 * pair + 1, n] = jnp.where(low, swapped(gate), up)


def join_cols(y_ref, own, low, high, far, *refs):
    outs, parts = refs[:-1], refs[-1]
    y = y_ref[0]
    parts[y] = own[...]
    parts[(y + 3) % Y] = low[...]
    parts[(y + 1) % Y] = high[...]
    parts[(y + 2) % Y] = far[...]
    lanes = own.shape[-1]
    half = outs[0].shape[-1] // 2
    for n, out in enumerate(outs):
        for pair in range(Y // 2):
            a, b = parts[2 * pair, n], parts[2 * pair + 1, n]
            first = lower_half(a)
            out[:, :, pair * lanes : (pair + 1) * lanes] = jnp.where(first, a, swapped(b))
            out[:, :, half + pair * lanes : half + (pair + 1) * lanes] = jnp.where(
                first, swapped(a), b
            )


def pick_old(slots, state, out, table):
    for e in range(table.shape[0]):
        table[e] = jnp.concatenate([state[y, 0, e] for y in range(Y)], axis=0).astype(jnp.bfloat16)
    for p in range(PLACES):
        out[p] = table[slots[p]]


def adam(old, new, total, got, state, out, after, acc, table):
    experts = acc.shape[0]
    rows = state.shape[3]
    acc[...] = jnp.zeros_like(acc)
    for p in range(PLACES):
        acc[old[p]] += got[p]
    for e in range(experts):
        master, first, second = (
            jnp.concatenate([state[y, n, e] for y in range(Y)], axis=0) for n in range(3)
        )
        grad = acc[e] / total[e]
        new_first = decay_first * first + (1.0 - decay_first) * grad
        new_second = decay_second * second + (1.0 - decay_second) * grad * grad
        first_hat = new_first / (1.0 - decay_first**step_number)
        second_hat = new_second / (1.0 - decay_second**step_number)
        new_master = master - learn_rate * (
            first_hat / (jnp.sqrt(second_hat) + epsilon) + weight_decay * master
        )
        table[e] = new_master.astype(jnp.bfloat16)
        for n, value in enumerate((new_master, new_first, new_second)):
            for y in range(Y):
                after[y, n, e] = value[y * rows : (y + 1) * rows]
    for p in range(PLACES):
        out[p] = table[new[p]]


def group_grad(core_ref, mine, theirs, h0_ref, h1_ref, *refs):
    chunks, (out_ref, tok, w_ref, local_ref, sems) = refs[:-5], refs[-5:]
    starts, row = [], 0
    copies = []
    for k, chunk in enumerate(chunks):
        rows = chunk.shape[0]
        copy = pltpu.make_async_copy(chunk, tok.at[pl.ds(row, rows)], sems.at[k])
        copy.start()
        copies.append(copy)
        starts.append((row, rows))
        row += rows
    core = core_ref[0]
    wide = mine.shape[1]
    for y in range(Y):
        w_ref[pl.ds(pl.multiple_of((2 * y + core) * wide, wide), wide), :] = mine[y]
        w_ref[pl.ds(pl.multiple_of((2 * y + 1 - core) * wide, wide), wide), :] = theirs[y]
    for k, (row, rows) in enumerate(starts):
        copies[k].wait()
        h_ref = h0_ref if k < len(chunks) // 2 else h1_ref
        at = row % h_ref.shape[0]
        both = jnp.dot(
            tok[row : row + rows, :], w_ref[...], preferred_element_type=jnp.float32
        )
        other = swapped(both)
        first = lower_half(both)
        gate = jnp.where(first, both, other)
        sigma = jax.nn.sigmoid(gate)
        active = gate * sigma
        slope = sigma * (1.0 + gate * (1.0 - sigma))
        incoming = h_ref[at : at + rows, :].astype(jnp.float32)
        local = jnp.where(first, incoming * other * slope, incoming * active)
        local_ref[:, row : row + rows] = local.T.astype(jnp.bfloat16)
    for y in range(Y):
        at = pl.multiple_of((2 * y + core) * wide, wide)
        total = jnp.dot(
            local_ref[...], tok[:, pl.ds(at, wide)], preferred_element_type=jnp.float32
        )
        out_ref[:, 4 * y : 4 * y + 4, :] = total.T.reshape(wide // 4, 4, -1)


def join_weights(core_ref, mine, theirs, out):
    core = core_ref[0]
    lanes = mine.shape[-1]
    half = out.shape[-1] // 2
    for which, source in ((core, mine), (1 - core, theirs)):
        for pair in range(Y // 2):
            a = source[2 * pair, 0].astype(jnp.float32)
            b = source[2 * pair + 1, 0].astype(jnp.float32)
            first = lower_half(a)
            out[0, which, :, pair * lanes : (pair + 1) * lanes] = jnp.where(
                first, a, swapped(b)
            ).astype(jnp.bfloat16)
            out[0, which, :, half + pair * lanes : half + (pair + 1) * lanes] = jnp.where(
                first, swapped(a), b
            ).astype(jnp.bfloat16)


def shards(
    tokens, hidden_grad, routing, row_count, old_slots, new_slots, master, first_moment, second_moment
):
    y, core = lax.axis_index("y"), lax.axis_index("core")
    group_here = y * C + core
    place_here = lax.axis_index("x") * Z + lax.axis_index("z")
    experts, rows_shard, width = master.shape
    hid = width // 2
    part = hid // Y
    lanes = 2 * part
    f32, bf16 = jnp.float32, jnp.bfloat16
    core_id = core.astype(jnp.int32).reshape(1)
    y_id = y.astype(jnp.int32).reshape(1)

    own = tokens[0, 0]
    rows = own.shape[0]
    low = lax.ppermute(own, "y", UP)
    high = lax.ppermute(own, "y", DOWN)
    own_c = lax.ppermute(own, "core", SWAP)

    columns = pl.pallas_call(
        split_cols,
        out_shape=jax.ShapeDtypeStruct((Y, 3, experts, rows_shard, lanes), f32),
        in_specs=[VMEM] * 3,
        out_specs=VMEM,
        compiler_params=grant(4),
        name="split_cols",
    )(master, first_moment, second_moment)
    state = lax.all_to_all(
        columns.reshape(Y, 3 * experts, rows_shard, lanes), "y", 0, 0, tiled=True
    ).reshape(Y, 3, experts, rows_shard, lanes)
    picked = pl.pallas_call(
        pick_old,
        out_shape=jax.ShapeDtypeStruct((PLACES, Y * rows_shard, lanes), bf16),
        in_specs=[SMEM, VMEM],
        out_specs=VMEM,
        scratch_shapes=[pltpu.VMEM((experts, Y * rows_shard, lanes), bf16)],
        compiler_params=grant(4),
        name="pick_old",
    )(old_slots, state)
    landed = lax.all_to_all(picked, ("x", "z"), 0, 0, tiled=True)

    def by_rows(x):
        return (
            x.reshape(PLACES, Y, rows_shard, lanes)
            .transpose(1, 0, 2, 3)
            .reshape(Y, PLACES * rows_shard, lanes)
        )

    w_mine = by_rows(landed)
    w_theirs = lax.ppermute(w_mine, "core", SWAP)

    order = routing[0, 0]
    batches, batch_rows = order.shape
    count = row_count[group_here, place_here]
    live = jnp.arange(rows, dtype=jnp.int32) < count
    masked = jnp.where(live[:, None], hidden_grad[0, 0], jnp.zeros((), bf16))
    slot_of = (
        order[:, None, :] == jnp.arange(batch_rows, dtype=jnp.int32)[None, :, None]
    ).astype(bf16)
    moved = lax.dot_general(
        slot_of,
        masked.reshape(batches, batch_rows, hid),
        (((2,), (1,)), ((0,), (0,))),
        preferred_element_type=f32,
    ).astype(bf16).reshape(rows, hid)
    slices = [moved[:, k * part : (k + 1) * part] for k in range(Y)]
    by_chip = jnp.stack([jnp.concatenate([s, s], axis=1) for s in slices])

    def for_chip(step, x=by_chip):
        return lax.dynamic_index_in_dim(x, (y + step) % Y, keepdims=False)

    h_low = lax.ppermute(for_chip(1), "y", UP)
    h_high = lax.ppermute(for_chip(3), "y", DOWN)
    h_far = lax.ppermute(for_chip(2), "y", ACROSS)
    h_own = jnp.concatenate([for_chip(0), h_low, h_high, h_far], axis=0)
    h_own_c = lax.ppermute(h_own, "core", SWAP)

    half_rows = rows // 2
    far_a = lax.ppermute(low[:half_rows], "y", UP)
    far_b = lax.ppermute(high[half_rows:], "y", DOWN)
    low_c = lax.ppermute(low, "core", SWAP)
    high_c = lax.ppermute(high, "core", SWAP)
    far_a_c = lax.ppermute(far_a, "core", SWAP)
    far_b_c = lax.ppermute(far_b, "core", SWAP)

    chunks = [own, low, high, far_a, far_b, own_c, low_c, high_c, far_a_c, far_b_c]
    group_rows = sum(c.shape[0] for c in chunks)
    deep = own.shape[1]
    summed = pl.pallas_call(
        group_grad,
        out_shape=jax.ShapeDtypeStruct((PLACES, Y * rows_shard, lanes), f32),
        in_specs=[SMEM] + [VMEM] * 4 + [ANY] * len(chunks),
        out_specs=VMEM,
        scratch_shapes=[
            pltpu.VMEM((group_rows, deep), bf16),
            pltpu.VMEM((deep, lanes), bf16),
            pltpu.VMEM((lanes, group_rows), bf16),
            pltpu.SemaphoreType.DMA((len(chunks),)),
        ],
        compiler_params=grant(24),
        name="group_grad",
    )(core_id, w_mine, w_theirs, h_own, h_own_c, *chunks)

    got = lax.all_to_all(summed, ("x", "z"), 0, 0, tiled=True)
    select = (old_slots[:, None] == jnp.arange(experts, dtype=jnp.int32)[None, :]).astype(f32)
    per_slot = jnp.sum(row_count.astype(f32), axis=0)
    total = jnp.dot(per_slot, select, precision=lax.Precision.HIGHEST)
    picked, after = pl.pallas_call(
        adam,
        out_shape=(
            jax.ShapeDtypeStruct((PLACES, Y * rows_shard, lanes), bf16),
            jax.ShapeDtypeStruct((Y, 3, experts, rows_shard, lanes), f32),
        ),
        in_specs=[SMEM] * 3 + [VMEM] * 2,
        out_specs=(VMEM, VMEM),
        scratch_shapes=[
            pltpu.VMEM((experts, Y * rows_shard, lanes), f32),
            pltpu.VMEM((experts, Y * rows_shard, lanes), bf16),
        ],
        compiler_params=grant(6),
        name="adam",
    )(old_slots, new_slots, total, got, state)
    landed = lax.all_to_all(picked, ("x", "z"), 0, 0, tiled=True)

    s_low = lax.ppermute(for_chip(1, after), "y", UP)
    s_high = lax.ppermute(for_chip(3, after), "y", DOWN)
    s_far = lax.ppermute(for_chip(2, after), "y", ACROSS)
    whole = jax.ShapeDtypeStruct((experts, rows_shard, width), f32)
    new_master, new_first, new_second = pl.pallas_call(
        join_cols,
        out_shape=(whole,) * 3,
        in_specs=[SMEM] + [VMEM] * 4,
        out_specs=(VMEM,) * 3,
        scratch_shapes=[pltpu.VMEM((Y, 3, experts, rows_shard, lanes), f32)],
        compiler_params=grant(6),
        name="join_cols",
    )(y_id, for_chip(0, after), s_low, s_high, s_far)

    landed = by_rows(landed)
    copies = jnp.broadcast_to(landed[None], (Y, *landed.shape))
    mine = lax.all_to_all(copies, "y", 0, 0, tiled=True)
    theirs = lax.ppermute(mine, "core", SWAP)
    block = pl.BlockSpec((Y, 1, PLACES * rows_shard, lanes), lambda i: (0, i, 0, 0))
    new_weights = pl.pallas_call(
        join_weights,
        grid=(Y,),
        out_shape=jax.ShapeDtypeStruct((Y, C, PLACES * rows_shard, width), bf16),
        in_specs=[SMEM, block, block],
        out_specs=pl.BlockSpec((1, C, PLACES * rows_shard, width), lambda i: (i, 0, 0, 0)),
        compiler_params=grant(8),
        name="join_weights",
    )(core_id, mine, theirs)
    return (new_weights.reshape(1, -1, width), new_master, new_first, new_second)


def solution(mesh):
    fine = Mesh(mesh.devices.reshape(Y, C, X, Z), ("y", "core", "x", "z"))
    dp, place = ("y", "core"), ("x", "z")
    placed = (
        P(dp, place, None, None),
        P(dp, place, None, None),
        P(dp, place, None, None),
        P(),
        P(),
        P(),
        P(None, dp + place, None),
        P(None, dp + place, None),
        P(None, dp + place, None),
    )

    return jax.shard_map(
        shards,
        mesh=fine,
        in_specs=placed,
        out_specs=(
            P(place, None, None),
            P(None, dp + place, None),
            P(None, dp + place, None),
            P(None, dp + place, None),
        ),
        check_vma=False,
    )
```

time: 208 us -> 209 us (level)
  starting transfers between devices: 83.7 us -> 99.6 us
  blocking collectives: 55.7 us -> 40.9 us
  Pallas kernels: 7.76 us -> 14.1 us
  local copies, waits for them, and re-layouts: 11.2 us -> 6.29 us
  waiting for transfers between devices: 37.5 us -> 42.3 us
  matrix products: 3.88 us -> 1.36 us
  other arithmetic: 4.01 us -> 1.66 us
    all_to_all x3 -> x2, blocking collectives: 55.7 us -> 40.9 us  [the longest x1 26.5 us: shards(): landed = lax.all_to_all(picked, ('x', 'z'), 0, 0, tiled=True)]
    ppermute x0 -> x4, starting transfers between devices: none -> 10.3 us  [the longest x1 4.3 us: shards(): s_high = lax.ppermute(for_chip(3, after), 'y', DOWN)]
    ppermute x1, starting transfers between devices: 2.48 us -> 9.54 us  [shards(): own_c = lax.ppermute(own, 'core', SWAP)]
    ppermute x0 -> x4, waiting for transfers between devices: none -> 6.73 us  [the longest x1 5.23 us: shards(): s_far = lax.ppermute(for_chip(2, after), 'y', ACROSS)]
    pallas_call x1 -> x6, Pallas kernels: 7.76 us -> 14.1 us  [the longest x1 8.06 us: shards(): pl.pallas_call(group_grad, out_shape=jax.ShapeDtypeStruct((PLACES, Y * ro...]
    ppermute x1, waiting for transfers between devices: 4.45 us -> 0.01 us  [shards(): h_far = lax.ppermute(for_chip(2), 'y', ACROSS)]
    ppermute x1, waiting for transfers between devices: 2.01 us -> 5.68 us  [shards(): far_a = lax.ppermute(low[:half_rows], 'y', UP)]
    ppermute x1, starting transfers between devices: 9.77 us -> 6.48 us  [shards(): theirs = lax.ppermute(mine, 'core', SWAP)]
  transfers between devices with their start and end apart: 17 -> 21, of which waited for: 4 -> 4; matrix products, arithmetic and copies ran while one was open for 6% -> 3% of each run, Pallas kernels for 0% -> 1%
where the time goes in v2:
time: 209 us; the launch traced here: 207 us
  starting transfers between devices  99.6 us (48%)
  waiting for transfers between devices  42.3 us (20%)
  blocking collectives  40.9 us (20%)
  Pallas kernels  14.1 us (7%)
  local copies, waits for them, and re-layouts  6.29 us (3%)
    all_to_all x1, waiting for transfers between devices, shards(): got = lax.all_to_all(summed, ('x', 'z'), 0, 0, tiled=True)  29.9 us
    all_to_all x1, blocking collectives, shards(): landed = lax.all_to_all(picked, ('x', 'z'), 0, 0, tiled=True)  26.5 us
    all_to_all x1, starting transfers between devices, shards(): landed = lax.all_to_all(picked, ('x', 'z'), 0, 0, tiled=True)  17 us
    all_to_all x1, starting transfers between devices, shards(): got = lax.all_to_all(summed, ('x', 'z'), 0, 0, tiled=True)  14.5 us
    all_to_all x1, blocking collectives, shards(): mine = lax.all_to_all(copies, 'y', 0, 0, tiled=True)  14.4 us
    ppermute x1, starting transfers between devices, shards(): own_c = lax.ppermute(own, 'core', SWAP)  9.54 us
    pallas_call x1, Pallas kernels, shards(): pl.pallas_call(group_grad, out_shape=jax.ShapeDtypeStruct((PLACES, Y * ro...  8.06 us
    ppermute x1, starting transfers between devices, shards(): theirs = lax.ppermute(mine, 'core', SWAP)  6.48 us
  transfers between devices with their start and end apart: 21, of which 4 were waited for; matrix products, arithmetic and copies ran while one was open for 3% of the time, Pallas kernels for 1%

profile of v2, /device:TPU:1, one launch (start us, length us, event | category | flops | bytes accessed | tf_op | source)
XLA Modules:
  0.0 207.4 jit_solution(4240731770542296584)
XLA Ops:
  0.6 4.2 %collective-permute-start.5 = (bf16[256,2048]{1,0:T(8,128)(2,1)}, bf16[256,2048]{1,0:T(8,128)(2,1)S(1)}, u32[]{:S(2)}, u32[]{:S(2)}) collective-permute-start(bf16[256,2048]{1,0:T(8,128)(2,1)} %bitcast.49), channel_id=1, source_target_pairs={{0,128},{128,256},{256,384},{384,0},{1,129},{129,257},{257,385},{3... | collective-permute-start | bytes 3145736 | tf_op jit(solution)/shard_map/ppermute | solution.py:178
  4.8 3.4 %collective-permute-start.6 = (bf16[256,2048]{1,0:T(8,128)(2,1)}, bf16[256,2048]{1,0:T(8,128)(2,1)S(1)}, u32[]{:S(2)}, u32[]{:S(2)}) collective-permute-start(bf16[256,2048]{1,0:T(8,128)(2,1)} %bitcast.50), channel_id=1, source_target_pairs={{0,384},{128,0},{256,128},{384,256},{1,385},{129,1},{257,129},{385... | collective-permute-start | bytes 3145736 | tf_op jit(solution)/shard_map/ppermute | solution.py:179
  11.9 3.6 %all-to-all-start = ((f32[4,48,4,128]{3,2,1,0:T(4,128)}), f32[4,48,4,128]{3,2,1,0:T(4,128)S(1)}, u32[]{:S(2)}, u32[]{:S(2)}) async-start(f32[4,48,4,128]{3,2,1,0:T(4,128)} %bitcast.3), calls=%async_computation | async-start | bytes 786432 | tf_op jit(solution)/shard_map/all_to_all | solution.py:190
  15.6 1.3 dynamic_slice.29
  17.5 1.2 convolution_convert_fusion
  19.1 3.3 %collective-permute-start.1 = (bf16[256,128]{1,0:T(8,128)(2,1)S(1)}, bf16[256,128]{1,0:T(8,128)(2,1)S(1)}, u32[]{:S(2)}, u32[]{:S(2)}) collective-permute-start(bf16[256,128]{1,0:T(8,128)(2,1)S(1)} %get-tuple-element.21), channel_id=1, source_target_pairs={{0,128},{128,256},{256,384},{384,0},{1,129},{129,257},{257,385},{3... | collective-permute-start | bytes 196616 | tf_op jit(solution)/shard_map/ppermute | solution.py:234
  22.4 3.2 %collective-permute-start.2 = (bf16[256,128]{1,0:T(8,128)(2,1)S(1)}, bf16[256,128]{1,0:T(8,128)(2,1)S(1)}, u32[]{:S(2)}, u32[]{:S(2)}) collective-permute-start(bf16[256,128]{1,0:T(8,128)(2,1)S(1)} %get-tuple-element.20), channel_id=1, source_target_pairs={{0,384},{128,0},{256,128},{384,256},{1,385},{129,1},{257,129},{385... | collective-permute-start | bytes 196616 | tf_op jit(solution)/shard_map/ppermute | solution.py:235
  25.6 3.6 %collective-permute-start.3 = (bf16[256,128]{1,0:T(8,128)(2,1)S(1)}, bf16[256,128]{1,0:T(8,128)(2,1)S(1)}, u32[]{:S(2)}, u32[]{:S(2)}) collective-permute-start(bf16[256,128]{1,0:T(8,128)(2,1)S(1)} %get-tuple-element.19), channel_id=1, source_target_pairs={{0,256},{128,384},{256,0},{384,128},{1,257},{129,385},{257,1},{385... | collective-permute-start | bytes 196616 | tf_op jit(solution)/shard_map/ppermute | solution.py:236
  29.2 9.5 %collective-permute-start.9 = (bf16[256,2048]{1,0:T(8,128)(2,1)S(1)}, bf16[256,2048]{1,0:T(8,128)(2,1)}, u32[]{:S(2)}, u32[]{:S(2)}) collective-permute-start(bf16[256,2048]{1,0:T(8,128)(2,1)S(1)} %bitcast.51), channel_id=1, source_target_pairs={{0,64},{64,0},{1,65},{65,1},{2,66},{66,2},{3,67},{67,3},{4,68},{68... | collective-permute-start | bytes 3145736 | tf_op jit(solution)/shard_map/ppermute | solution.py:180
  39.5 3.5 %collective-permute-start.4 = (bf16[1024,128]{1,0:T(8,128)(2,1)}, bf16[1024,128]{1,0:T(8,128)(2,1)}, u32[]{:S(2)}, u32[]{:S(2)}) collective-permute-start(bf16[1024,128]{1,0:T(8,128)(2,1)} %pad_maximum_fusion.1.h0_ref), channel_id=1, source_target_pairs={{0,64},{64,0},{1,65},{65,1},{2,66},{66,2},{3,67},{67,3},{4,68},{68... | collective-permute-start | bytes 786440 | tf_op jit(solution)/shard_map/ppermute | solution.py:238
  44.3 17.0 %all-to-all-start.1 = ((bf16[64,16,128]{2,1,0:T(8,128)(2,1)}), bf16[64,16,128]{2,1,0:T(8,128)(2,1)}, u32[]{:S(2)}, u32[]{:S(2)}) async-start(bf16[64,16,128]{2,1,0:T(8,128)(2,1)} %copy-done.1), calls=%async_computation.1 | async-start | bytes 524288 | tf_op jit(solution)/shard_map/all_to_all | solution.py:202
  61.4 4.6 %collective-permute-start.7 = (bf16[128,2048]{1,0:T(8,128)(2,1)S(1)}, bf16[128,2048]{1,0:T(8,128)(2,1)}, u32[]{:S(2)}, u32[]{:S(2)}) collective-permute-start(bf16[128,2048]{1,0:T(8,128)(2,1)S(1)} %slice.28), channel_id=1, source_target_pairs={{0,128},{128,256},{256,384},{384,0},{1,129},{129,257},{257,385},{3... | collective-permute-start | bytes 1572872 | tf_op jit(solution)/shard_map/ppermute | solution.py:241
  66.1 2.6 %collective-permute-start.8 = (bf16[128,2048]{1,0:T(8,128)(2,1)S(1)}, bf16[128,2048]{1,0:T(8,128)(2,1)}, u32[]{:S(2)}, u32[]{:S(2)}) collective-permute-start(bf16[128,2048]{1,0:T(8,128)(2,1)S(1)} %slice.29), channel_id=1, source_target_pairs={{0,384},{128,0},{256,128},{384,256},{1,385},{129,1},{257,129},{385... | collective-permute-start | bytes 1572872 | tf_op jit(solution)/shard_map/ppermute | solution.py:242
  68.6 2.5 %collective-permute-start.10 = (bf16[256,2048]{1,0:T(8,128)(2,1)S(1)}, bf16[256,2048]{1,0:T(8,128)(2,1)}, u32[]{:S(2)}, u32[]{:S(2)}) collective-permute-start(bf16[256,2048]{1,0:T(8,128)(2,1)S(1)} %collective-permute-done.5.refs_1_), channel_id=1, source_target_pairs={{0,64},{64,0},{1,65},{65,1},{2,66},{66,2},{3,67},{67,3},{4,68},{68... | collective-permute-start | bytes 3145736 | tf_op jit(solution)/shard_map/ppermute | solution.py:243
  71.1 1.9 collective-permute-start.11
  73.1 5.7 %collective-permute-done.7.refs_3_ = bf16[128,2048]{1,0:T(8,128)(2,1)} collective-permute-done((bf16[128,2048]{1,0:T(8,128)(2,1)S(1)}, bf16[128,2048]{1,0:T(8,128)(2,1)}, u32[]{:S(2)}, u32[]{:S(2)}) %collective-permute-start.7) | collective-permute-done | bytes 524320 | tf_op jit(solution)/shard_map/ppermute | solution.py:241
  78.8 2.8 %collective-permute-start.12 = (bf16[128,2048]{1,0:T(8,128)(2,1)}, bf16[128,2048]{1,0:T(8,128)(2,1)}, u32[]{:S(2)}, u32[]{:S(2)}) collective-permute-start(bf16[128,2048]{1,0:T(8,128)(2,1)} %collective-permute-done.7.refs_3_), channel_id=1, source_target_pairs={{0,64},{64,0},{1,65},{65,1},{2,66},{66,2},{3,67},{67,3},{4,68},{68... | collective-permute-start | bytes 1572872 | tf_op jit(solution)/shard_map/ppermute | solution.py:245
  81.5 2.8 %collective-permute-start.13 = (bf16[128,2048]{1,0:T(8,128)(2,1)}, bf16[128,2048]{1,0:T(8,128)(2,1)}, u32[]{:S(2)}, u32[]{:S(2)}) collective-permute-start(bf16[128,2048]{1,0:T(8,128)(2,1)} %collective-permute-done.8.refs_4_), channel_id=1, source_target_pairs={{0,64},{64,0},{1,65},{65,1},{2,66},{66,2},{3,67},{67,3},{4,68},{68... | collective-permute-start | bytes 1572872 | tf_op jit(solution)/shard_map/ppermute | solution.py:246
  84.3 1.0 copy.13
  85.4 1.9 collective-permute-start
  87.3 1.5 collective-permute-done.theirs
  88.9 8.1 %group_grad.1 = f32[64,16,128]{2,1,0:T(8,128)} custom-call(s32[1]{0:T(128)} %bitcast.core_ref, bf16[4,256,128]{2,1,0:T(8,128)(2,1)S(1)} %bitcast.54, bf16[4,256,128]{2,1,0:T(8,128)(2,1)S(1)} %collective-permute-done.theirs, bf16[1024,128]{1,0:T(8,128)(2,1)} %pad_maximum_fusion.1.h0_ref, bf16[1024,128]{1,0:T(8,128)(2,1)} %collective-permute-done.4.h1_ref, ...), custom_call_target="tpu_custom_call" | custom-call | tf_op jit(solution)/shard_map/group_grad/pallas_call | solution.py:251
  96.9 14.5 %all-to-all-start.2 = ((f32[64,16,128]{2,1,0:T(8,128)}), f32[64,16,128]{2,1,0:T(8,128)S(1)}, u32[]{:S(2)}, u32[]{:S(2)}) async-start(f32[64,16,128]{2,1,0:T(8,128)} %group_grad.1), calls=%async_computation.2 | async-start | bytes 1048576 | tf_op jit(solution)/shard_map/all_to_all | solution.py:266
  111.7 29.9 %all-to-all-done.2.got = f32[64,16,128]{2,1,0:T(8,128)S(1)} async-done(((f32[64,16,128]{2,1,0:T(8,128)}), f32[64,16,128]{2,1,0:T(8,128)S(1)}, u32[]{:S(2)}, u32[]{:S(2)}) %all-to-all-start.2) | async-done | bytes 524320 | tf_op jit(solution)/shard_map/all_to_all | solution.py:266
  142.6 26.5 %all_to_all.25 = bf16[64,16,128]{2,1,0:T(8,128)(2,1)S(1)} all-to-all(bf16[64,16,128]{2,1,0:T(8,128)(2,1)S(1)} %get-tuple-element.9), channel_id=1, replica_groups=mesh['y'=4,'core'=2,'x'=4,'z'=16] {'x','z'}, dimensions={0} | all-to-all | bytes 524288 | tf_op jit(solution)/shard_map/all_to_all | solution.py:285
  169.4 14.4 %all_to_all.26.mine = bf16[4,4,256,128]{3,2,1,0:T(8,128)(2,1)S(1)} all-to-all(bf16[4,4,256,128]{3,2,1,0:T(8,128)(2,1)S(1)} %broadcast_in_dim.26), channel_id=1, replica_groups=mesh['y'=4,'core'=2,'x'=4,'z'=16] {'y'}, dimensions={0} | all-to-all | bytes 2097152 | tf_op jit(solution)/shard_map/all_to_all | solution.py:303
  183.8 6.5 %collective-permute-start.14 = (bf16[4,4,256,128]{3,2,1,0:T(8,128)(2,1)S(1)}, bf16[4,4,256,128]{3,2,1,0:T(8,128)(2,1)S(1)}, u32[]{:S(2)}, u32[]{:S(2)}) collective-permute-start(bf16[4,4,256,128]{3,2,1,0:T(8,128)(2,1)S(1)} %all_to_all.26.mine), channel_id=1, source_target_pairs={{0,64},{64,0},{1,65},{65,1},{2,66},{66,2},{3,67},{67,3},{4,68},{68... | collective-permute-start | bytes 3145736 | tf_op jit(solution)/shard_map/ppermute | solution.py:304
  190.3 2.2 %collective-permute-start.15 = (f32[3,16,4,128]{3,2,1,0:T(4,128)S(1)}, f32[3,16,4,128]{3,2,1,0:T(4,128)S(1)}, u32[]{:S(2)}, u32[]{:S(2)}) collective-permute-start(f32[3,16,4,128]{3,2,1,0:T(4,128)S(1)} %get-tuple-element.16), channel_id=1, source_target_pairs={{0,128},{128,256},{256,384},{384,0},{1,129},{129,257},{257,385},{3... | collective-permute-start | bytes 294920 | tf_op jit(solution)/shard_map/ppermute | solution.py:287
  192.5 4.3 %collective-permute-start.16 = (f32[3,16,4,128]{3,2,1,0:T(4,128)S(1)}, f32[3,16,4,128]{3,2,1,0:T(4,128)S(1)}, u32[]{:S(2)}, u32[]{:S(2)}) collective-permute-start(f32[3,16,4,128]{3,2,1,0:T(4,128)S(1)} %get-tuple-element.15), channel_id=1, source_target_pairs={{0,384},{128,0},{256,128},{384,256},{1,385},{129,1},{257,129},{385... | collective-permute-start | bytes 294920 | tf_op jit(solution)/shard_map/ppermute | solution.py:288
  196.9 1.9 collective-permute-start.17
  198.8 5.2 %collective-permute-done.17.far = f32[3,16,4,128]{3,2,1,0:T(4,128)S(1)} collective-permute-done((f32[3,16,4,128]{3,2,1,0:T(4,128)S(1)}, f32[3,16,4,128]{3,2,1,0:T(4,128)S(1)}, u32[]{:S(2)}, u32[]{:S(2)}) %collective-permute-start.17) | collective-permute-done | bytes 98336 | tf_op jit(solution)/shard_map/ppermute | solution.py:289
  205.0 2.4 %join_weights.1 = bf16[4,2,256,512]{3,2,1,0:T(8,128)(2,1)} custom-call(s32[1]{0:T(128)} %bitcast.core_ref, bf16[4,4,256,128]{3,2,1,0:T(8,128)(2,1)S(1)} %all_to_all.26.mine, bf16[4,4,256,128]{3,2,1,0:T(8,128)(2,1)S(1)} %collective-permute-done.14.theirs), custom_call_target="tpu_custom_call" | custom-call | tf_op jit(solution)/shard_map/join_weights/pallas_call | solution.py:306
  (51 shorter events, 9.5 us)
Async XLA Ops:
  0.6 28.6 %copy-start = (bf16[1,1,256,2048]{3,2,1,0:T(8,128)(2,1)S(1)}, bf16[1,1,256,2048]{3,2,1,0:T(8,128)(2,1)}, u32[]{:S(2)}) copy-start(bf16[1,1,256,2048]{3,2,1,0:T(8,128)(2,1)} %param.9) | copy-start | bytes 3145732
  0.6 60.7 %collective-permute-start.5 = (bf16[256,2048]{1,0:T(8,128)(2,1)}, bf16[256,2048]{1,0:T(8,128)(2,1)S(1)}, u32[]{:S(2)}, u32[]{:S(2)}) collective-permute-start(bf16[256,2048]{1,0:T(8,128)(2,1)} %bitcast.49), channel_id=1, source_target_pairs={{0,128},{128,256},{256,384},{384,0},{1,129},{129,257},{257,385},{3... | collective-permute-start | bytes 3145736 | tf_op jit(solution)/shard_map/ppermute | solution.py:178
  4.8 61.2 %collective-permute-start.6 = (bf16[256,2048]{1,0:T(8,128)(2,1)}, bf16[256,2048]{1,0:T(8,128)(2,1)S(1)}, u32[]{:S(2)}, u32[]{:S(2)}) collective-permute-start(bf16[256,2048]{1,0:T(8,128)(2,1)} %bitcast.50), channel_id=1, source_target_pairs={{0,384},{128,0},{256,128},{384,256},{1,385},{129,1},{257,129},{385... | collective-permute-start | bytes 3145736 | tf_op jit(solution)/shard_map/ppermute | solution.py:179
  8.2 0.9 copy-start.2
  9.1 0.9 copy-start.3
  10.0 0.9 copy-start.4
  11.9 31.1 %copy-start.5 = (s32[64]{0:T(128)S(1)}, s32[64]{0:T(128)}, u32[]{:S(2)}) copy-start(s32[64]{0:T(128)} %old.1) | copy-start | bytes 772
  11.9 31.1 %all-to-all-start = ((f32[4,48,4,128]{3,2,1,0:T(4,128)}), f32[4,48,4,128]{3,2,1,0:T(4,128)S(1)}, u32[]{:S(2)}, u32[]{:S(2)}) async-start(f32[4,48,4,128]{3,2,1,0:T(4,128)} %bitcast.3), calls=%async_computation | async-start | bytes 786432 | tf_op jit(solution)/shard_map/all_to_all | solution.py:190
  19.1 10.1 %collective-permute-start.1 = (bf16[256,128]{1,0:T(8,128)(2,1)S(1)}, bf16[256,128]{1,0:T(8,128)(2,1)S(1)}, u32[]{:S(2)}, u32[]{:S(2)}) collective-permute-start(bf16[256,128]{1,0:T(8,128)(2,1)S(1)} %get-tuple-element.21), channel_id=1, source_target_pairs={{0,128},{128,256},{256,384},{384,0},{1,129},{129,257},{257,385},{3... | collective-permute-start | bytes 196616 | tf_op jit(solution)/shard_map/ppermute | solution.py:234
  22.4 16.4 %collective-permute-start.2 = (bf16[256,128]{1,0:T(8,128)(2,1)S(1)}, bf16[256,128]{1,0:T(8,128)(2,1)S(1)}, u32[]{:S(2)}, u32[]{:S(2)}) collective-permute-start(bf16[256,128]{1,0:T(8,128)(2,1)S(1)} %get-tuple-element.20), channel_id=1, source_target_pairs={{0,384},{128,0},{256,128},{384,256},{1,385},{129,1},{257,129},{385... | collective-permute-start | bytes 196616 | tf_op jit(solution)/shard_map/ppermute | solution.py:235
  25.6 13.2 %collective-permute-start.3 = (bf16[256,128]{1,0:T(8,128)(2,1)S(1)}, bf16[256,128]{1,0:T(8,128)(2,1)S(1)}, u32[]{:S(2)}, u32[]{:S(2)}) collective-permute-start(bf16[256,128]{1,0:T(8,128)(2,1)S(1)} %get-tuple-element.19), channel_id=1, source_target_pairs={{0,256},{128,384},{256,0},{384,128},{1,257},{129,385},{257,1},{385... | collective-permute-start | bytes 196616 | tf_op jit(solution)/shard_map/ppermute | solution.py:236
  29.2 56.1 %collective-permute-start.9 = (bf16[256,2048]{1,0:T(8,128)(2,1)S(1)}, bf16[256,2048]{1,0:T(8,128)(2,1)}, u32[]{:S(2)}, u32[]{:S(2)}) collective-permute-start(bf16[256,2048]{1,0:T(8,128)(2,1)S(1)} %bitcast.51), channel_id=1, source_target_pairs={{0,64},{64,0},{1,65},{65,1},{2,66},{66,2},{3,67},{67,3},{4,68},{68... | collective-permute-start | bytes 3145736 | tf_op jit(solution)/shard_map/ppermute | solution.py:180
  39.5 31.6 %collective-permute-start.4 = (bf16[1024,128]{1,0:T(8,128)(2,1)}, bf16[1024,128]{1,0:T(8,128)(2,1)}, u32[]{:S(2)}, u32[]{:S(2)}) collective-permute-start(bf16[1024,128]{1,0:T(8,128)(2,1)} %pad_maximum_fusion.1.h0_ref), channel_id=1, source_target_pairs={{0,64},{64,0},{1,65},{65,1},{2,66},{66,2},{3,67},{67,3},{4,68},{68... | collective-permute-start | bytes 786440 | tf_op jit(solution)/shard_map/ppermute | solution.py:238
  43.6 0.7 copy-start.1
  44.3 40.0 %all-to-all-start.1 = ((bf16[64,16,128]{2,1,0:T(8,128)(2,1)}), bf16[64,16,128]{2,1,0:T(8,128)(2,1)}, u32[]{:S(2)}, u32[]{:S(2)}) async-start(bf16[64,16,128]{2,1,0:T(8,128)(2,1)} %copy-done.1), calls=%async_computation.1 | async-start | bytes 524288 | tf_op jit(solution)/shard_map/all_to_all | solution.py:202
  61.4 17.3 %collective-permute-start.7 = (bf16[128,2048]{1,0:T(8,128)(2,1)S(1)}, bf16[128,2048]{1,0:T(8,128)(2,1)}, u32[]{:S(2)}, u32[]{:S(2)}) collective-permute-start(bf16[128,2048]{1,0:T(8,128)(2,1)S(1)} %slice.28), channel_id=1, source_target_pairs={{0,128},{128,256},{256,384},{384,0},{1,129},{129,257},{257,385},{3... | collective-permute-start | bytes 1572872 | tf_op jit(solution)/shard_map/ppermute | solution.py:241
  66.1 15.5 %collective-permute-start.8 = (bf16[128,2048]{1,0:T(8,128)(2,1)S(1)}, bf16[128,2048]{1,0:T(8,128)(2,1)}, u32[]{:S(2)}, u32[]{:S(2)}) collective-permute-start(bf16[128,2048]{1,0:T(8,128)(2,1)S(1)} %slice.29), channel_id=1, source_target_pairs={{0,384},{128,0},{256,128},{384,256},{1,385},{129,1},{257,129},{385... | collective-permute-start | bytes 1572872 | tf_op jit(solution)/shard_map/ppermute | solution.py:242
  68.6 20.2 %collective-permute-start.10 = (bf16[256,2048]{1,0:T(8,128)(2,1)S(1)}, bf16[256,2048]{1,0:T(8,128)(2,1)}, u32[]{:S(2)}, u32[]{:S(2)}) collective-permute-start(bf16[256,2048]{1,0:T(8,128)(2,1)S(1)} %collective-permute-done.5.refs_1_), channel_id=1, source_target_pairs={{0,64},{64,0},{1,65},{65,1},{2,66},{66,2},{3,67},{67,3},{4,68},{68... | collective-permute-start | bytes 3145736 | tf_op jit(solution)/shard_map/ppermute | solution.py:243
  71.1 17.7 %collective-permute-start.11 = (bf16[256,2048]{1,0:T(8,128)(2,1)S(1)}, bf16[256,2048]{1,0:T(8,128)(2,1)}, u32[]{:S(2)}, u32[]{:S(2)}) collective-permute-start(bf16[256,2048]{1,0:T(8,128)(2,1)S(1)} %collective-permute-done.6.refs_2_), channel_id=1, source_target_pairs={{0,64},{64,0},{1,65},{65,1},{2,66},{66,2},{3,67},{67,3},{4,68},{68... | collective-permute-start | bytes 3145736 | tf_op jit(solution)/shard_map/ppermute | solution.py:244
  78.8 10.1 %collective-permute-start.12 = (bf16[128,2048]{1,0:T(8,128)(2,1)}, bf16[128,2048]{1,0:T(8,128)(2,1)}, u32[]{:S(2)}, u32[]{:S(2)}) collective-permute-start(bf16[128,2048]{1,0:T(8,128)(2,1)} %collective-permute-done.7.refs_3_), channel_id=1, source_target_pairs={{0,64},{64,0},{1,65},{65,1},{2,66},{66,2},{3,67},{67,3},{4,68},{68... | collective-permute-start | bytes 1572872 | tf_op jit(solution)/shard_map/ppermute | solution.py:245
  81.5 7.3 %collective-permute-start.13 = (bf16[128,2048]{1,0:T(8,128)(2,1)}, bf16[128,2048]{1,0:T(8,128)(2,1)}, u32[]{:S(2)}, u32[]{:S(2)}) collective-permute-start(bf16[128,2048]{1,0:T(8,128)(2,1)} %collective-permute-done.8.refs_4_), channel_id=1, source_target_pairs={{0,64},{64,0},{1,65},{65,1},{2,66},{66,2},{3,67},{67,3},{4,68},{68... | collective-permute-start | bytes 1572872 | tf_op jit(solution)/shard_map/ppermute | solution.py:246
  85.4 3.4 %collective-permute-start = (bf16[4,256,128]{2,1,0:T(8,128)(2,1)S(1)}, bf16[4,256,128]{2,1,0:T(8,128)(2,1)S(1)}, u32[]{:S(2)}, u32[]{:S(2)}) collective-permute-start(bf16[4,256,128]{2,1,0:T(8,128)(2,1)S(1)} %bitcast.53), channel_id=1, source_target_pairs={{0,64},{64,0},{1,65},{65,1},{2,66},{66,2},{3,67},{67,3},{4,68},{68... | collective-permute-start | bytes 786440 | tf_op jit(solution)/shard_map/ppermute | solution.py:212
  88.8 22.6 %copy-start.7 = (s32[8,64]{1,0:T(8,128)S(1)}, s32[8,64]{1,0:T(8,128)}, u32[]{:S(2)}) copy-start(s32[8,64]{1,0:T(8,128)} %param.12) | copy-start | bytes 6148
  88.8 52.7 %copy-start.6 = (s32[64]{0:T(128)S(1)}, s32[64]{0:T(128)}, u32[]{:S(2)}) copy-start(s32[64]{0:T(128)} %new.1) | copy-start | bytes 772
  96.9 44.6 %all-to-all-start.2 = ((f32[64,16,128]{2,1,0:T(8,128)}), f32[64,16,128]{2,1,0:T(8,128)S(1)}, u32[]{:S(2)}, u32[]{:S(2)}) async-start(f32[64,16,128]{2,1,0:T(8,128)} %group_grad.1), calls=%async_computation.2 | async-start | bytes 1048576 | tf_op jit(solution)/shard_map/all_to_all | solution.py:266
  183.8 21.2 %collective-permute-start.14 = (bf16[4,4,256,128]{3,2,1,0:T(8,128)(2,1)S(1)}, bf16[4,4,256,128]{3,2,1,0:T(8,128)(2,1)S(1)}, u32[]{:S(2)}, u32[]{:S(2)}) collective-permute-start(bf16[4,4,256,128]{3,2,1,0:T(8,128)(2,1)S(1)} %all_to_all.26.mine), channel_id=1, source_target_pairs={{0,64},{64,0},{1,65},{65,1},{2,66},{66,2},{3,67},{67,3},{4,68},{68... | collective-permute-start | bytes 3145736 | tf_op jit(solution)/shard_map/ppermute | solution.py:304
  190.3 8.4 %collective-permute-start.15 = (f32[3,16,4,128]{3,2,1,0:T(4,128)S(1)}, f32[3,16,4,128]{3,2,1,0:T(4,128)S(1)}, u32[]{:S(2)}, u32[]{:S(2)}) collective-permute-start(f32[3,16,4,128]{3,2,1,0:T(4,128)S(1)} %get-tuple-element.16), channel_id=1, source_target_pairs={{0,128},{128,256},{256,384},{384,0},{1,129},{129,257},{257,385},{3... | collective-permute-start | bytes 294920 | tf_op jit(solution)/shard_map/ppermute | solution.py:287
  192.5 6.2 %collective-permute-start.16 = (f32[3,16,4,128]{3,2,1,0:T(4,128)S(1)}, f32[3,16,4,128]{3,2,1,0:T(4,128)S(1)}, u32[]{:S(2)}, u32[]{:S(2)}) collective-permute-start(f32[3,16,4,128]{3,2,1,0:T(4,128)S(1)} %get-tuple-element.15), channel_id=1, source_target_pairs={{0,384},{128,0},{256,128},{384,256},{1,385},{129,1},{257,129},{385... | collective-permute-start | bytes 294920 | tf_op jit(solution)/shard_map/ppermute | solution.py:288
  196.9 7.2 %collective-permute-start.17 = (f32[3,16,4,128]{3,2,1,0:T(4,128)S(1)}, f32[3,16,4,128]{3,2,1,0:T(4,128)S(1)}, u32[]{:S(2)}, u32[]{:S(2)}) collective-permute-start(f32[3,16,4,128]{3,2,1,0:T(4,128)S(1)} %get-tuple-element.14), channel_id=1, source_target_pairs={{0,256},{128,384},{256,0},{384,128},{1,257},{129,385},{257,1},{385... | collective-permute-start | bytes 294920 | tf_op jit(solution)/shard_map/ppermute | solution.py:289

commit v3 on v2

v3 whole, which is shorter than its diff:
```python
import jax
import jax.numpy as jnp
from jax import lax
from jax.experimental import pallas as pl
from jax.experimental.pallas import tpu as pltpu
from jax.sharding import Mesh
from jax.sharding import PartitionSpec as P


decay_first = 0.9
decay_second = 0.95
learn_rate = 0.001
weight_decay = 0.1
epsilon = 1e-08
step_number = 20.0

Y, C, X, Z = 4, 2, 4, 16
PLACES = X * Z
UP = [(i, (i + 1) % Y) for i in range(Y)]
DOWN = [(i, (i - 1) % Y) for i in range(Y)]
ACROSS = [(i, (i + 2) % Y) for i in range(Y)]
SWAP = [(0, 1), (1, 0)]
VMEM = pl.BlockSpec(memory_space=pltpu.VMEM)
SMEM = pl.BlockSpec(memory_space=pltpu.SMEM)
ANY = pl.BlockSpec(memory_space=pl.ANY)


def grant(mib):
    return pltpu.CompilerParams(vmem_limit_bytes=mib << 20)


def lower_half(x):
    return lax.broadcasted_iota(jnp.int32, x.shape, x.ndim - 1) < x.shape[-1] // 2


def swapped(x):
    return pltpu.roll(x, x.shape[-1] // 2, x.ndim - 1)


def split_cols(*refs):
    ins, out = refs[:-1], refs[-1]
    lanes = out.shape[-1]
    half = ins[0].shape[-1] // 2
    for n, x in enumerate(ins):
        for pair in range(Y // 2):
            gate = x[:, :, pair * lanes : (pair + 1) * lanes]
            up = x[:, :, half + pair * lanes : half + (pair + 1) * lanes]
            low = lower_half(gate)
            out[2 * pair, n] = jnp.where(low, gate, swapped(up))
            out[2 * pair + 1, n] = jnp.where(low, swapped(gate), up)


def join_cols(y_ref, own, low, high, far, *refs):
    outs, parts = refs[:-1], refs[-1]
    y = y_ref[0]
    parts[y] = own[...]
    parts[(y + 3) % Y] = low[...]
    parts[(y + 1) % Y] = high[...]
    parts[(y + 2) % Y] = far[...]
    lanes = own.shape[-1]
    half = outs[0].shape[-1] // 2
    for n, out in enumerate(outs):
        for pair in range(Y // 2):
            a, b = parts[2 * pair, n], parts[2 * pair + 1, n]
            first = lower_half(a)
            out[:, :, pair * lanes : (pair + 1) * lanes] = jnp.where(first, a, swapped(b))
            out[:, :, half + pair * lanes : half + (pair + 1) * lanes] = jnp.where(
                first, swapped(a), b
            )


def prepare(where, counts, order, hidden, master, out):
    batches, batch_rows = order.shape
    experts, rows_shard, width = master.shape
    lanes = out.shape[-1]
    half = width // 2
    count = counts[where[0], where[1]]
    blocks = []
    for m in range(batches):
        at = m * batch_rows
        slot = lax.broadcasted_iota(jnp.int32, (batch_rows, hidden.shape[1]), 0) + at
        live = jnp.where(slot < count, hidden[at : at + batch_rows, :].astype(jnp.float32), 0.0)
        row = lax.broadcasted_iota(jnp.int32, (batch_rows, batch_rows), 0)
        moves = (jnp.broadcast_to(order[m : m + 1, :], row.shape) == row).astype(jnp.bfloat16)
        blocks.append(
            jnp.dot(moves, live.astype(jnp.bfloat16), preferred_element_type=jnp.float32)
        )
    upper = jnp.concatenate(blocks[: batches // 2], axis=0)
    lower = jnp.concatenate(blocks[batches // 2 :], axis=0)
    weights = experts * rows_shard
    for pair in range(Y // 2):
        cut = slice(pair * lanes, (pair + 1) * lanes)
        first = lower_half(upper[:, cut])
        out[2 * pair, weights:, :] = jnp.where(
            first, upper[:, cut], swapped(lower[:, cut])
        ).astype(jnp.bfloat16)
        out[2 * pair + 1, weights:, :] = jnp.where(
            first, swapped(upper[:, cut]), lower[:, cut]
        ).astype(jnp.bfloat16)
        gate = jnp.concatenate([master[e, :, cut] for e in range(experts)], axis=0)
        up_cut = slice(half + pair * lanes, half + (pair + 1) * lanes)
        up = jnp.concatenate([master[e, :, up_cut] for e in range(experts)], axis=0)
        first = lower_half(gate)
        out[2 * pair, :weights, :] = jnp.where(first, gate, swapped(up)).astype(jnp.bfloat16)
        out[2 * pair + 1, :weights, :] = jnp.where(first, swapped(gate), up).astype(jnp.bfloat16)


def pick_old(slots, payload, out, table):
    experts, rows, _ = table.shape
    rows_shard = rows // Y
    parts = [payload[y, : experts * rows_shard, :].astype(jnp.float32) for y in range(Y)]
    for e in range(experts):
        table[e] = jnp.concatenate(
            [part[e * rows_shard : (e + 1) * rows_shard] for part in parts], axis=0
        ).astype(jnp.bfloat16)
    for p in range(PLACES):
        out[p] = table[slots[p]]


def adam(old, new, total, y_ref, got, own, low, high, far, out, after, state, acc, table):
    experts = acc.shape[0]
    rows = state.shape[3]
    y_here = y_ref[0]
    state[y_here] = own[...]
    state[(y_here + 3) % Y] = low[...]
    state[(y_here + 1) % Y] = high[...]
    state[(y_here + 2) % Y] = far[...]
    acc[...] = jnp.zeros_like(acc)
    for p in range(PLACES):
        acc[old[p]] += got[p]
    for e in range(experts):
        master, first, second = (
            jnp.concatenate([state[y, n, e] for y in range(Y)], axis=0) for n in range(3)
        )
        grad = acc[e] / total[e]
        new_first = decay_first * first + (1.0 - decay_first) * grad
        new_second = decay_second * second + (1.0 - decay_second) * grad * grad
        first_hat = new_first / (1.0 - decay_first**step_number)
        second_hat = new_second / (1.0 - decay_second**step_number)
        new_master = master - learn_rate * (
            first_hat / (jnp.sqrt(second_hat) + epsilon) + weight_decay * master
        )
        table[e] = new_master.astype(jnp.bfloat16)
        for n, value in enumerate((new_master, new_first, new_second)):
            for y in range(Y):
                after[y, n, e] = value[y * rows : (y + 1) * rows]
    for p in range(PLACES):
        out[p] = table[new[p]]


def half_grad(out_ref, local_ref, chunks, half, wide):
    for y in range(Y):
        at = pl.multiple_of((2 * y + half) * wide, wide)
        total, row = None, 0
        for chunk in chunks:
            rows = chunk.shape[0]
            term = jnp.dot(
                local_ref[:, row : row + rows],
                chunk[:, pl.ds(at, wide)],
                preferred_element_type=jnp.float32,
            )
            total = term if total is None else total + term
            row += rows
        out_ref[:, 4 * y : 4 * y + 4, :] = total.T.reshape(wide // 4, 4, -1)


def grad_theirs(where, mine, theirs, payload, *refs):
    chunks, (out_ref, local_ref, w_ref) = refs[:-3], refs[-3:]
    y_here, core = where[0], where[1]
    wide = mine.shape[1]
    for y in range(Y):
        w_ref[pl.ds(pl.multiple_of((2 * y + core) * wide, wide), wide), :] = mine[y]
        w_ref[pl.ds(pl.multiple_of((2 * y + 1 - core) * wide, wide), wide), :] = theirs[y]
    sources = [y_here, (y_here + 3) % Y, (y_here + 1) % Y, (y_here + 2) % Y, (y_here + 2) % Y]
    packed = chunks[-1].shape[0]
    weights = payload.shape[1] - packed
    row = 0
    for k, chunk in enumerate(chunks):
        rows = chunk.shape[0]
        both = jnp.dot(chunk[...], w_ref[...], preferred_element_type=jnp.float32)
        other = swapped(both)
        first = lower_half(both)
        gate = jnp.where(first, both, other)
        sigma = jax.nn.sigmoid(gate)
        active = gate * sigma
        slope = sigma * (1.0 + gate * (1.0 - sigma))
        hidden = payload[sources[k], weights:, :].astype(jnp.float32)
        around = swapped(hidden)
        begin = lower_half(hidden)
        halves = [jnp.where(begin, hidden, around), jnp.where(begin, around, hidden)]
        if rows > packed:
            incoming = jnp.concatenate(halves, axis=0)
        else:
            incoming = halves[k - 3]
        local = jnp.where(first, incoming * other * slope, incoming * active)
        local_ref[:, row : row + rows] = local.T.astype(jnp.bfloat16)
        row += rows
    half_grad(out_ref, local_ref, chunks, 1 - core, wide)


def grad_mine(where, local_ref, *refs):
    chunks, out_ref = refs[:-1], refs[-1]
    half_grad(out_ref, local_ref, chunks, where[1], out_ref.shape[0] * 4)


def joined(out, source):
    lanes = source.shape[-1]
    half = out.shape[-1] // 2
    for pair in range(Y // 2):
        a = source[2 * pair, 0].astype(jnp.float32)
        b = source[2 * pair + 1, 0].astype(jnp.float32)
        first = lower_half(a)
        out[0, 0, :, pair * lanes : (pair + 1) * lanes] = jnp.where(
            first, a, swapped(b)
        ).astype(jnp.bfloat16)
        out[0, 0, :, half + pair * lanes : half + (pair + 1) * lanes] = jnp.where(
            first, swapped(a), b
        ).astype(jnp.bfloat16)


def join_mine(where, source, out):
    joined(out, source)


def join_theirs(where, source, begun, out):
    joined(out, source)


def shards(
    tokens, hidden_grad, routing, row_count, old_slots, new_slots, master, first_moment, second_moment
):
    y, core = lax.axis_index("y"), lax.axis_index("core")
    group_here = y * C + core
    place_here = lax.axis_index("x") * Z + lax.axis_index("z")
    experts, rows_shard, width = master.shape
    hid = width // 2
    part = hid // Y
    lanes = 2 * part
    f32, bf16 = jnp.float32, jnp.bfloat16
    where = jnp.stack([y, core]).astype(jnp.int32)
    y_id = y.astype(jnp.int32).reshape(1)
    spot = jnp.stack([group_here, place_here]).astype(jnp.int32)

    own = tokens[0, 0]
    rows = own.shape[0]
    half_rows = rows // 2
    low = lax.ppermute(own, "y", UP)
    high = lax.ppermute(own, "y", DOWN)

    payload = pl.pallas_call(
        prepare,
        out_shape=jax.ShapeDtypeStruct((Y, experts * rows_shard + half_rows, lanes), bf16),
        in_specs=[SMEM, SMEM, VMEM, VMEM, VMEM],
        out_specs=VMEM,
        name="prepare",
    )(spot, row_count, routing[0, 0], hidden_grad[0, 0], master)
    payload = lax.all_to_all(payload, "y", 0, 0, tiled=True)
    picked = pl.pallas_call(
        pick_old,
        out_shape=jax.ShapeDtypeStruct((PLACES, Y * rows_shard, lanes), bf16),
        in_specs=[SMEM, VMEM],
        out_specs=VMEM,
        scratch_shapes=[pltpu.VMEM((experts, Y * rows_shard, lanes), bf16)],
        compiler_params=grant(4),
        name="pick_old",
    )(old_slots, payload)
    landed = lax.all_to_all(picked, ("x", "z"), 0, 0, tiled=True)
    far_a = lax.ppermute(low[:half_rows], "y", UP)
    far_b = lax.ppermute(high[half_rows:], "y", DOWN)

    def by_rows(x):
        return (
            x.reshape(PLACES, Y, rows_shard, lanes)
            .transpose(1, 0, 2, 3)
            .reshape(Y, PLACES * rows_shard, lanes)
        )

    w_mine = by_rows(landed)
    w_theirs = lax.ppermute(w_mine, "core", SWAP)

    chunks = [own, low, high, far_a, far_b]
    line_rows = sum(c.shape[0] for c in chunks)
    deep = own.shape[1]
    grad_shape = jax.ShapeDtypeStruct((PLACES, Y * rows_shard, lanes), f32)
    sent, local = pl.pallas_call(
        grad_theirs,
        out_shape=(grad_shape, jax.ShapeDtypeStruct((lanes, line_rows), bf16)),
        in_specs=[SMEM] + [VMEM] * (3 + len(chunks)),
        out_specs=(VMEM, VMEM),
        scratch_shapes=[pltpu.VMEM((deep, lanes), bf16)],
        compiler_params=grant(24),
        name="grad_theirs",
    )(where, w_mine, w_theirs, payload, *chunks)
    received = lax.ppermute(sent, "core", SWAP)
    summed = pl.pallas_call(
        grad_mine,
        out_shape=grad_shape,
        in_specs=[SMEM] + [VMEM] * (1 + len(chunks)),
        out_specs=VMEM,
        compiler_params=grant(24),
        name="grad_mine",
    )(where, local, *chunks)
    summed = summed + received

    columns = pl.pallas_call(
        split_cols,
        out_shape=jax.ShapeDtypeStruct((Y, 3, experts, rows_shard, lanes), f32),
        in_specs=[VMEM] * 3,
        out_specs=VMEM,
        compiler_params=grant(4),
        name="split_cols",
    )(master, first_moment, second_moment)

    def for_chip(step, x):
        return lax.dynamic_index_in_dim(x, (y + step) % Y, keepdims=False)

    m_low = lax.ppermute(for_chip(1, columns), "y", UP)
    m_high = lax.ppermute(for_chip(3, columns), "y", DOWN)
    m_far = lax.ppermute(for_chip(2, columns), "y", ACROSS)
    m_own = for_chip(0, columns)

    got = lax.all_to_all(summed, ("x", "z"), 0, 0, tiled=True)
    select = (old_slots[:, None] == jnp.arange(experts, dtype=jnp.int32)[None, :]).astype(f32)
    per_slot = jnp.sum(row_count.astype(f32), axis=0)
    total = jnp.dot(per_slot, select, precision=lax.Precision.HIGHEST)
    picked, after = pl.pallas_call(
        adam,
        out_shape=(
            jax.ShapeDtypeStruct((PLACES, Y * rows_shard, lanes), bf16),
            jax.ShapeDtypeStruct((Y, 3, experts, rows_shard, lanes), f32),
        ),
        in_specs=[SMEM] * 4 + [VMEM] * 5,
        out_specs=(VMEM, VMEM),
        scratch_shapes=[
            pltpu.VMEM((Y, 3, experts, rows_shard, lanes), f32),
            pltpu.VMEM((experts, Y * rows_shard, lanes), f32),
            pltpu.VMEM((experts, Y * rows_shard, lanes), bf16),
        ],
        compiler_params=grant(6),
        name="adam",
    )(old_slots, new_slots, total, y_id, got, m_own, m_low, m_high, m_far)
    landed = lax.all_to_all(picked, ("x", "z"), 0, 0, tiled=True)

    s_low = lax.ppermute(for_chip(1, after), "y", UP)
    s_high = lax.ppermute(for_chip(3, after), "y", DOWN)
    s_far = lax.ppermute(for_chip(2, after), "y", ACROSS)
    whole = jax.ShapeDtypeStruct((experts, rows_shard, width), f32)
    new_master, new_first, new_second = pl.pallas_call(
        join_cols,
        out_shape=(whole,) * 3,
        in_specs=[SMEM] + [VMEM] * 4,
        out_specs=(VMEM,) * 3,
        scratch_shapes=[pltpu.VMEM((Y, 3, experts, rows_shard, lanes), f32)],
        compiler_params=grant(6),
        name="join_cols",
    )(y_id, for_chip(0, after), s_low, s_high, s_far)

    landed = by_rows(landed)
    copies = jnp.broadcast_to(landed[None], (Y, *landed.shape))
    mine = lax.all_to_all(copies, "y", 0, 0, tiled=True)
    theirs = lax.ppermute(mine, "core", SWAP)
    block_rows = PLACES * rows_shard
    whole = jax.ShapeDtypeStruct((Y, C, block_rows, width), bf16)
    block = pl.BlockSpec((Y, 1, block_rows, lanes), lambda i, at: (0, i, 0, 0))
    begun = pl.pallas_call(
        join_mine,
        out_shape=whole,
        grid_spec=pltpu.PrefetchScalarGridSpec(
            num_scalar_prefetch=1,
            grid=(Y,),
            in_specs=[block],
            out_specs=pl.BlockSpec((1, 1, block_rows, width), lambda i, at: (i, at[1], 0, 0)),
        ),
        compiler_params=grant(8),
        name="join_mine",
    )(where, mine)
    new_weights = pl.pallas_call(
        join_theirs,
        out_shape=whole,
        grid_spec=pltpu.PrefetchScalarGridSpec(
            num_scalar_prefetch=1,
            grid=(Y,),
            in_specs=[block, ANY],
            out_specs=pl.BlockSpec((1, 1, block_rows, width), lambda i, at: (i, 1 - at[1], 0, 0)),
        ),
        input_output_aliases={2: 0},
        compiler_params=grant(8),
        name="join_theirs",
    )(where, theirs, begun)
    return (new_weights.reshape(1, -1, width), new_master, new_first, new_second)


def solution(mesh):
    fine = Mesh(mesh.devices.reshape(Y, C, X, Z), ("y", "core", "x", "z"))
    dp, place = ("y", "core"), ("x", "z")
    placed = (
        P(dp, place, None, None),
        P(dp, place, None, None),
        P(dp, place, None, None),
        P(),
        P(),
        P(),
        P(None, dp + place, None),
        P(None, dp + place, None),
        P(None, dp + place, None),
    )

    return jax.shard_map(
        shards,
        mesh=fine,
        in_specs=placed,
        out_specs=(
            P(place, None, None),
            P(None, dp + place, None),
            P(None, dp + place, None),
            P(None, dp + place, None),
        ),
        check_vma=False,
    )
```

time: 209 us -> 198 us (0.947)
  starting transfers between devices: 99.6 us -> 72.6 us
  blocking collectives: 40.9 us -> 64.5 us
  waiting for transfers between devices: 42.3 us -> 37.7 us
    all_to_all x0 -> x1, blocking collectives: none -> 23.3 us  [shards(): payload = lax.all_to_all(payload, 'y', 0, 0, tiled=True)]
    ppermute x9 -> x4, starting transfers between devices: 33 us -> 10.7 us  [the longest x1 3.97 us: shards(): m_high = lax.ppermute(for_chip(3, columns), 'y', DOWN)]
    all_to_all x1, waiting for transfers between devices: 29.9 us -> 16.3 us  [shards(): got = lax.all_to_all(summed, ('x', 'z'), 0, 0, tiled=True)]
    all_to_all x1, waiting for transfers between devices: 0.01 us -> 10.6 us  [shards(): landed = lax.all_to_all(picked, ('x', 'z'), 0, 0, tiled=True)]
    ppermute x1, waiting for transfers between devices: 5.68 us -> 0.01 us  [shards(): far_a = lax.ppermute(low[:half_rows], 'y', UP)]
    ppermute x1, waiting for transfers between devices: 5.23 us -> 0.01 us  [shards(): s_far = lax.ppermute(for_chip(2, after), 'y', ACROSS)]
    all_to_all x1, starting transfers between devices: 14.5 us -> 9.57 us  [shards(): got = lax.all_to_all(summed, ('x', 'z'), 0, 0, tiled=True)]
    ppermute x1, waiting for transfers between devices: 0.01 us -> 4.93 us  [shards(): s_low = lax.ppermute(for_chip(1, after), 'y', UP)]
  transfers between devices with their start and end apart: 21 -> 15, of which waited for: 4 -> 5; matrix products, arithmetic and copies ran while one was open for 3% -> 2% of each run, Pallas kernels for 1% -> 4%
where the time goes in v3:
time: 198 us; the launch traced here: 197 us
  starting transfers between devices  72.6 us (37%)
  blocking collectives  64.5 us (33%)
  waiting for transfers between devices  37.7 us (19%)
  Pallas kernels  14.7 us (7%)
  local copies, waits for them, and re-layouts  4.47 us (2%)
    all_to_all x1, blocking collectives, shards(): landed = lax.all_to_all(picked, ('x', 'z'), 0, 0, tiled=True)  26.7 us
    all_to_all x1, blocking collectives, shards(): payload = lax.all_to_all(payload, 'y', 0, 0, tiled=True)  23.3 us
    all_to_all x1, starting transfers between devices, shards(): landed = lax.all_to_all(picked, ('x', 'z'), 0, 0, tiled=True)  19.3 us
    all_to_all x1, waiting for transfers between devices, shards(): got = lax.all_to_all(summed, ('x', 'z'), 0, 0, tiled=True)  16.3 us
    all_to_all x1, blocking collectives, shards(): mine = lax.all_to_all(copies, 'y', 0, 0, tiled=True)  14.5 us
    all_to_all x1, waiting for transfers between devices, shards(): landed = lax.all_to_all(picked, ('x', 'z'), 0, 0, tiled=True)  10.6 us
    all_to_all x1, starting transfers between devices, shards(): got = lax.all_to_all(summed, ('x', 'z'), 0, 0, tiled=True)  9.57 us
    ppermute x1, starting transfers between devices, shards(): w_theirs = lax.ppermute(w_mine, 'core', SWAP)  6.1 us
  transfers between devices with their start and end apart: 15, of which 5 were waited for; matrix products, arithmetic and copies ran while one was open for 2% of the time, Pallas kernels for 4%

profile of v3, /device:TPU:1, one launch (start us, length us, event | category | flops | bytes accessed | tf_op | source)
XLA Modules:
  0.0 196.8 jit_solution(14615199568620167877)
XLA Ops:
  0.6 5.5 %collective-permute-start.2 = (bf16[256,2048]{1,0:T(8,128)(2,1)}, bf16[256,2048]{1,0:T(8,128)(2,1)S(1)}, u32[]{:S(2)}, u32[]{:S(2)}) collective-permute-start(bf16[256,2048]{1,0:T(8,128)(2,1)} %bitcast.37), channel_id=1, source_target_pairs={{0,384},{128,0},{256,128},{384,256},{1,385},{129,1},{257,129},{385... | collective-permute-start | bytes 3145736 | tf_op jit(solution)/shard_map/ppermute | solution.py:248
  6.1 1.9 collective-permute-start.1
  8.7 1.9 prepare.1
  10.6 23.3 %all_to_all.25.payload = bf16[4,192,128]{2,1,0:T(8,128)(2,1)S(1)} all-to-all(bf16[4,192,128]{2,1,0:T(8,128)(2,1)} %prepare.1), channel_id=1, replica_groups=mesh['y'=4,'core'=2,'x'=4,'z'=16] {'y'}, dimensions={0} | all-to-all | bytes 393216 | tf_op jit(solution)/shard_map/all_to_all | solution.py:257
  35.9 19.3 %all-to-all-start.1 = ((bf16[64,16,128]{2,1,0:T(8,128)(2,1)}), bf16[64,16,128]{2,1,0:T(8,128)(2,1)}, u32[]{:S(2)}, u32[]{:S(2)}) async-start(bf16[64,16,128]{2,1,0:T(8,128)(2,1)} %copy-done.1), calls=%async_computation.1 | async-start | bytes 524288 | tf_op jit(solution)/shard_map/all_to_all | solution.py:267
  56.1 1.9 collective-permute-start.4
  58.9 3.4 %collective-permute-start.3 = (bf16[128,2048]{1,0:T(8,128)(2,1)}, bf16[128,2048]{1,0:T(8,128)(2,1)}, u32[]{:S(2)}, u32[]{:S(2)}) collective-permute-start(bf16[128,2048]{1,0:T(8,128)(2,1)} %slice.8), channel_id=1, source_target_pairs={{0,128},{128,256},{256,384},{384,0},{1,129},{129,257},{257,385},{3... | collective-permute-start | bytes 1572872 | tf_op jit(solution)/shard_map/ppermute | solution.py:268
  62.2 10.6 %all-to-all-done.1 = bf16[64,16,128]{2,1,0:T(8,128)(2,1)} async-done(((bf16[64,16,128]{2,1,0:T(8,128)(2,1)}), bf16[64,16,128]{2,1,0:T(8,128)(2,1)}, u32[]{:S(2)}, u32[]{:S(2)}) %all-to-all-start.1) | async-done | bytes 262176 | tf_op jit(solution)/shard_map/all_to_all | solution.py:267
  72.9 1.0 copy.14
  73.9 6.1 %collective-permute-start = (bf16[4,256,128]{2,1,0:T(8,128)(2,1)S(1)}, bf16[4,256,128]{2,1,0:T(8,128)(2,1)S(1)}, u32[]{:S(2)}, u32[]{:S(2)}) collective-permute-start(bf16[4,256,128]{2,1,0:T(8,128)(2,1)S(1)} %bitcast.41), channel_id=1, source_target_pairs={{0,64},{64,0},{1,65},{65,1},{2,66},{66,2},{3,67},{67,3},{4,68},{68... | collective-permute-start | bytes 786440 | tf_op jit(solution)/shard_map/ppermute | solution.py:279
  80.1 1.1 collective-permute-done.theirs
  81.2 3.2 %grad_theirs.1 = (f32[64,16,128]{2,1,0:T(8,128)S(1)}, bf16[128,1024]{1,0:T(8,128)(2,1)S(1)}) custom-call(s32[2]{0:T(128)S(1)} %pad_add_fusion.where, bf16[4,256,128]{2,1,0:T(8,128)(2,1)S(1)} %bitcast.42, bf16[4,256,128]{2,1,0:T(8,128)(2,1)S(1)} %collective-permute-done.theirs, bf16[4,192,128]{2,1,0:T(8,128)(2,1)S(1)} %all_to_all.25.payload, ...), custom_call_target="tpu_custom_call" | custom-call | tf_op jit(solution)/shard_map/grad_theirs/pallas_call | solution.py:285
  84.4 2.3 %collective-permute-start.5 = (f32[64,16,128]{2,1,0:T(8,128)S(1)}, f32[64,16,128]{2,1,0:T(8,128)S(1)}, u32[]{:S(2)}, u32[]{:S(2)}) collective-permute-start(f32[64,16,128]{2,1,0:T(8,128)S(1)} %get-tuple-element.12), channel_id=1, source_target_pairs={{0,64},{64,0},{1,65},{65,1},{2,66},{66,2},{3,67},{67,3},{4,68},{68... | collective-permute-start | bytes 1572872 | tf_op jit(solution)/shard_map/ppermute | solution.py:294
  86.7 1.9 grad_mine.1
  88.6 0.9 add.57
  89.5 9.6 %all-to-all-start.2 = ((f32[64,16,128]{2,1,0:T(8,128)}), f32[64,16,128]{2,1,0:T(8,128)S(1)}, u32[]{:S(2)}, u32[]{:S(2)}) async-start(f32[64,16,128]{2,1,0:T(8,128)} %add.57), calls=%async_computation.2 | async-start | bytes 1048576 | tf_op jit(solution)/shard_map/all_to_all | solution.py:322
  99.5 2.5 %collective-permute-start.8 = (f32[3,16,4,128]{3,2,1,0:T(4,128)S(1)}, f32[3,16,4,128]{3,2,1,0:T(4,128)S(1)}, u32[]{:S(2)}, u32[]{:S(2)}) collective-permute-start(f32[3,16,4,128]{3,2,1,0:T(4,128)S(1)} %get-tuple-element.22), channel_id=1, source_target_pairs={{0,256},{128,384},{256,0},{384,128},{1,257},{129,385},{257,1},{385... | collective-permute-start | bytes 294920 | tf_op jit(solution)/shard_map/ppermute | solution.py:319
  101.9 4.0 %collective-permute-start.7 = (f32[3,16,4,128]{3,2,1,0:T(4,128)S(1)}, f32[3,16,4,128]{3,2,1,0:T(4,128)S(1)}, u32[]{:S(2)}, u32[]{:S(2)}) collective-permute-start(f32[3,16,4,128]{3,2,1,0:T(4,128)S(1)} %get-tuple-element.23), channel_id=1, source_target_pairs={{0,384},{128,0},{256,128},{384,256},{1,385},{129,1},{257,129},{385... | collective-permute-start | bytes 294920 | tf_op jit(solution)/shard_map/ppermute | solution.py:318
  105.9 1.9 collective-permute-start.6
  108.1 4.7 %collective-permute-done.6.low = f32[3,16,4,128]{3,2,1,0:T(4,128)S(1)} collective-permute-done((f32[3,16,4,128]{3,2,1,0:T(4,128)S(1)}, f32[3,16,4,128]{3,2,1,0:T(4,128)S(1)}, u32[]{:S(2)}, u32[]{:S(2)}) %collective-permute-start.6) | collective-permute-done | bytes 98336 | tf_op jit(solution)/shard_map/ppermute | solution.py:317
  112.8 16.3 %all-to-all-done.2.got = f32[64,16,128]{2,1,0:T(8,128)S(1)} async-done(((f32[64,16,128]{2,1,0:T(8,128)}), f32[64,16,128]{2,1,0:T(8,128)S(1)}, u32[]{:S(2)}, u32[]{:S(2)}) %all-to-all-start.2) | async-done | bytes 524320 | tf_op jit(solution)/shard_map/all_to_all | solution.py:322
  129.1 1.0 adam.1
  130.1 26.7 %all_to_all.26 = bf16[64,16,128]{2,1,0:T(8,128)(2,1)S(1)} all-to-all(bf16[64,16,128]{2,1,0:T(8,128)(2,1)S(1)} %get-tuple-element.13), channel_id=1, replica_groups=mesh['y'=4,'core'=2,'x'=4,'z'=16] {'x','z'}, dimensions={0} | all-to-all | bytes 524288 | tf_op jit(solution)/shard_map/all_to_all | solution.py:342
  157.1 14.5 %all_to_all.27.source = bf16[4,4,256,128]{3,2,1,0:T(8,128)(2,1)S(1)} all-to-all(bf16[4,4,256,128]{3,2,1,0:T(8,128)(2,1)S(1)} %broadcast_in_dim.10), channel_id=1, replica_groups=mesh['y'=4,'core'=2,'x'=4,'z'=16] {'y'}, dimensions={0} | all-to-all | bytes 2097152 | tf_op jit(solution)/shard_map/all_to_all | solution.py:360
  171.6 5.8 %collective-permute-start.9 = (bf16[4,4,256,128]{3,2,1,0:T(8,128)(2,1)S(1)}, bf16[4,4,256,128]{3,2,1,0:T(8,128)(2,1)S(1)}, u32[]{:S(2)}, u32[]{:S(2)}) collective-permute-start(bf16[4,4,256,128]{3,2,1,0:T(8,128)(2,1)S(1)} %all_to_all.27.source), channel_id=1, source_target_pairs={{0,64},{64,0},{1,65},{65,1},{2,66},{66,2},{3,67},{67,3},{4,68},{68... | collective-permute-start | bytes 3145736 | tf_op jit(solution)/shard_map/ppermute | solution.py:361
  177.5 2.4 %collective-permute-start.12 = (f32[3,16,4,128]{3,2,1,0:T(4,128)S(1)}, f32[3,16,4,128]{3,2,1,0:T(4,128)S(1)}, u32[]{:S(2)}, u32[]{:S(2)}) collective-permute-start(f32[3,16,4,128]{3,2,1,0:T(4,128)S(1)} %get-tuple-element.18), channel_id=1, source_target_pairs={{0,256},{128,384},{256,0},{384,128},{1,257},{129,385},{257,1},{385... | collective-permute-start | bytes 294920 | tf_op jit(solution)/shard_map/ppermute | solution.py:346
  180.0 4.0 %collective-permute-start.11 = (f32[3,16,4,128]{3,2,1,0:T(4,128)S(1)}, f32[3,16,4,128]{3,2,1,0:T(4,128)S(1)}, u32[]{:S(2)}, u32[]{:S(2)}) collective-permute-start(f32[3,16,4,128]{3,2,1,0:T(4,128)S(1)} %get-tuple-element.19), channel_id=1, source_target_pairs={{0,384},{128,0},{256,128},{384,256},{1,385},{129,1},{257,129},{385... | collective-permute-start | bytes 294920 | tf_op jit(solution)/shard_map/ppermute | solution.py:345
  184.0 1.9 collective-permute-start.10
  186.0 4.9 %collective-permute-done.10.low = f32[3,16,4,128]{3,2,1,0:T(4,128)S(1)} collective-permute-done((f32[3,16,4,128]{3,2,1,0:T(4,128)S(1)}, f32[3,16,4,128]{3,2,1,0:T(4,128)S(1)}, u32[]{:S(2)}, u32[]{:S(2)}) %collective-permute-start.10) | collective-permute-done | bytes 98336 | tf_op jit(solution)/shard_map/ppermute | solution.py:344
  190.9 1.0 join_cols.1
  191.9 2.5 %join_mine.1.begun = bf16[4,2,256,512]{3,2,1,0:T(8,128)(2,1)} custom-call(s32[2]{0:T(128)S(1)} %pad_add_fusion.where, bf16[4,4,256,128]{3,2,1,0:T(8,128)(2,1)S(1)} %all_to_all.27.source), custom_call_target="tpu_custom_call" | custom-call | tf_op jit(solution)/shard_map/join_mine/pallas_call | solution.py:365
  194.3 2.5 %join_theirs.1 = bf16[4,2,256,512]{3,2,1,0:T(8,128)(2,1)} custom-call(s32[2]{0:T(128)S(1)} %pad_add_fusion.where, bf16[4,4,256,128]{3,2,1,0:T(8,128)(2,1)S(1)} %collective-permute-done.9.source, bf16[4,2,256,512]{3,2,1,0:T(8,128)(2,1)} %join_mine.1.begun), custom_call_target="tpu_custom_call", output_to_operand_aliasing={{}: (2, {})} | custom-call | tf_op jit(solution)/shard_map/join_theirs/pallas_call | solution.py:377
  (40 shorter events, 5.3 us)
Async XLA Ops:
  0.6 54.6 %collective-permute-start.2 = (bf16[256,2048]{1,0:T(8,128)(2,1)}, bf16[256,2048]{1,0:T(8,128)(2,1)S(1)}, u32[]{:S(2)}, u32[]{:S(2)}) collective-permute-start(bf16[256,2048]{1,0:T(8,128)(2,1)} %bitcast.37), channel_id=1, source_target_pairs={{0,384},{128,0},{256,128},{384,256},{1,385},{129,1},{257,129},{385... | collective-permute-start | bytes 3145736 | tf_op jit(solution)/shard_map/ppermute | solution.py:248
  6.1 51.9 %collective-permute-start.1 = (bf16[256,2048]{1,0:T(8,128)(2,1)}, bf16[256,2048]{1,0:T(8,128)(2,1)S(1)}, u32[]{:S(2)}, u32[]{:S(2)}) collective-permute-start(bf16[256,2048]{1,0:T(8,128)(2,1)} %bitcast.38), channel_id=1, source_target_pairs={{0,128},{128,256},{256,384},{384,0},{1,129},{129,257},{257,385},{3... | collective-permute-start | bytes 3145736 | tf_op jit(solution)/shard_map/ppermute | solution.py:247
  10.6 70.5 %copy-start = (bf16[1,1,256,2048]{3,2,1,0:T(8,128)(2,1)S(1)}, bf16[1,1,256,2048]{3,2,1,0:T(8,128)(2,1)}, u32[]{:S(2)}) copy-start(bf16[1,1,256,2048]{3,2,1,0:T(8,128)(2,1)} %param.9) | copy-start | bytes 3145732
  34.0 0.7 copy-start.5
  35.2 0.7 copy-start.1
  35.9 37.0 %all-to-all-start.1 = ((bf16[64,16,128]{2,1,0:T(8,128)(2,1)}), bf16[64,16,128]{2,1,0:T(8,128)(2,1)}, u32[]{:S(2)}, u32[]{:S(2)}) async-start(bf16[64,16,128]{2,1,0:T(8,128)(2,1)} %copy-done.1), calls=%async_computation.1 | async-start | bytes 524288 | tf_op jit(solution)/shard_map/all_to_all | solution.py:267
  56.1 25.0 %collective-permute-start.4 = (bf16[128,2048]{1,0:T(8,128)(2,1)}, bf16[128,2048]{1,0:T(8,128)(2,1)}, u32[]{:S(2)}, u32[]{:S(2)}) collective-permute-start(bf16[128,2048]{1,0:T(8,128)(2,1)} %slice.9), channel_id=1, source_target_pairs={{0,384},{128,0},{256,128},{384,256},{1,385},{129,1},{257,129},{385... | collective-permute-start | bytes 1572872 | tf_op jit(solution)/shard_map/ppermute | solution.py:269
  58.9 22.3 %collective-permute-start.3 = (bf16[128,2048]{1,0:T(8,128)(2,1)}, bf16[128,2048]{1,0:T(8,128)(2,1)}, u32[]{:S(2)}, u32[]{:S(2)}) collective-permute-start(bf16[128,2048]{1,0:T(8,128)(2,1)} %slice.8), channel_id=1, source_target_pairs={{0,128},{128,256},{256,384},{384,0},{1,129},{129,257},{257,385},{3... | collective-permute-start | bytes 1572872 | tf_op jit(solution)/shard_map/ppermute | solution.py:268
  73.9 7.2 %collective-permute-start = (bf16[4,256,128]{2,1,0:T(8,128)(2,1)S(1)}, bf16[4,256,128]{2,1,0:T(8,128)(2,1)S(1)}, u32[]{:S(2)}, u32[]{:S(2)}) collective-permute-start(bf16[4,256,128]{2,1,0:T(8,128)(2,1)S(1)} %bitcast.41), channel_id=1, source_target_pairs={{0,64},{64,0},{1,65},{65,1},{2,66},{66,2},{3,67},{67,3},{4,68},{68... | collective-permute-start | bytes 786440 | tf_op jit(solution)/shard_map/ppermute | solution.py:279
  84.4 4.2 %collective-permute-start.5 = (f32[64,16,128]{2,1,0:T(8,128)S(1)}, f32[64,16,128]{2,1,0:T(8,128)S(1)}, u32[]{:S(2)}, u32[]{:S(2)}) collective-permute-start(f32[64,16,128]{2,1,0:T(8,128)S(1)} %get-tuple-element.12), channel_id=1, source_target_pairs={{0,64},{64,0},{1,65},{65,1},{2,66},{66,2},{3,67},{67,3},{4,68},{68... | collective-permute-start | bytes 1572872 | tf_op jit(solution)/shard_map/ppermute | solution.py:294
  88.5 10.6 %copy-start.2 = (f32[16,4,512]{2,1,0:T(4,128)S(1)}, f32[16,4,512]{2,1,0:T(4,128)}, u32[]{:S(2)}) copy-start(f32[16,4,512]{2,1,0:T(4,128)} %refs_0_.1) | copy-start | bytes 393220
  88.5 10.6 %copy-start.3 = (f32[16,4,512]{2,1,0:T(4,128)S(1)}, f32[16,4,512]{2,1,0:T(4,128)}, u32[]{:S(2)}) copy-start(f32[16,4,512]{2,1,0:T(4,128)} %refs_1_.1) | copy-start | bytes 393220
  88.5 10.6 %copy-start.4 = (f32[16,4,512]{2,1,0:T(4,128)S(1)}, f32[16,4,512]{2,1,0:T(4,128)}, u32[]{:S(2)}) copy-start(f32[16,4,512]{2,1,0:T(4,128)} %refs_2_.1) | copy-start | bytes 393220
  88.6 19.3 %copy-start.8 = (s32[8,64]{1,0:T(8,128)S(1)}, s32[8,64]{1,0:T(8,128)}, u32[]{:S(2)}) copy-start(s32[8,64]{1,0:T(8,128)} %counts.1) | copy-start | bytes 6148
  88.6 19.3 %copy-start.6 = (s32[64]{0:T(128)S(1)}, s32[64]{0:T(128)}, u32[]{:S(2)}) copy-start(s32[64]{0:T(128)} %old.1) | copy-start | bytes 772
  88.6 40.5 %copy-start.7 = (s32[64]{0:T(128)S(1)}, s32[64]{0:T(128)}, u32[]{:S(2)}) copy-start(s32[64]{0:T(128)} %new.1) | copy-start | bytes 772
  89.5 39.7 %all-to-all-start.2 = ((f32[64,16,128]{2,1,0:T(8,128)}), f32[64,16,128]{2,1,0:T(8,128)S(1)}, u32[]{:S(2)}, u32[]{:S(2)}) async-start(f32[64,16,128]{2,1,0:T(8,128)} %add.57), calls=%async_computation.2 | async-start | bytes 1048576 | tf_op jit(solution)/shard_map/all_to_all | solution.py:322
  99.5 8.6 %collective-permute-start.8 = (f32[3,16,4,128]{3,2,1,0:T(4,128)S(1)}, f32[3,16,4,128]{3,2,1,0:T(4,128)S(1)}, u32[]{:S(2)}, u32[]{:S(2)}) collective-permute-start(f32[3,16,4,128]{3,2,1,0:T(4,128)S(1)} %get-tuple-element.22), channel_id=1, source_target_pairs={{0,256},{128,384},{256,0},{384,128},{1,257},{129,385},{257,1},{385... | collective-permute-start | bytes 294920 | tf_op jit(solution)/shard_map/ppermute | solution.py:319
  101.9 6.1 %collective-permute-start.7 = (f32[3,16,4,128]{3,2,1,0:T(4,128)S(1)}, f32[3,16,4,128]{3,2,1,0:T(4,128)S(1)}, u32[]{:S(2)}, u32[]{:S(2)}) collective-permute-start(f32[3,16,4,128]{3,2,1,0:T(4,128)S(1)} %get-tuple-element.23), channel_id=1, source_target_pairs={{0,384},{128,0},{256,128},{384,256},{1,385},{129,1},{257,129},{385... | collective-permute-start | bytes 294920 | tf_op jit(solution)/shard_map/ppermute | solution.py:318
  105.9 6.9 %collective-permute-start.6 = (f32[3,16,4,128]{3,2,1,0:T(4,128)S(1)}, f32[3,16,4,128]{3,2,1,0:T(4,128)S(1)}, u32[]{:S(2)}, u32[]{:S(2)}) collective-permute-start(f32[3,16,4,128]{3,2,1,0:T(4,128)S(1)} %get-tuple-element.24), channel_id=1, source_target_pairs={{0,128},{128,256},{256,384},{384,0},{1,129},{129,257},{257,385},{3... | collective-permute-start | bytes 294920 | tf_op jit(solution)/shard_map/ppermute | solution.py:317
  171.6 22.7 %collective-permute-start.9 = (bf16[4,4,256,128]{3,2,1,0:T(8,128)(2,1)S(1)}, bf16[4,4,256,128]{3,2,1,0:T(8,128)(2,1)S(1)}, u32[]{:S(2)}, u32[]{:S(2)}) collective-permute-start(bf16[4,4,256,128]{3,2,1,0:T(8,128)(2,1)S(1)} %all_to_all.27.source), channel_id=1, source_target_pairs={{0,64},{64,0},{1,65},{65,1},{2,66},{66,2},{3,67},{67,3},{4,68},{68... | collective-permute-start | bytes 3145736 | tf_op jit(solution)/shard_map/ppermute | solution.py:361
  177.5 8.4 %collective-permute-start.12 = (f32[3,16,4,128]{3,2,1,0:T(4,128)S(1)}, f32[3,16,4,128]{3,2,1,0:T(4,128)S(1)}, u32[]{:S(2)}, u32[]{:S(2)}) collective-permute-start(f32[3,16,4,128]{3,2,1,0:T(4,128)S(1)} %get-tuple-element.18), channel_id=1, source_target_pairs={{0,256},{128,384},{256,0},{384,128},{1,257},{129,385},{257,1},{385... | collective-permute-start | bytes 294920 | tf_op jit(solution)/shard_map/ppermute | solution.py:346
  180.0 6.0 %collective-permute-start.11 = (f32[3,16,4,128]{3,2,1,0:T(4,128)S(1)}, f32[3,16,4,128]{3,2,1,0:T(4,128)S(1)}, u32[]{:S(2)}, u32[]{:S(2)}) collective-permute-start(f32[3,16,4,128]{3,2,1,0:T(4,128)S(1)} %get-tuple-element.19), channel_id=1, source_target_pairs={{0,384},{128,0},{256,128},{384,256},{1,385},{129,1},{257,129},{385... | collective-permute-start | bytes 294920 | tf_op jit(solution)/shard_map/ppermute | solution.py:345
  184.0 6.9 %collective-permute-start.10 = (f32[3,16,4,128]{3,2,1,0:T(4,128)S(1)}, f32[3,16,4,128]{3,2,1,0:T(4,128)S(1)}, u32[]{:S(2)}, u32[]{:S(2)}) collective-permute-start(f32[3,16,4,128]{3,2,1,0:T(4,128)S(1)} %get-tuple-element.20), channel_id=1, source_target_pairs={{0,128},{128,256},{256,384},{384,0},{1,129},{129,257},{257,385},{3... | collective-permute-start | bytes 294920 | tf_op jit(solution)/shard_map/ppermute | solution.py:344

commit v4 on v3

--- a/solution.py
+++ b/solution.py
@@ -20,6 +20,7 @@
 DOWN = [(i, (i - 1) % Y) for i in range(Y)]
 ACROSS = [(i, (i + 2) % Y) for i in range(Y)]
 SWAP = [(0, 1), (1, 0)]
+LINE = ((0, None), (3, 0), (3, 1), (1, 0), (1, 1), (2, 0), (2, 1))
 VMEM = pl.BlockSpec(memory_space=pltpu.VMEM)
 SMEM = pl.BlockSpec(memory_space=pltpu.SMEM)
 ANY = pl.BlockSpec(memory_space=pl.ANY)
@@ -50,9 +51,9 @@
             out[2 * pair + 1, n] = jnp.where(low, swapped(gate), up)
 
 
-def join_cols(y_ref, own, low, high, far, *refs):
+def join_cols(own, low, high, far, *refs):
     outs, parts = refs[:-1], refs[-1]
-    y = y_ref[0]
+    y = lax.axis_index("y")
     parts[y] = own[...]
     parts[(y + 3) % Y] = low[...]
     parts[(y + 1) % Y] = high[...]
@@ -69,12 +70,13 @@
             )
 
 
-def prepare(where, counts, order, hidden, master, out):
+def prepare(counts, order, hidden, master, out):
     batches, batch_rows = order.shape
     experts, rows_shard, width = master.shape
     lanes = out.shape[-1]
     half = width // 2
-    count = counts[where[0], where[1]]
+    group_here = lax.axis_index("y") * C + lax.axis_index("core")
+    count = counts[group_here, lax.axis_index("x") * Z + lax.axis_index("z")]
     blocks = []
     for m in range(batches):
         at = m * batch_rows
@@ -105,7 +107,7 @@
         out[2 * pair + 1, :weights, :] = jnp.where(first, swapped(gate), up).astype(jnp.bfloat16)
 
 
-def pick_old(slots, payload, out, table):
+def pick_old(slots, payload, out, table, picked, sem):
     experts, rows, _ = table.shape
     rows_shard = rows // Y
     parts = [payload[y, : experts * rows_shard, :].astype(jnp.float32) for y in range(Y)]
@@ -114,13 +116,16 @@
             [part[e * rows_shard : (e + 1) * rows_shard] for part in parts], axis=0
         ).astype(jnp.bfloat16)
     for p in range(PLACES):
-        out[p] = table[slots[p]]
-
-
-def adam(old, new, total, y_ref, got, own, low, high, far, out, after, state, acc, table):
+        picked[p] = table[slots[p]]
+    copy = pltpu.make_async_copy(picked, out, sem)
+    copy.start()
+    copy.wait()
+
+
+def adam(old, new, total, got, own, low, high, far, out, after, state, acc, table):
     experts = acc.shape[0]
     rows = state.shape[3]
-    y_here = y_ref[0]
+    y_here = lax.axis_index("y")
     state[y_here] = own[...]
     state[(y_here + 3) % Y] = low[...]
     state[(y_here + 1) % Y] = high[...]
@@ -148,7 +153,9 @@
         out[p] = table[new[p]]
 
 
-def half_grad(out_ref, local_ref, chunks, half, wide):
+def half_grad(out_ref, local_ref, chunks, half):
+    rows_shard = out_ref.shape[1] // Y
+    wide = PLACES * rows_shard
     for y in range(Y):
         at = pl.multiple_of((2 * y + half) * wide, wide)
         total, row = None, 0
@@ -161,21 +168,28 @@
             )
             total = term if total is None else total + term
             row += rows
-        out_ref[:, 4 * y : 4 * y + 4, :] = total.T.reshape(wide // 4, 4, -1)
-
-
-def grad_theirs(where, mine, theirs, payload, *refs):
+        out_ref[:, y * rows_shard : (y + 1) * rows_shard, :] = total.T.reshape(
+            PLACES, rows_shard, -1
+        )
+
+
+def grad_theirs(mine, theirs, payload, *refs):
     chunks, (out_ref, local_ref, w_ref) = refs[:-3], refs[-3:]
-    y_here, core = where[0], where[1]
-    wide = mine.shape[1]
-    for y in range(Y):
-        w_ref[pl.ds(pl.multiple_of((2 * y + core) * wide, wide), wide), :] = mine[y]
-        w_ref[pl.ds(pl.multiple_of((2 * y + 1 - core) * wide, wide), wide), :] = theirs[y]
-    sources = [y_here, (y_here + 3) % Y, (y_here + 1) % Y, (y_here + 2) % Y, (y_here + 2) % Y]
+    y_here, core = lax.axis_index("y"), lax.axis_index("core")
+    rows_shard = mine.shape[1] // Y
+    wide = PLACES * rows_shard
+    for source, which in ((mine, core), (theirs, 1 - core)):
+        block = source[...].astype(jnp.float32)
+        for y in range(Y):
+            w_ref[pl.ds(pl.multiple_of((2 * y + which) * wide, wide), wide), :] = (
+                block[:, y * rows_shard : (y + 1) * rows_shard, :]
+                .reshape(wide, -1)
+                .astype(jnp.bfloat16)
+            )
     packed = chunks[-1].shape[0]
     weights = payload.shape[1] - packed
     row = 0
-    for k, chunk in enumerate(chunks):
+    for (step, part), chunk in zip(LINE, chunks):
         rows = chunk.shape[0]
         both = jnp.dot(chunk[...], w_ref[...], preferred_element_type=jnp.float32)
         other = swapped(both)
@@ -184,89 +198,94 @@
         sigma = jax.nn.sigmoid(gate)
         active = gate * sigma
         slope = sigma * (1.0 + gate * (1.0 - sigma))
-        hidden = payload[sources[k], weights:, :].astype(jnp.float32)
+        hidden = payload[(y_here + step) % Y, weights:, :].astype(jnp.float32)
         around = swapped(hidden)
         begin = lower_half(hidden)
         halves = [jnp.where(begin, hidden, around), jnp.where(begin, around, hidden)]
-        if rows > packed:
-            incoming = jnp.concatenate(halves, axis=0)
-        else:
-            incoming = halves[k - 3]
+        incoming = jnp.concatenate(halves, axis=0) if part is None else halves[part]
         local = jnp.where(first, incoming * other * slope, incoming * active)
         local_ref[:, row : row + rows] = local.T.astype(jnp.bfloat16)
         row += rows
-    half_grad(out_ref, local_ref, chunks, 1 - core, wide)
-
-
-def grad_mine(where, local_ref, *refs):
+    half_grad(out_ref, local_ref, chunks, 1 - core)
+
+
+def grad_mine(local_ref, *refs):
     chunks, out_ref = refs[:-1], refs[-1]
-    half_grad(out_ref, local_ref, chunks, where[1], out_ref.shape[0] * 4)
-
-
-def joined(out, source):
+    half_grad(out_ref, local_ref, chunks, lax.axis_index("core"))
+
+
+def join(source, out, which, blocks, sems):
     lanes = source.shape[-1]
     half = out.shape[-1] // 2
-    for pair in range(Y // 2):
-        a = source[2 * pair, 0].astype(jnp.float32)
-        b = source[2 * pair + 1, 0].astype(jnp.float32)
-        first = lower_half(a)
-        out[0, 0, :, pair * lanes : (pair + 1) * lanes] = jnp.where(
-            first, a, swapped(b)
-        ).astype(jnp.bfloat16)
-        out[0, 0, :, half + pair * lanes : half + (pair + 1) * lanes] = jnp.where(
-            first, swapped(a), b
-        ).astype(jnp.bfloat16)
-
-
-def join_mine(where, source, out):
-    joined(out, source)
-
-
-def join_theirs(where, source, begun, out):
-    joined(out, source)
+    copies = []
+    for y in range(Y):
+        for pair in range(Y // 2):
+            a = source[2 * pair, y].astype(jnp.float32)
+            b = source[2 * pair + 1, y].astype(jnp.float32)
+            first = lower_half(a)
+            blocks[y, :, pair * lanes : (pair + 1) * lanes] = jnp.where(
+                first, a, swapped(b)
+            ).astype(jnp.bfloat16)
+            blocks[y, :, half + pair * lanes : half + (pair + 1) * lanes] = jnp.where(
+                first, swapped(a), b
+            ).astype(jnp.bfloat16)
+        copy = pltpu.make_async_copy(blocks.at[y], out.at[y, which], sems.at[y])
+        copy.start()
+        copies.append(copy)
+    for copy in copies:
+        copy.wait()
+
+
+def join_mine(source, out, blocks, sems):
+    join(source, out, lax.axis_index("core"), blocks, sems)
+
+
+def join_theirs(source, begun, out, blocks, sems):
+    join(source, out, 1 - lax.axis_index("core"), blocks, sems)
 
 
 def shards(
     tokens, hidden_grad, routing, row_count, old_slots, new_slots, master, first_moment, second_moment
 ):
-    y, core = lax.axis_index("y"), lax.axis_index("core")
-    group_here = y * C + core
-    place_here = lax.axis_index("x") * Z + lax.axis_index("z")
+    y = lax.axis_index("y")
     experts, rows_shard, width = master.shape
     hid = width // 2
     part = hid // Y
     lanes = 2 * part
     f32, bf16 = jnp.float32, jnp.bfloat16
-    where = jnp.stack([y, core]).astype(jnp.int32)
-    y_id = y.astype(jnp.int32).reshape(1)
-    spot = jnp.stack([group_here, place_here]).astype(jnp.int32)
-
     own = tokens[0, 0]
     rows = own.shape[0]
     half_rows = rows // 2
-    low = lax.ppermute(own, "y", UP)
-    high = lax.ppermute(own, "y", DOWN)
+    own_a, own_b = own[:half_rows], own[half_rows:]
 
     payload = pl.pallas_call(
         prepare,
         out_shape=jax.ShapeDtypeStruct((Y, experts * rows_shard + half_rows, lanes), bf16),
-        in_specs=[SMEM, SMEM, VMEM, VMEM, VMEM],
+        in_specs=[SMEM, VMEM, VMEM, VMEM],
         out_specs=VMEM,
         name="prepare",
-    )(spot, row_count, routing[0, 0], hidden_grad[0, 0], master)
+    )(row_count, routing[0, 0], hidden_grad[0, 0], master)
     payload = lax.all_to_all(payload, "y", 0, 0, tiled=True)
+    low_a = lax.ppermute(own_a, "y", UP)
+    high_b = lax.ppermute(own_b, "y", DOWN)
+    low_b = lax.ppermute(own_b, "y", UP)
+    high_a = lax.ppermute(own_a, "y", DOWN)
     picked = pl.pallas_call(
         pick_old,
         out_shape=jax.ShapeDtypeStruct((PLACES, Y * rows_shard, lanes), bf16),
         in_specs=[SMEM, VMEM],
-        out_specs=VMEM,
-        scratch_shapes=[pltpu.VMEM((experts, Y * rows_shard, lanes), bf16)],
+        out_specs=pl.BlockSpec(memory_space=pltpu.MemorySpace.HBM),
+        scratch_shapes=[
+            pltpu.VMEM((experts, Y * rows_shard, lanes), bf16),
+            pltpu.VMEM((PLACES, Y * rows_shard, lanes), bf16),
+            pltpu.SemaphoreType.DMA(()),
+        ],
         compiler_params=grant(4),
         name="pick_old",
     )(old_slots, payload)
     landed = lax.all_to_all(picked, ("x", "z"), 0, 0, tiled=True)
-    far_a = lax.ppermute(low[:half_rows], "y", UP)
-    far_b = lax.ppermute(high[half_rows:], "y", DOWN)
+    far_a = lax.ppermute(low_a, "y", UP)
+    far_b = lax.ppermute(high_b, "y", DOWN)
 
     def by_rows(x):
         return (
@@ -275,31 +294,31 @@
             .reshape(Y, PLACES * rows_shard, lanes)
         )
 
-    w_mine = by_rows(landed)
+    w_mine = landed
     w_theirs = lax.ppermute(w_mine, "core", SWAP)
 
-    chunks = [own, low, high, far_a, far_b]
+    chunks = [own, low_a, low_b, high_a, high_b, far_a, far_b]
     line_rows = sum(c.shape[0] for c in chunks)
     deep = own.shape[1]
     grad_shape = jax.ShapeDtypeStruct((PLACES, Y * rows_shard, lanes), f32)
     sent, local = pl.pallas_call(
         grad_theirs,
         out_shape=(grad_shape, jax.ShapeDtypeStruct((lanes, line_rows), bf16)),
-        in_specs=[SMEM] + [VMEM] * (3 + len(chunks)),
+        in_specs=[VMEM] * (3 + len(chunks)),
         out_specs=(VMEM, VMEM),
         scratch_shapes=[pltpu.VMEM((deep, lanes), bf16)],
         compiler_params=grant(24),
         name="grad_theirs",
-    )(where, w_mine, w_theirs, payload, *chunks)
+    )(w_mine, w_theirs, payload, *chunks)
     received = lax.ppermute(sent, "core", SWAP)
     summed = pl.pallas_call(
         grad_mine,
         out_shape=grad_shape,
-        in_specs=[SMEM] + [VMEM] * (1 + len(chunks)),
+        in_specs=[VMEM] * (1 + len(chunks)),
         out_specs=VMEM,
         compiler_params=grant(24),
         name="grad_mine",
-    )(where, local, *chunks)
+    )(local, *chunks)
     summed = summed + received
 
     columns = pl.pallas_call(
@@ -329,7 +348,7 @@
             jax.ShapeDtypeStruct((PLACES, Y * rows_shard, lanes), bf16),
             jax.ShapeDtypeStruct((Y, 3, experts, rows_shard, lanes), f32),
         ),
-        in_specs=[SMEM] * 4 + [VMEM] * 5,
+        in_specs=[SMEM] * 3 + [VMEM] * 5,
         out_specs=(VMEM, VMEM),
         scratch_shapes=[
             pltpu.VMEM((Y, 3, experts, rows_shard, lanes), f32),
@@ -338,7 +357,7 @@
         ],
         compiler_params=grant(6),
         name="adam",
-    )(old_slots, new_slots, total, y_id, got, m_own, m_low, m_high, m_far)
+    )(old_slots, new_slots, total, got, m_own, m_low, m_high, m_far)
     landed = lax.all_to_all(picked, ("x", "z"), 0, 0, tiled=True)
 
     s_low = lax.ppermute(for_chip(1, after), "y", UP)
@@ -348,45 +367,40 @@
     new_master, new_first, new_second = pl.pallas_call(
         join_cols,
         out_shape=(whole,) * 3,
-        in_specs=[SMEM] + [VMEM] * 4,
+        in_specs=[VMEM] * 4,
         out_specs=(VMEM,) * 3,
         scratch_shapes=[pltpu.VMEM((Y, 3, experts, rows_shard, lanes), f32)],
         compiler_params=grant(6),
         name="join_cols",
-    )(y_id, for_chip(0, after), s_low, s_high, s_far)
+    )(for_chip(0, after), s_low, s_high, s_far)
 
     landed = by_rows(landed)
     copies = jnp.broadcast_to(landed[None], (Y, *landed.shape))
     mine = lax.all_to_all(copies, "y", 0, 0, tiled=True)
     theirs = lax.ppermute(mine, "core", SWAP)
     block_rows = PLACES * rows_shard
+    hbm = pl.BlockSpec(memory_space=pltpu.MemorySpace.HBM)
+    scratch = [pltpu.VMEM((Y, block_rows, width), bf16), pltpu.SemaphoreType.DMA((Y,))]
     whole = jax.ShapeDtypeStruct((Y, C, block_rows, width), bf16)
-    block = pl.BlockSpec((Y, 1, block_rows, lanes), lambda i, at: (0, i, 0, 0))
     begun = pl.pallas_call(
         join_mine,
         out_shape=whole,
-        grid_spec=pltpu.PrefetchScalarGridSpec(
-            num_scalar_prefetch=1,
-            grid=(Y,),
-            in_specs=[block],
-            out_specs=pl.BlockSpec((1, 1, block_rows, width), lambda i, at: (i, at[1], 0, 0)),
-        ),
+        in_specs=[VMEM],
+        out_specs=hbm,
+        scratch_shapes=scratch,
         compiler_params=grant(8),
         name="join_mine",
-    )(where, mine)
+    )(mine)
     new_weights = pl.pallas_call(
         join_theirs,
         out_shape=whole,
-        grid_spec=pltpu.PrefetchScalarGridSpec(
-            num_scalar_prefetch=1,
-            grid=(Y,),
-            in_specs=[block, ANY],
-            out_specs=pl.BlockSpec((1, 1, block_rows, width), lambda i, at: (i, 1 - at[1], 0, 0)),
-        ),
-        input_output_aliases={2: 0},
+        in_specs=[VMEM, hbm],
+        out_specs=hbm,
+        scratch_shapes=scratch,
+        input_output_aliases={1: 0},
         compiler_params=grant(8),
         name="join_theirs",
-    )(where, theirs, begun)
+    )(theirs, begun)
     return (new_weights.reshape(1, -1, width), new_master, new_first, new_second)
 
 

time: 198 us -> 197 us (level)
  starting transfers between devices: 72.6 us -> 86.1 us
  blocking collectives: 64.5 us -> 51.4 us
  waiting for transfers between devices: 37.7 us -> 40.5 us
  local copies, waits for them, and re-layouts: 4.47 us -> 2.13 us
    ppermute x4 -> x6, waiting for transfers between devices: 0.01 us -> 13.6 us  [the longest x1 7.6 us: shards(): far_b = lax.ppermute(high_b, 'y', DOWN)]
    all_to_all x1, blocking collectives: 23.3 us -> 10.2 us  [shards(): payload = lax.all_to_all(payload, 'y', 0, 0, tiled=True)]
    all_to_all x1, waiting for transfers between devices: 10.6 us -> 0.01 us  [shards(): landed = lax.all_to_all(picked, ('x', 'z'), 0, 0, tiled=True)]
    ppermute x4 -> x6, starting transfers between devices: 12.6 us -> 17.7 us  [the longest x1 4.2 us: shards(): high_a = lax.ppermute(own_a, 'y', DOWN)]
    all_to_all x1, starting transfers between devices: 9.57 us -> 14.5 us  [shards(): got = lax.all_to_all(summed, ('x', 'z'), 0, 0, tiled=True)]
    ppermute x1, starting transfers between devices: 2.28 us -> 5.43 us  [shards(): received = lax.ppermute(sent, 'core', SWAP)]
    pallas_call x4, Pallas kernels: 7.74 us -> 5.31 us  [the longest x1 1.96 us: shards(): pl.pallas_call(grad_mine, out_shape=grad_shape, in_specs=[VMEM] * (1 + le...]
    ppermute x1, starting transfers between devices: 6.1 us -> 8.15 us  [shards(): w_theirs = lax.ppermute(w_mine, 'core', SWAP)]
  transfers between devices with their start and end apart: 15 -> 17, of which waited for: 5 -> 7; matrix products, arithmetic and copies ran while one was open for 2% -> 1% of each run, Pallas kernels for 4% -> 2%
where the time goes in v4:
time: 197 us; the launch traced here: 195 us
  starting transfers between devices  86.1 us (44%)
  blocking collectives  51.4 us (26%)
  waiting for transfers between devices  40.5 us (21%)
  Pallas kernels  13.3 us (7%)
  local copies, waits for them, and re-layouts  2.13 us (1%)
    all_to_all x1, blocking collectives, shards(): landed = lax.all_to_all(picked, ('x', 'z'), 0, 0, tiled=True)  26.7 us
    all_to_all x1, starting transfers between devices, shards(): landed = lax.all_to_all(picked, ('x', 'z'), 0, 0, tiled=True)  18.6 us
    all_to_all x1, waiting for transfers between devices, shards(): got = lax.all_to_all(summed, ('x', 'z'), 0, 0, tiled=True)  17.2 us
    all_to_all x1, blocking collectives, shards(): mine = lax.all_to_all(copies, 'y', 0, 0, tiled=True)  14.5 us
    all_to_all x1, starting transfers between devices, shards(): got = lax.all_to_all(summed, ('x', 'z'), 0, 0, tiled=True)  14.5 us
    all_to_all x1, blocking collectives, shards(): payload = lax.all_to_all(payload, 'y', 0, 0, tiled=True)  10.2 us
    ppermute x1, starting transfers between devices, shards(): w_theirs = lax.ppermute(w_mine, 'core', SWAP)  8.15 us
    ppermute x1, waiting for transfers between devices, shards(): far_b = lax.ppermute(high_b, 'y', DOWN)  7.6 us
  transfers between devices with their start and end apart: 17, of which 7 were waited for; matrix products, arithmetic and copies ran while one was open for 1% of the time, Pallas kernels for 2%

profile of v4, /device:TPU:1, one launch (start us, length us, event | category | flops | bytes accessed | tf_op | source)
XLA Modules:
  0.0 195.4 jit_solution(3640643417014519335)
XLA Ops:
  0.6 2.0 %prepare.1 = bf16[4,192,128]{2,1,0:T(8,128)(2,1)} custom-call(s32[8,64]{1,0:T(8,128)} %counts.1, s32[4,64]{1,0:T(4,128)} %bitcast.39, bf16[256,256]{1,0:T(8,128)(2,1)} %bitcast.38, f32[16,4,512]{2,1,0:T(4,128)} %refs_0_.1), custom_call_target="tpu_custom_call" | custom-call | tf_op jit(solution)/shard_map/prepare/pallas_call | solution.py:261
  2.7 10.2 %all_to_all.25.payload = bf16[4,192,128]{2,1,0:T(8,128)(2,1)S(1)} all-to-all(bf16[4,192,128]{2,1,0:T(8,128)(2,1)} %prepare.1), channel_id=1, replica_groups=mesh['y'=4,'core'=2,'x'=4,'z'=16] {'y'}, dimensions={0} | all-to-all | bytes 393216 | tf_op jit(solution)/shard_map/all_to_all | solution.py:268
  13.5 1.3 pick_old.1
  14.8 18.6 %all-to-all-start.1 = ((bf16[64,16,128]{2,1,0:T(8,128)(2,1)}), bf16[64,16,128]{2,1,0:T(8,128)(2,1)}, u32[]{:S(2)}, u32[]{:S(2)}) async-start(bf16[64,16,128]{2,1,0:T(8,128)(2,1)} %pick_old.1), calls=%async_computation.1 | async-start | bytes 524288 | tf_op jit(solution)/shard_map/all_to_all | solution.py:286
  34.5 2.8 %collective-permute-start.4 = (bf16[128,2048]{1,0:T(8,128)(2,1)}, bf16[128,2048]{1,0:T(8,128)(2,1)S(1)}, u32[]{:S(2)}, u32[]{:S(2)}) collective-permute-start(bf16[128,2048]{1,0:T(8,128)(2,1)} %get-tuple-element.18), channel_id=1, source_target_pairs={{0,384},{128,0},{256,128},{384,256},{1,385},{129,1},{257,129},{385... | collective-permute-start | bytes 1572872 | tf_op jit(solution)/shard_map/ppermute | solution.py:270
  37.3 2.5 %collective-permute-start.1 = (bf16[128,2048]{1,0:T(8,128)(2,1)}, bf16[128,2048]{1,0:T(8,128)(2,1)S(1)}, u32[]{:S(2)}, u32[]{:S(2)}) collective-permute-start(bf16[128,2048]{1,0:T(8,128)(2,1)} %get-tuple-element.19), channel_id=1, source_target_pairs={{0,128},{128,256},{256,384},{384,0},{1,129},{129,257},{257,385},{3... | collective-permute-start | bytes 1572872 | tf_op jit(solution)/shard_map/ppermute | solution.py:269
  39.7 2.3 %collective-permute-start.2 = (bf16[128,2048]{1,0:T(8,128)(2,1)}, bf16[128,2048]{1,0:T(8,128)(2,1)S(1)}, u32[]{:S(2)}, u32[]{:S(2)}) collective-permute-start(bf16[128,2048]{1,0:T(8,128)(2,1)} %get-tuple-element.18), channel_id=1, source_target_pairs={{0,128},{128,256},{256,384},{384,0},{1,129},{129,257},{257,385},{3... | collective-permute-start | bytes 1572872 | tf_op jit(solution)/shard_map/ppermute | solution.py:271
  42.0 4.2 %collective-permute-start.3 = (bf16[128,2048]{1,0:T(8,128)(2,1)}, bf16[128,2048]{1,0:T(8,128)(2,1)S(1)}, u32[]{:S(2)}, u32[]{:S(2)}) collective-permute-start(bf16[128,2048]{1,0:T(8,128)(2,1)} %get-tuple-element.19), channel_id=1, source_target_pairs={{0,384},{128,0},{256,128},{384,256},{1,385},{129,1},{257,129},{385... | collective-permute-start | bytes 1572872 | tf_op jit(solution)/shard_map/ppermute | solution.py:272
  46.3 1.5 collective-permute-done.4.refs_4_
  47.8 4.0 %collective-permute-start.6 = (bf16[128,2048]{1,0:T(8,128)(2,1)S(1)}, bf16[128,2048]{1,0:T(8,128)(2,1)}, u32[]{:S(2)}, u32[]{:S(2)}) collective-permute-start(bf16[128,2048]{1,0:T(8,128)(2,1)S(1)} %collective-permute-done.4.refs_4_), channel_id=1, source_target_pairs={{0,384},{128,0},{256,128},{384,256},{1,385},{129,1},{257,129},{385... | collective-permute-start | bytes 1572872 | tf_op jit(solution)/shard_map/ppermute | solution.py:288
  51.8 1.9 collective-permute-start.5
  53.7 8.2 %collective-permute-start = (bf16[64,16,128]{2,1,0:T(8,128)(2,1)}, bf16[64,16,128]{2,1,0:T(8,128)(2,1)S(1)}, u32[]{:S(2)}, u32[]{:S(2)}) collective-permute-start(bf16[64,16,128]{2,1,0:T(8,128)(2,1)} %all-to-all-done.1.mine), channel_id=1, source_target_pairs={{0,64},{64,0},{1,65},{65,1},{2,66},{66,2},{3,67},{67,3},{4,68},{68... | collective-permute-start | bytes 786440 | tf_op jit(solution)/shard_map/ppermute | solution.py:298
  62.6 7.6 %collective-permute-done.6.refs_6_ = bf16[128,2048]{1,0:T(8,128)(2,1)} collective-permute-done((bf16[128,2048]{1,0:T(8,128)(2,1)S(1)}, bf16[128,2048]{1,0:T(8,128)(2,1)}, u32[]{:S(2)}, u32[]{:S(2)}) %collective-permute-start.6) | collective-permute-done | bytes 524320 | tf_op jit(solution)/shard_map/ppermute | solution.py:288
  70.2 3.7 %collective-permute-done.5.refs_5_ = bf16[128,2048]{1,0:T(8,128)(2,1)} collective-permute-done((bf16[128,2048]{1,0:T(8,128)(2,1)S(1)}, bf16[128,2048]{1,0:T(8,128)(2,1)}, u32[]{:S(2)}, u32[]{:S(2)}) %collective-permute-start.5) | collective-permute-done | bytes 524320 | tf_op jit(solution)/shard_map/ppermute | solution.py:287
  74.0 3.4 %grad_theirs.1 = (f32[64,16,128]{2,1,0:T(8,128)S(1)}, bf16[128,1024]{1,0:T(8,128)(2,1)S(1)}) custom-call(bf16[64,16,128]{2,1,0:T(8,128)(2,1)} %all-to-all-done.1.mine, bf16[64,16,128]{2,1,0:T(8,128)(2,1)S(1)} %collective-permute-done.theirs, bf16[4,192,128]{2,1,0:T(8,128)(2,1)S(1)} %all_to_all.25.payload, bf16[256,2048]{1,0:T(8,128)(2,1)S(1)} %bitcast.33, ...), custom_call_target="tpu_custom_call" | custom-call | tf_op jit(solution)/shard_map/grad_theirs/pallas_call | solution.py:304
  77.4 5.4 %collective-permute-start.7 = (f32[64,16,128]{2,1,0:T(8,128)S(1)}, f32[64,16,128]{2,1,0:T(8,128)S(1)}, u32[]{:S(2)}, u32[]{:S(2)}) collective-permute-start(f32[64,16,128]{2,1,0:T(8,128)S(1)} %get-tuple-element.12), channel_id=1, source_target_pairs={{0,64},{64,0},{1,65},{65,1},{2,66},{66,2},{3,67},{67,3},{4,68},{68... | collective-permute-start | bytes 1572872 | tf_op jit(solution)/shard_map/ppermute | solution.py:313
  82.8 2.0 %grad_mine.1 = f32[64,16,128]{2,1,0:T(8,128)S(1)} custom-call(bf16[128,1024]{1,0:T(8,128)(2,1)S(1)} %get-tuple-element.11.local_ref, bf16[256,2048]{1,0:T(8,128)(2,1)S(1)} %bitcast.34, bf16[128,2048]{1,0:T(8,128)(2,1)S(1)} %collective-permute-done.1.refs_1_, bf16[128,2048]{1,0:T(8,128)(2,1)S(1)} %collective-permute-done.2.refs_2_, ...), custom_call_target="tpu_custom_call" | custom-call | tf_op jit(solution)/shard_map/grad_mine/pallas_call | solution.py:314
  85.7 14.5 %all-to-all-start.2 = ((f32[64,16,128]{2,1,0:T(8,128)}), f32[64,16,128]{2,1,0:T(8,128)S(1)}, u32[]{:S(2)}, u32[]{:S(2)}) async-start(f32[64,16,128]{2,1,0:T(8,128)} %add.49), calls=%async_computation.2 | async-start | bytes 1048576 | tf_op jit(solution)/shard_map/all_to_all | solution.py:341
  100.6 2.0 %collective-permute-start.10 = (f32[3,16,4,128]{3,2,1,0:T(4,128)S(1)}, f32[3,16,4,128]{3,2,1,0:T(4,128)S(1)}, u32[]{:S(2)}, u32[]{:S(2)}) collective-permute-start(f32[3,16,4,128]{3,2,1,0:T(4,128)S(1)} %get-tuple-element.24), channel_id=1, source_target_pairs={{0,256},{128,384},{256,0},{384,128},{1,257},{129,385},{257,1},{385... | collective-permute-start | bytes 294920 | tf_op jit(solution)/shard_map/ppermute | solution.py:338
  102.6 3.6 %collective-permute-start.9 = (f32[3,16,4,128]{3,2,1,0:T(4,128)S(1)}, f32[3,16,4,128]{3,2,1,0:T(4,128)S(1)}, u32[]{:S(2)}, u32[]{:S(2)}) collective-permute-start(f32[3,16,4,128]{3,2,1,0:T(4,128)S(1)} %get-tuple-element.25), channel_id=1, source_target_pairs={{0,384},{128,0},{256,128},{384,256},{1,385},{129,1},{257,129},{385... | collective-permute-start | bytes 294920 | tf_op jit(solution)/shard_map/ppermute | solution.py:337
  106.2 1.9 collective-permute-start.8
  108.4 4.7 %collective-permute-done.8.low = f32[3,16,4,128]{3,2,1,0:T(4,128)S(1)} collective-permute-done((f32[3,16,4,128]{3,2,1,0:T(4,128)S(1)}, f32[3,16,4,128]{3,2,1,0:T(4,128)S(1)}, u32[]{:S(2)}, u32[]{:S(2)}) %collective-permute-start.8) | collective-permute-done | bytes 98336 | tf_op jit(solution)/shard_map/ppermute | solution.py:336
  113.1 17.2 %all-to-all-done.2.got = f32[64,16,128]{2,1,0:T(8,128)S(1)} async-done(((f32[64,16,128]{2,1,0:T(8,128)}), f32[64,16,128]{2,1,0:T(8,128)S(1)}, u32[]{:S(2)}, u32[]{:S(2)}) %all-to-all-start.2) | async-done | bytes 524320 | tf_op jit(solution)/shard_map/all_to_all | solution.py:341
  131.3 26.7 %all_to_all.26 = bf16[64,16,128]{2,1,0:T(8,128)(2,1)S(1)} all-to-all(bf16[64,16,128]{2,1,0:T(8,128)(2,1)S(1)} %get-tuple-element.13), channel_id=1, replica_groups=mesh['y'=4,'core'=2,'x'=4,'z'=16] {'x','z'}, dimensions={0} | all-to-all | bytes 524288 | tf_op jit(solution)/shard_map/all_to_all | solution.py:361
  158.2 14.5 %all_to_all.27.source = bf16[4,4,256,128]{3,2,1,0:T(8,128)(2,1)S(1)} all-to-all(bf16[4,4,256,128]{3,2,1,0:T(8,128)(2,1)S(1)} %broadcast_in_dim.10), channel_id=1, replica_groups=mesh['y'=4,'core'=2,'x'=4,'z'=16] {'y'}, dimensions={0} | all-to-all | bytes 2097152 | tf_op jit(solution)/shard_map/all_to_all | solution.py:379
  172.8 5.8 %collective-permute-start.11 = (bf16[4,4,256,128]{3,2,1,0:T(8,128)(2,1)S(1)}, bf16[4,4,256,128]{3,2,1,0:T(8,128)(2,1)S(1)}, u32[]{:S(2)}, u32[]{:S(2)}) collective-permute-start(bf16[4,4,256,128]{3,2,1,0:T(8,128)(2,1)S(1)} %all_to_all.27.source), channel_id=1, source_target_pairs={{0,64},{64,0},{1,65},{65,1},{2,66},{66,2},{3,67},{67,3},{4,68},{68... | collective-permute-start | bytes 3145736 | tf_op jit(solution)/shard_map/ppermute | solution.py:380
  178.7 2.4 %collective-permute-start.14 = (f32[3,16,4,128]{3,2,1,0:T(4,128)S(1)}, f32[3,16,4,128]{3,2,1,0:T(4,128)S(1)}, u32[]{:S(2)}, u32[]{:S(2)}) collective-permute-start(f32[3,16,4,128]{3,2,1,0:T(4,128)S(1)} %get-tuple-element.20), channel_id=1, source_target_pairs={{0,256},{128,384},{256,0},{384,128},{1,257},{129,385},{257,1},{385... | collective-permute-start | bytes 294920 | tf_op jit(solution)/shard_map/ppermute | solution.py:365
  181.1 4.0 %collective-permute-start.13 = (f32[3,16,4,128]{3,2,1,0:T(4,128)S(1)}, f32[3,16,4,128]{3,2,1,0:T(4,128)S(1)}, u32[]{:S(2)}, u32[]{:S(2)}) collective-permute-start(f32[3,16,4,128]{3,2,1,0:T(4,128)S(1)} %get-tuple-element.21), channel_id=1, source_target_pairs={{0,384},{128,0},{256,128},{384,256},{1,385},{129,1},{257,129},{385... | collective-permute-start | bytes 294920 | tf_op jit(solution)/shard_map/ppermute | solution.py:364
  185.2 1.9 collective-permute-start.12
  187.1 4.9 %collective-permute-done.12.low = f32[3,16,4,128]{3,2,1,0:T(4,128)S(1)} collective-permute-done((f32[3,16,4,128]{3,2,1,0:T(4,128)S(1)}, f32[3,16,4,128]{3,2,1,0:T(4,128)S(1)}, u32[]{:S(2)}, u32[]{:S(2)}) %collective-permute-start.12) | collective-permute-done | bytes 98336 | tf_op jit(solution)/shard_map/ppermute | solution.py:363
  193.0 1.2 join_mine.1.begun
  194.2 1.2 join_theirs.1
  (38 shorter events, 6.2 us)
Async XLA Ops:
  0.6 32.8 %copy-start = (bf16[1,1,256,2048]{3,2,1,0:T(8,128)(2,1)S(1)}, bf16[1,1,256,2048]{3,2,1,0:T(8,128)(2,1)}, u32[]{:S(2)}) copy-start(bf16[1,1,256,2048]{3,2,1,0:T(8,128)(2,1)} %param.9) | copy-start | bytes 3145732
  12.8 0.7 copy-start.4
  14.8 38.9 %all-to-all-start.1 = ((bf16[64,16,128]{2,1,0:T(8,128)(2,1)}), bf16[64,16,128]{2,1,0:T(8,128)(2,1)}, u32[]{:S(2)}, u32[]{:S(2)}) async-start(bf16[64,16,128]{2,1,0:T(8,128)(2,1)} %pick_old.1), calls=%async_computation.1 | async-start | bytes 524288 | tf_op jit(solution)/shard_map/all_to_all | solution.py:286
  34.5 13.3 %collective-permute-start.4 = (bf16[128,2048]{1,0:T(8,128)(2,1)}, bf16[128,2048]{1,0:T(8,128)(2,1)S(1)}, u32[]{:S(2)}, u32[]{:S(2)}) collective-permute-start(bf16[128,2048]{1,0:T(8,128)(2,1)} %get-tuple-element.18), channel_id=1, source_target_pairs={{0,384},{128,0},{256,128},{384,256},{1,385},{129,1},{257,129},{385... | collective-permute-start | bytes 1572872 | tf_op jit(solution)/shard_map/ppermute | solution.py:270
  37.3 14.5 %collective-permute-start.1 = (bf16[128,2048]{1,0:T(8,128)(2,1)}, bf16[128,2048]{1,0:T(8,128)(2,1)S(1)}, u32[]{:S(2)}, u32[]{:S(2)}) collective-permute-start(bf16[128,2048]{1,0:T(8,128)(2,1)} %get-tuple-element.19), channel_id=1, source_target_pairs={{0,128},{128,256},{256,384},{384,0},{1,129},{129,257},{257,385},{3... | collective-permute-start | bytes 1572872 | tf_op jit(solution)/shard_map/ppermute | solution.py:269
  39.7 22.9 %collective-permute-start.2 = (bf16[128,2048]{1,0:T(8,128)(2,1)}, bf16[128,2048]{1,0:T(8,128)(2,1)S(1)}, u32[]{:S(2)}, u32[]{:S(2)}) collective-permute-start(bf16[128,2048]{1,0:T(8,128)(2,1)} %get-tuple-element.18), channel_id=1, source_target_pairs={{0,128},{128,256},{256,384},{384,0},{1,129},{129,257},{257,385},{3... | collective-permute-start | bytes 1572872 | tf_op jit(solution)/shard_map/ppermute | solution.py:271
  42.0 20.6 %collective-permute-start.3 = (bf16[128,2048]{1,0:T(8,128)(2,1)}, bf16[128,2048]{1,0:T(8,128)(2,1)S(1)}, u32[]{:S(2)}, u32[]{:S(2)}) collective-permute-start(bf16[128,2048]{1,0:T(8,128)(2,1)} %get-tuple-element.19), channel_id=1, source_target_pairs={{0,384},{128,0},{256,128},{384,256},{1,385},{129,1},{257,129},{385... | collective-permute-start | bytes 1572872 | tf_op jit(solution)/shard_map/ppermute | solution.py:272
  47.8 22.5 %collective-permute-start.6 = (bf16[128,2048]{1,0:T(8,128)(2,1)S(1)}, bf16[128,2048]{1,0:T(8,128)(2,1)}, u32[]{:S(2)}, u32[]{:S(2)}) collective-permute-start(bf16[128,2048]{1,0:T(8,128)(2,1)S(1)} %collective-permute-done.4.refs_4_), channel_id=1, source_target_pairs={{0,384},{128,0},{256,128},{384,256},{1,385},{129,1},{257,129},{385... | collective-permute-start | bytes 1572872 | tf_op jit(solution)/shard_map/ppermute | solution.py:288
  51.8 22.2 %collective-permute-start.5 = (bf16[128,2048]{1,0:T(8,128)(2,1)S(1)}, bf16[128,2048]{1,0:T(8,128)(2,1)}, u32[]{:S(2)}, u32[]{:S(2)}) collective-permute-start(bf16[128,2048]{1,0:T(8,128)(2,1)S(1)} %collective-permute-done.1.refs_1_), channel_id=1, source_target_pairs={{0,128},{128,256},{256,384},{384,0},{1,129},{129,257},{257,385},{3... | collective-permute-start | bytes 1572872 | tf_op jit(solution)/shard_map/ppermute | solution.py:287
  53.7 20.3 %collective-permute-start = (bf16[64,16,128]{2,1,0:T(8,128)(2,1)}, bf16[64,16,128]{2,1,0:T(8,128)(2,1)S(1)}, u32[]{:S(2)}, u32[]{:S(2)}) collective-permute-start(bf16[64,16,128]{2,1,0:T(8,128)(2,1)} %all-to-all-done.1.mine), channel_id=1, source_target_pairs={{0,64},{64,0},{1,65},{65,1},{2,66},{66,2},{3,67},{67,3},{4,68},{68... | collective-permute-start | bytes 786440 | tf_op jit(solution)/shard_map/ppermute | solution.py:298
  77.4 7.5 %collective-permute-start.7 = (f32[64,16,128]{2,1,0:T(8,128)S(1)}, f32[64,16,128]{2,1,0:T(8,128)S(1)}, u32[]{:S(2)}, u32[]{:S(2)}) collective-permute-start(f32[64,16,128]{2,1,0:T(8,128)S(1)} %get-tuple-element.12), channel_id=1, source_target_pairs={{0,64},{64,0},{1,65},{65,1},{2,66},{66,2},{3,67},{67,3},{4,68},{68... | collective-permute-start | bytes 1572872 | tf_op jit(solution)/shard_map/ppermute | solution.py:313
  84.8 15.5 %copy-start.1 = (f32[16,4,512]{2,1,0:T(4,128)S(1)}, f32[16,4,512]{2,1,0:T(4,128)}, u32[]{:S(2)}) copy-start(f32[16,4,512]{2,1,0:T(4,128)} %refs_0_.1) | copy-start | bytes 393220
  84.8 15.5 %copy-start.2 = (f32[16,4,512]{2,1,0:T(4,128)S(1)}, f32[16,4,512]{2,1,0:T(4,128)}, u32[]{:S(2)}) copy-start(f32[16,4,512]{2,1,0:T(4,128)} %refs_1_.1) | copy-start | bytes 393220
  84.8 15.5 %copy-start.3 = (f32[16,4,512]{2,1,0:T(4,128)S(1)}, f32[16,4,512]{2,1,0:T(4,128)}, u32[]{:S(2)}) copy-start(f32[16,4,512]{2,1,0:T(4,128)} %refs_2_.1) | copy-start | bytes 393220
  84.8 23.3 %copy-start.7 = (s32[8,64]{1,0:T(8,128)S(1)}, s32[8,64]{1,0:T(8,128)}, u32[]{:S(2)}) copy-start(s32[8,64]{1,0:T(8,128)} %counts.1) | copy-start | bytes 6148
  84.8 23.4 %copy-start.5 = (s32[64]{0:T(128)S(1)}, s32[64]{0:T(128)}, u32[]{:S(2)}) copy-start(s32[64]{0:T(128)} %old.1) | copy-start | bytes 772
  84.8 45.5 %copy-start.6 = (s32[64]{0:T(128)S(1)}, s32[64]{0:T(128)}, u32[]{:S(2)}) copy-start(s32[64]{0:T(128)} %new.1) | copy-start | bytes 772
  85.7 44.6 %all-to-all-start.2 = ((f32[64,16,128]{2,1,0:T(8,128)}), f32[64,16,128]{2,1,0:T(8,128)S(1)}, u32[]{:S(2)}, u32[]{:S(2)}) async-start(f32[64,16,128]{2,1,0:T(8,128)} %add.49), calls=%async_computation.2 | async-start | bytes 1048576 | tf_op jit(solution)/shard_map/all_to_all | solution.py:341
  100.6 7.7 %collective-permute-start.10 = (f32[3,16,4,128]{3,2,1,0:T(4,128)S(1)}, f32[3,16,4,128]{3,2,1,0:T(4,128)S(1)}, u32[]{:S(2)}, u32[]{:S(2)}) collective-permute-start(f32[3,16,4,128]{3,2,1,0:T(4,128)S(1)} %get-tuple-element.24), channel_id=1, source_target_pairs={{0,256},{128,384},{256,0},{384,128},{1,257},{129,385},{257,1},{385... | collective-permute-start | bytes 294920 | tf_op jit(solution)/shard_map/ppermute | solution.py:338
  102.6 5.8 %collective-permute-start.9 = (f32[3,16,4,128]{3,2,1,0:T(4,128)S(1)}, f32[3,16,4,128]{3,2,1,0:T(4,128)S(1)}, u32[]{:S(2)}, u32[]{:S(2)}) collective-permute-start(f32[3,16,4,128]{3,2,1,0:T(4,128)S(1)} %get-tuple-element.25), channel_id=1, source_target_pairs={{0,384},{128,0},{256,128},{384,256},{1,385},{129,1},{257,129},{385... | collective-permute-start | bytes 294920 | tf_op jit(solution)/shard_map/ppermute | solution.py:337
  106.2 6.9 %collective-permute-start.8 = (f32[3,16,4,128]{3,2,1,0:T(4,128)S(1)}, f32[3,16,4,128]{3,2,1,0:T(4,128)S(1)}, u32[]{:S(2)}, u32[]{:S(2)}) collective-permute-start(f32[3,16,4,128]{3,2,1,0:T(4,128)S(1)} %get-tuple-element.26), channel_id=1, source_target_pairs={{0,128},{128,256},{256,384},{384,0},{1,129},{129,257},{257,385},{3... | collective-permute-start | bytes 294920 | tf_op jit(solution)/shard_map/ppermute | solution.py:336
  172.8 21.4 %collective-permute-start.11 = (bf16[4,4,256,128]{3,2,1,0:T(8,128)(2,1)S(1)}, bf16[4,4,256,128]{3,2,1,0:T(8,128)(2,1)S(1)}, u32[]{:S(2)}, u32[]{:S(2)}) collective-permute-start(bf16[4,4,256,128]{3,2,1,0:T(8,128)(2,1)S(1)} %all_to_all.27.source), channel_id=1, source_target_pairs={{0,64},{64,0},{1,65},{65,1},{2,66},{66,2},{3,67},{67,3},{4,68},{68... | collective-permute-start | bytes 3145736 | tf_op jit(solution)/shard_map/ppermute | solution.py:380
  178.7 8.4 %collective-permute-start.14 = (f32[3,16,4,128]{3,2,1,0:T(4,128)S(1)}, f32[3,16,4,128]{3,2,1,0:T(4,128)S(1)}, u32[]{:S(2)}, u32[]{:S(2)}) collective-permute-start(f32[3,16,4,128]{3,2,1,0:T(4,128)S(1)} %get-tuple-element.20), channel_id=1, source_target_pairs={{0,256},{128,384},{256,0},{384,128},{1,257},{129,385},{257,1},{385... | collective-permute-start | bytes 294920 | tf_op jit(solution)/shard_map/ppermute | solution.py:365
  181.1 6.0 %collective-permute-start.13 = (f32[3,16,4,128]{3,2,1,0:T(4,128)S(1)}, f32[3,16,4,128]{3,2,1,0:T(4,128)S(1)}, u32[]{:S(2)}, u32[]{:S(2)}) collective-permute-start(f32[3,16,4,128]{3,2,1,0:T(4,128)S(1)} %get-tuple-element.21), channel_id=1, source_target_pairs={{0,384},{128,0},{256,128},{384,256},{1,385},{129,1},{257,129},{385... | collective-permute-start | bytes 294920 | tf_op jit(solution)/shard_map/ppermute | solution.py:364
  185.2 6.9 %collective-permute-start.12 = (f32[3,16,4,128]{3,2,1,0:T(4,128)S(1)}, f32[3,16,4,128]{3,2,1,0:T(4,128)S(1)}, u32[]{:S(2)}, u32[]{:S(2)}) collective-permute-start(f32[3,16,4,128]{3,2,1,0:T(4,128)S(1)} %get-tuple-element.22), channel_id=1, source_target_pairs={{0,128},{128,256},{256,384},{384,0},{1,129},{129,257},{257,385},{3... | collective-permute-start | bytes 294920 | tf_op jit(solution)/shard_map/ppermute | solution.py:363

commit v5 on v4

--- a/solution.py
+++ b/solution.py
@@ -123,7 +123,7 @@
 
 
 def adam(old, new, total, got, own, low, high, far, out, after, state, acc, table):
-    experts = acc.shape[0]
+    experts, pairs = acc.shape[:2]
     rows = state.shape[3]
     y_here = lax.axis_index("y")
     state[y_here] = own[...]
@@ -132,12 +132,12 @@
     state[(y_here + 2) % Y] = far[...]
     acc[...] = jnp.zeros_like(acc)
     for p in range(PLACES):
-        acc[old[p]] += got[p]
+        acc[old[p]] += got[p, :pairs] * jnp.exp2(got[p, pairs:] - 14.0)
     for e in range(experts):
         master, first, second = (
             jnp.concatenate([state[y, n, e] for y in range(Y)], axis=0) for n in range(3)
         )
-        grad = acc[e] / total[e]
+        grad = jnp.concatenate([acc[e, t] for t in range(pairs)], axis=0) / total[e]
         new_first = decay_first * first + (1.0 - decay_first) * grad
         new_second = decay_second * second + (1.0 - decay_second) * grad * grad
         first_hat = new_first / (1.0 - decay_first**step_number)
@@ -156,6 +156,7 @@
 def half_grad(out_ref, local_ref, chunks, half):
     rows_shard = out_ref.shape[1] // Y
     wide = PLACES * rows_shard
+    peak = None
     for y in range(Y):
         at = pl.multiple_of((2 * y + half) * wide, wide)
         total, row = None, 0
@@ -168,37 +169,57 @@
             )
             total = term if total is None else total + term
             row += rows
-        out_ref[:, y * rows_shard : (y + 1) * rows_shard, :] = total.T.reshape(
+        size = jnp.abs(total)
+        peak = size if peak is None else jnp.maximum(peak, size)
+        out_ref[:PLACES, y * rows_shard : (y + 1) * rows_shard, :] = total.T.reshape(
             PLACES, rows_shard, -1
         )
-
-
-def grad_theirs(mine, theirs, payload, *refs):
-    chunks, (out_ref, local_ref, w_ref) = refs[:-3], refs[-3:]
+    out_ref[PLACES] = jnp.broadcast_to(jnp.max(peak, keepdims=True), out_ref.shape[1:])
+
+
+def forward_part(chunk, weights, which):
+    rows_shard = weights.shape[1] // Y
+    wide = PLACES * rows_shard
+    total = None
+    for y in range(Y):
+        at = pl.multiple_of((2 * y + which) * wide, wide)
+        block = weights[:, y * rows_shard : (y + 1) * rows_shard, :].astype(jnp.float32)
+        term = jnp.dot(
+            chunk[:, pl.ds(at, wide)],
+            block.reshape(wide, -1).astype(jnp.bfloat16),
+            preferred_element_type=jnp.float32,
+        )
+        total = term if total is None else total + term
+    return total
+
+
+def forward_mine(mine, *refs):
+    chunks, out_ref = refs[:-1], refs[-1]
+    weights = mine[...]
+    row = 0
+    for chunk in chunks:
+        rows = chunk.shape[0]
+        out_ref[row : row + rows, :] = forward_part(chunk, weights, lax.axis_index("core"))
+        row += rows
+
+
+def grad_theirs(part_ref, theirs, payload, *refs):
+    chunks, (out_ref, local_ref) = refs[:-2], refs[-2:]
     y_here, core = lax.axis_index("y"), lax.axis_index("core")
-    rows_shard = mine.shape[1] // Y
-    wide = PLACES * rows_shard
-    for source, which in ((mine, core), (theirs, 1 - core)):
-        block = source[...].astype(jnp.float32)
-        for y in range(Y):
-            w_ref[pl.ds(pl.multiple_of((2 * y + which) * wide, wide), wide), :] = (
-                block[:, y * rows_shard : (y + 1) * rows_shard, :]
-                .reshape(wide, -1)
-                .astype(jnp.bfloat16)
-            )
+    weights = theirs[...]
     packed = chunks[-1].shape[0]
-    weights = payload.shape[1] - packed
+    head = payload.shape[1] - packed
     row = 0
     for (step, part), chunk in zip(LINE, chunks):
         rows = chunk.shape[0]
-        both = jnp.dot(chunk[...], w_ref[...], preferred_element_type=jnp.float32)
+        both = part_ref[row : row + rows, :] + forward_part(chunk, weights, 1 - core)
         other = swapped(both)
         first = lower_half(both)
         gate = jnp.where(first, both, other)
         sigma = jax.nn.sigmoid(gate)
         active = gate * sigma
         slope = sigma * (1.0 + gate * (1.0 - sigma))
-        hidden = payload[(y_here + step) % Y, weights:, :].astype(jnp.float32)
+        hidden = payload[(y_here + step) % Y, head:, :].astype(jnp.float32)
         around = swapped(hidden)
         begin = lower_half(hidden)
         halves = [jnp.where(begin, hidden, around), jnp.where(begin, around, hidden)]
@@ -212,6 +233,16 @@
 def grad_mine(local_ref, *refs):
     chunks, out_ref = refs[:-1], refs[-1]
     half_grad(out_ref, local_ref, chunks, lax.axis_index("core"))
+
+
+def combine(mine, theirs, out):
+    pairs = out.shape[1] - 1
+    bits = jnp.ceil(jnp.log2(jnp.maximum(mine[PLACES] + theirs[PLACES], 1e-30)))
+    scale = jnp.exp2(14.0 - bits)
+    for t in range(pairs):
+        cut = slice(2 * t, 2 * t + 2)
+        out[:, t] = (mine[:PLACES, cut, :] + theirs[:PLACES, cut, :]) * scale[cut]
+    out[:, pairs] = jnp.broadcast_to(bits[:2], (PLACES, 2, bits.shape[1]))
 
 
 def join(source, out, which, blocks, sems):
@@ -299,17 +330,23 @@
 
     chunks = [own, low_a, low_b, high_a, high_b, far_a, far_b]
     line_rows = sum(c.shape[0] for c in chunks)
-    deep = own.shape[1]
-    grad_shape = jax.ShapeDtypeStruct((PLACES, Y * rows_shard, lanes), f32)
+    forward = pl.pallas_call(
+        forward_mine,
+        out_shape=jax.ShapeDtypeStruct((line_rows, lanes), f32),
+        in_specs=[VMEM] * (1 + len(chunks)),
+        out_specs=VMEM,
+        compiler_params=grant(24),
+        name="forward_mine",
+    )(w_mine, *chunks)
+    grad_shape = jax.ShapeDtypeStruct((PLACES + 1, Y * rows_shard, lanes), f32)
     sent, local = pl.pallas_call(
         grad_theirs,
         out_shape=(grad_shape, jax.ShapeDtypeStruct((lanes, line_rows), bf16)),
         in_specs=[VMEM] * (3 + len(chunks)),
         out_specs=(VMEM, VMEM),
-        scratch_shapes=[pltpu.VMEM((deep, lanes), bf16)],
         compiler_params=grant(24),
         name="grad_theirs",
-    )(w_mine, w_theirs, payload, *chunks)
+    )(forward, w_theirs, payload, *chunks)
     received = lax.ppermute(sent, "core", SWAP)
     summed = pl.pallas_call(
         grad_mine,
@@ -319,7 +356,15 @@
         compiler_params=grant(24),
         name="grad_mine",
     )(local, *chunks)
-    summed = summed + received
+    pairs = Y * rows_shard // 2
+    scaled = pl.pallas_call(
+        combine,
+        out_shape=jax.ShapeDtypeStruct((PLACES, pairs + 1, 2, lanes), f32),
+        in_specs=[VMEM] * 2,
+        out_specs=VMEM,
+        compiler_params=grant(6),
+        name="combine",
+    )(summed, received)
 
     columns = pl.pallas_call(
         split_cols,
@@ -338,7 +383,8 @@
     m_far = lax.ppermute(for_chip(2, columns), "y", ACROSS)
     m_own = for_chip(0, columns)
 
-    got = lax.all_to_all(summed, ("x", "z"), 0, 0, tiled=True)
+    got = lax.all_to_all(scaled.astype(jnp.float16), ("x", "z"), 0, 0, tiled=True)
+    got = got.astype(f32)
     select = (old_slots[:, None] == jnp.arange(experts, dtype=jnp.int32)[None, :]).astype(f32)
     per_slot = jnp.sum(row_count.astype(f32), axis=0)
     total = jnp.dot(per_slot, select, precision=lax.Precision.HIGHEST)
@@ -352,7 +398,7 @@
         out_specs=(VMEM, VMEM),
         scratch_shapes=[
             pltpu.VMEM((Y, 3, experts, rows_shard, lanes), f32),
-            pltpu.VMEM((experts, Y * rows_shard, lanes), f32),
+            pltpu.VMEM((experts, pairs, 2, lanes), f32),
             pltpu.VMEM((experts, Y * rows_shard, lanes), bf16),
         ],
         compiler_params=grant(6),

time: 197 us -> 189 us (0.959)
  waiting for transfers between devices: 40.5 us -> 31.5 us
  Pallas kernels: 13.3 us -> 15.5 us
    ppermute x1, waiting for transfers between devices: 4.69 us -> 0.01 us  [shards(): m_low = lax.ppermute(for_chip(1, columns), 'y', UP)]
    all_to_all x1, waiting for transfers between devices: 17.2 us -> 13 us  [shards(): lax.all_to_all(scaled.astype(jnp.float16), ('x', 'z'), 0, 0, tiled=True)]
    pallas_call x0 -> x2, Pallas kernels: none -> 2.48 us  [the longest x1 2 us: shards(): pl.pallas_call(forward_mine, out_shape=jax.ShapeDtypeStruct((line_rows, l...]
  transfers between devices with their start and end apart: 17 -> 17, of which waited for: 7 -> 6; matrix products, arithmetic and copies ran while one was open for 1% -> 1% of each run, Pallas kernels for 2% -> 3%
where the time goes in v5:
time: 189 us; the launch traced here: 188 us
  starting transfers between devices  86.1 us (46%)
  blocking collectives  50.4 us (27%)
  waiting for transfers between devices  31.5 us (17%)
  Pallas kernels  15.5 us (8%)
  local copies, waits for them, and re-layouts  2.13 us (1%)
    all_to_all x1, blocking collectives, shards(): landed = lax.all_to_all(picked, ('x', 'z'), 0, 0, tiled=True)  25.7 us
    all_to_all x1, starting transfers between devices, shards(): landed = lax.all_to_all(picked, ('x', 'z'), 0, 0, tiled=True)  18.6 us
    all_to_all x1, blocking collectives, shards(): mine = lax.all_to_all(copies, 'y', 0, 0, tiled=True)  14.5 us
    all_to_all x1, starting transfers between devices, shards(): lax.all_to_all(scaled.astype(jnp.float16), ('x', 'z'), 0, 0, tiled=True)  14.5 us
    all_to_all x1, waiting for transfers between devices, shards(): lax.all_to_all(scaled.astype(jnp.float16), ('x', 'z'), 0, 0, tiled=True)  13 us
    all_to_all x1, blocking collectives, shards(): payload = lax.all_to_all(payload, 'y', 0, 0, tiled=True)  10.2 us
    ppermute x1, starting transfers between devices, shards(): w_theirs = lax.ppermute(w_mine, 'core', SWAP)  8.15 us
    ppermute x1, waiting for transfers between devices, shards(): far_b = lax.ppermute(high_b, 'y', DOWN)  7.6 us
  transfers between devices with their start and end apart: 17, of which 6 were waited for; matrix products, arithmetic and copies ran while one was open for 1% of the time, Pallas kernels for 3%

profile of v5, /device:TPU:1, one launch (start us, length us, event | category | flops | bytes accessed | tf_op | source)
XLA Modules:
  0.0 188.1 jit_solution(3429662630057458237)
XLA Ops:
  0.6 2.0 %prepare.1 = bf16[4,192,128]{2,1,0:T(8,128)(2,1)} custom-call(s32[8,64]{1,0:T(8,128)} %counts.1, s32[4,64]{1,0:T(4,128)} %bitcast.40, bf16[256,256]{1,0:T(8,128)(2,1)} %bitcast.39, f32[16,4,512]{2,1,0:T(4,128)} %refs_0_.1), custom_call_target="tpu_custom_call" | custom-call | tf_op jit(solution)/shard_map/prepare/pallas_call | solution.py:292
  2.7 10.2 %all_to_all.25.payload = bf16[4,192,128]{2,1,0:T(8,128)(2,1)S(1)} all-to-all(bf16[4,192,128]{2,1,0:T(8,128)(2,1)} %prepare.1), channel_id=1, replica_groups=mesh['y'=4,'core'=2,'x'=4,'z'=16] {'y'}, dimensions={0} | all-to-all | bytes 393216 | tf_op jit(solution)/shard_map/all_to_all | solution.py:299
  13.5 1.3 pick_old.1
  14.8 18.6 %all-to-all-start.1 = ((bf16[64,16,128]{2,1,0:T(8,128)(2,1)}), bf16[64,16,128]{2,1,0:T(8,128)(2,1)}, u32[]{:S(2)}, u32[]{:S(2)}) async-start(bf16[64,16,128]{2,1,0:T(8,128)(2,1)} %pick_old.1), calls=%async_computation.1 | async-start | bytes 524288 | tf_op jit(solution)/shard_map/all_to_all | solution.py:317
  34.5 2.8 %collective-permute-start.3 = (bf16[128,2048]{1,0:T(8,128)(2,1)}, bf16[128,2048]{1,0:T(8,128)(2,1)S(1)}, u32[]{:S(2)}, u32[]{:S(2)}) collective-permute-start(bf16[128,2048]{1,0:T(8,128)(2,1)} %get-tuple-element.18), channel_id=1, source_target_pairs={{0,384},{128,0},{256,128},{384,256},{1,385},{129,1},{257,129},{385... | collective-permute-start | bytes 1572872 | tf_op jit(solution)/shard_map/ppermute | solution.py:301
  37.3 2.5 %collective-permute-start = (bf16[128,2048]{1,0:T(8,128)(2,1)}, bf16[128,2048]{1,0:T(8,128)(2,1)S(1)}, u32[]{:S(2)}, u32[]{:S(2)}) collective-permute-start(bf16[128,2048]{1,0:T(8,128)(2,1)} %get-tuple-element.19), channel_id=1, source_target_pairs={{0,128},{128,256},{256,384},{384,0},{1,129},{129,257},{257,385},{3... | collective-permute-start | bytes 1572872 | tf_op jit(solution)/shard_map/ppermute | solution.py:300
  39.7 2.3 %collective-permute-start.1 = (bf16[128,2048]{1,0:T(8,128)(2,1)}, bf16[128,2048]{1,0:T(8,128)(2,1)S(1)}, u32[]{:S(2)}, u32[]{:S(2)}) collective-permute-start(bf16[128,2048]{1,0:T(8,128)(2,1)} %get-tuple-element.18), channel_id=1, source_target_pairs={{0,128},{128,256},{256,384},{384,0},{1,129},{129,257},{257,385},{3... | collective-permute-start | bytes 1572872 | tf_op jit(solution)/shard_map/ppermute | solution.py:302
  42.0 4.2 %collective-permute-start.2 = (bf16[128,2048]{1,0:T(8,128)(2,1)}, bf16[128,2048]{1,0:T(8,128)(2,1)S(1)}, u32[]{:S(2)}, u32[]{:S(2)}) collective-permute-start(bf16[128,2048]{1,0:T(8,128)(2,1)} %get-tuple-element.19), channel_id=1, source_target_pairs={{0,384},{128,0},{256,128},{384,256},{1,385},{129,1},{257,129},{385... | collective-permute-start | bytes 1572872 | tf_op jit(solution)/shard_map/ppermute | solution.py:303
  46.3 1.5 collective-permute-done.3.refs_4_
  47.8 4.0 %collective-permute-start.5 = (bf16[128,2048]{1,0:T(8,128)(2,1)S(1)}, bf16[128,2048]{1,0:T(8,128)(2,1)}, u32[]{:S(2)}, u32[]{:S(2)}) collective-permute-start(bf16[128,2048]{1,0:T(8,128)(2,1)S(1)} %collective-permute-done.3.refs_4_), channel_id=1, source_target_pairs={{0,384},{128,0},{256,128},{384,256},{1,385},{129,1},{257,129},{385... | collective-permute-start | bytes 1572872 | tf_op jit(solution)/shard_map/ppermute | solution.py:319
  51.8 1.9 %collective-permute-start.4 = (bf16[128,2048]{1,0:T(8,128)(2,1)S(1)}, bf16[128,2048]{1,0:T(8,128)(2,1)}, u32[]{:S(2)}, u32[]{:S(2)}) collective-permute-start(bf16[128,2048]{1,0:T(8,128)(2,1)S(1)} %collective-permute-done.refs_1_), channel_id=1, source_target_pairs={{0,128},{128,256},{256,384},{384,0},{1,129},{129,257},{257,385},{3... | collective-permute-start | bytes 1572872 | tf_op jit(solution)/shard_map/ppermute | solution.py:318
  53.7 8.2 %collective-permute-start.6 = (bf16[64,16,128]{2,1,0:T(8,128)(2,1)}, bf16[64,16,128]{2,1,0:T(8,128)(2,1)S(1)}, u32[]{:S(2)}, u32[]{:S(2)}) collective-permute-start(bf16[64,16,128]{2,1,0:T(8,128)(2,1)} %all-to-all-done.1.mine), channel_id=1, source_target_pairs={{0,64},{64,0},{1,65},{65,1},{2,66},{66,2},{3,67},{67,3},{4,68},{68... | collective-permute-start | bytes 786440 | tf_op jit(solution)/shard_map/ppermute | solution.py:329
  62.6 7.6 %collective-permute-done.5.refs_6_ = bf16[128,2048]{1,0:T(8,128)(2,1)} collective-permute-done((bf16[128,2048]{1,0:T(8,128)(2,1)S(1)}, bf16[128,2048]{1,0:T(8,128)(2,1)}, u32[]{:S(2)}, u32[]{:S(2)}) %collective-permute-start.5) | collective-permute-done | bytes 524320 | tf_op jit(solution)/shard_map/ppermute | solution.py:319
  70.2 3.7 %collective-permute-done.4.refs_5_ = bf16[128,2048]{1,0:T(8,128)(2,1)} collective-permute-done((bf16[128,2048]{1,0:T(8,128)(2,1)S(1)}, bf16[128,2048]{1,0:T(8,128)(2,1)}, u32[]{:S(2)}, u32[]{:S(2)}) %collective-permute-start.4) | collective-permute-done | bytes 524320 | tf_op jit(solution)/shard_map/ppermute | solution.py:318
  74.0 2.0 %forward_mine.1.part_ref = f32[1024,128]{1,0:T(8,128)S(1)} custom-call(bf16[64,16,128]{2,1,0:T(8,128)(2,1)} %all-to-all-done.1.mine, bf16[256,2048]{1,0:T(8,128)(2,1)S(1)} %bitcast.33, bf16[128,2048]{1,0:T(8,128)(2,1)S(1)} %collective-permute-done.refs_1_, bf16[128,2048]{1,0:T(8,128)(2,1)S(1)} %collective-permute-done.1.refs_2_, ...), custom_call_target="tpu_custom_call" | custom-call | tf_op jit(solution)/shard_map/forward_mine/pallas_call | solution.py:333
  76.0 2.8 %grad_theirs.1 = (f32[65,16,128]{2,1,0:T(8,128)S(1)}, bf16[128,1024]{1,0:T(8,128)(2,1)S(1)}) custom-call(f32[1024,128]{1,0:T(8,128)S(1)} %forward_mine.1.part_ref, bf16[64,16,128]{2,1,0:T(8,128)(2,1)S(1)} %collective-permute-done.6.theirs, bf16[4,192,128]{2,1,0:T(8,128)(2,1)S(1)} %all_to_all.25.payload, bf16[256,2048]{1,0:T(8,128)(2,1)S(1)} %bitcast.34, ...), custom_call_target="tpu_custom_call" | custom-call | tf_op jit(solution)/shard_map/grad_theirs/pallas_call | solution.py:342
  78.8 5.5 %collective-permute-start.7 = (f32[65,16,128]{2,1,0:T(8,128)S(1)}, f32[65,16,128]{2,1,0:T(8,128)S(1)}, u32[]{:S(2)}, u32[]{:S(2)}) collective-permute-start(f32[65,16,128]{2,1,0:T(8,128)S(1)} %get-tuple-element.12), channel_id=1, source_target_pairs={{0,64},{64,0},{1,65},{65,1},{2,66},{66,2},{3,67},{67,3},{4,68},{68... | collective-permute-start | bytes 1597448 | tf_op jit(solution)/shard_map/ppermute | solution.py:350
  84.3 2.0 %grad_mine.1.mine = f32[65,16,128]{2,1,0:T(8,128)S(1)} custom-call(bf16[128,1024]{1,0:T(8,128)(2,1)S(1)} %get-tuple-element.11.local_ref, bf16[256,2048]{1,0:T(8,128)(2,1)S(1)} %bitcast.35, bf16[128,2048]{1,0:T(8,128)(2,1)S(1)} %collective-permute-done.refs_1_, bf16[128,2048]{1,0:T(8,128)(2,1)S(1)} %collective-permute-done.1.refs_2_, ...), custom_call_target="tpu_custom_call" | custom-call | tf_op jit(solution)/shard_map/grad_mine/pallas_call | solution.py:351
  87.7 14.5 %all-to-all-start.2 = ((f16[64,9,2,128]{3,2,1,0:T(2,128)(2,1)}), f16[64,9,2,128]{3,2,1,0:T(2,128)(2,1)S(1)}, u32[]{:S(2)}, u32[]{:S(2)}) async-start(f16[64,9,2,128]{3,2,1,0:T(2,128)(2,1)} %convert_element_type.11), calls=%async_computation.2 | async-start | bytes 589824 | tf_op jit(solution)/shard_map/all_to_all | solution.py:386
  102.7 2.0 %collective-permute-start.10 = (f32[3,16,4,128]{3,2,1,0:T(4,128)S(1)}, f32[3,16,4,128]{3,2,1,0:T(4,128)S(1)}, u32[]{:S(2)}, u32[]{:S(2)}) collective-permute-start(f32[3,16,4,128]{3,2,1,0:T(4,128)S(1)} %get-tuple-element.24), channel_id=1, source_target_pairs={{0,256},{128,384},{256,0},{384,128},{1,257},{129,385},{257,1},{385... | collective-permute-start | bytes 294920 | tf_op jit(solution)/shard_map/ppermute | solution.py:383
  104.7 3.6 %collective-permute-start.9 = (f32[3,16,4,128]{3,2,1,0:T(4,128)S(1)}, f32[3,16,4,128]{3,2,1,0:T(4,128)S(1)}, u32[]{:S(2)}, u32[]{:S(2)}) collective-permute-start(f32[3,16,4,128]{3,2,1,0:T(4,128)S(1)} %get-tuple-element.25), channel_id=1, source_target_pairs={{0,384},{128,0},{256,128},{384,256},{1,385},{129,1},{257,129},{385... | collective-permute-start | bytes 294920 | tf_op jit(solution)/shard_map/ppermute | solution.py:382
  108.3 1.9 %collective-permute-start.8 = (f32[3,16,4,128]{3,2,1,0:T(4,128)S(1)}, f32[3,16,4,128]{3,2,1,0:T(4,128)S(1)}, u32[]{:S(2)}, u32[]{:S(2)}) collective-permute-start(f32[3,16,4,128]{3,2,1,0:T(4,128)S(1)} %get-tuple-element.26), channel_id=1, source_target_pairs={{0,128},{128,256},{256,384},{384,0},{1,129},{129,257},{257,385},{3... | collective-permute-start | bytes 294920 | tf_op jit(solution)/shard_map/ppermute | solution.py:381
  110.4 13.0 %all-to-all-done.2 = f16[64,9,2,128]{3,2,1,0:T(2,128)(2,1)S(1)} async-done(((f16[64,9,2,128]{3,2,1,0:T(2,128)(2,1)}), f16[64,9,2,128]{3,2,1,0:T(2,128)(2,1)S(1)}, u32[]{:S(2)}, u32[]{:S(2)}) %all-to-all-start.2) | async-done | bytes 294944 | tf_op jit(solution)/shard_map/all_to_all | solution.py:386
  123.7 1.3 adam.1
  124.9 25.7 %all_to_all.26 = bf16[64,16,128]{2,1,0:T(8,128)(2,1)S(1)} all-to-all(bf16[64,16,128]{2,1,0:T(8,128)(2,1)S(1)} %get-tuple-element.13), channel_id=1, replica_groups=mesh['y'=4,'core'=2,'x'=4,'z'=16] {'x','z'}, dimensions={0} | all-to-all | bytes 524288 | tf_op jit(solution)/shard_map/all_to_all | solution.py:407
  150.9 14.5 %all_to_all.27.source = bf16[4,4,256,128]{3,2,1,0:T(8,128)(2,1)S(1)} all-to-all(bf16[4,4,256,128]{3,2,1,0:T(8,128)(2,1)S(1)} %broadcast_in_dim.10), channel_id=1, replica_groups=mesh['y'=4,'core'=2,'x'=4,'z'=16] {'y'}, dimensions={0} | all-to-all | bytes 2097152 | tf_op jit(solution)/shard_map/all_to_all | solution.py:425
  165.5 5.8 %collective-permute-start.11 = (bf16[4,4,256,128]{3,2,1,0:T(8,128)(2,1)S(1)}, bf16[4,4,256,128]{3,2,1,0:T(8,128)(2,1)S(1)}, u32[]{:S(2)}, u32[]{:S(2)}) collective-permute-start(bf16[4,4,256,128]{3,2,1,0:T(8,128)(2,1)S(1)} %all_to_all.27.source), channel_id=1, source_target_pairs={{0,64},{64,0},{1,65},{65,1},{2,66},{66,2},{3,67},{67,3},{4,68},{68... | collective-permute-start | bytes 3145736 | tf_op jit(solution)/shard_map/ppermute | solution.py:426
  171.4 2.4 %collective-permute-start.14 = (f32[3,16,4,128]{3,2,1,0:T(4,128)S(1)}, f32[3,16,4,128]{3,2,1,0:T(4,128)S(1)}, u32[]{:S(2)}, u32[]{:S(2)}) collective-permute-start(f32[3,16,4,128]{3,2,1,0:T(4,128)S(1)} %get-tuple-element.20), channel_id=1, source_target_pairs={{0,256},{128,384},{256,0},{384,128},{1,257},{129,385},{257,1},{385... | collective-permute-start | bytes 294920 | tf_op jit(solution)/shard_map/ppermute | solution.py:411
  173.8 4.0 %collective-permute-start.13 = (f32[3,16,4,128]{3,2,1,0:T(4,128)S(1)}, f32[3,16,4,128]{3,2,1,0:T(4,128)S(1)}, u32[]{:S(2)}, u32[]{:S(2)}) collective-permute-start(f32[3,16,4,128]{3,2,1,0:T(4,128)S(1)} %get-tuple-element.21), channel_id=1, source_target_pairs={{0,384},{128,0},{256,128},{384,256},{1,385},{129,1},{257,129},{385... | collective-permute-start | bytes 294920 | tf_op jit(solution)/shard_map/ppermute | solution.py:410
  177.9 1.9 %collective-permute-start.12 = (f32[3,16,4,128]{3,2,1,0:T(4,128)S(1)}, f32[3,16,4,128]{3,2,1,0:T(4,128)S(1)}, u32[]{:S(2)}, u32[]{:S(2)}) collective-permute-start(f32[3,16,4,128]{3,2,1,0:T(4,128)S(1)} %get-tuple-element.22), channel_id=1, source_target_pairs={{0,128},{128,256},{256,384},{384,0},{1,129},{129,257},{257,385},{3... | collective-permute-start | bytes 294920 | tf_op jit(solution)/shard_map/ppermute | solution.py:409
  179.8 4.9 %collective-permute-done.12.low = f32[3,16,4,128]{3,2,1,0:T(4,128)S(1)} collective-permute-done((f32[3,16,4,128]{3,2,1,0:T(4,128)S(1)}, f32[3,16,4,128]{3,2,1,0:T(4,128)S(1)}, u32[]{:S(2)}, u32[]{:S(2)}) %collective-permute-start.12) | collective-permute-done | bytes 98336 | tf_op jit(solution)/shard_map/ppermute | solution.py:409
  186.9 1.2 join_theirs.1
  (41 shorter events, 7.1 us)
Async XLA Ops:
  0.6 32.8 %copy-start = (bf16[1,1,256,2048]{3,2,1,0:T(8,128)(2,1)S(1)}, bf16[1,1,256,2048]{3,2,1,0:T(8,128)(2,1)}, u32[]{:S(2)}) copy-start(bf16[1,1,256,2048]{3,2,1,0:T(8,128)(2,1)} %param.9) | copy-start | bytes 3145732
  12.8 0.7 copy-start.4
  14.8 38.9 %all-to-all-start.1 = ((bf16[64,16,128]{2,1,0:T(8,128)(2,1)}), bf16[64,16,128]{2,1,0:T(8,128)(2,1)}, u32[]{:S(2)}, u32[]{:S(2)}) async-start(bf16[64,16,128]{2,1,0:T(8,128)(2,1)} %pick_old.1), calls=%async_computation.1 | async-start | bytes 524288 | tf_op jit(solution)/shard_map/all_to_all | solution.py:317
  34.5 13.3 %collective-permute-start.3 = (bf16[128,2048]{1,0:T(8,128)(2,1)}, bf16[128,2048]{1,0:T(8,128)(2,1)S(1)}, u32[]{:S(2)}, u32[]{:S(2)}) collective-permute-start(bf16[128,2048]{1,0:T(8,128)(2,1)} %get-tuple-element.18), channel_id=1, source_target_pairs={{0,384},{128,0},{256,128},{384,256},{1,385},{129,1},{257,129},{385... | collective-permute-start | bytes 1572872 | tf_op jit(solution)/shard_map/ppermute | solution.py:301
  37.3 14.5 %collective-permute-start = (bf16[128,2048]{1,0:T(8,128)(2,1)}, bf16[128,2048]{1,0:T(8,128)(2,1)S(1)}, u32[]{:S(2)}, u32[]{:S(2)}) collective-permute-start(bf16[128,2048]{1,0:T(8,128)(2,1)} %get-tuple-element.19), channel_id=1, source_target_pairs={{0,128},{128,256},{256,384},{384,0},{1,129},{129,257},{257,385},{3... | collective-permute-start | bytes 1572872 | tf_op jit(solution)/shard_map/ppermute | solution.py:300
  39.7 22.9 %collective-permute-start.1 = (bf16[128,2048]{1,0:T(8,128)(2,1)}, bf16[128,2048]{1,0:T(8,128)(2,1)S(1)}, u32[]{:S(2)}, u32[]{:S(2)}) collective-permute-start(bf16[128,2048]{1,0:T(8,128)(2,1)} %get-tuple-element.18), channel_id=1, source_target_pairs={{0,128},{128,256},{256,384},{384,0},{1,129},{129,257},{257,385},{3... | collective-permute-start | bytes 1572872 | tf_op jit(solution)/shard_map/ppermute | solution.py:302
  42.0 20.6 %collective-permute-start.2 = (bf16[128,2048]{1,0:T(8,128)(2,1)}, bf16[128,2048]{1,0:T(8,128)(2,1)S(1)}, u32[]{:S(2)}, u32[]{:S(2)}) collective-permute-start(bf16[128,2048]{1,0:T(8,128)(2,1)} %get-tuple-element.19), channel_id=1, source_target_pairs={{0,384},{128,0},{256,128},{384,256},{1,385},{129,1},{257,129},{385... | collective-permute-start | bytes 1572872 | tf_op jit(solution)/shard_map/ppermute | solution.py:303
  47.8 22.5 %collective-permute-start.5 = (bf16[128,2048]{1,0:T(8,128)(2,1)S(1)}, bf16[128,2048]{1,0:T(8,128)(2,1)}, u32[]{:S(2)}, u32[]{:S(2)}) collective-permute-start(bf16[128,2048]{1,0:T(8,128)(2,1)S(1)} %collective-permute-done.3.refs_4_), channel_id=1, source_target_pairs={{0,384},{128,0},{256,128},{384,256},{1,385},{129,1},{257,129},{385... | collective-permute-start | bytes 1572872 | tf_op jit(solution)/shard_map/ppermute | solution.py:319
  51.8 22.2 %collective-permute-start.4 = (bf16[128,2048]{1,0:T(8,128)(2,1)S(1)}, bf16[128,2048]{1,0:T(8,128)(2,1)}, u32[]{:S(2)}, u32[]{:S(2)}) collective-permute-start(bf16[128,2048]{1,0:T(8,128)(2,1)S(1)} %collective-permute-done.refs_1_), channel_id=1, source_target_pairs={{0,128},{128,256},{256,384},{384,0},{1,129},{129,257},{257,385},{3... | collective-permute-start | bytes 1572872 | tf_op jit(solution)/shard_map/ppermute | solution.py:318
  53.7 22.3 %collective-permute-start.6 = (bf16[64,16,128]{2,1,0:T(8,128)(2,1)}, bf16[64,16,128]{2,1,0:T(8,128)(2,1)S(1)}, u32[]{:S(2)}, u32[]{:S(2)}) collective-permute-start(bf16[64,16,128]{2,1,0:T(8,128)(2,1)} %all-to-all-done.1.mine), channel_id=1, source_target_pairs={{0,64},{64,0},{1,65},{65,1},{2,66},{66,2},{3,67},{67,3},{4,68},{68... | collective-permute-start | bytes 786440 | tf_op jit(solution)/shard_map/ppermute | solution.py:329
  78.8 7.6 %collective-permute-start.7 = (f32[65,16,128]{2,1,0:T(8,128)S(1)}, f32[65,16,128]{2,1,0:T(8,128)S(1)}, u32[]{:S(2)}, u32[]{:S(2)}) collective-permute-start(f32[65,16,128]{2,1,0:T(8,128)S(1)} %get-tuple-element.12), channel_id=1, source_target_pairs={{0,64},{64,0},{1,65},{65,1},{2,66},{66,2},{3,67},{67,3},{4,68},{68... | collective-permute-start | bytes 1597448 | tf_op jit(solution)/shard_map/ppermute | solution.py:350
  86.3 16.0 %copy-start.1 = (f32[16,4,512]{2,1,0:T(4,128)S(1)}, f32[16,4,512]{2,1,0:T(4,128)}, u32[]{:S(2)}) copy-start(f32[16,4,512]{2,1,0:T(4,128)} %refs_0_.1) | copy-start | bytes 393220
  86.3 16.0 %copy-start.2 = (f32[16,4,512]{2,1,0:T(4,128)S(1)}, f32[16,4,512]{2,1,0:T(4,128)}, u32[]{:S(2)}) copy-start(f32[16,4,512]{2,1,0:T(4,128)} %refs_1_.1) | copy-start | bytes 393220
  86.3 16.0 %copy-start.3 = (f32[16,4,512]{2,1,0:T(4,128)S(1)}, f32[16,4,512]{2,1,0:T(4,128)}, u32[]{:S(2)}) copy-start(f32[16,4,512]{2,1,0:T(4,128)} %refs_2_.1) | copy-start | bytes 393220
  86.3 23.9 %copy-start.7 = (s32[8,64]{1,0:T(8,128)S(1)}, s32[8,64]{1,0:T(8,128)}, u32[]{:S(2)}) copy-start(s32[8,64]{1,0:T(8,128)} %counts.1) | copy-start | bytes 6148
  86.3 23.9 %copy-start.5 = (s32[64]{0:T(128)S(1)}, s32[64]{0:T(128)}, u32[]{:S(2)}) copy-start(s32[64]{0:T(128)} %old.1) | copy-start | bytes 772
  86.8 36.8 %copy-start.6 = (s32[64]{0:T(128)S(1)}, s32[64]{0:T(128)}, u32[]{:S(2)}) copy-start(s32[64]{0:T(128)} %new.1) | copy-start | bytes 772
  87.7 35.7 %all-to-all-start.2 = ((f16[64,9,2,128]{3,2,1,0:T(2,128)(2,1)}), f16[64,9,2,128]{3,2,1,0:T(2,128)(2,1)S(1)}, u32[]{:S(2)}, u32[]{:S(2)}) async-start(f16[64,9,2,128]{3,2,1,0:T(2,128)(2,1)} %convert_element_type.11), calls=%async_computation.2 | async-start | bytes 589824 | tf_op jit(solution)/shard_map/all_to_all | solution.py:386
  102.7 21.0 %collective-permute-start.10 = (f32[3,16,4,128]{3,2,1,0:T(4,128)S(1)}, f32[3,16,4,128]{3,2,1,0:T(4,128)S(1)}, u32[]{:S(2)}, u32[]{:S(2)}) collective-permute-start(f32[3,16,4,128]{3,2,1,0:T(4,128)S(1)} %get-tuple-element.24), channel_id=1, source_target_pairs={{0,256},{128,384},{256,0},{384,128},{1,257},{129,385},{257,1},{385... | collective-permute-start | bytes 294920 | tf_op jit(solution)/shard_map/ppermute | solution.py:383
  104.7 19.0 %collective-permute-start.9 = (f32[3,16,4,128]{3,2,1,0:T(4,128)S(1)}, f32[3,16,4,128]{3,2,1,0:T(4,128)S(1)}, u32[]{:S(2)}, u32[]{:S(2)}) collective-permute-start(f32[3,16,4,128]{3,2,1,0:T(4,128)S(1)} %get-tuple-element.25), channel_id=1, source_target_pairs={{0,384},{128,0},{256,128},{384,256},{1,385},{129,1},{257,129},{385... | collective-permute-start | bytes 294920 | tf_op jit(solution)/shard_map/ppermute | solution.py:382
  108.3 15.4 %collective-permute-start.8 = (f32[3,16,4,128]{3,2,1,0:T(4,128)S(1)}, f32[3,16,4,128]{3,2,1,0:T(4,128)S(1)}, u32[]{:S(2)}, u32[]{:S(2)}) collective-permute-start(f32[3,16,4,128]{3,2,1,0:T(4,128)S(1)} %get-tuple-element.26), channel_id=1, source_target_pairs={{0,128},{128,256},{256,384},{384,0},{1,129},{129,257},{257,385},{3... | collective-permute-start | bytes 294920 | tf_op jit(solution)/shard_map/ppermute | solution.py:381
  165.5 21.4 %collective-permute-start.11 = (bf16[4,4,256,128]{3,2,1,0:T(8,128)(2,1)S(1)}, bf16[4,4,256,128]{3,2,1,0:T(8,128)(2,1)S(1)}, u32[]{:S(2)}, u32[]{:S(2)}) collective-permute-start(bf16[4,4,256,128]{3,2,1,0:T(8,128)(2,1)S(1)} %all_to_all.27.source), channel_id=1, source_target_pairs={{0,64},{64,0},{1,65},{65,1},{2,66},{66,2},{3,67},{67,3},{4,68},{68... | collective-permute-start | bytes 3145736 | tf_op jit(solution)/shard_map/ppermute | solution.py:426
  171.4 8.4 %collective-permute-start.14 = (f32[3,16,4,128]{3,2,1,0:T(4,128)S(1)}, f32[3,16,4,128]{3,2,1,0:T(4,128)S(1)}, u32[]{:S(2)}, u32[]{:S(2)}) collective-permute-start(f32[3,16,4,128]{3,2,1,0:T(4,128)S(1)} %get-tuple-element.20), channel_id=1, source_target_pairs={{0,256},{128,384},{256,0},{384,128},{1,257},{129,385},{257,1},{385... | collective-permute-start | bytes 294920 | tf_op jit(solution)/shard_map/ppermute | solution.py:411
  173.8 6.0 %collective-permute-start.13 = (f32[3,16,4,128]{3,2,1,0:T(4,128)S(1)}, f32[3,16,4,128]{3,2,1,0:T(4,128)S(1)}, u32[]{:S(2)}, u32[]{:S(2)}) collective-permute-start(f32[3,16,4,128]{3,2,1,0:T(4,128)S(1)} %get-tuple-element.21), channel_id=1, source_target_pairs={{0,384},{128,0},{256,128},{384,256},{1,385},{129,1},{257,129},{385... | collective-permute-start | bytes 294920 | tf_op jit(solution)/shard_map/ppermute | solution.py:410
  177.9 6.9 %collective-permute-start.12 = (f32[3,16,4,128]{3,2,1,0:T(4,128)S(1)}, f32[3,16,4,128]{3,2,1,0:T(4,128)S(1)}, u32[]{:S(2)}, u32[]{:S(2)}) collective-permute-start(f32[3,16,4,128]{3,2,1,0:T(4,128)S(1)} %get-tuple-element.22), channel_id=1, source_target_pairs={{0,128},{128,256},{256,384},{384,0},{1,129},{129,257},{257,385},{3... | collective-permute-start | bytes 294920 | tf_op jit(solution)/shard_map/ppermute | solution.py:409

commit v6 on v5

--- a/solution.py
+++ b/solution.py
@@ -70,7 +70,9 @@
             )
 
 
-def prepare(counts, order, hidden, master, out):
+def prepare(counts, order, hidden, master, tokens, out, upper_out, lower_out, held, sems):
+    whole = pltpu.make_async_copy(tokens, held, sems.at[0])
+    whole.start()
     batches, batch_rows = order.shape
     experts, rows_shard, width = master.shape
     lanes = out.shape[-1]
@@ -105,6 +107,14 @@
         first = lower_half(gate)
         out[2 * pair, :weights, :] = jnp.where(first, gate, swapped(up)).astype(jnp.bfloat16)
         out[2 * pair + 1, :weights, :] = jnp.where(first, swapped(gate), up).astype(jnp.bfloat16)
+    whole.wait()
+    cut = held.shape[0] // 2
+    upper_copy = pltpu.make_async_copy(held.at[pl.ds(0, cut)], upper_out, sems.at[0])
+    lower_copy = pltpu.make_async_copy(held.at[pl.ds(cut, cut)], lower_out, sems.at[1])
+    upper_copy.start()
+    lower_copy.start()
+    upper_copy.wait()
+    lower_copy.wait()
 
 
 def pick_old(slots, payload, out, table, picked, sem):
@@ -123,8 +133,8 @@
 
 
 def adam(old, new, total, got, own, low, high, far, out, after, state, acc, table):
-    experts, pairs = acc.shape[:2]
-    rows = state.shape[3]
+    experts, _, data = acc.shape
+    rows, lanes = state.shape[3:]
     y_here = lax.axis_index("y")
     state[y_here] = own[...]
     state[(y_here + 3) % Y] = low[...]
@@ -132,12 +142,16 @@
     state[(y_here + 2) % Y] = far[...]
     acc[...] = jnp.zeros_like(acc)
     for p in range(PLACES):
-        acc[old[p]] += got[p, :pairs] * jnp.exp2(got[p, pairs:] - 14.0)
+        undo = jnp.exp2(got[p, :, data:] - 14.0)
+        acc[old[p]] += got[p, :, :data] * jnp.concatenate([undo] * (data // lanes), axis=1)
     for e in range(experts):
         master, first, second = (
             jnp.concatenate([state[y, n, e] for y in range(Y)], axis=0) for n in range(3)
         )
-        grad = jnp.concatenate([acc[e, t] for t in range(pairs)], axis=0) / total[e]
+        grad = jnp.concatenate(
+            [acc[e, :, at : at + lanes] for at in range(0, data, lanes)], axis=0
+        )
+        grad = grad / total[e]
         new_first = decay_first * first + (1.0 - decay_first) * grad
         new_second = decay_second * second + (1.0 - decay_second) * grad * grad
         first_hat = new_first / (1.0 - decay_first**step_number)
@@ -203,7 +217,7 @@
         row += rows
 
 
-def grad_theirs(part_ref, theirs, payload, *refs):
+def grad_theirs(part_ref, mine, theirs, payload, *refs):
     chunks, (out_ref, local_ref) = refs[:-2], refs[-2:]
     y_here, core = lax.axis_index("y"), lax.axis_index("core")
     weights = theirs[...]
@@ -212,7 +226,11 @@
     row = 0
     for (step, part), chunk in zip(LINE, chunks):
         rows = chunk.shape[0]
-        both = part_ref[row : row + rows, :] + forward_part(chunk, weights, 1 - core)
+        if row < part_ref.shape[0]:
+            both = part_ref[row : row + rows, :]
+        else:
+            both = forward_part(chunk, mine[...], core)
+        both = both + forward_part(chunk, weights, 1 - core)
         other = swapped(both)
         first = lower_half(both)
         gate = jnp.where(first, both, other)
@@ -236,13 +254,16 @@
 
 
 def combine(mine, theirs, out):
-    pairs = out.shape[1] - 1
+    lanes = mine.shape[-1]
+    pairs = out.shape[2] // lanes - 1
     bits = jnp.ceil(jnp.log2(jnp.maximum(mine[PLACES] + theirs[PLACES], 1e-30)))
     scale = jnp.exp2(14.0 - bits)
     for t in range(pairs):
         cut = slice(2 * t, 2 * t + 2)
-        out[:, t] = (mine[:PLACES, cut, :] + theirs[:PLACES, cut, :]) * scale[cut]
-    out[:, pairs] = jnp.broadcast_to(bits[:2], (PLACES, 2, bits.shape[1]))
+        out[:, :, t * lanes : (t + 1) * lanes] = (
+            mine[:PLACES, cut, :] + theirs[:PLACES, cut, :]
+        ) * scale[cut]
+    out[:, :, pairs * lanes :] = jnp.broadcast_to(bits[:2], (PLACES, 2, bits.shape[1]))
 
 
 def join(source, out, which, blocks, sems):
@@ -287,15 +308,20 @@
     own = tokens[0, 0]
     rows = own.shape[0]
     half_rows = rows // 2
-    own_a, own_b = own[:half_rows], own[half_rows:]
-
-    payload = pl.pallas_call(
+    half_shape = jax.ShapeDtypeStruct((half_rows, own.shape[1]), bf16)
+    hbm = pl.BlockSpec(memory_space=pltpu.MemorySpace.HBM)
+    payload, own_a, own_b = pl.pallas_call(
         prepare,
-        out_shape=jax.ShapeDtypeStruct((Y, experts * rows_shard + half_rows, lanes), bf16),
-        in_specs=[SMEM, VMEM, VMEM, VMEM],
-        out_specs=VMEM,
+        out_shape=(
+            jax.ShapeDtypeStruct((Y, experts * rows_shard + half_rows, lanes), bf16),
+            half_shape,
+            half_shape,
+        ),
+        in_specs=[SMEM, VMEM, VMEM, VMEM, hbm],
+        out_specs=(VMEM, hbm, hbm),
+        scratch_shapes=[pltpu.VMEM(own.shape, bf16), pltpu.SemaphoreType.DMA((2,))],
         name="prepare",
-    )(row_count, routing[0, 0], hidden_grad[0, 0], master)
+    )(row_count, routing[0, 0], hidden_grad[0, 0], master, own)
     payload = lax.all_to_all(payload, "y", 0, 0, tiled=True)
     low_a = lax.ppermute(own_a, "y", UP)
     high_b = lax.ppermute(own_b, "y", DOWN)
@@ -332,21 +358,21 @@
     line_rows = sum(c.shape[0] for c in chunks)
     forward = pl.pallas_call(
         forward_mine,
-        out_shape=jax.ShapeDtypeStruct((line_rows, lanes), f32),
-        in_specs=[VMEM] * (1 + len(chunks)),
+        out_shape=jax.ShapeDtypeStruct((line_rows - rows, lanes), f32),
+        in_specs=[VMEM] * (len(chunks) - 1),
         out_specs=VMEM,
         compiler_params=grant(24),
         name="forward_mine",
-    )(w_mine, *chunks)
+    )(w_mine, *chunks[:-2])
     grad_shape = jax.ShapeDtypeStruct((PLACES + 1, Y * rows_shard, lanes), f32)
     sent, local = pl.pallas_call(
         grad_theirs,
         out_shape=(grad_shape, jax.ShapeDtypeStruct((lanes, line_rows), bf16)),
-        in_specs=[VMEM] * (3 + len(chunks)),
+        in_specs=[VMEM] * (4 + len(chunks)),
         out_specs=(VMEM, VMEM),
         compiler_params=grant(24),
         name="grad_theirs",
-    )(forward, w_theirs, payload, *chunks)
+    )(forward, w_mine, w_theirs, payload, *chunks)
     received = lax.ppermute(sent, "core", SWAP)
     summed = pl.pallas_call(
         grad_mine,
@@ -359,7 +385,7 @@
     pairs = Y * rows_shard // 2
     scaled = pl.pallas_call(
         combine,
-        out_shape=jax.ShapeDtypeStruct((PLACES, pairs + 1, 2, lanes), f32),
+        out_shape=jax.ShapeDtypeStruct((PLACES, 2, (pairs + 1) * lanes), f32),
         in_specs=[VMEM] * 2,
         out_specs=VMEM,
         compiler_params=grant(6),
@@ -398,7 +424,7 @@
         out_specs=(VMEM, VMEM),
         scratch_shapes=[
             pltpu.VMEM((Y, 3, experts, rows_shard, lanes), f32),
-            pltpu.VMEM((experts, pairs, 2, lanes), f32),
+            pltpu.VMEM((experts, 2, pairs * lanes), f32),
             pltpu.VMEM((experts, Y * rows_shard, lanes), bf16),
         ],
         compiler_params=grant(6),
@@ -425,7 +451,6 @@
     mine = lax.all_to_all(copies, "y", 0, 0, tiled=True)
     theirs = lax.ppermute(mine, "core", SWAP)
     block_rows = PLACES * rows_shard
-    hbm = pl.BlockSpec(memory_space=pltpu.MemorySpace.HBM)
     scratch = [pltpu.VMEM((Y, block_rows, width), bf16), pltpu.SemaphoreType.DMA((Y,))]
     whole = jax.ShapeDtypeStruct((Y, C, block_rows, width), bf16)
     begun = pl.pallas_call(

time: 189 us -> 189 us (level)
  waiting for transfers between devices: 31.5 us -> 25.9 us
  starting transfers between devices: 86.1 us -> 89.4 us
  blocking collectives: 50.4 us -> 52.3 us
    ppermute x1, waiting for transfers between devices: 7.6 us -> 0.87 us  [shards(): far_b = lax.ppermute(high_b, 'y', DOWN)]
    ppermute x1, waiting for transfers between devices: 3.73 us -> 6.8 us  [shards(): far_a = lax.ppermute(low_a, 'y', UP)]
    ppermute x1, waiting for transfers between devices: 0.01 us -> 2.61 us  [shards(): low_a = lax.ppermute(own_a, 'y', UP)]
    all_to_all x1, waiting for transfers between devices: 13 us -> 10.7 us  [shards(): lax.all_to_all(scaled.astype(jnp.float16), ('x', 'z'), 0, 0, tiled=True)]
    ppermute x1, starting transfers between devices: 4.2 us -> 1.92 us  [shards(): high_a = lax.ppermute(own_a, 'y', DOWN)]
    all_to_all x1, blocking collectives: 14.5 us -> 16.6 us  [shards(): mine = lax.all_to_all(copies, 'y', 0, 0, tiled=True)]
    ppermute x1, starting transfers between devices: 1.99 us -> 3.93 us  [shards(): m_far = lax.ppermute(for_chip(2, columns), 'y', ACROSS)]
  transfers between devices with their start and end apart: 17 -> 17, of which waited for: 6 -> 5; matrix products, arithmetic and copies ran while one was open for 1% -> 0% of each run, Pallas kernels for 3% -> 3%
where the time goes in v6:
time: 189 us; the launch traced here: 188 us
  starting transfers between devices  89.4 us (47%)
  blocking collectives  52.3 us (28%)
  waiting for transfers between devices  25.9 us (14%)
  Pallas kernels  16.1 us (9%)
    all_to_all x1, blocking collectives, shards(): landed = lax.all_to_all(picked, ('x', 'z'), 0, 0, tiled=True)  25.5 us
    all_to_all x1, starting transfers between devices, shards(): landed = lax.all_to_all(picked, ('x', 'z'), 0, 0, tiled=True)  18.3 us
    all_to_all x1, blocking collectives, shards(): mine = lax.all_to_all(copies, 'y', 0, 0, tiled=True)  16.6 us
    all_to_all x1, starting transfers between devices, shards(): lax.all_to_all(scaled.astype(jnp.float16), ('x', 'z'), 0, 0, tiled=True)  14.6 us
    all_to_all x1, waiting for transfers between devices, shards(): lax.all_to_all(scaled.astype(jnp.float16), ('x', 'z'), 0, 0, tiled=True)  10.7 us
    all_to_all x1, blocking collectives, shards(): payload = lax.all_to_all(payload, 'y', 0, 0, tiled=True)  10.2 us
    ppermute x1, starting transfers between devices, shards(): w_theirs = lax.ppermute(w_mine, 'core', SWAP)  8.67 us
    ppermute x1, waiting for transfers between devices, shards(): far_a = lax.ppermute(low_a, 'y', UP)  6.8 us
  transfers between devices with their start and end apart: 17, of which 5 were waited for; matrix products, arithmetic and copies ran while one was open for 0% of the time, Pallas kernels for 3%

profile of v6, /device:TPU:1, one launch (start us, length us, event | category | flops | bytes accessed | tf_op | source)
XLA Modules:
  0.0 187.9 jit_solution(13057754796485819103)
XLA Ops:
  0.6 4.0 %prepare.1 = (bf16[4,192,128]{2,1,0:T(8,128)(2,1)}, bf16[128,2048]{1,0:T(8,128)(2,1)}, bf16[128,2048]{1,0:T(8,128)(2,1)}) custom-call(s32[8,64]{1,0:T(8,128)} %counts.1, s32[4,64]{1,0:T(4,128)} %bitcast.37, bf16[256,256]{1,0:T(8,128)(2,1)} %bitcast.36, f32[16,4,512]{2,1,0:T(4,128)} %refs_0_.1, bf16[256,2048]{1,0:T(8,128)(2,1)} %bitcast.29), custom_call_target="tpu_custom_call" | custom-call | tf_op jit(solution)/shard_map/prepare/pallas_call | solution.py:313
  4.7 10.2 %all_to_all.25.payload = bf16[4,192,128]{2,1,0:T(8,128)(2,1)S(1)} all-to-all(bf16[4,192,128]{2,1,0:T(8,128)(2,1)} %get-tuple-element.14), channel_id=1, replica_groups=mesh['y'=4,'core'=2,'x'=4,'z'=16] {'y'}, dimensions={0} | all-to-all | bytes 393216 | tf_op jit(solution)/shard_map/all_to_all | solution.py:325
  15.5 1.3 pick_old.1
  17.5 18.3 %all-to-all-start.1 = ((bf16[64,16,128]{2,1,0:T(8,128)(2,1)}), bf16[64,16,128]{2,1,0:T(8,128)(2,1)S(1)}, u32[]{:S(2)}, u32[]{:S(2)}) async-start(bf16[64,16,128]{2,1,0:T(8,128)(2,1)} %pick_old.1), calls=%async_computation.1 | async-start | bytes 524288 | tf_op jit(solution)/shard_map/all_to_all | solution.py:343
  35.8 2.3 %collective-permute-start = (bf16[128,2048]{1,0:T(8,128)(2,1)}, bf16[128,2048]{1,0:T(8,128)(2,1)S(1)}, u32[]{:S(2)}, u32[]{:S(2)}) collective-permute-start(bf16[128,2048]{1,0:T(8,128)(2,1)} %get-tuple-element.15), channel_id=1, source_target_pairs={{0,128},{128,256},{256,384},{384,0},{1,129},{129,257},{257,385},{3... | collective-permute-start | bytes 1572872 | tf_op jit(solution)/shard_map/ppermute | solution.py:326
  38.1 4.2 %collective-permute-start.3 = (bf16[128,2048]{1,0:T(8,128)(2,1)}, bf16[128,2048]{1,0:T(8,128)(2,1)S(1)}, u32[]{:S(2)}, u32[]{:S(2)}) collective-permute-start(bf16[128,2048]{1,0:T(8,128)(2,1)} %get-tuple-element.16), channel_id=1, source_target_pairs={{0,384},{128,0},{256,128},{384,256},{1,385},{129,1},{257,129},{385... | collective-permute-start | bytes 1572872 | tf_op jit(solution)/shard_map/ppermute | solution.py:327
  42.3 1.9 %collective-permute-start.2 = (bf16[128,2048]{1,0:T(8,128)(2,1)}, bf16[128,2048]{1,0:T(8,128)(2,1)S(1)}, u32[]{:S(2)}, u32[]{:S(2)}) collective-permute-start(bf16[128,2048]{1,0:T(8,128)(2,1)} %get-tuple-element.15), channel_id=1, source_target_pairs={{0,384},{128,0},{256,128},{384,256},{1,385},{129,1},{257,129},{385... | collective-permute-start | bytes 1572872 | tf_op jit(solution)/shard_map/ppermute | solution.py:329
  44.2 3.4 %collective-permute-start.1 = (bf16[128,2048]{1,0:T(8,128)(2,1)}, bf16[128,2048]{1,0:T(8,128)(2,1)S(1)}, u32[]{:S(2)}, u32[]{:S(2)}) collective-permute-start(bf16[128,2048]{1,0:T(8,128)(2,1)} %get-tuple-element.16), channel_id=1, source_target_pairs={{0,128},{128,256},{256,384},{384,0},{1,129},{129,257},{257,385},{3... | collective-permute-start | bytes 1572872 | tf_op jit(solution)/shard_map/ppermute | solution.py:328
  47.6 2.6 %collective-permute-done.refs_1_ = bf16[128,2048]{1,0:T(8,128)(2,1)S(1)} collective-permute-done((bf16[128,2048]{1,0:T(8,128)(2,1)}, bf16[128,2048]{1,0:T(8,128)(2,1)S(1)}, u32[]{:S(2)}, u32[]{:S(2)}) %collective-permute-start) | collective-permute-done | bytes 524320 | tf_op jit(solution)/shard_map/ppermute | solution.py:326
  50.2 1.9 %collective-permute-start.5 = (bf16[128,2048]{1,0:T(8,128)(2,1)S(1)}, bf16[128,2048]{1,0:T(8,128)(2,1)}, u32[]{:S(2)}, u32[]{:S(2)}) collective-permute-start(bf16[128,2048]{1,0:T(8,128)(2,1)S(1)} %collective-permute-done.refs_1_), channel_id=1, source_target_pairs={{0,128},{128,256},{256,384},{384,0},{1,129},{129,257},{257,385},{3... | collective-permute-start | bytes 1572872 | tf_op jit(solution)/shard_map/ppermute | solution.py:344
  52.2 4.6 %collective-permute-start.6 = (bf16[128,2048]{1,0:T(8,128)(2,1)S(1)}, bf16[128,2048]{1,0:T(8,128)(2,1)}, u32[]{:S(2)}, u32[]{:S(2)}) collective-permute-start(bf16[128,2048]{1,0:T(8,128)(2,1)S(1)} %collective-permute-done.3.refs_4_), channel_id=1, source_target_pairs={{0,384},{128,0},{256,128},{384,256},{1,385},{129,1},{257,129},{385... | collective-permute-start | bytes 1572872 | tf_op jit(solution)/shard_map/ppermute | solution.py:345
  56.8 8.7 %collective-permute-start.4 = (bf16[64,16,128]{2,1,0:T(8,128)(2,1)S(1)}, bf16[64,16,128]{2,1,0:T(8,128)(2,1)S(1)}, u32[]{:S(2)}, u32[]{:S(2)}) collective-permute-start(bf16[64,16,128]{2,1,0:T(8,128)(2,1)S(1)} %all-to-all-done.1.mine), channel_id=1, source_target_pairs={{0,64},{64,0},{1,65},{65,1},{2,66},{66,2},{3,67},{67,3},{4,68},{68... | collective-permute-start | bytes 786440 | tf_op jit(solution)/shard_map/ppermute | solution.py:355
  66.0 6.8 %collective-permute-done.5.refs_5_ = bf16[128,2048]{1,0:T(8,128)(2,1)} collective-permute-done((bf16[128,2048]{1,0:T(8,128)(2,1)S(1)}, bf16[128,2048]{1,0:T(8,128)(2,1)}, u32[]{:S(2)}, u32[]{:S(2)}) %collective-permute-start.5) | collective-permute-done | bytes 524320 | tf_op jit(solution)/shard_map/ppermute | solution.py:344
  73.7 3.0 %grad_theirs.1 = (f32[65,16,128]{2,1,0:T(8,128)S(1)}, bf16[128,1024]{1,0:T(8,128)(2,1)S(1)}) custom-call(f32[768,128]{1,0:T(8,128)S(1)} %forward_mine.1.part_ref, bf16[64,16,128]{2,1,0:T(8,128)(2,1)S(1)} %all-to-all-done.1.mine, bf16[64,16,128]{2,1,0:T(8,128)(2,1)S(1)} %collective-permute-done.4.theirs, bf16[4,192,128]{2,1,0:T(8,128)(2,1)S(1)} %copy-done.2, ...), custom_call_target="tpu_custom_call" | custom-call | tf_op jit(solution)/shard_map/grad_theirs/pallas_call | solution.py:368
  76.7 5.3 %collective-permute-start.7 = (f32[65,16,128]{2,1,0:T(8,128)S(1)}, f32[65,16,128]{2,1,0:T(8,128)S(1)}, u32[]{:S(2)}, u32[]{:S(2)}) collective-permute-start(f32[65,16,128]{2,1,0:T(8,128)S(1)} %get-tuple-element.18), channel_id=1, source_target_pairs={{0,64},{64,0},{1,65},{65,1},{2,66},{66,2},{3,67},{67,3},{4,68},{68... | collective-permute-start | bytes 1597448 | tf_op jit(solution)/shard_map/ppermute | solution.py:376
  82.0 2.0 %grad_mine.1.mine = f32[65,16,128]{2,1,0:T(8,128)S(1)} custom-call(bf16[128,1024]{1,0:T(8,128)(2,1)S(1)} %get-tuple-element.17.local_ref, bf16[256,2048]{1,0:T(8,128)(2,1)S(1)} %bitcast.32, bf16[128,2048]{1,0:T(8,128)(2,1)S(1)} %collective-permute-done.refs_1_, bf16[128,2048]{1,0:T(8,128)(2,1)S(1)} %collective-permute-done.1.refs_2_, ...), custom_call_target="tpu_custom_call" | custom-call | tf_op jit(solution)/shard_map/grad_mine/pallas_call | solution.py:377
  85.5 14.6 %all-to-all-start.2 = ((f16[64,2,1152]{2,1,0:T(2,128)(2,1)}), f16[64,2,1152]{2,1,0:T(2,128)(2,1)S(1)}, u32[]{:S(2)}, u32[]{:S(2)}) async-start(f16[64,2,1152]{2,1,0:T(2,128)(2,1)} %convert_element_type.11), calls=%async_computation.2 | async-start | bytes 589824 | tf_op jit(solution)/shard_map/all_to_all | solution.py:412
  100.5 3.9 %collective-permute-start.10 = (f32[3,16,4,128]{3,2,1,0:T(4,128)S(1)}, f32[3,16,4,128]{3,2,1,0:T(4,128)S(1)}, u32[]{:S(2)}, u32[]{:S(2)}) collective-permute-start(f32[3,16,4,128]{3,2,1,0:T(4,128)S(1)} %get-tuple-element.28), channel_id=1, source_target_pairs={{0,256},{128,384},{256,0},{384,128},{1,257},{129,385},{257,1},{385... | collective-permute-start | bytes 294920 | tf_op jit(solution)/shard_map/ppermute | solution.py:409
  104.4 3.4 %collective-permute-start.9 = (f32[3,16,4,128]{3,2,1,0:T(4,128)S(1)}, f32[3,16,4,128]{3,2,1,0:T(4,128)S(1)}, u32[]{:S(2)}, u32[]{:S(2)}) collective-permute-start(f32[3,16,4,128]{3,2,1,0:T(4,128)S(1)} %get-tuple-element.29), channel_id=1, source_target_pairs={{0,384},{128,0},{256,128},{384,256},{1,385},{129,1},{257,129},{385... | collective-permute-start | bytes 294920 | tf_op jit(solution)/shard_map/ppermute | solution.py:408
  107.8 2.5 %collective-permute-start.8 = (f32[3,16,4,128]{3,2,1,0:T(4,128)S(1)}, f32[3,16,4,128]{3,2,1,0:T(4,128)S(1)}, u32[]{:S(2)}, u32[]{:S(2)}) collective-permute-start(f32[3,16,4,128]{3,2,1,0:T(4,128)S(1)} %get-tuple-element.30), channel_id=1, source_target_pairs={{0,128},{128,256},{256,384},{384,0},{1,129},{129,257},{257,385},{3... | collective-permute-start | bytes 294920 | tf_op jit(solution)/shard_map/ppermute | solution.py:407
  110.6 10.7 %all-to-all-done.2 = f16[64,2,1152]{2,1,0:T(2,128)(2,1)S(1)} async-done(((f16[64,2,1152]{2,1,0:T(2,128)(2,1)}), f16[64,2,1152]{2,1,0:T(2,128)(2,1)S(1)}, u32[]{:S(2)}, u32[]{:S(2)}) %all-to-all-start.2) | async-done | bytes 294944 | tf_op jit(solution)/shard_map/all_to_all | solution.py:412
  121.5 1.1 adam.1
  122.6 25.5 %all_to_all.26 = bf16[64,16,128]{2,1,0:T(8,128)(2,1)S(1)} all-to-all(bf16[64,16,128]{2,1,0:T(8,128)(2,1)S(1)} %get-tuple-element.19), channel_id=1, replica_groups=mesh['y'=4,'core'=2,'x'=4,'z'=16] {'x','z'}, dimensions={0} | all-to-all | bytes 524288 | tf_op jit(solution)/shard_map/all_to_all | solution.py:433
  148.4 16.6 %all_to_all.27.source = bf16[4,4,256,128]{3,2,1,0:T(8,128)(2,1)S(1)} all-to-all(bf16[4,4,256,128]{3,2,1,0:T(8,128)(2,1)S(1)} %broadcast_in_dim.10), channel_id=1, replica_groups=mesh['y'=4,'core'=2,'x'=4,'z'=16] {'y'}, dimensions={0} | all-to-all | bytes 2097152 | tf_op jit(solution)/shard_map/all_to_all | solution.py:451
  165.0 6.1 %collective-permute-start.11 = (bf16[4,4,256,128]{3,2,1,0:T(8,128)(2,1)S(1)}, bf16[4,4,256,128]{3,2,1,0:T(8,128)(2,1)S(1)}, u32[]{:S(2)}, u32[]{:S(2)}) collective-permute-start(bf16[4,4,256,128]{3,2,1,0:T(8,128)(2,1)S(1)} %all_to_all.27.source), channel_id=1, source_target_pairs={{0,64},{64,0},{1,65},{65,1},{2,66},{66,2},{3,67},{67,3},{4,68},{68... | collective-permute-start | bytes 3145736 | tf_op jit(solution)/shard_map/ppermute | solution.py:452
  171.2 2.4 %collective-permute-start.14 = (f32[3,16,4,128]{3,2,1,0:T(4,128)S(1)}, f32[3,16,4,128]{3,2,1,0:T(4,128)S(1)}, u32[]{:S(2)}, u32[]{:S(2)}) collective-permute-start(f32[3,16,4,128]{3,2,1,0:T(4,128)S(1)} %get-tuple-element.24), channel_id=1, source_target_pairs={{0,256},{128,384},{256,0},{384,128},{1,257},{129,385},{257,1},{385... | collective-permute-start | bytes 294920 | tf_op jit(solution)/shard_map/ppermute | solution.py:437
  173.6 4.0 %collective-permute-start.13 = (f32[3,16,4,128]{3,2,1,0:T(4,128)S(1)}, f32[3,16,4,128]{3,2,1,0:T(4,128)S(1)}, u32[]{:S(2)}, u32[]{:S(2)}) collective-permute-start(f32[3,16,4,128]{3,2,1,0:T(4,128)S(1)} %get-tuple-element.25), channel_id=1, source_target_pairs={{0,384},{128,0},{256,128},{384,256},{1,385},{129,1},{257,129},{385... | collective-permute-start | bytes 294920 | tf_op jit(solution)/shard_map/ppermute | solution.py:436
  177.7 1.9 %collective-permute-start.12 = (f32[3,16,4,128]{3,2,1,0:T(4,128)S(1)}, f32[3,16,4,128]{3,2,1,0:T(4,128)S(1)}, u32[]{:S(2)}, u32[]{:S(2)}) collective-permute-start(f32[3,16,4,128]{3,2,1,0:T(4,128)S(1)} %get-tuple-element.26), channel_id=1, source_target_pairs={{0,128},{128,256},{256,384},{384,0},{1,129},{129,257},{257,385},{3... | collective-permute-start | bytes 294920 | tf_op jit(solution)/shard_map/ppermute | solution.py:435
  179.6 4.9 %collective-permute-done.12.low = f32[3,16,4,128]{3,2,1,0:T(4,128)S(1)} collective-permute-done((f32[3,16,4,128]{3,2,1,0:T(4,128)S(1)}, f32[3,16,4,128]{3,2,1,0:T(4,128)S(1)}, u32[]{:S(2)}, u32[]{:S(2)}) %collective-permute-start.12) | collective-permute-done | bytes 98336 | tf_op jit(solution)/shard_map/ppermute | solution.py:435
  184.6 1.0 join_cols.1
  185.5 1.2 join_mine.1.begun
  186.7 1.2 join_theirs.1
  (44 shorter events, 5.3 us)
Async XLA Ops:
  0.6 64.8 %copy-start = (bf16[1,1,256,2048]{3,2,1,0:T(8,128)(2,1)S(1)}, bf16[1,1,256,2048]{3,2,1,0:T(8,128)(2,1)}, u32[]{:S(2)}) copy-start(bf16[1,1,256,2048]{3,2,1,0:T(8,128)(2,1)} %param.9) | copy-start | bytes 3145732
  14.8 0.7 copy-start.6
  16.9 0.7 copy-start.1
  17.5 39.2 %all-to-all-start.1 = ((bf16[64,16,128]{2,1,0:T(8,128)(2,1)}), bf16[64,16,128]{2,1,0:T(8,128)(2,1)S(1)}, u32[]{:S(2)}, u32[]{:S(2)}) async-start(bf16[64,16,128]{2,1,0:T(8,128)(2,1)} %pick_old.1), calls=%async_computation.1 | async-start | bytes 524288 | tf_op jit(solution)/shard_map/all_to_all | solution.py:343
  35.8 14.4 %collective-permute-start = (bf16[128,2048]{1,0:T(8,128)(2,1)}, bf16[128,2048]{1,0:T(8,128)(2,1)S(1)}, u32[]{:S(2)}, u32[]{:S(2)}) collective-permute-start(bf16[128,2048]{1,0:T(8,128)(2,1)} %get-tuple-element.15), channel_id=1, source_target_pairs={{0,128},{128,256},{256,384},{384,0},{1,129},{129,257},{257,385},{3... | collective-permute-start | bytes 1572872 | tf_op jit(solution)/shard_map/ppermute | solution.py:326
  38.1 14.0 %collective-permute-start.3 = (bf16[128,2048]{1,0:T(8,128)(2,1)}, bf16[128,2048]{1,0:T(8,128)(2,1)S(1)}, u32[]{:S(2)}, u32[]{:S(2)}) collective-permute-start(bf16[128,2048]{1,0:T(8,128)(2,1)} %get-tuple-element.16), channel_id=1, source_target_pairs={{0,384},{128,0},{256,128},{384,256},{1,385},{129,1},{257,129},{385... | collective-permute-start | bytes 1572872 | tf_op jit(solution)/shard_map/ppermute | solution.py:327
  42.3 23.1 %collective-permute-start.2 = (bf16[128,2048]{1,0:T(8,128)(2,1)}, bf16[128,2048]{1,0:T(8,128)(2,1)S(1)}, u32[]{:S(2)}, u32[]{:S(2)}) collective-permute-start(bf16[128,2048]{1,0:T(8,128)(2,1)} %get-tuple-element.15), channel_id=1, source_target_pairs={{0,384},{128,0},{256,128},{384,256},{1,385},{129,1},{257,129},{385... | collective-permute-start | bytes 1572872 | tf_op jit(solution)/shard_map/ppermute | solution.py:329
  44.2 21.2 %collective-permute-start.1 = (bf16[128,2048]{1,0:T(8,128)(2,1)}, bf16[128,2048]{1,0:T(8,128)(2,1)S(1)}, u32[]{:S(2)}, u32[]{:S(2)}) collective-permute-start(bf16[128,2048]{1,0:T(8,128)(2,1)} %get-tuple-element.16), channel_id=1, source_target_pairs={{0,128},{128,256},{256,384},{384,0},{1,129},{129,257},{257,385},{3... | collective-permute-start | bytes 1572872 | tf_op jit(solution)/shard_map/ppermute | solution.py:328
  50.2 22.6 %collective-permute-start.5 = (bf16[128,2048]{1,0:T(8,128)(2,1)S(1)}, bf16[128,2048]{1,0:T(8,128)(2,1)}, u32[]{:S(2)}, u32[]{:S(2)}) collective-permute-start(bf16[128,2048]{1,0:T(8,128)(2,1)S(1)} %collective-permute-done.refs_1_), channel_id=1, source_target_pairs={{0,128},{128,256},{256,384},{384,0},{1,129},{129,257},{257,385},{3... | collective-permute-start | bytes 1572872 | tf_op jit(solution)/shard_map/ppermute | solution.py:344
  52.2 21.6 %collective-permute-start.6 = (bf16[128,2048]{1,0:T(8,128)(2,1)S(1)}, bf16[128,2048]{1,0:T(8,128)(2,1)}, u32[]{:S(2)}, u32[]{:S(2)}) collective-permute-start(bf16[128,2048]{1,0:T(8,128)(2,1)S(1)} %collective-permute-done.3.refs_4_), channel_id=1, source_target_pairs={{0,384},{128,0},{256,128},{384,256},{1,385},{129,1},{257,129},{385... | collective-permute-start | bytes 1572872 | tf_op jit(solution)/shard_map/ppermute | solution.py:345
  56.7 17.0 %copy-start.2 = (bf16[4,192,128]{2,1,0:T(8,128)(2,1)S(1)}, bf16[4,192,128]{2,1,0:T(8,128)(2,1)}, u32[]{:S(2)}) copy-start(bf16[4,192,128]{2,1,0:T(8,128)(2,1)} %copy-done.1) | copy-start | bytes 589828
  56.8 17.0 %collective-permute-start.4 = (bf16[64,16,128]{2,1,0:T(8,128)(2,1)S(1)}, bf16[64,16,128]{2,1,0:T(8,128)(2,1)S(1)}, u32[]{:S(2)}, u32[]{:S(2)}) collective-permute-start(bf16[64,16,128]{2,1,0:T(8,128)(2,1)S(1)} %all-to-all-done.1.mine), channel_id=1, source_target_pairs={{0,64},{64,0},{1,65},{65,1},{2,66},{66,2},{3,67},{67,3},{4,68},{68... | collective-permute-start | bytes 786440 | tf_op jit(solution)/shard_map/ppermute | solution.py:355
  76.7 7.4 %collective-permute-start.7 = (f32[65,16,128]{2,1,0:T(8,128)S(1)}, f32[65,16,128]{2,1,0:T(8,128)S(1)}, u32[]{:S(2)}, u32[]{:S(2)}) collective-permute-start(f32[65,16,128]{2,1,0:T(8,128)S(1)} %get-tuple-element.18), channel_id=1, source_target_pairs={{0,64},{64,0},{1,65},{65,1},{2,66},{66,2},{3,67},{67,3},{4,68},{68... | collective-permute-start | bytes 1597448 | tf_op jit(solution)/shard_map/ppermute | solution.py:376
  84.0 16.1 %copy-start.3 = (f32[16,4,512]{2,1,0:T(4,128)S(1)}, f32[16,4,512]{2,1,0:T(4,128)}, u32[]{:S(2)}) copy-start(f32[16,4,512]{2,1,0:T(4,128)} %refs_0_.1) | copy-start | bytes 393220
  84.0 16.1 %copy-start.4 = (f32[16,4,512]{2,1,0:T(4,128)S(1)}, f32[16,4,512]{2,1,0:T(4,128)}, u32[]{:S(2)}) copy-start(f32[16,4,512]{2,1,0:T(4,128)} %refs_1_.1) | copy-start | bytes 393220
  84.1 16.1 %copy-start.5 = (f32[16,4,512]{2,1,0:T(4,128)S(1)}, f32[16,4,512]{2,1,0:T(4,128)}, u32[]{:S(2)}) copy-start(f32[16,4,512]{2,1,0:T(4,128)} %refs_2_.1) | copy-start | bytes 393220
  84.1 26.3 %copy-start.9 = (s32[8,64]{1,0:T(8,128)S(1)}, s32[8,64]{1,0:T(8,128)}, u32[]{:S(2)}) copy-start(s32[8,64]{1,0:T(8,128)} %counts.1) | copy-start | bytes 6148
  84.1 26.3 %copy-start.7 = (s32[64]{0:T(128)S(1)}, s32[64]{0:T(128)}, u32[]{:S(2)}) copy-start(s32[64]{0:T(128)} %old.1) | copy-start | bytes 772
  84.6 36.9 %copy-start.8 = (s32[64]{0:T(128)S(1)}, s32[64]{0:T(128)}, u32[]{:S(2)}) copy-start(s32[64]{0:T(128)} %new.1) | copy-start | bytes 772
  85.5 35.7 %all-to-all-start.2 = ((f16[64,2,1152]{2,1,0:T(2,128)(2,1)}), f16[64,2,1152]{2,1,0:T(2,128)(2,1)S(1)}, u32[]{:S(2)}, u32[]{:S(2)}) async-start(f16[64,2,1152]{2,1,0:T(2,128)(2,1)} %convert_element_type.11), calls=%async_computation.2 | async-start | bytes 589824 | tf_op jit(solution)/shard_map/all_to_all | solution.py:412
  100.5 21.0 %collective-permute-start.10 = (f32[3,16,4,128]{3,2,1,0:T(4,128)S(1)}, f32[3,16,4,128]{3,2,1,0:T(4,128)S(1)}, u32[]{:S(2)}, u32[]{:S(2)}) collective-permute-start(f32[3,16,4,128]{3,2,1,0:T(4,128)S(1)} %get-tuple-element.28), channel_id=1, source_target_pairs={{0,256},{128,384},{256,0},{384,128},{1,257},{129,385},{257,1},{385... | collective-permute-start | bytes 294920 | tf_op jit(solution)/shard_map/ppermute | solution.py:409
  104.4 17.0 %collective-permute-start.9 = (f32[3,16,4,128]{3,2,1,0:T(4,128)S(1)}, f32[3,16,4,128]{3,2,1,0:T(4,128)S(1)}, u32[]{:S(2)}, u32[]{:S(2)}) collective-permute-start(f32[3,16,4,128]{3,2,1,0:T(4,128)S(1)} %get-tuple-element.29), channel_id=1, source_target_pairs={{0,384},{128,0},{256,128},{384,256},{1,385},{129,1},{257,129},{385... | collective-permute-start | bytes 294920 | tf_op jit(solution)/shard_map/ppermute | solution.py:408
  107.8 13.6 %collective-permute-start.8 = (f32[3,16,4,128]{3,2,1,0:T(4,128)S(1)}, f32[3,16,4,128]{3,2,1,0:T(4,128)S(1)}, u32[]{:S(2)}, u32[]{:S(2)}) collective-permute-start(f32[3,16,4,128]{3,2,1,0:T(4,128)S(1)} %get-tuple-element.30), channel_id=1, source_target_pairs={{0,128},{128,256},{256,384},{384,0},{1,129},{129,257},{257,385},{3... | collective-permute-start | bytes 294920 | tf_op jit(solution)/shard_map/ppermute | solution.py:407
  165.0 21.7 %collective-permute-start.11 = (bf16[4,4,256,128]{3,2,1,0:T(8,128)(2,1)S(1)}, bf16[4,4,256,128]{3,2,1,0:T(8,128)(2,1)S(1)}, u32[]{:S(2)}, u32[]{:S(2)}) collective-permute-start(bf16[4,4,256,128]{3,2,1,0:T(8,128)(2,1)S(1)} %all_to_all.27.source), channel_id=1, source_target_pairs={{0,64},{64,0},{1,65},{65,1},{2,66},{66,2},{3,67},{67,3},{4,68},{68... | collective-permute-start | bytes 3145736 | tf_op jit(solution)/shard_map/ppermute | solution.py:452
  171.2 8.4 %collective-permute-start.14 = (f32[3,16,4,128]{3,2,1,0:T(4,128)S(1)}, f32[3,16,4,128]{3,2,1,0:T(4,128)S(1)}, u32[]{:S(2)}, u32[]{:S(2)}) collective-permute-start(f32[3,16,4,128]{3,2,1,0:T(4,128)S(1)} %get-tuple-element.24), channel_id=1, source_target_pairs={{0,256},{128,384},{256,0},{384,128},{1,257},{129,385},{257,1},{385... | collective-permute-start | bytes 294920 | tf_op jit(solution)/shard_map/ppermute | solution.py:437
  173.6 6.0 %collective-permute-start.13 = (f32[3,16,4,128]{3,2,1,0:T(4,128)S(1)}, f32[3,16,4,128]{3,2,1,0:T(4,128)S(1)}, u32[]{:S(2)}, u32[]{:S(2)}) collective-permute-start(f32[3,16,4,128]{3,2,1,0:T(4,128)S(1)} %get-tuple-element.25), channel_id=1, source_target_pairs={{0,384},{128,0},{256,128},{384,256},{1,385},{129,1},{257,129},{385... | collective-permute-start | bytes 294920 | tf_op jit(solution)/shard_map/ppermute | solution.py:436
  177.7 6.9 %collective-permute-start.12 = (f32[3,16,4,128]{3,2,1,0:T(4,128)S(1)}, f32[3,16,4,128]{3,2,1,0:T(4,128)S(1)}, u32[]{:S(2)}, u32[]{:S(2)}) collective-permute-start(f32[3,16,4,128]{3,2,1,0:T(4,128)S(1)} %get-tuple-element.26), channel_id=1, source_target_pairs={{0,128},{128,256},{256,384},{384,0},{1,129},{129,257},{257,385},{3... | collective-permute-start | bytes 294920 | tf_op jit(solution)/shard_map/ppermute | solution.py:435

commit v7 on v5

--- a/solution.py
+++ b/solution.py
@@ -20,7 +20,8 @@
 DOWN = [(i, (i - 1) % Y) for i in range(Y)]
 ACROSS = [(i, (i + 2) % Y) for i in range(Y)]
 SWAP = [(0, 1), (1, 0)]
-LINE = ((0, None), (3, 0), (3, 1), (1, 0), (1, 1), (2, 0), (2, 1))
+APART = [(i * C + c, (i + 1 - 2 * c) % Y * C + c) for i in range(Y) for c in range(C)]
+BACK = [(t, s) for s, t in APART]
 VMEM = pl.BlockSpec(memory_space=pltpu.VMEM)
 SMEM = pl.BlockSpec(memory_space=pltpu.SMEM)
 ANY = pl.BlockSpec(memory_space=pl.ANY)
@@ -123,8 +124,8 @@
 
 
 def adam(old, new, total, got, own, low, high, far, out, after, state, acc, table):
-    experts, pairs = acc.shape[:2]
-    rows = state.shape[3]
+    experts, _, data = acc.shape
+    rows, lanes = state.shape[3:]
     y_here = lax.axis_index("y")
     state[y_here] = own[...]
     state[(y_here + 3) % Y] = low[...]
@@ -132,12 +133,16 @@
     state[(y_here + 2) % Y] = far[...]
     acc[...] = jnp.zeros_like(acc)
     for p in range(PLACES):
-        acc[old[p]] += got[p, :pairs] * jnp.exp2(got[p, pairs:] - 14.0)
+        undo = jnp.exp2(got[p, :, data:] - 14.0)
+        acc[old[p]] += got[p, :, :data] * jnp.concatenate([undo] * (data // lanes), axis=1)
     for e in range(experts):
         master, first, second = (
             jnp.concatenate([state[y, n, e] for y in range(Y)], axis=0) for n in range(3)
         )
-        grad = jnp.concatenate([acc[e, t] for t in range(pairs)], axis=0) / total[e]
+        grad = jnp.concatenate(
+            [acc[e, :, at : at + lanes] for at in range(0, data, lanes)], axis=0
+        )
+        grad = grad / total[e]
         new_first = decay_first * first + (1.0 - decay_first) * grad
         new_second = decay_second * second + (1.0 - decay_second) * grad * grad
         first_hat = new_first / (1.0 - decay_first**step_number)
@@ -151,30 +156,6 @@
                 after[y, n, e] = value[y * rows : (y + 1) * rows]
     for p in range(PLACES):
         out[p] = table[new[p]]
-
-
-def half_grad(out_ref, local_ref, chunks, half):
-    rows_shard = out_ref.shape[1] // Y
-    wide = PLACES * rows_shard
-    peak = None
-    for y in range(Y):
-        at = pl.multiple_of((2 * y + half) * wide, wide)
-        total, row = None, 0
-        for chunk in chunks:
-            rows = chunk.shape[0]
-            term = jnp.dot(
-                local_ref[:, row : row + rows],
-                chunk[:, pl.ds(at, wide)],
-                preferred_element_type=jnp.float32,
-            )
-            total = term if total is None else total + term
-            row += rows
-        size = jnp.abs(total)
-        peak = size if peak is None else jnp.maximum(peak, size)
-        out_ref[:PLACES, y * rows_shard : (y + 1) * rows_shard, :] = total.T.reshape(
-            PLACES, rows_shard, -1
-        )
-    out_ref[PLACES] = jnp.broadcast_to(jnp.max(peak, keepdims=True), out_ref.shape[1:])
 
 
 def forward_part(chunk, weights, which):
@@ -193,56 +174,94 @@
     return total
 
 
+def local_part(both, payload, source):
+    packed = both.shape[0] // 2
+    other = swapped(both)
+    first = lower_half(both)
+    gate = jnp.where(first, both, other)
+    sigma = jax.nn.sigmoid(gate)
+    active = gate * sigma
+    slope = sigma * (1.0 + gate * (1.0 - sigma))
+    hidden = payload[source, payload.shape[1] - packed :, :].astype(jnp.float32)
+    around = swapped(hidden)
+    begin = lower_half(hidden)
+    incoming = jnp.concatenate(
+        [jnp.where(begin, hidden, around), jnp.where(begin, around, hidden)], axis=0
+    )
+    local = jnp.where(first, incoming * other * slope, incoming * active)
+    return local.T.astype(jnp.bfloat16)
+
+
+def grad_part(local, chunk, y, half, wide):
+    at = pl.multiple_of((2 * y + half) * wide, wide)
+    return jnp.dot(local, chunk[:, pl.ds(at, wide)], preferred_element_type=jnp.float32)
+
+
+def finish_grad(out_ref, begun, local, chunk, half):
+    rows_shard = out_ref.shape[1] // Y
+    wide = PLACES * rows_shard
+    peak = None
+    for y in range(Y):
+        total = begun[y] + grad_part(local, chunk, y, half, wide)
+        size = jnp.abs(total)
+        peak = size if peak is None else jnp.maximum(peak, size)
+        out_ref[:PLACES, y * rows_shard : (y + 1) * rows_shard, :] = total.T.reshape(
+            PLACES, rows_shard, -1
+        )
+    out_ref[PLACES] = jnp.broadcast_to(jnp.max(peak, keepdims=True), out_ref.shape[1:])
+
+
 def forward_mine(mine, *refs):
     chunks, out_ref = refs[:-1], refs[-1]
     weights = mine[...]
-    row = 0
-    for chunk in chunks:
-        rows = chunk.shape[0]
-        out_ref[row : row + rows, :] = forward_part(chunk, weights, lax.axis_index("core"))
-        row += rows
-
-
-def grad_theirs(part_ref, theirs, payload, *refs):
-    chunks, (out_ref, local_ref) = refs[:-2], refs[-2:]
+    for k, chunk in enumerate(chunks):
+        out_ref[k] = forward_part(chunk, weights, lax.axis_index("core"))
+
+
+def near_grad(part_ref, theirs, payload, *refs):
+    chunks, (theirs_ref, mine_ref) = refs[:-2], refs[-2:]
     y_here, core = lax.axis_index("y"), lax.axis_index("core")
     weights = theirs[...]
-    packed = chunks[-1].shape[0]
-    head = payload.shape[1] - packed
-    row = 0
-    for (step, part), chunk in zip(LINE, chunks):
-        rows = chunk.shape[0]
-        both = part_ref[row : row + rows, :] + forward_part(chunk, weights, 1 - core)
-        other = swapped(both)
-        first = lower_half(both)
-        gate = jnp.where(first, both, other)
-        sigma = jax.nn.sigmoid(gate)
-        active = gate * sigma
-        slope = sigma * (1.0 + gate * (1.0 - sigma))
-        hidden = payload[(y_here + step) % Y, head:, :].astype(jnp.float32)
-        around = swapped(hidden)
-        begin = lower_half(hidden)
-        halves = [jnp.where(begin, hidden, around), jnp.where(begin, around, hidden)]
-        incoming = jnp.concatenate(halves, axis=0) if part is None else halves[part]
-        local = jnp.where(first, incoming * other * slope, incoming * active)
-        local_ref[:, row : row + rows] = local.T.astype(jnp.bfloat16)
-        row += rows
-    half_grad(out_ref, local_ref, chunks, 1 - core)
-
-
-def grad_mine(local_ref, *refs):
-    chunks, out_ref = refs[:-1], refs[-1]
-    half_grad(out_ref, local_ref, chunks, lax.axis_index("core"))
+    steps = (0, 3 + 2 * core, 1 + 2 * core)
+    locals_ = [
+        local_part(
+            part_ref[k] + forward_part(chunk, weights, 1 - core), payload, (y_here + step) % Y
+        )
+        for k, (step, chunk) in enumerate(zip(steps, chunks))
+    ]
+    wide = theirs_ref.shape[2]
+    for out_ref, half in ((theirs_ref, 1 - core), (mine_ref, core)):
+        for y in range(Y):
+            total = None
+            for local, chunk in zip(locals_, chunks):
+                term = grad_part(local, chunk, y, half, wide)
+                total = term if total is None else total + term
+            out_ref[y] = total
+
+
+def grad_theirs(begun, mine, theirs, payload, chunk, out_ref, local_ref):
+    core = lax.axis_index("core")
+    both = forward_part(chunk, mine[...], core) + forward_part(chunk, theirs[...], 1 - core)
+    local = local_part(both, payload, (lax.axis_index("y") + 2) % Y)
+    local_ref[...] = local
+    finish_grad(out_ref, begun, local, chunk, 1 - core)
+
+
+def grad_mine(begun, local_ref, chunk, out_ref):
+    finish_grad(out_ref, begun, local_ref[...], chunk, lax.axis_index("core"))
 
 
 def combine(mine, theirs, out):
-    pairs = out.shape[1] - 1
+    lanes = mine.shape[-1]
+    pairs = out.shape[2] // lanes - 1
     bits = jnp.ceil(jnp.log2(jnp.maximum(mine[PLACES] + theirs[PLACES], 1e-30)))
     scale = jnp.exp2(14.0 - bits)
     for t in range(pairs):
         cut = slice(2 * t, 2 * t + 2)
-        out[:, t] = (mine[:PLACES, cut, :] + theirs[:PLACES, cut, :]) * scale[cut]
-    out[:, pairs] = jnp.broadcast_to(bits[:2], (PLACES, 2, bits.shape[1]))
+        out[:, :, t * lanes : (t + 1) * lanes] = (
+            mine[:PLACES, cut, :] + theirs[:PLACES, cut, :]
+        ) * scale[cut]
+    out[:, :, pairs * lanes :] = jnp.broadcast_to(bits[:2], (PLACES, 2, bits.shape[1]))
 
 
 def join(source, out, which, blocks, sems):
@@ -287,8 +306,7 @@
     own = tokens[0, 0]
     rows = own.shape[0]
     half_rows = rows // 2
-    own_a, own_b = own[:half_rows], own[half_rows:]
-
+    hbm = pl.BlockSpec(memory_space=pltpu.MemorySpace.HBM)
     payload = pl.pallas_call(
         prepare,
         out_shape=jax.ShapeDtypeStruct((Y, experts * rows_shard + half_rows, lanes), bf16),
@@ -297,10 +315,8 @@
         name="prepare",
     )(row_count, routing[0, 0], hidden_grad[0, 0], master)
     payload = lax.all_to_all(payload, "y", 0, 0, tiled=True)
-    low_a = lax.ppermute(own_a, "y", UP)
-    high_b = lax.ppermute(own_b, "y", DOWN)
-    low_b = lax.ppermute(own_b, "y", UP)
-    high_a = lax.ppermute(own_a, "y", DOWN)
+    near_one = lax.ppermute(own, ("y", "core"), APART)
+    near_two = lax.ppermute(own, ("y", "core"), BACK)
     picked = pl.pallas_call(
         pick_old,
         out_shape=jax.ShapeDtypeStruct((PLACES, Y * rows_shard, lanes), bf16),
@@ -315,8 +331,7 @@
         name="pick_old",
     )(old_slots, payload)
     landed = lax.all_to_all(picked, ("x", "z"), 0, 0, tiled=True)
-    far_a = lax.ppermute(low_a, "y", UP)
-    far_b = lax.ppermute(high_b, "y", DOWN)
+    far = lax.ppermute(near_one, ("y", "core"), APART)
 
     def by_rows(x):
         return (
@@ -328,38 +343,46 @@
     w_mine = landed
     w_theirs = lax.ppermute(w_mine, "core", SWAP)
 
-    chunks = [own, low_a, low_b, high_a, high_b, far_a, far_b]
-    line_rows = sum(c.shape[0] for c in chunks)
+    near = [own, near_one, near_two]
     forward = pl.pallas_call(
         forward_mine,
-        out_shape=jax.ShapeDtypeStruct((line_rows, lanes), f32),
-        in_specs=[VMEM] * (1 + len(chunks)),
+        out_shape=jax.ShapeDtypeStruct((len(near), rows, lanes), f32),
+        in_specs=[VMEM] * (1 + len(near)),
         out_specs=VMEM,
         compiler_params=grant(24),
         name="forward_mine",
-    )(w_mine, *chunks)
+    )(w_mine, *near)
+    begun_shape = jax.ShapeDtypeStruct((Y, lanes, PLACES * rows_shard), f32)
+    begun_theirs, begun_mine = pl.pallas_call(
+        near_grad,
+        out_shape=(begun_shape, begun_shape),
+        in_specs=[VMEM] * (3 + len(near)),
+        out_specs=(VMEM, VMEM),
+        compiler_params=grant(24),
+        name="near_grad",
+    )(forward, w_theirs, payload, *near)
     grad_shape = jax.ShapeDtypeStruct((PLACES + 1, Y * rows_shard, lanes), f32)
     sent, local = pl.pallas_call(
         grad_theirs,
-        out_shape=(grad_shape, jax.ShapeDtypeStruct((lanes, line_rows), bf16)),
-        in_specs=[VMEM] * (3 + len(chunks)),
+        out_shape=(grad_shape, jax.ShapeDtypeStruct((lanes, rows), bf16)),
+        in_specs=[VMEM] * 5,
         out_specs=(VMEM, VMEM),
         compiler_params=grant(24),
         name="grad_theirs",
-    )(forward, w_theirs, payload, *chunks)
+    )(begun_theirs, w_mine, w_theirs, payload, far)
     received = lax.ppermute(sent, "core", SWAP)
     summed = pl.pallas_call(
         grad_mine,
         out_shape=grad_shape,
-        in_specs=[VMEM] * (1 + len(chunks)),
+        in_specs=[VMEM] * 3,
         out_specs=VMEM,
         compiler_params=grant(24),
         name="grad_mine",
-    )(local, *chunks)
+    )(begun_mine, local, far)
     pairs = Y * rows_shard // 2
     scaled = pl.pallas_call(
         combine,
-        out_shape=jax.ShapeDtypeStruct((PLACES, pairs + 1, 2, lanes), f32),
+        out_shape=jax.ShapeDtypeStruct((PLACES, 2, (pairs + 1) * lanes), f32),
         in_specs=[VMEM] * 2,
         out_specs=VMEM,
         compiler_params=grant(6),
@@ -398,7 +421,7 @@
         out_specs=(VMEM, VMEM),
         scratch_shapes=[
             pltpu.VMEM((Y, 3, experts, rows_shard, lanes), f32),
-            pltpu.VMEM((experts, pairs, 2, lanes), f32),
+            pltpu.VMEM((experts, 2, pairs * lanes), f32),
             pltpu.VMEM((experts, Y * rows_shard, lanes), bf16),
         ],
         compiler_params=grant(6),
@@ -425,7 +448,6 @@
     mine = lax.all_to_all(copies, "y", 0, 0, tiled=True)
     theirs = lax.ppermute(mine, "core", SWAP)
     block_rows = PLACES * rows_shard
-    hbm = pl.BlockSpec(memory_space=pltpu.MemorySpace.HBM)
     scratch = [pltpu.VMEM((Y, block_rows, width), bf16), pltpu.SemaphoreType.DMA((Y,))]
     whole = jax.ShapeDtypeStruct((Y, C, block_rows, width), bf16)
     begun = pl.pallas_call(

time: 189 us -> 185 us (0.979)
  starting transfers between devices: 86.1 us -> 83.3 us
  blocking collectives: 50.4 us -> 53.1 us
  waiting for transfers between devices: 31.5 us -> 29.1 us
    ppermute x6 -> x3, waiting for transfers between devices: 13.6 us -> 1.65 us  [the longest x1 1.64 us: shards(): far = lax.ppermute(near_one, ('y', 'core'), APART)]
    all_to_all x1, waiting for transfers between devices: 0.01 us -> 9.66 us  [shards(): landed = lax.all_to_all(picked, ('x', 'z'), 0, 0, tiled=True)]
    ppermute x6 -> x3, starting transfers between devices: 17.7 us -> 12.5 us  [the longest x1 5.59 us: shards(): near_one = lax.ppermute(own, ('y', 'core'), APART)]
    ppermute x1, starting transfers between devices: 5.47 us -> 7.68 us  [shards(): received = lax.ppermute(sent, 'core', SWAP)]
    all_to_all x1, blocking collectives: 10.2 us -> 12.1 us  [shards(): payload = lax.all_to_all(payload, 'y', 0, 0, tiled=True)]
    pallas_call x3 -> x4, Pallas kernels: 4.48 us -> 5.27 us  [the longest x1 2.46 us: shards(): pl.pallas_call(near_grad, out_shape=(begun_shape, begun_shape), in_specs=...]
  transfers between devices with their start and end apart: 17 -> 14, of which waited for: 6 -> 5; matrix products, arithmetic and copies ran while one was open for 1% -> 0% of each run, Pallas kernels for 3% -> 6%
where the time goes in v7:
time: 185 us; the launch traced here: 184 us
  starting transfers between devices  83.3 us (45%)
  blocking collectives  53.1 us (29%)
  waiting for transfers between devices  29.1 us (16%)
  Pallas kernels  15.1 us (8%)
    all_to_all x1, blocking collectives, shards(): landed = lax.all_to_all(picked, ('x', 'z'), 0, 0, tiled=True)  25.1 us
    all_to_all x1, starting transfers between devices, shards(): landed = lax.all_to_all(picked, ('x', 'z'), 0, 0, tiled=True)  18.5 us
    all_to_all x1, blocking collectives, shards(): mine = lax.all_to_all(copies, 'y', 0, 0, tiled=True)  15.9 us
    all_to_all x1, starting transfers between devices, shards(): lax.all_to_all(scaled.astype(jnp.float16), ('x', 'z'), 0, 0, tiled=True)  14.5 us
    all_to_all x1, blocking collectives, shards(): payload = lax.all_to_all(payload, 'y', 0, 0, tiled=True)  12.1 us
    all_to_all x1, waiting for transfers between devices, shards(): lax.all_to_all(scaled.astype(jnp.float16), ('x', 'z'), 0, 0, tiled=True)  11.8 us
    all_to_all x1, waiting for transfers between devices, shards(): landed = lax.all_to_all(picked, ('x', 'z'), 0, 0, tiled=True)  9.66 us
    ppermute x1, starting transfers between devices, shards(): received = lax.ppermute(sent, 'core', SWAP)  7.68 us
  transfers between devices with their start and end apart: 14, of which 5 were waited for; matrix products, arithmetic and copies ran while one was open for 0% of the time, Pallas kernels for 6%

profile of v7, /device:TPU:1, one launch (start us, length us, event | category | flops | bytes accessed | tf_op | source)
XLA Modules:
  0.0 184.1 jit_solution(5061241056724805781)
XLA Ops:
  0.6 5.6 %collective-permute-start = (bf16[256,2048]{1,0:T(8,128)(2,1)}, bf16[256,2048]{1,0:T(8,128)(2,1)S(1)}, u32[]{:S(2)}, u32[]{:S(2)}) collective-permute-start(bf16[256,2048]{1,0:T(8,128)(2,1)} %bitcast.29), channel_id=1, source_target_pairs={{0,128},{64,448},{128,256},{192,64},{256,384},{320,192},{384,0},{4... | collective-permute-start | bytes 3145736 | tf_op jit(solution)/shard_map/ppermute | solution.py:318
  6.2 1.9 %prepare.1 = bf16[4,192,128]{2,1,0:T(8,128)(2,1)} custom-call(s32[8,64]{1,0:T(8,128)} %counts.1, s32[4,64]{1,0:T(4,128)} %bitcast.37, bf16[256,256]{1,0:T(8,128)(2,1)} %bitcast.36, f32[16,4,512]{2,1,0:T(4,128)} %refs_0_.1), custom_call_target="tpu_custom_call" | custom-call | tf_op jit(solution)/shard_map/prepare/pallas_call | solution.py:310
  8.2 12.1 %all_to_all.25.payload = bf16[4,192,128]{2,1,0:T(8,128)(2,1)S(1)} all-to-all(bf16[4,192,128]{2,1,0:T(8,128)(2,1)} %prepare.1), channel_id=1, replica_groups=mesh['y'=4,'core'=2,'x'=4,'z'=16] {'y'}, dimensions={0} | all-to-all | bytes 393216 | tf_op jit(solution)/shard_map/all_to_all | solution.py:317
  21.0 1.3 pick_old.1
  22.3 18.5 %all-to-all-start.1 = ((bf16[64,16,128]{2,1,0:T(8,128)(2,1)}), bf16[64,16,128]{2,1,0:T(8,128)(2,1)}, u32[]{:S(2)}, u32[]{:S(2)}) async-start(bf16[64,16,128]{2,1,0:T(8,128)(2,1)} %pick_old.1), calls=%async_computation.1 | async-start | bytes 524288 | tf_op jit(solution)/shard_map/all_to_all | solution.py:333
  40.8 3.4 %collective-permute-start.1 = (bf16[256,2048]{1,0:T(8,128)(2,1)}, bf16[256,2048]{1,0:T(8,128)(2,1)}, u32[]{:S(2)}, u32[]{:S(2)}) collective-permute-start(bf16[256,2048]{1,0:T(8,128)(2,1)} %bitcast.30), channel_id=1, source_target_pairs={{128,0},{448,64},{256,128},{64,192},{384,256},{192,320},{0,384},{3... | collective-permute-start | bytes 3145736 | tf_op jit(solution)/shard_map/ppermute | solution.py:319
  44.2 3.6 %collective-permute-start.3 = (bf16[256,2048]{1,0:T(8,128)(2,1)S(1)}, bf16[256,2048]{1,0:T(8,128)(2,1)S(1)}, u32[]{:S(2)}, u32[]{:S(2)}) collective-permute-start(bf16[256,2048]{1,0:T(8,128)(2,1)S(1)} %collective-permute-done.refs_1_), channel_id=1, source_target_pairs={{0,128},{64,448},{128,256},{192,64},{256,384},{320,192},{384,0},{4... | collective-permute-start | bytes 3145736 | tf_op jit(solution)/shard_map/ppermute | solution.py:334
  47.8 9.7 %all-to-all-done.1.mine = bf16[64,16,128]{2,1,0:T(8,128)(2,1)} async-done(((bf16[64,16,128]{2,1,0:T(8,128)(2,1)}), bf16[64,16,128]{2,1,0:T(8,128)(2,1)}, u32[]{:S(2)}, u32[]{:S(2)}) %all-to-all-start.1) | async-done | bytes 262176 | tf_op jit(solution)/shard_map/all_to_all | solution.py:333
  57.5 6.9 %collective-permute-start.2 = (bf16[64,16,128]{2,1,0:T(8,128)(2,1)}, bf16[64,16,128]{2,1,0:T(8,128)(2,1)S(1)}, u32[]{:S(2)}, u32[]{:S(2)}) collective-permute-start(bf16[64,16,128]{2,1,0:T(8,128)(2,1)} %all-to-all-done.1.mine), channel_id=1, source_target_pairs={{0,64},{64,0},{1,65},{65,1},{2,66},{66,2},{3,67},{67,3},{4,68},{68... | collective-permute-start | bytes 786440 | tf_op jit(solution)/shard_map/ppermute | solution.py:344
  64.4 1.9 %forward_mine.1.part_ref = f32[3,256,128]{2,1,0:T(8,128)S(1)} custom-call(bf16[64,16,128]{2,1,0:T(8,128)(2,1)} %all-to-all-done.1.mine, bf16[256,2048]{1,0:T(8,128)(2,1)S(1)} %bitcast.31, bf16[256,2048]{1,0:T(8,128)(2,1)S(1)} %collective-permute-done.refs_1_, bf16[256,2048]{1,0:T(8,128)(2,1)} %collective-permute-done.1.refs_2_), custom_call_target="tpu_custom_call" | custom-call | tf_op jit(solution)/shard_map/forward_mine/pallas_call | solution.py:347
  66.3 2.5 %near_grad.1 = (f32[4,128,256]{2,1,0:T(8,128)S(1)}, f32[4,128,256]{2,1,0:T(8,128)S(1)}) custom-call(f32[3,256,128]{2,1,0:T(8,128)S(1)} %forward_mine.1.part_ref, bf16[64,16,128]{2,1,0:T(8,128)(2,1)S(1)} %collective-permute-done.2.theirs, bf16[4,192,128]{2,1,0:T(8,128)(2,1)S(1)} %all_to_all.25.payload, bf16[256,2048]{1,0:T(8,128)(2,1)S(1)} %bitcast.32, ...), custom_call_target="tpu_custom_call" | custom-call | tf_op jit(solution)/shard_map/near_grad/pallas_call | solution.py:356
  68.8 1.6 collective-permute-done.3.chunk
  70.4 1.9 %grad_theirs.1 = (f32[65,16,128]{2,1,0:T(8,128)S(1)}, bf16[128,256]{1,0:T(8,128)(2,1)S(1)}) custom-call(f32[4,128,256]{2,1,0:T(8,128)S(1)} %get-tuple-element.14.begun, bf16[64,16,128]{2,1,0:T(8,128)(2,1)} %all-to-all-done.1.mine, bf16[64,16,128]{2,1,0:T(8,128)(2,1)S(1)} %collective-permute-done.2.theirs, bf16[4,192,128]{2,1,0:T(8,128)(2,1)S(1)} %all_to_all.25.payload, ...), custom_call_target="tpu_custom_call" | custom-call | tf_op jit(solution)/shard_map/grad_theirs/pallas_call | solution.py:365
  72.3 7.7 %collective-permute-start.4 = (f32[65,16,128]{2,1,0:T(8,128)S(1)}, f32[65,16,128]{2,1,0:T(8,128)S(1)}, u32[]{:S(2)}, u32[]{:S(2)}) collective-permute-start(f32[65,16,128]{2,1,0:T(8,128)S(1)} %get-tuple-element.16), channel_id=1, source_target_pairs={{0,64},{64,0},{1,65},{65,1},{2,66},{66,2},{3,67},{67,3},{4,68},{68... | collective-permute-start | bytes 1597448 | tf_op jit(solution)/shard_map/ppermute | solution.py:373
  80.5 1.0 collective-permute-done.4.theirs
  82.1 0.9 convert_element_type.11
  83.0 14.5 %all-to-all-start.2 = ((f16[64,2,1152]{2,1,0:T(2,128)(2,1)}), f16[64,2,1152]{2,1,0:T(2,128)(2,1)S(1)}, u32[]{:S(2)}, u32[]{:S(2)}) async-start(f16[64,2,1152]{2,1,0:T(2,128)(2,1)} %convert_element_type.11), calls=%async_computation.2 | async-start | bytes 589824 | tf_op jit(solution)/shard_map/all_to_all | solution.py:409
  97.9 2.6 %collective-permute-start.7 = (f32[3,16,4,128]{3,2,1,0:T(4,128)S(1)}, f32[3,16,4,128]{3,2,1,0:T(4,128)S(1)}, u32[]{:S(2)}, u32[]{:S(2)}) collective-permute-start(f32[3,16,4,128]{3,2,1,0:T(4,128)S(1)} %get-tuple-element.26), channel_id=1, source_target_pairs={{0,256},{128,384},{256,0},{384,128},{1,257},{129,385},{257,1},{385... | collective-permute-start | bytes 294920 | tf_op jit(solution)/shard_map/ppermute | solution.py:406
  100.5 3.6 %collective-permute-start.6 = (f32[3,16,4,128]{3,2,1,0:T(4,128)S(1)}, f32[3,16,4,128]{3,2,1,0:T(4,128)S(1)}, u32[]{:S(2)}, u32[]{:S(2)}) collective-permute-start(f32[3,16,4,128]{3,2,1,0:T(4,128)S(1)} %get-tuple-element.27), channel_id=1, source_target_pairs={{0,384},{128,0},{256,128},{384,256},{1,385},{129,1},{257,129},{385... | collective-permute-start | bytes 294920 | tf_op jit(solution)/shard_map/ppermute | solution.py:405
  104.0 2.5 %collective-permute-start.5 = (f32[3,16,4,128]{3,2,1,0:T(4,128)S(1)}, f32[3,16,4,128]{3,2,1,0:T(4,128)S(1)}, u32[]{:S(2)}, u32[]{:S(2)}) collective-permute-start(f32[3,16,4,128]{3,2,1,0:T(4,128)S(1)} %get-tuple-element.28), channel_id=1, source_target_pairs={{0,128},{128,256},{256,384},{384,0},{1,129},{129,257},{257,385},{3... | collective-permute-start | bytes 294920 | tf_op jit(solution)/shard_map/ppermute | solution.py:404
  106.8 11.8 %all-to-all-done.2 = f16[64,2,1152]{2,1,0:T(2,128)(2,1)S(1)} async-done(((f16[64,2,1152]{2,1,0:T(2,128)(2,1)}), f16[64,2,1152]{2,1,0:T(2,128)(2,1)S(1)}, u32[]{:S(2)}, u32[]{:S(2)}) %all-to-all-start.2) | async-done | bytes 294944 | tf_op jit(solution)/shard_map/all_to_all | solution.py:409
  118.8 1.1 adam.1
  119.9 25.1 %all_to_all.26 = bf16[64,16,128]{2,1,0:T(8,128)(2,1)S(1)} all-to-all(bf16[64,16,128]{2,1,0:T(8,128)(2,1)S(1)} %get-tuple-element.17), channel_id=1, replica_groups=mesh['y'=4,'core'=2,'x'=4,'z'=16] {'x','z'}, dimensions={0} | all-to-all | bytes 524288 | tf_op jit(solution)/shard_map/all_to_all | solution.py:430
  145.3 15.9 %all_to_all.27.source = bf16[4,4,256,128]{3,2,1,0:T(8,128)(2,1)S(1)} all-to-all(bf16[4,4,256,128]{3,2,1,0:T(8,128)(2,1)S(1)} %broadcast_in_dim.10), channel_id=1, replica_groups=mesh['y'=4,'core'=2,'x'=4,'z'=16] {'y'}, dimensions={0} | all-to-all | bytes 2097152 | tf_op jit(solution)/shard_map/all_to_all | solution.py:448
  161.2 6.1 %collective-permute-start.8 = (bf16[4,4,256,128]{3,2,1,0:T(8,128)(2,1)S(1)}, bf16[4,4,256,128]{3,2,1,0:T(8,128)(2,1)S(1)}, u32[]{:S(2)}, u32[]{:S(2)}) collective-permute-start(bf16[4,4,256,128]{3,2,1,0:T(8,128)(2,1)S(1)} %all_to_all.27.source), channel_id=1, source_target_pairs={{0,64},{64,0},{1,65},{65,1},{2,66},{66,2},{3,67},{67,3},{4,68},{68... | collective-permute-start | bytes 3145736 | tf_op jit(solution)/shard_map/ppermute | solution.py:449
  167.3 2.4 %collective-permute-start.11 = (f32[3,16,4,128]{3,2,1,0:T(4,128)S(1)}, f32[3,16,4,128]{3,2,1,0:T(4,128)S(1)}, u32[]{:S(2)}, u32[]{:S(2)}) collective-permute-start(f32[3,16,4,128]{3,2,1,0:T(4,128)S(1)} %get-tuple-element.22), channel_id=1, source_target_pairs={{0,256},{128,384},{256,0},{384,128},{1,257},{129,385},{257,1},{385... | collective-permute-start | bytes 294920 | tf_op jit(solution)/shard_map/ppermute | solution.py:434
  169.8 4.0 %collective-permute-start.10 = (f32[3,16,4,128]{3,2,1,0:T(4,128)S(1)}, f32[3,16,4,128]{3,2,1,0:T(4,128)S(1)}, u32[]{:S(2)}, u32[]{:S(2)}) collective-permute-start(f32[3,16,4,128]{3,2,1,0:T(4,128)S(1)} %get-tuple-element.23), channel_id=1, source_target_pairs={{0,384},{128,0},{256,128},{384,256},{1,385},{129,1},{257,129},{385... | collective-permute-start | bytes 294920 | tf_op jit(solution)/shard_map/ppermute | solution.py:433
  173.9 1.9 %collective-permute-start.9 = (f32[3,16,4,128]{3,2,1,0:T(4,128)S(1)}, f32[3,16,4,128]{3,2,1,0:T(4,128)S(1)}, u32[]{:S(2)}, u32[]{:S(2)}) collective-permute-start(f32[3,16,4,128]{3,2,1,0:T(4,128)S(1)} %get-tuple-element.24), channel_id=1, source_target_pairs={{0,128},{128,256},{256,384},{384,0},{1,129},{129,257},{257,385},{3... | collective-permute-start | bytes 294920 | tf_op jit(solution)/shard_map/ppermute | solution.py:432
  175.8 4.9 %collective-permute-done.9.low = f32[3,16,4,128]{3,2,1,0:T(4,128)S(1)} collective-permute-done((f32[3,16,4,128]{3,2,1,0:T(4,128)S(1)}, f32[3,16,4,128]{3,2,1,0:T(4,128)S(1)}, u32[]{:S(2)}, u32[]{:S(2)}) %collective-permute-start.9) | collective-permute-done | bytes 98336 | tf_op jit(solution)/shard_map/ppermute | solution.py:432
  180.7 1.0 join_cols.1
  181.7 1.2 join_mine.1.begun
  182.9 1.2 join_theirs.1
  (35 shorter events, 2.7 us)
Async XLA Ops:
  0.6 63.8 %copy-start = (bf16[1,1,256,2048]{3,2,1,0:T(8,128)(2,1)S(1)}, bf16[1,1,256,2048]{3,2,1,0:T(8,128)(2,1)}, u32[]{:S(2)}) copy-start(bf16[1,1,256,2048]{3,2,1,0:T(8,128)(2,1)} %param.9) | copy-start | bytes 3145732
  0.6 43.6 %collective-permute-start = (bf16[256,2048]{1,0:T(8,128)(2,1)}, bf16[256,2048]{1,0:T(8,128)(2,1)S(1)}, u32[]{:S(2)}, u32[]{:S(2)}) collective-permute-start(bf16[256,2048]{1,0:T(8,128)(2,1)} %bitcast.29), channel_id=1, source_target_pairs={{0,128},{64,448},{128,256},{192,64},{256,384},{320,192},{384,0},{4... | collective-permute-start | bytes 3145736 | tf_op jit(solution)/shard_map/ppermute | solution.py:318
  20.3 0.7 copy-start.4
  22.3 35.2 %all-to-all-start.1 = ((bf16[64,16,128]{2,1,0:T(8,128)(2,1)}), bf16[64,16,128]{2,1,0:T(8,128)(2,1)}, u32[]{:S(2)}, u32[]{:S(2)}) async-start(bf16[64,16,128]{2,1,0:T(8,128)(2,1)} %pick_old.1), calls=%async_computation.1 | async-start | bytes 524288 | tf_op jit(solution)/shard_map/all_to_all | solution.py:333
  40.8 23.6 %collective-permute-start.1 = (bf16[256,2048]{1,0:T(8,128)(2,1)}, bf16[256,2048]{1,0:T(8,128)(2,1)}, u32[]{:S(2)}, u32[]{:S(2)}) collective-permute-start(bf16[256,2048]{1,0:T(8,128)(2,1)} %bitcast.30), channel_id=1, source_target_pairs={{128,0},{448,64},{256,128},{64,192},{384,256},{192,320},{0,384},{3... | collective-permute-start | bytes 3145736 | tf_op jit(solution)/shard_map/ppermute | solution.py:319
  44.2 26.2 %collective-permute-start.3 = (bf16[256,2048]{1,0:T(8,128)(2,1)S(1)}, bf16[256,2048]{1,0:T(8,128)(2,1)S(1)}, u32[]{:S(2)}, u32[]{:S(2)}) collective-permute-start(bf16[256,2048]{1,0:T(8,128)(2,1)S(1)} %collective-permute-done.refs_1_), channel_id=1, source_target_pairs={{0,128},{64,448},{128,256},{192,64},{256,384},{320,192},{384,0},{4... | collective-permute-start | bytes 3145736 | tf_op jit(solution)/shard_map/ppermute | solution.py:334
  57.5 8.8 %collective-permute-start.2 = (bf16[64,16,128]{2,1,0:T(8,128)(2,1)}, bf16[64,16,128]{2,1,0:T(8,128)(2,1)S(1)}, u32[]{:S(2)}, u32[]{:S(2)}) collective-permute-start(bf16[64,16,128]{2,1,0:T(8,128)(2,1)} %all-to-all-done.1.mine), channel_id=1, source_target_pairs={{0,64},{64,0},{1,65},{65,1},{2,66},{66,2},{3,67},{67,3},{4,68},{68... | collective-permute-start | bytes 786440 | tf_op jit(solution)/shard_map/ppermute | solution.py:344
  72.3 9.2 %collective-permute-start.4 = (f32[65,16,128]{2,1,0:T(8,128)S(1)}, f32[65,16,128]{2,1,0:T(8,128)S(1)}, u32[]{:S(2)}, u32[]{:S(2)}) collective-permute-start(f32[65,16,128]{2,1,0:T(8,128)S(1)} %get-tuple-element.16), channel_id=1, source_target_pairs={{0,64},{64,0},{1,65},{65,1},{2,66},{66,2},{3,67},{67,3},{4,68},{68... | collective-permute-start | bytes 1597448 | tf_op jit(solution)/shard_map/ppermute | solution.py:373
  80.5 17.1 %copy-start.1 = (f32[16,4,512]{2,1,0:T(4,128)S(1)}, f32[16,4,512]{2,1,0:T(4,128)}, u32[]{:S(2)}) copy-start(f32[16,4,512]{2,1,0:T(4,128)} %refs_0_.1) | copy-start | bytes 393220
  80.5 17.1 %copy-start.2 = (f32[16,4,512]{2,1,0:T(4,128)S(1)}, f32[16,4,512]{2,1,0:T(4,128)}, u32[]{:S(2)}) copy-start(f32[16,4,512]{2,1,0:T(4,128)} %refs_1_.1) | copy-start | bytes 393220
  80.5 17.1 %copy-start.3 = (f32[16,4,512]{2,1,0:T(4,128)S(1)}, f32[16,4,512]{2,1,0:T(4,128)}, u32[]{:S(2)}) copy-start(f32[16,4,512]{2,1,0:T(4,128)} %refs_2_.1) | copy-start | bytes 393220
  80.5 26.0 %copy-start.7 = (s32[8,64]{1,0:T(8,128)S(1)}, s32[8,64]{1,0:T(8,128)}, u32[]{:S(2)}) copy-start(s32[8,64]{1,0:T(8,128)} %counts.1) | copy-start | bytes 6148
  80.5 26.1 %copy-start.5 = (s32[64]{0:T(128)S(1)}, s32[64]{0:T(128)}, u32[]{:S(2)}) copy-start(s32[64]{0:T(128)} %old.1) | copy-start | bytes 772
  82.0 36.7 %copy-start.6 = (s32[64]{0:T(128)S(1)}, s32[64]{0:T(128)}, u32[]{:S(2)}) copy-start(s32[64]{0:T(128)} %new.1) | copy-start | bytes 772
  83.0 35.6 %all-to-all-start.2 = ((f16[64,2,1152]{2,1,0:T(2,128)(2,1)}), f16[64,2,1152]{2,1,0:T(2,128)(2,1)S(1)}, u32[]{:S(2)}, u32[]{:S(2)}) async-start(f16[64,2,1152]{2,1,0:T(2,128)(2,1)} %convert_element_type.11), calls=%async_computation.2 | async-start | bytes 589824 | tf_op jit(solution)/shard_map/all_to_all | solution.py:409
  97.9 20.9 %collective-permute-start.7 = (f32[3,16,4,128]{3,2,1,0:T(4,128)S(1)}, f32[3,16,4,128]{3,2,1,0:T(4,128)S(1)}, u32[]{:S(2)}, u32[]{:S(2)}) collective-permute-start(f32[3,16,4,128]{3,2,1,0:T(4,128)S(1)} %get-tuple-element.26), channel_id=1, source_target_pairs={{0,256},{128,384},{256,0},{384,128},{1,257},{129,385},{257,1},{385... | collective-permute-start | bytes 294920 | tf_op jit(solution)/shard_map/ppermute | solution.py:406
  100.5 18.3 %collective-permute-start.6 = (f32[3,16,4,128]{3,2,1,0:T(4,128)S(1)}, f32[3,16,4,128]{3,2,1,0:T(4,128)S(1)}, u32[]{:S(2)}, u32[]{:S(2)}) collective-permute-start(f32[3,16,4,128]{3,2,1,0:T(4,128)S(1)} %get-tuple-element.27), channel_id=1, source_target_pairs={{0,384},{128,0},{256,128},{384,256},{1,385},{129,1},{257,129},{385... | collective-permute-start | bytes 294920 | tf_op jit(solution)/shard_map/ppermute | solution.py:405
  104.0 14.7 %collective-permute-start.5 = (f32[3,16,4,128]{3,2,1,0:T(4,128)S(1)}, f32[3,16,4,128]{3,2,1,0:T(4,128)S(1)}, u32[]{:S(2)}, u32[]{:S(2)}) collective-permute-start(f32[3,16,4,128]{3,2,1,0:T(4,128)S(1)} %get-tuple-element.28), channel_id=1, source_target_pairs={{0,128},{128,256},{256,384},{384,0},{1,129},{129,257},{257,385},{3... | collective-permute-start | bytes 294920 | tf_op jit(solution)/shard_map/ppermute | solution.py:404
  161.2 21.7 %collective-permute-start.8 = (bf16[4,4,256,128]{3,2,1,0:T(8,128)(2,1)S(1)}, bf16[4,4,256,128]{3,2,1,0:T(8,128)(2,1)S(1)}, u32[]{:S(2)}, u32[]{:S(2)}) collective-permute-start(bf16[4,4,256,128]{3,2,1,0:T(8,128)(2,1)S(1)} %all_to_all.27.source), channel_id=1, source_target_pairs={{0,64},{64,0},{1,65},{65,1},{2,66},{66,2},{3,67},{67,3},{4,68},{68... | collective-permute-start | bytes 3145736 | tf_op jit(solution)/shard_map/ppermute | solution.py:449
  167.3 8.4 %collective-permute-start.11 = (f32[3,16,4,128]{3,2,1,0:T(4,128)S(1)}, f32[3,16,4,128]{3,2,1,0:T(4,128)S(1)}, u32[]{:S(2)}, u32[]{:S(2)}) collective-permute-start(f32[3,16,4,128]{3,2,1,0:T(4,128)S(1)} %get-tuple-element.22), channel_id=1, source_target_pairs={{0,256},{128,384},{256,0},{384,128},{1,257},{129,385},{257,1},{385... | collective-permute-start | bytes 294920 | tf_op jit(solution)/shard_map/ppermute | solution.py:434
  169.8 6.0 %collective-permute-start.10 = (f32[3,16,4,128]{3,2,1,0:T(4,128)S(1)}, f32[3,16,4,128]{3,2,1,0:T(4,128)S(1)}, u32[]{:S(2)}, u32[]{:S(2)}) collective-permute-start(f32[3,16,4,128]{3,2,1,0:T(4,128)S(1)} %get-tuple-element.23), channel_id=1, source_target_pairs={{0,384},{128,0},{256,128},{384,256},{1,385},{129,1},{257,129},{385... | collective-permute-start | bytes 294920 | tf_op jit(solution)/shard_map/ppermute | solution.py:433
  173.9 6.9 %collective-permute-start.9 = (f32[3,16,4,128]{3,2,1,0:T(4,128)S(1)}, f32[3,16,4,128]{3,2,1,0:T(4,128)S(1)}, u32[]{:S(2)}, u32[]{:S(2)}) collective-permute-start(f32[3,16,4,128]{3,2,1,0:T(4,128)S(1)} %get-tuple-element.24), channel_id=1, source_target_pairs={{0,128},{128,256},{256,384},{384,0},{1,129},{129,257},{257,385},{3... | collective-permute-start | bytes 294920 | tf_op jit(solution)/shard_map/ppermute | solution.py:432

commit v8 on v7

--- a/solution.py
+++ b/solution.py
@@ -155,7 +155,7 @@
             for y in range(Y):
                 after[y, n, e] = value[y * rows : (y + 1) * rows]
     for p in range(PLACES):
-        out[p] = table[new[p]]
+        out[p % Z * X + p // Z] = table[new[p]]
 
 
 def forward_part(chunk, weights, which):
@@ -265,20 +265,22 @@
 
 
 def join(source, out, which, blocks, sems):
-    lanes = source.shape[-1]
+    rows, lanes = source.shape[3:]
     half = out.shape[-1] // 2
     copies = []
     for y in range(Y):
-        for pair in range(Y // 2):
-            a = source[2 * pair, y].astype(jnp.float32)
-            b = source[2 * pair + 1, y].astype(jnp.float32)
-            first = lower_half(a)
-            blocks[y, :, pair * lanes : (pair + 1) * lanes] = jnp.where(
-                first, a, swapped(b)
-            ).astype(jnp.bfloat16)
-            blocks[y, :, half + pair * lanes : half + (pair + 1) * lanes] = jnp.where(
-                first, swapped(a), b
-            ).astype(jnp.bfloat16)
+        for x in range(X):
+            at = slice(x * rows, (x + 1) * rows)
+            for pair in range(Y // 2):
+                a = source[2 * pair, x, y].astype(jnp.float32)
+                b = source[2 * pair + 1, x, y].astype(jnp.float32)
+                first = lower_half(a)
+                blocks[y, at, pair * lanes : (pair + 1) * lanes] = jnp.where(
+                    first, a, swapped(b)
+                ).astype(jnp.bfloat16)
+                blocks[y, at, half + pair * lanes : half + (pair + 1) * lanes] = jnp.where(
+                    first, swapped(a), b
+                ).astype(jnp.bfloat16)
         copy = pltpu.make_async_copy(blocks.at[y], out.at[y, which], sems.at[y])
         copy.start()
         copies.append(copy)
@@ -332,13 +334,6 @@
     )(old_slots, payload)
     landed = lax.all_to_all(picked, ("x", "z"), 0, 0, tiled=True)
     far = lax.ppermute(near_one, ("y", "core"), APART)
-
-    def by_rows(x):
-        return (
-            x.reshape(PLACES, Y, rows_shard, lanes)
-            .transpose(1, 0, 2, 3)
-            .reshape(Y, PLACES * rows_shard, lanes)
-        )
 
     w_mine = landed
     w_theirs = lax.ppermute(w_mine, "core", SWAP)
@@ -427,7 +422,10 @@
         compiler_params=grant(6),
         name="adam",
     )(old_slots, new_slots, total, got, m_own, m_low, m_high, m_far)
-    landed = lax.all_to_all(picked, ("x", "z"), 0, 0, tiled=True)
+    block_rows = PLACES * rows_shard
+    landed = lax.all_to_all(
+        picked.reshape(Z, X * Y * rows_shard, lanes), "z", 0, 0, tiled=True
+    )
 
     s_low = lax.ppermute(for_chip(1, after), "y", UP)
     s_high = lax.ppermute(for_chip(3, after), "y", DOWN)
@@ -443,11 +441,16 @@
         name="join_cols",
     )(for_chip(0, after), s_low, s_high, s_far)
 
-    landed = by_rows(landed)
+    landed = (
+        landed.reshape(Z, X, Y, rows_shard, lanes)
+        .transpose(1, 2, 0, 3, 4)
+        .reshape(X, Y * Z * rows_shard, lanes)
+    )
     copies = jnp.broadcast_to(landed[None], (Y, *landed.shape))
-    mine = lax.all_to_all(copies, "y", 0, 0, tiled=True)
+    mine = lax.all_to_all(
+        copies.reshape(Y * X, Y * Z * rows_shard, lanes), ("y", "x"), 0, 0, tiled=True
+    ).reshape(Y, X, Y, Z * rows_shard, lanes)
     theirs = lax.ppermute(mine, "core", SWAP)
-    block_rows = PLACES * rows_shard
     scratch = [pltpu.VMEM((Y, block_rows, width), bf16), pltpu.SemaphoreType.DMA((Y,))]
     whole = jax.ShapeDtypeStruct((Y, C, block_rows, width), bf16)
     begun = pl.pallas_call(

time: 185 us -> 184 us (level); the launches traced: 184 us -> 181 us
  blocking collectives: 53.1 us -> 46.2 us
  starting transfers between devices: 83.3 us -> 86.9 us
    all_to_all x2, blocking collectives: 41 us -> 34.1 us  [the longest x1 17.8 us: shards(): lax.all_to_all(picked.reshape(Z, X * Y * rows_shard, lanes), 'z', 0, 0, t...]
    ppermute x1, starting transfers between devices: 6.1 us -> 10.3 us  [shards(): theirs = lax.ppermute(mine, 'core', SWAP)]
  transfers between devices with their start and end apart: 14 -> 14, of which waited for: 5 -> 6; matrix products, arithmetic and copies ran while one was open for 0% -> 0% of each run, Pallas kernels for 6% -> 6%
where the time goes in v8:
time: 184 us; the launch traced here: 181 us
  starting transfers between devices  86.9 us (47%)
  blocking collectives  46.2 us (25%)
  waiting for transfers between devices  28.9 us (16%)
  Pallas kernels  15.1 us (8%)
    all_to_all x1, starting transfers between devices, shards(): landed = lax.all_to_all(picked, ('x', 'z'), 0, 0, tiled=True)  18.5 us
    all_to_all x1, blocking collectives, shards(): lax.all_to_all(picked.reshape(Z, X * Y * rows_shard, lanes), 'z', 0, 0, t...  17.8 us
    all_to_all x1, blocking collectives, shards(): lax.all_to_all(copies.reshape(Y * X, Y * Z * rows_shard, lanes), ('y', 'x...  16.2 us
    all_to_all x1, starting transfers between devices, shards(): lax.all_to_all(scaled.astype(jnp.float16), ('x', 'z'), 0, 0, tiled=True)  14.5 us
    all_to_all x1, blocking collectives, shards(): payload = lax.all_to_all(payload, 'y', 0, 0, tiled=True)  12.1 us
    all_to_all x1, waiting for transfers between devices, shards(): lax.all_to_all(scaled.astype(jnp.float16), ('x', 'z'), 0, 0, tiled=True)  11.8 us
    ppermute x1, starting transfers between devices, shards(): theirs = lax.ppermute(mine, 'core', SWAP)  10.3 us
    all_to_all x1, waiting for transfers between devices, shards(): landed = lax.all_to_all(picked, ('x', 'z'), 0, 0, tiled=True)  9.66 us
  transfers between devices with their start and end apart: 14, of which 6 were waited for; matrix products, arithmetic and copies ran while one was open for 0% of the time, Pallas kernels for 6%

profile of v8, /device:TPU:1, one launch (start us, length us, event | category | flops | bytes accessed | tf_op | source)
XLA Modules:
  0.0 180.8 jit_solution(12524690583651057420)
XLA Ops:
  0.6 5.6 %collective-permute-start = (bf16[256,2048]{1,0:T(8,128)(2,1)}, bf16[256,2048]{1,0:T(8,128)(2,1)S(1)}, u32[]{:S(2)}, u32[]{:S(2)}) collective-permute-start(bf16[256,2048]{1,0:T(8,128)(2,1)} %bitcast.34), channel_id=1, source_target_pairs={{0,128},{64,448},{128,256},{192,64},{256,384},{320,192},{384,0},{4... | collective-permute-start | bytes 3145736 | tf_op jit(solution)/shard_map/ppermute | solution.py:320
  6.2 1.9 %prepare.1 = bf16[4,192,128]{2,1,0:T(8,128)(2,1)} custom-call(s32[8,64]{1,0:T(8,128)} %counts.1, s32[4,64]{1,0:T(4,128)} %bitcast.44, bf16[256,256]{1,0:T(8,128)(2,1)} %bitcast.43, f32[16,4,512]{2,1,0:T(4,128)} %refs_0_.1), custom_call_target="tpu_custom_call" | custom-call | tf_op jit(solution)/shard_map/prepare/pallas_call | solution.py:312
  8.2 12.1 %all_to_all.25.payload = bf16[4,192,128]{2,1,0:T(8,128)(2,1)S(1)} all-to-all(bf16[4,192,128]{2,1,0:T(8,128)(2,1)} %prepare.1), channel_id=1, replica_groups=mesh['y'=4,'core'=2,'x'=4,'z'=16] {'y'}, dimensions={0} | all-to-all | bytes 393216 | tf_op jit(solution)/shard_map/all_to_all | solution.py:319
  21.0 1.3 pick_old.1
  22.3 18.5 %all-to-all-start.1 = ((bf16[64,16,128]{2,1,0:T(8,128)(2,1)}), bf16[64,16,128]{2,1,0:T(8,128)(2,1)}, u32[]{:S(2)}, u32[]{:S(2)}) async-start(bf16[64,16,128]{2,1,0:T(8,128)(2,1)} %pick_old.1), calls=%async_computation.1 | async-start | bytes 524288 | tf_op jit(solution)/shard_map/all_to_all | solution.py:335
  40.8 3.4 %collective-permute-start.1 = (bf16[256,2048]{1,0:T(8,128)(2,1)}, bf16[256,2048]{1,0:T(8,128)(2,1)}, u32[]{:S(2)}, u32[]{:S(2)}) collective-permute-start(bf16[256,2048]{1,0:T(8,128)(2,1)} %bitcast.35), channel_id=1, source_target_pairs={{128,0},{448,64},{256,128},{64,192},{384,256},{192,320},{0,384},{3... | collective-permute-start | bytes 3145736 | tf_op jit(solution)/shard_map/ppermute | solution.py:321
  44.2 3.6 %collective-permute-start.3 = (bf16[256,2048]{1,0:T(8,128)(2,1)S(1)}, bf16[256,2048]{1,0:T(8,128)(2,1)S(1)}, u32[]{:S(2)}, u32[]{:S(2)}) collective-permute-start(bf16[256,2048]{1,0:T(8,128)(2,1)S(1)} %collective-permute-done.refs_1_), channel_id=1, source_target_pairs={{0,128},{64,448},{128,256},{192,64},{256,384},{320,192},{384,0},{4... | collective-permute-start | bytes 3145736 | tf_op jit(solution)/shard_map/ppermute | solution.py:336
  47.8 9.7 %all-to-all-done.1.mine = bf16[64,16,128]{2,1,0:T(8,128)(2,1)} async-done(((bf16[64,16,128]{2,1,0:T(8,128)(2,1)}), bf16[64,16,128]{2,1,0:T(8,128)(2,1)}, u32[]{:S(2)}, u32[]{:S(2)}) %all-to-all-start.1) | async-done | bytes 262176 | tf_op jit(solution)/shard_map/all_to_all | solution.py:335
  57.5 6.9 %collective-permute-start.2 = (bf16[64,16,128]{2,1,0:T(8,128)(2,1)}, bf16[64,16,128]{2,1,0:T(8,128)(2,1)S(1)}, u32[]{:S(2)}, u32[]{:S(2)}) collective-permute-start(bf16[64,16,128]{2,1,0:T(8,128)(2,1)} %all-to-all-done.1.mine), channel_id=1, source_target_pairs={{0,64},{64,0},{1,65},{65,1},{2,66},{66,2},{3,67},{67,3},{4,68},{68... | collective-permute-start | bytes 786440 | tf_op jit(solution)/shard_map/ppermute | solution.py:339
  64.4 1.9 %forward_mine.1.part_ref = f32[3,256,128]{2,1,0:T(8,128)S(1)} custom-call(bf16[64,16,128]{2,1,0:T(8,128)(2,1)} %all-to-all-done.1.mine, bf16[256,2048]{1,0:T(8,128)(2,1)S(1)} %bitcast.36, bf16[256,2048]{1,0:T(8,128)(2,1)S(1)} %collective-permute-done.refs_1_, bf16[256,2048]{1,0:T(8,128)(2,1)} %collective-permute-done.1.refs_2_), custom_call_target="tpu_custom_call" | custom-call | tf_op jit(solution)/shard_map/forward_mine/pallas_call | solution.py:342
  66.3 2.5 %near_grad.1 = (f32[4,128,256]{2,1,0:T(8,128)S(1)}, f32[4,128,256]{2,1,0:T(8,128)S(1)}) custom-call(f32[3,256,128]{2,1,0:T(8,128)S(1)} %forward_mine.1.part_ref, bf16[64,16,128]{2,1,0:T(8,128)(2,1)S(1)} %collective-permute-done.2.theirs, bf16[4,192,128]{2,1,0:T(8,128)(2,1)S(1)} %all_to_all.25.payload, bf16[256,2048]{1,0:T(8,128)(2,1)S(1)} %bitcast.37, ...), custom_call_target="tpu_custom_call" | custom-call | tf_op jit(solution)/shard_map/near_grad/pallas_call | solution.py:351
  68.8 1.6 collective-permute-done.3.chunk
  70.4 1.9 %grad_theirs.1 = (f32[65,16,128]{2,1,0:T(8,128)S(1)}, bf16[128,256]{1,0:T(8,128)(2,1)S(1)}) custom-call(f32[4,128,256]{2,1,0:T(8,128)S(1)} %get-tuple-element.14.begun, bf16[64,16,128]{2,1,0:T(8,128)(2,1)} %all-to-all-done.1.mine, bf16[64,16,128]{2,1,0:T(8,128)(2,1)S(1)} %collective-permute-done.2.theirs, bf16[4,192,128]{2,1,0:T(8,128)(2,1)S(1)} %all_to_all.25.payload, ...), custom_call_target="tpu_custom_call" | custom-call | tf_op jit(solution)/shard_map/grad_theirs/pallas_call | solution.py:360
  72.3 7.7 %collective-permute-start.4 = (f32[65,16,128]{2,1,0:T(8,128)S(1)}, f32[65,16,128]{2,1,0:T(8,128)S(1)}, u32[]{:S(2)}, u32[]{:S(2)}) collective-permute-start(f32[65,16,128]{2,1,0:T(8,128)S(1)} %get-tuple-element.16), channel_id=1, source_target_pairs={{0,64},{64,0},{1,65},{65,1},{2,66},{66,2},{3,67},{67,3},{4,68},{68... | collective-permute-start | bytes 1597448 | tf_op jit(solution)/shard_map/ppermute | solution.py:368
  80.5 1.0 collective-permute-done.4.theirs
  82.1 0.9 convert_element_type.11
  83.0 14.5 %all-to-all-start.2 = ((f16[64,2,1152]{2,1,0:T(2,128)(2,1)}), f16[64,2,1152]{2,1,0:T(2,128)(2,1)S(1)}, u32[]{:S(2)}, u32[]{:S(2)}) async-start(f16[64,2,1152]{2,1,0:T(2,128)(2,1)} %convert_element_type.11), calls=%async_computation.2 | async-start | bytes 589824 | tf_op jit(solution)/shard_map/all_to_all | solution.py:404
  97.9 2.6 %collective-permute-start.7 = (f32[3,16,4,128]{3,2,1,0:T(4,128)S(1)}, f32[3,16,4,128]{3,2,1,0:T(4,128)S(1)}, u32[]{:S(2)}, u32[]{:S(2)}) collective-permute-start(f32[3,16,4,128]{3,2,1,0:T(4,128)S(1)} %get-tuple-element.26), channel_id=1, source_target_pairs={{0,256},{128,384},{256,0},{384,128},{1,257},{129,385},{257,1},{385... | collective-permute-start | bytes 294920 | tf_op jit(solution)/shard_map/ppermute | solution.py:401
  100.5 3.6 %collective-permute-start.6 = (f32[3,16,4,128]{3,2,1,0:T(4,128)S(1)}, f32[3,16,4,128]{3,2,1,0:T(4,128)S(1)}, u32[]{:S(2)}, u32[]{:S(2)}) collective-permute-start(f32[3,16,4,128]{3,2,1,0:T(4,128)S(1)} %get-tuple-element.27), channel_id=1, source_target_pairs={{0,384},{128,0},{256,128},{384,256},{1,385},{129,1},{257,129},{385... | collective-permute-start | bytes 294920 | tf_op jit(solution)/shard_map/ppermute | solution.py:400
  104.1 2.5 %collective-permute-start.5 = (f32[3,16,4,128]{3,2,1,0:T(4,128)S(1)}, f32[3,16,4,128]{3,2,1,0:T(4,128)S(1)}, u32[]{:S(2)}, u32[]{:S(2)}) collective-permute-start(f32[3,16,4,128]{3,2,1,0:T(4,128)S(1)} %get-tuple-element.28), channel_id=1, source_target_pairs={{0,128},{128,256},{256,384},{384,0},{1,129},{129,257},{257,385},{3... | collective-permute-start | bytes 294920 | tf_op jit(solution)/shard_map/ppermute | solution.py:399
  106.8 11.8 %all-to-all-done.2 = f16[64,2,1152]{2,1,0:T(2,128)(2,1)S(1)} async-done(((f16[64,2,1152]{2,1,0:T(2,128)(2,1)}), f16[64,2,1152]{2,1,0:T(2,128)(2,1)S(1)}, u32[]{:S(2)}, u32[]{:S(2)}) %all-to-all-start.2) | async-done | bytes 294944 | tf_op jit(solution)/shard_map/all_to_all | solution.py:404
  118.8 1.1 adam.1
  119.9 17.8 %all_to_all.26 = bf16[16,64,128]{2,1,0:T(8,128)(2,1)S(1)} all-to-all(bf16[16,64,128]{2,1,0:T(8,128)(2,1)S(1)} %bitcast.38), channel_id=1, replica_groups=mesh['y'=4,'core'=2,'x'=4,'z'=16] {'z'}, dimensions={0} | all-to-all | bytes 524288 | tf_op jit(solution)/shard_map/all_to_all | solution.py:426
  138.2 16.2 %all_to_all.27 = bf16[16,256,128]{2,1,0:T(8,128)(2,1)S(1)} all-to-all(bf16[16,256,128]{2,1,0:T(8,128)(2,1)S(1)} %bitcast.40), channel_id=1, replica_groups=mesh['y'=4,'core'=2,'x'=4,'z'=16] {'y','x'}, dimensions={0} | all-to-all | bytes 2097152 | tf_op jit(solution)/shard_map/all_to_all | solution.py:450
  154.5 10.3 %collective-permute-start.8 = (bf16[4,4,4,64,128]{4,3,2,1,0:T(8,128)(2,1)S(1)}, bf16[4,4,4,64,128]{4,3,2,1,0:T(8,128)(2,1)S(1)}, u32[]{:S(2)}, u32[]{:S(2)}) collective-permute-start(bf16[4,4,4,64,128]{4,3,2,1,0:T(8,128)(2,1)S(1)} %bitcast.32), channel_id=1, source_target_pairs={{0,64},{64,0},{1,65},{65,1},{2,66},{66,2},{3,67},{67,3},{4,68},{68... | collective-permute-start | bytes 3145736 | tf_op jit(solution)/shard_map/ppermute | solution.py:453
  164.8 2.5 %collective-permute-start.11 = (f32[3,16,4,128]{3,2,1,0:T(4,128)S(1)}, f32[3,16,4,128]{3,2,1,0:T(4,128)S(1)}, u32[]{:S(2)}, u32[]{:S(2)}) collective-permute-start(f32[3,16,4,128]{3,2,1,0:T(4,128)S(1)} %get-tuple-element.22), channel_id=1, source_target_pairs={{0,256},{128,384},{256,0},{384,128},{1,257},{129,385},{257,1},{385... | collective-permute-start | bytes 294920 | tf_op jit(solution)/shard_map/ppermute | solution.py:432
  167.3 3.2 %collective-permute-start.10 = (f32[3,16,4,128]{3,2,1,0:T(4,128)S(1)}, f32[3,16,4,128]{3,2,1,0:T(4,128)S(1)}, u32[]{:S(2)}, u32[]{:S(2)}) collective-permute-start(f32[3,16,4,128]{3,2,1,0:T(4,128)S(1)} %get-tuple-element.23), channel_id=1, source_target_pairs={{0,384},{128,0},{256,128},{384,256},{1,385},{129,1},{257,129},{385... | collective-permute-start | bytes 294920 | tf_op jit(solution)/shard_map/ppermute | solution.py:431
  170.6 2.0 %collective-permute-start.9 = (f32[3,16,4,128]{3,2,1,0:T(4,128)S(1)}, f32[3,16,4,128]{3,2,1,0:T(4,128)S(1)}, u32[]{:S(2)}, u32[]{:S(2)}) collective-permute-start(f32[3,16,4,128]{3,2,1,0:T(4,128)S(1)} %get-tuple-element.24), channel_id=1, source_target_pairs={{0,128},{128,256},{256,384},{384,0},{1,129},{129,257},{257,385},{3... | collective-permute-start | bytes 294920 | tf_op jit(solution)/shard_map/ppermute | solution.py:430
  173.3 4.2 %collective-permute-done.9.low = f32[3,16,4,128]{3,2,1,0:T(4,128)S(1)} collective-permute-done((f32[3,16,4,128]{3,2,1,0:T(4,128)S(1)}, f32[3,16,4,128]{3,2,1,0:T(4,128)S(1)}, u32[]{:S(2)}, u32[]{:S(2)}) %collective-permute-start.9) | collective-permute-done | bytes 98336 | tf_op jit(solution)/shard_map/ppermute | solution.py:430
  177.5 1.0 join_cols.1
  178.4 1.2 join_mine.1.begun
  179.6 1.2 join_theirs.1
  (36 shorter events, 3.5 us)
Async XLA Ops:
  0.6 63.8 %copy-start = (bf16[1,1,256,2048]{3,2,1,0:T(8,128)(2,1)S(1)}, bf16[1,1,256,2048]{3,2,1,0:T(8,128)(2,1)}, u32[]{:S(2)}) copy-start(bf16[1,1,256,2048]{3,2,1,0:T(8,128)(2,1)} %param.9) | copy-start | bytes 3145732
  0.6 43.6 %collective-permute-start = (bf16[256,2048]{1,0:T(8,128)(2,1)}, bf16[256,2048]{1,0:T(8,128)(2,1)S(1)}, u32[]{:S(2)}, u32[]{:S(2)}) collective-permute-start(bf16[256,2048]{1,0:T(8,128)(2,1)} %bitcast.34), channel_id=1, source_target_pairs={{0,128},{64,448},{128,256},{192,64},{256,384},{320,192},{384,0},{4... | collective-permute-start | bytes 3145736 | tf_op jit(solution)/shard_map/ppermute | solution.py:320
  20.3 0.7 copy-start.4
  22.3 35.2 %all-to-all-start.1 = ((bf16[64,16,128]{2,1,0:T(8,128)(2,1)}), bf16[64,16,128]{2,1,0:T(8,128)(2,1)}, u32[]{:S(2)}, u32[]{:S(2)}) async-start(bf16[64,16,128]{2,1,0:T(8,128)(2,1)} %pick_old.1), calls=%async_computation.1 | async-start | bytes 524288 | tf_op jit(solution)/shard_map/all_to_all | solution.py:335
  40.8 23.6 %collective-permute-start.1 = (bf16[256,2048]{1,0:T(8,128)(2,1)}, bf16[256,2048]{1,0:T(8,128)(2,1)}, u32[]{:S(2)}, u32[]{:S(2)}) collective-permute-start(bf16[256,2048]{1,0:T(8,128)(2,1)} %bitcast.35), channel_id=1, source_target_pairs={{128,0},{448,64},{256,128},{64,192},{384,256},{192,320},{0,384},{3... | collective-permute-start | bytes 3145736 | tf_op jit(solution)/shard_map/ppermute | solution.py:321
  44.2 26.2 %collective-permute-start.3 = (bf16[256,2048]{1,0:T(8,128)(2,1)S(1)}, bf16[256,2048]{1,0:T(8,128)(2,1)S(1)}, u32[]{:S(2)}, u32[]{:S(2)}) collective-permute-start(bf16[256,2048]{1,0:T(8,128)(2,1)S(1)} %collective-permute-done.refs_1_), channel_id=1, source_target_pairs={{0,128},{64,448},{128,256},{192,64},{256,384},{320,192},{384,0},{4... | collective-permute-start | bytes 3145736 | tf_op jit(solution)/shard_map/ppermute | solution.py:336
  57.5 8.8 %collective-permute-start.2 = (bf16[64,16,128]{2,1,0:T(8,128)(2,1)}, bf16[64,16,128]{2,1,0:T(8,128)(2,1)S(1)}, u32[]{:S(2)}, u32[]{:S(2)}) collective-permute-start(bf16[64,16,128]{2,1,0:T(8,128)(2,1)} %all-to-all-done.1.mine), channel_id=1, source_target_pairs={{0,64},{64,0},{1,65},{65,1},{2,66},{66,2},{3,67},{67,3},{4,68},{68... | collective-permute-start | bytes 786440 | tf_op jit(solution)/shard_map/ppermute | solution.py:339
  72.3 9.2 %collective-permute-start.4 = (f32[65,16,128]{2,1,0:T(8,128)S(1)}, f32[65,16,128]{2,1,0:T(8,128)S(1)}, u32[]{:S(2)}, u32[]{:S(2)}) collective-permute-start(f32[65,16,128]{2,1,0:T(8,128)S(1)} %get-tuple-element.16), channel_id=1, source_target_pairs={{0,64},{64,0},{1,65},{65,1},{2,66},{66,2},{3,67},{67,3},{4,68},{68... | collective-permute-start | bytes 1597448 | tf_op jit(solution)/shard_map/ppermute | solution.py:368
  80.5 17.1 %copy-start.1 = (f32[16,4,512]{2,1,0:T(4,128)S(1)}, f32[16,4,512]{2,1,0:T(4,128)}, u32[]{:S(2)}) copy-start(f32[16,4,512]{2,1,0:T(4,128)} %refs_0_.1) | copy-start | bytes 393220
  80.5 17.1 %copy-start.2 = (f32[16,4,512]{2,1,0:T(4,128)S(1)}, f32[16,4,512]{2,1,0:T(4,128)}, u32[]{:S(2)}) copy-start(f32[16,4,512]{2,1,0:T(4,128)} %refs_1_.1) | copy-start | bytes 393220
  80.5 17.1 %copy-start.3 = (f32[16,4,512]{2,1,0:T(4,128)S(1)}, f32[16,4,512]{2,1,0:T(4,128)}, u32[]{:S(2)}) copy-start(f32[16,4,512]{2,1,0:T(4,128)} %refs_2_.1) | copy-start | bytes 393220
  80.5 26.0 %copy-start.7 = (s32[8,64]{1,0:T(8,128)S(1)}, s32[8,64]{1,0:T(8,128)}, u32[]{:S(2)}) copy-start(s32[8,64]{1,0:T(8,128)} %counts.1) | copy-start | bytes 6148
  80.5 26.1 %copy-start.5 = (s32[64]{0:T(128)S(1)}, s32[64]{0:T(128)}, u32[]{:S(2)}) copy-start(s32[64]{0:T(128)} %old.1) | copy-start | bytes 772
  82.1 36.7 %copy-start.6 = (s32[64]{0:T(128)S(1)}, s32[64]{0:T(128)}, u32[]{:S(2)}) copy-start(s32[64]{0:T(128)} %new.1) | copy-start | bytes 772
  83.0 35.6 %all-to-all-start.2 = ((f16[64,2,1152]{2,1,0:T(2,128)(2,1)}), f16[64,2,1152]{2,1,0:T(2,128)(2,1)S(1)}, u32[]{:S(2)}, u32[]{:S(2)}) async-start(f16[64,2,1152]{2,1,0:T(2,128)(2,1)} %convert_element_type.11), calls=%async_computation.2 | async-start | bytes 589824 | tf_op jit(solution)/shard_map/all_to_all | solution.py:404
  97.9 20.9 %collective-permute-start.7 = (f32[3,16,4,128]{3,2,1,0:T(4,128)S(1)}, f32[3,16,4,128]{3,2,1,0:T(4,128)S(1)}, u32[]{:S(2)}, u32[]{:S(2)}) collective-permute-start(f32[3,16,4,128]{3,2,1,0:T(4,128)S(1)} %get-tuple-element.26), channel_id=1, source_target_pairs={{0,256},{128,384},{256,0},{384,128},{1,257},{129,385},{257,1},{385... | collective-permute-start | bytes 294920 | tf_op jit(solution)/shard_map/ppermute | solution.py:401
  100.5 18.3 %collective-permute-start.6 = (f32[3,16,4,128]{3,2,1,0:T(4,128)S(1)}, f32[3,16,4,128]{3,2,1,0:T(4,128)S(1)}, u32[]{:S(2)}, u32[]{:S(2)}) collective-permute-start(f32[3,16,4,128]{3,2,1,0:T(4,128)S(1)} %get-tuple-element.27), channel_id=1, source_target_pairs={{0,384},{128,0},{256,128},{384,256},{1,385},{129,1},{257,129},{385... | collective-permute-start | bytes 294920 | tf_op jit(solution)/shard_map/ppermute | solution.py:400
  104.1 14.7 %collective-permute-start.5 = (f32[3,16,4,128]{3,2,1,0:T(4,128)S(1)}, f32[3,16,4,128]{3,2,1,0:T(4,128)S(1)}, u32[]{:S(2)}, u32[]{:S(2)}) collective-permute-start(f32[3,16,4,128]{3,2,1,0:T(4,128)S(1)} %get-tuple-element.28), channel_id=1, source_target_pairs={{0,128},{128,256},{256,384},{384,0},{1,129},{129,257},{257,385},{3... | collective-permute-start | bytes 294920 | tf_op jit(solution)/shard_map/ppermute | solution.py:399
  154.5 25.2 %collective-permute-start.8 = (bf16[4,4,4,64,128]{4,3,2,1,0:T(8,128)(2,1)S(1)}, bf16[4,4,4,64,128]{4,3,2,1,0:T(8,128)(2,1)S(1)}, u32[]{:S(2)}, u32[]{:S(2)}) collective-permute-start(bf16[4,4,4,64,128]{4,3,2,1,0:T(8,128)(2,1)S(1)} %bitcast.32), channel_id=1, source_target_pairs={{0,64},{64,0},{1,65},{65,1},{2,66},{66,2},{3,67},{67,3},{4,68},{68... | collective-permute-start | bytes 3145736 | tf_op jit(solution)/shard_map/ppermute | solution.py:453
  164.8 7.8 %collective-permute-start.11 = (f32[3,16,4,128]{3,2,1,0:T(4,128)S(1)}, f32[3,16,4,128]{3,2,1,0:T(4,128)S(1)}, u32[]{:S(2)}, u32[]{:S(2)}) collective-permute-start(f32[3,16,4,128]{3,2,1,0:T(4,128)S(1)} %get-tuple-element.22), channel_id=1, source_target_pairs={{0,256},{128,384},{256,0},{384,128},{1,257},{129,385},{257,1},{385... | collective-permute-start | bytes 294920 | tf_op jit(solution)/shard_map/ppermute | solution.py:432
  167.3 6.0 %collective-permute-start.10 = (f32[3,16,4,128]{3,2,1,0:T(4,128)S(1)}, f32[3,16,4,128]{3,2,1,0:T(4,128)S(1)}, u32[]{:S(2)}, u32[]{:S(2)}) collective-permute-start(f32[3,16,4,128]{3,2,1,0:T(4,128)S(1)} %get-tuple-element.23), channel_id=1, source_target_pairs={{0,384},{128,0},{256,128},{384,256},{1,385},{129,1},{257,129},{385... | collective-permute-start | bytes 294920 | tf_op jit(solution)/shard_map/ppermute | solution.py:431
  170.6 6.9 %collective-permute-start.9 = (f32[3,16,4,128]{3,2,1,0:T(4,128)S(1)}, f32[3,16,4,128]{3,2,1,0:T(4,128)S(1)}, u32[]{:S(2)}, u32[]{:S(2)}) collective-permute-start(f32[3,16,4,128]{3,2,1,0:T(4,128)S(1)} %get-tuple-element.24), channel_id=1, source_target_pairs={{0,128},{128,256},{256,384},{384,0},{1,129},{129,257},{257,385},{3... | collective-permute-start | bytes 294920 | tf_op jit(solution)/shard_map/ppermute | solution.py:430

commit v9 on v8

--- a/solution.py
+++ b/solution.py
@@ -158,18 +158,23 @@
         out[p % Z * X + p // Z] = table[new[p]]
 
 
+def natural(weights):
+    rows_shard = weights.shape[1] // Y
+    wide = weights[...].astype(jnp.float32)
+    return [
+        wide[:, y * rows_shard : (y + 1) * rows_shard, :]
+        .reshape(PLACES * rows_shard, -1)
+        .astype(jnp.bfloat16)
+        for y in range(Y)
+    ]
+
+
 def forward_part(chunk, weights, which):
-    rows_shard = weights.shape[1] // Y
-    wide = PLACES * rows_shard
+    wide = weights.shape[1]
     total = None
     for y in range(Y):
         at = pl.multiple_of((2 * y + which) * wide, wide)
-        block = weights[:, y * rows_shard : (y + 1) * rows_shard, :].astype(jnp.float32)
-        term = jnp.dot(
-            chunk[:, pl.ds(at, wide)],
-            block.reshape(wide, -1).astype(jnp.bfloat16),
-            preferred_element_type=jnp.float32,
-        )
+        term = jnp.dot(chunk[:, pl.ds(at, wide)], weights[y], preferred_element_type=jnp.float32)
         total = term if total is None else total + term
     return total
 
@@ -211,24 +216,32 @@
     out_ref[PLACES] = jnp.broadcast_to(jnp.max(peak, keepdims=True), out_ref.shape[1:])
 
 
-def forward_mine(mine, *refs):
-    chunks, out_ref = refs[:-1], refs[-1]
-    weights = mine[...]
-    for k, chunk in enumerate(chunks):
-        out_ref[k] = forward_part(chunk, weights, lax.axis_index("core"))
-
-
-def near_grad(part_ref, theirs, payload, *refs):
-    chunks, (theirs_ref, mine_ref) = refs[:-2], refs[-2:]
+def forward_mine(mine, own, one, two, out_ref, weights_ref, held, sem):
+    copy = pltpu.make_async_copy(two, held, sem)
+    copy.start()
+    for y, block in enumerate(natural(mine)):
+        weights_ref[y] = block
+    core = lax.axis_index("core")
+    out_ref[0] = forward_part(own, weights_ref, core)
+    out_ref[1] = forward_part(one, weights_ref, core)
+    copy.wait()
+    out_ref[2] = forward_part(held, weights_ref, core)
+
+
+def near_grad(part_ref, theirs, payload, own, one, two, theirs_ref, mine_ref, weights_ref, held, sem):
+    copy = pltpu.make_async_copy(two, held, sem)
+    copy.start()
+    for y, block in enumerate(natural(theirs)):
+        weights_ref[y] = block
     y_here, core = lax.axis_index("y"), lax.axis_index("core")
-    weights = theirs[...]
+    chunks = (own, one, held)
     steps = (0, 3 + 2 * core, 1 + 2 * core)
-    locals_ = [
-        local_part(
-            part_ref[k] + forward_part(chunk, weights, 1 - core), payload, (y_here + step) % Y
-        )
-        for k, (step, chunk) in enumerate(zip(steps, chunks))
-    ]
+    locals_ = []
+    for k, (step, chunk) in enumerate(zip(steps, chunks)):
+        if k == 2:
+            copy.wait()
+        both = part_ref[k] + forward_part(chunk, weights_ref, 1 - core)
+        locals_.append(local_part(both, payload, (y_here + step) % Y))
     wide = theirs_ref.shape[2]
     for out_ref, half in ((theirs_ref, 1 - core), (mine_ref, core)):
         for y in range(Y):
@@ -241,7 +254,7 @@
 
 def grad_theirs(begun, mine, theirs, payload, chunk, out_ref, local_ref):
     core = lax.axis_index("core")
-    both = forward_part(chunk, mine[...], core) + forward_part(chunk, theirs[...], 1 - core)
+    both = forward_part(chunk, mine, core) + forward_part(chunk, theirs, 1 - core)
     local = local_part(both, payload, (lax.axis_index("y") + 2) % Y)
     local_ref[...] = local
     finish_grad(out_ref, begun, local, chunk, 1 - core)
@@ -338,24 +351,28 @@
     w_mine = landed
     w_theirs = lax.ppermute(w_mine, "core", SWAP)
 
-    near = [own, near_one, near_two]
-    forward = pl.pallas_call(
+    wide = PLACES * rows_shard
+    weights_shape = jax.ShapeDtypeStruct((Y, wide, lanes), bf16)
+    held = [pltpu.VMEM(own.shape, bf16), pltpu.SemaphoreType.DMA(())]
+    forward, w_mine = pl.pallas_call(
         forward_mine,
-        out_shape=jax.ShapeDtypeStruct((len(near), rows, lanes), f32),
-        in_specs=[VMEM] * (1 + len(near)),
-        out_specs=VMEM,
+        out_shape=(jax.ShapeDtypeStruct((3, rows, lanes), f32), weights_shape),
+        in_specs=[VMEM] * 3 + [ANY],
+        out_specs=(VMEM, VMEM),
+        scratch_shapes=held,
         compiler_params=grant(24),
         name="forward_mine",
-    )(w_mine, *near)
-    begun_shape = jax.ShapeDtypeStruct((Y, lanes, PLACES * rows_shard), f32)
-    begun_theirs, begun_mine = pl.pallas_call(
+    )(w_mine, own, near_one, near_two)
+    begun_shape = jax.ShapeDtypeStruct((Y, lanes, wide), f32)
+    begun_theirs, begun_mine, w_theirs = pl.pallas_call(
         near_grad,
-        out_shape=(begun_shape, begun_shape),
-        in_specs=[VMEM] * (3 + len(near)),
-        out_specs=(VMEM, VMEM),
+        out_shape=(begun_shape, begun_shape, weights_shape),
+        in_specs=[VMEM] * 5 + [ANY],
+        out_specs=(VMEM, VMEM, VMEM),
+        scratch_shapes=held,
         compiler_params=grant(24),
         name="near_grad",
-    )(forward, w_theirs, payload, *near)
+    )(forward, w_theirs, payload, own, near_one, near_two)
     grad_shape = jax.ShapeDtypeStruct((PLACES + 1, Y * rows_shard, lanes), f32)
     sent, local = pl.pallas_call(
         grad_theirs,

time: 184 us -> 184 us (level)
  no operation moved by 1% of the time
where the time goes in v9:
time: 184 us; the launch traced here: 181 us
  starting transfers between devices  88 us (48%)
  blocking collectives  46.2 us (25%)
  waiting for transfers between devices  27.8 us (15%)
  Pallas kernels  15.3 us (8%)
    all_to_all x1, starting transfers between devices, shards(): landed = lax.all_to_all(picked, ('x', 'z'), 0, 0, tiled=True)  18.5 us
    all_to_all x1, blocking collectives, shards(): lax.all_to_all(picked.reshape(Z, X * Y * rows_shard, lanes), 'z', 0, 0, t...  17.8 us
    all_to_all x1, blocking collectives, shards(): lax.all_to_all(copies.reshape(Y * X, Y * Z * rows_shard, lanes), ('y', 'x...  16.2 us
    all_to_all x1, starting transfers between devices, shards(): lax.all_to_all(scaled.astype(jnp.float16), ('x', 'z'), 0, 0, tiled=True)  14.5 us
    all_to_all x1, blocking collectives, shards(): payload = lax.all_to_all(payload, 'y', 0, 0, tiled=True)  12.1 us
    all_to_all x1, waiting for transfers between devices, shards(): lax.all_to_all(scaled.astype(jnp.float16), ('x', 'z'), 0, 0, tiled=True)  11.8 us
    ppermute x1, starting transfers between devices, shards(): theirs = lax.ppermute(mine, 'core', SWAP)  10.3 us
    all_to_all x1, waiting for transfers between devices, shards(): landed = lax.all_to_all(picked, ('x', 'z'), 0, 0, tiled=True)  9.66 us
  transfers between devices with their start and end apart: 14, of which 6 were waited for; matrix products, arithmetic and copies ran while one was open for 0% of the time, Pallas kernels for 6%

profile of v9, /device:TPU:1, one launch (start us, length us, event | category | flops | bytes accessed | tf_op | source)
XLA Modules:
  0.0 181.0 jit_solution(13997435497077408076)
XLA Ops:
  0.6 5.6 %collective-permute-start = (bf16[256,2048]{1,0:T(8,128)(2,1)}, bf16[256,2048]{1,0:T(8,128)(2,1)S(1)}, u32[]{:S(2)}, u32[]{:S(2)}) collective-permute-start(bf16[256,2048]{1,0:T(8,128)(2,1)} %bitcast.34), channel_id=1, source_target_pairs={{0,128},{64,448},{128,256},{192,64},{256,384},{320,192},{384,0},{4... | collective-permute-start | bytes 3145736 | tf_op jit(solution)/shard_map/ppermute | solution.py:333
  6.2 1.9 %prepare.1 = bf16[4,192,128]{2,1,0:T(8,128)(2,1)} custom-call(s32[8,64]{1,0:T(8,128)} %counts.1, s32[4,64]{1,0:T(4,128)} %bitcast.44, bf16[256,256]{1,0:T(8,128)(2,1)} %bitcast.43, f32[16,4,512]{2,1,0:T(4,128)} %refs_0_.1), custom_call_target="tpu_custom_call" | custom-call | tf_op jit(solution)/shard_map/prepare/pallas_call | solution.py:325
  8.2 12.1 %all_to_all.25.payload = bf16[4,192,128]{2,1,0:T(8,128)(2,1)S(1)} all-to-all(bf16[4,192,128]{2,1,0:T(8,128)(2,1)} %prepare.1), channel_id=1, replica_groups=mesh['y'=4,'core'=2,'x'=4,'z'=16] {'y'}, dimensions={0} | all-to-all | bytes 393216 | tf_op jit(solution)/shard_map/all_to_all | solution.py:332
  20.3 0.7 copy-done.4
  21.0 1.3 pick_old.1
  22.3 18.5 %all-to-all-start.1 = ((bf16[64,16,128]{2,1,0:T(8,128)(2,1)}), bf16[64,16,128]{2,1,0:T(8,128)(2,1)}, u32[]{:S(2)}, u32[]{:S(2)}) async-start(bf16[64,16,128]{2,1,0:T(8,128)(2,1)} %pick_old.1), calls=%async_computation.1 | async-start | bytes 524288 | tf_op jit(solution)/shard_map/all_to_all | solution.py:348
  40.8 3.4 %collective-permute-start.1 = (bf16[256,2048]{1,0:T(8,128)(2,1)}, bf16[256,2048]{1,0:T(8,128)(2,1)}, u32[]{:S(2)}, u32[]{:S(2)}) collective-permute-start(bf16[256,2048]{1,0:T(8,128)(2,1)} %bitcast.35), channel_id=1, source_target_pairs={{128,0},{448,64},{256,128},{64,192},{384,256},{192,320},{0,384},{3... | collective-permute-start | bytes 3145736 | tf_op jit(solution)/shard_map/ppermute | solution.py:334
  44.2 3.6 %collective-permute-start.3 = (bf16[256,2048]{1,0:T(8,128)(2,1)S(1)}, bf16[256,2048]{1,0:T(8,128)(2,1)S(1)}, u32[]{:S(2)}, u32[]{:S(2)}) collective-permute-start(bf16[256,2048]{1,0:T(8,128)(2,1)S(1)} %collective-permute-done.one), channel_id=1, source_target_pairs={{0,128},{64,448},{128,256},{192,64},{256,384},{320,192},{384,0},{4... | collective-permute-start | bytes 3145736 | tf_op jit(solution)/shard_map/ppermute | solution.py:349
  47.8 9.7 %all-to-all-done.1.mine = bf16[64,16,128]{2,1,0:T(8,128)(2,1)} async-done(((bf16[64,16,128]{2,1,0:T(8,128)(2,1)}), bf16[64,16,128]{2,1,0:T(8,128)(2,1)}, u32[]{:S(2)}, u32[]{:S(2)}) %all-to-all-start.1) | async-done | bytes 262176 | tf_op jit(solution)/shard_map/all_to_all | solution.py:348
  57.5 6.9 %collective-permute-start.2 = (bf16[64,16,128]{2,1,0:T(8,128)(2,1)}, bf16[64,16,128]{2,1,0:T(8,128)(2,1)S(1)}, u32[]{:S(2)}, u32[]{:S(2)}) collective-permute-start(bf16[64,16,128]{2,1,0:T(8,128)(2,1)} %all-to-all-done.1.mine), channel_id=1, source_target_pairs={{0,64},{64,0},{1,65},{65,1},{2,66},{66,2},{3,67},{67,3},{4,68},{68... | collective-permute-start | bytes 786440 | tf_op jit(solution)/shard_map/ppermute | solution.py:352
  64.4 2.8 %forward_mine.1 = (f32[3,256,128]{2,1,0:T(8,128)S(1)}, bf16[4,256,128]{2,1,0:T(8,128)(2,1)S(1)}) custom-call(bf16[64,16,128]{2,1,0:T(8,128)(2,1)} %all-to-all-done.1.mine, bf16[256,2048]{1,0:T(8,128)(2,1)S(1)} %bitcast.36, bf16[256,2048]{1,0:T(8,128)(2,1)S(1)} %collective-permute-done.one, bf16[256,2048]{1,0:T(8,128)(2,1)} %collective-permute-done.1.two), custom_call_target="tpu_custom_call" | custom-call | tf_op jit(solution)/shard_map/forward_mine/pallas_call | solution.py:357
  67.2 2.7 %near_grad.1 = (f32[4,128,256]{2,1,0:T(8,128)S(1)}, f32[4,128,256]{2,1,0:T(8,128)S(1)}, bf16[4,256,128]{2,1,0:T(8,128)(2,1)S(1)}) custom-call(f32[3,256,128]{2,1,0:T(8,128)S(1)} %get-tuple-element.16.part_ref, bf16[64,16,128]{2,1,0:T(8,128)(2,1)S(1)} %collective-permute-done.2.theirs, bf16[4,192,128]{2,1,0:T(8,128)(2,1)S(1)} %all_to_all.25.payload, ...), custom_call_target="tpu_custom_call" | custom-call | tf_op jit(solution)/shard_map/near_grad/pallas_call | solution.py:367
  70.4 1.0 grad_theirs.1
  71.4 8.8 %collective-permute-start.4 = (f32[65,16,128]{2,1,0:T(8,128)S(1)}, f32[65,16,128]{2,1,0:T(8,128)S(1)}, u32[]{:S(2)}, u32[]{:S(2)}) collective-permute-start(f32[65,16,128]{2,1,0:T(8,128)S(1)} %get-tuple-element.22), channel_id=1, source_target_pairs={{0,64},{64,0},{1,65},{65,1},{2,66},{66,2},{3,67},{67,3},{4,68},{68... | collective-permute-start | bytes 1597448 | tf_op jit(solution)/shard_map/ppermute | solution.py:385
  80.7 1.0 collective-permute-done.4.theirs
  82.2 0.9 convert_element_type.11
  83.1 14.5 %all-to-all-start.2 = ((f16[64,2,1152]{2,1,0:T(2,128)(2,1)}), f16[64,2,1152]{2,1,0:T(2,128)(2,1)S(1)}, u32[]{:S(2)}, u32[]{:S(2)}) async-start(f16[64,2,1152]{2,1,0:T(2,128)(2,1)} %convert_element_type.11), calls=%async_computation.2 | async-start | bytes 589824 | tf_op jit(solution)/shard_map/all_to_all | solution.py:421
  98.0 2.6 %collective-permute-start.7 = (f32[3,16,4,128]{3,2,1,0:T(4,128)S(1)}, f32[3,16,4,128]{3,2,1,0:T(4,128)S(1)}, u32[]{:S(2)}, u32[]{:S(2)}) collective-permute-start(f32[3,16,4,128]{3,2,1,0:T(4,128)S(1)} %get-tuple-element.32), channel_id=1, source_target_pairs={{0,256},{128,384},{256,0},{384,128},{1,257},{129,385},{257,1},{385... | collective-permute-start | bytes 294920 | tf_op jit(solution)/shard_map/ppermute | solution.py:418
  100.6 3.6 %collective-permute-start.6 = (f32[3,16,4,128]{3,2,1,0:T(4,128)S(1)}, f32[3,16,4,128]{3,2,1,0:T(4,128)S(1)}, u32[]{:S(2)}, u32[]{:S(2)}) collective-permute-start(f32[3,16,4,128]{3,2,1,0:T(4,128)S(1)} %get-tuple-element.33), channel_id=1, source_target_pairs={{0,384},{128,0},{256,128},{384,256},{1,385},{129,1},{257,129},{385... | collective-permute-start | bytes 294920 | tf_op jit(solution)/shard_map/ppermute | solution.py:417
  104.2 2.5 %collective-permute-start.5 = (f32[3,16,4,128]{3,2,1,0:T(4,128)S(1)}, f32[3,16,4,128]{3,2,1,0:T(4,128)S(1)}, u32[]{:S(2)}, u32[]{:S(2)}) collective-permute-start(f32[3,16,4,128]{3,2,1,0:T(4,128)S(1)} %get-tuple-element.34), channel_id=1, source_target_pairs={{0,128},{128,256},{256,384},{384,0},{1,129},{129,257},{257,385},{3... | collective-permute-start | bytes 294920 | tf_op jit(solution)/shard_map/ppermute | solution.py:416
  106.9 11.8 %all-to-all-done.2 = f16[64,2,1152]{2,1,0:T(2,128)(2,1)S(1)} async-done(((f16[64,2,1152]{2,1,0:T(2,128)(2,1)}), f16[64,2,1152]{2,1,0:T(2,128)(2,1)S(1)}, u32[]{:S(2)}, u32[]{:S(2)}) %all-to-all-start.2) | async-done | bytes 294944 | tf_op jit(solution)/shard_map/all_to_all | solution.py:421
  118.9 1.1 adam.1
  120.0 17.8 %all_to_all.26 = bf16[16,64,128]{2,1,0:T(8,128)(2,1)S(1)} all-to-all(bf16[16,64,128]{2,1,0:T(8,128)(2,1)S(1)} %bitcast.38), channel_id=1, replica_groups=mesh['y'=4,'core'=2,'x'=4,'z'=16] {'z'}, dimensions={0} | all-to-all | bytes 524288 | tf_op jit(solution)/shard_map/all_to_all | solution.py:443
  138.4 16.2 %all_to_all.27 = bf16[16,256,128]{2,1,0:T(8,128)(2,1)S(1)} all-to-all(bf16[16,256,128]{2,1,0:T(8,128)(2,1)S(1)} %bitcast.40), channel_id=1, replica_groups=mesh['y'=4,'core'=2,'x'=4,'z'=16] {'y','x'}, dimensions={0} | all-to-all | bytes 2097152 | tf_op jit(solution)/shard_map/all_to_all | solution.py:467
  154.6 10.3 %collective-permute-start.8 = (bf16[4,4,4,64,128]{4,3,2,1,0:T(8,128)(2,1)S(1)}, bf16[4,4,4,64,128]{4,3,2,1,0:T(8,128)(2,1)S(1)}, u32[]{:S(2)}, u32[]{:S(2)}) collective-permute-start(bf16[4,4,4,64,128]{4,3,2,1,0:T(8,128)(2,1)S(1)} %bitcast.32), channel_id=1, source_target_pairs={{0,64},{64,0},{1,65},{65,1},{2,66},{66,2},{3,67},{67,3},{4,68},{68... | collective-permute-start | bytes 3145736 | tf_op jit(solution)/shard_map/ppermute | solution.py:470
  165.0 2.5 %collective-permute-start.11 = (f32[3,16,4,128]{3,2,1,0:T(4,128)S(1)}, f32[3,16,4,128]{3,2,1,0:T(4,128)S(1)}, u32[]{:S(2)}, u32[]{:S(2)}) collective-permute-start(f32[3,16,4,128]{3,2,1,0:T(4,128)S(1)} %get-tuple-element.28), channel_id=1, source_target_pairs={{0,256},{128,384},{256,0},{384,128},{1,257},{129,385},{257,1},{385... | collective-permute-start | bytes 294920 | tf_op jit(solution)/shard_map/ppermute | solution.py:449
  167.5 3.2 %collective-permute-start.10 = (f32[3,16,4,128]{3,2,1,0:T(4,128)S(1)}, f32[3,16,4,128]{3,2,1,0:T(4,128)S(1)}, u32[]{:S(2)}, u32[]{:S(2)}) collective-permute-start(f32[3,16,4,128]{3,2,1,0:T(4,128)S(1)} %get-tuple-element.29), channel_id=1, source_target_pairs={{0,384},{128,0},{256,128},{384,256},{1,385},{129,1},{257,129},{385... | collective-permute-start | bytes 294920 | tf_op jit(solution)/shard_map/ppermute | solution.py:448
  170.7 2.0 %collective-permute-start.9 = (f32[3,16,4,128]{3,2,1,0:T(4,128)S(1)}, f32[3,16,4,128]{3,2,1,0:T(4,128)S(1)}, u32[]{:S(2)}, u32[]{:S(2)}) collective-permute-start(f32[3,16,4,128]{3,2,1,0:T(4,128)S(1)} %get-tuple-element.30), channel_id=1, source_target_pairs={{0,128},{128,256},{256,384},{384,0},{1,129},{129,257},{257,385},{3... | collective-permute-start | bytes 294920 | tf_op jit(solution)/shard_map/ppermute | solution.py:447
  173.4 4.2 %collective-permute-done.9.low = f32[3,16,4,128]{3,2,1,0:T(4,128)S(1)} collective-permute-done((f32[3,16,4,128]{3,2,1,0:T(4,128)S(1)}, f32[3,16,4,128]{3,2,1,0:T(4,128)S(1)}, u32[]{:S(2)}, u32[]{:S(2)}) %collective-permute-start.9) | collective-permute-done | bytes 98336 | tf_op jit(solution)/shard_map/ppermute | solution.py:447
  177.6 1.0 join_cols.1
  178.6 1.2 join_mine.1.begun
  179.8 1.2 join_theirs.1
  (36 shorter events, 3.4 us)
Async XLA Ops:
  0.6 63.8 %copy-start = (bf16[1,1,256,2048]{3,2,1,0:T(8,128)(2,1)S(1)}, bf16[1,1,256,2048]{3,2,1,0:T(8,128)(2,1)}, u32[]{:S(2)}) copy-start(bf16[1,1,256,2048]{3,2,1,0:T(8,128)(2,1)} %param.9) | copy-start | bytes 3145732
  0.6 43.6 %collective-permute-start = (bf16[256,2048]{1,0:T(8,128)(2,1)}, bf16[256,2048]{1,0:T(8,128)(2,1)S(1)}, u32[]{:S(2)}, u32[]{:S(2)}) collective-permute-start(bf16[256,2048]{1,0:T(8,128)(2,1)} %bitcast.34), channel_id=1, source_target_pairs={{0,128},{64,448},{128,256},{192,64},{256,384},{320,192},{384,0},{4... | collective-permute-start | bytes 3145736 | tf_op jit(solution)/shard_map/ppermute | solution.py:333
  20.3 0.7 copy-start.4
  22.3 35.2 %all-to-all-start.1 = ((bf16[64,16,128]{2,1,0:T(8,128)(2,1)}), bf16[64,16,128]{2,1,0:T(8,128)(2,1)}, u32[]{:S(2)}, u32[]{:S(2)}) async-start(bf16[64,16,128]{2,1,0:T(8,128)(2,1)} %pick_old.1), calls=%async_computation.1 | async-start | bytes 524288 | tf_op jit(solution)/shard_map/all_to_all | solution.py:348
  40.8 23.6 %collective-permute-start.1 = (bf16[256,2048]{1,0:T(8,128)(2,1)}, bf16[256,2048]{1,0:T(8,128)(2,1)}, u32[]{:S(2)}, u32[]{:S(2)}) collective-permute-start(bf16[256,2048]{1,0:T(8,128)(2,1)} %bitcast.35), channel_id=1, source_target_pairs={{128,0},{448,64},{256,128},{64,192},{384,256},{192,320},{0,384},{3... | collective-permute-start | bytes 3145736 | tf_op jit(solution)/shard_map/ppermute | solution.py:334
  44.2 26.2 %collective-permute-start.3 = (bf16[256,2048]{1,0:T(8,128)(2,1)S(1)}, bf16[256,2048]{1,0:T(8,128)(2,1)S(1)}, u32[]{:S(2)}, u32[]{:S(2)}) collective-permute-start(bf16[256,2048]{1,0:T(8,128)(2,1)S(1)} %collective-permute-done.one), channel_id=1, source_target_pairs={{0,128},{64,448},{128,256},{192,64},{256,384},{320,192},{384,0},{4... | collective-permute-start | bytes 3145736 | tf_op jit(solution)/shard_map/ppermute | solution.py:349
  57.5 9.8 %collective-permute-start.2 = (bf16[64,16,128]{2,1,0:T(8,128)(2,1)}, bf16[64,16,128]{2,1,0:T(8,128)(2,1)S(1)}, u32[]{:S(2)}, u32[]{:S(2)}) collective-permute-start(bf16[64,16,128]{2,1,0:T(8,128)(2,1)} %all-to-all-done.1.mine), channel_id=1, source_target_pairs={{0,64},{64,0},{1,65},{65,1},{2,66},{66,2},{3,67},{67,3},{4,68},{68... | collective-permute-start | bytes 786440 | tf_op jit(solution)/shard_map/ppermute | solution.py:352
  71.4 10.3 %collective-permute-start.4 = (f32[65,16,128]{2,1,0:T(8,128)S(1)}, f32[65,16,128]{2,1,0:T(8,128)S(1)}, u32[]{:S(2)}, u32[]{:S(2)}) collective-permute-start(f32[65,16,128]{2,1,0:T(8,128)S(1)} %get-tuple-element.22), channel_id=1, source_target_pairs={{0,64},{64,0},{1,65},{65,1},{2,66},{66,2},{3,67},{67,3},{4,68},{68... | collective-permute-start | bytes 1597448 | tf_op jit(solution)/shard_map/ppermute | solution.py:385
  80.6 17.1 %copy-start.1 = (f32[16,4,512]{2,1,0:T(4,128)S(1)}, f32[16,4,512]{2,1,0:T(4,128)}, u32[]{:S(2)}) copy-start(f32[16,4,512]{2,1,0:T(4,128)} %refs_0_.1) | copy-start | bytes 393220
  80.6 17.1 %copy-start.2 = (f32[16,4,512]{2,1,0:T(4,128)S(1)}, f32[16,4,512]{2,1,0:T(4,128)}, u32[]{:S(2)}) copy-start(f32[16,4,512]{2,1,0:T(4,128)} %refs_1_.1) | copy-start | bytes 393220
  80.7 17.1 %copy-start.3 = (f32[16,4,512]{2,1,0:T(4,128)S(1)}, f32[16,4,512]{2,1,0:T(4,128)}, u32[]{:S(2)}) copy-start(f32[16,4,512]{2,1,0:T(4,128)} %refs_2_.1) | copy-start | bytes 393220
  80.7 26.0 %copy-start.7 = (s32[8,64]{1,0:T(8,128)S(1)}, s32[8,64]{1,0:T(8,128)}, u32[]{:S(2)}) copy-start(s32[8,64]{1,0:T(8,128)} %counts.1) | copy-start | bytes 6148
  80.7 26.1 %copy-start.5 = (s32[64]{0:T(128)S(1)}, s32[64]{0:T(128)}, u32[]{:S(2)}) copy-start(s32[64]{0:T(128)} %old.1) | copy-start | bytes 772
  82.2 36.7 %copy-start.6 = (s32[64]{0:T(128)S(1)}, s32[64]{0:T(128)}, u32[]{:S(2)}) copy-start(s32[64]{0:T(128)} %new.1) | copy-start | bytes 772
  83.1 35.6 %all-to-all-start.2 = ((f16[64,2,1152]{2,1,0:T(2,128)(2,1)}), f16[64,2,1152]{2,1,0:T(2,128)(2,1)S(1)}, u32[]{:S(2)}, u32[]{:S(2)}) async-start(f16[64,2,1152]{2,1,0:T(2,128)(2,1)} %convert_element_type.11), calls=%async_computation.2 | async-start | bytes 589824 | tf_op jit(solution)/shard_map/all_to_all | solution.py:421
  98.0 20.9 %collective-permute-start.7 = (f32[3,16,4,128]{3,2,1,0:T(4,128)S(1)}, f32[3,16,4,128]{3,2,1,0:T(4,128)S(1)}, u32[]{:S(2)}, u32[]{:S(2)}) collective-permute-start(f32[3,16,4,128]{3,2,1,0:T(4,128)S(1)} %get-tuple-element.32), channel_id=1, source_target_pairs={{0,256},{128,384},{256,0},{384,128},{1,257},{129,385},{257,1},{385... | collective-permute-start | bytes 294920 | tf_op jit(solution)/shard_map/ppermute | solution.py:418
  100.6 18.3 %collective-permute-start.6 = (f32[3,16,4,128]{3,2,1,0:T(4,128)S(1)}, f32[3,16,4,128]{3,2,1,0:T(4,128)S(1)}, u32[]{:S(2)}, u32[]{:S(2)}) collective-permute-start(f32[3,16,4,128]{3,2,1,0:T(4,128)S(1)} %get-tuple-element.33), channel_id=1, source_target_pairs={{0,384},{128,0},{256,128},{384,256},{1,385},{129,1},{257,129},{385... | collective-permute-start | bytes 294920 | tf_op jit(solution)/shard_map/ppermute | solution.py:417
  104.2 14.7 %collective-permute-start.5 = (f32[3,16,4,128]{3,2,1,0:T(4,128)S(1)}, f32[3,16,4,128]{3,2,1,0:T(4,128)S(1)}, u32[]{:S(2)}, u32[]{:S(2)}) collective-permute-start(f32[3,16,4,128]{3,2,1,0:T(4,128)S(1)} %get-tuple-element.34), channel_id=1, source_target_pairs={{0,128},{128,256},{256,384},{384,0},{1,129},{129,257},{257,385},{3... | collective-permute-start | bytes 294920 | tf_op jit(solution)/shard_map/ppermute | solution.py:416
  154.6 25.2 %collective-permute-start.8 = (bf16[4,4,4,64,128]{4,3,2,1,0:T(8,128)(2,1)S(1)}, bf16[4,4,4,64,128]{4,3,2,1,0:T(8,128)(2,1)S(1)}, u32[]{:S(2)}, u32[]{:S(2)}) collective-permute-start(bf16[4,4,4,64,128]{4,3,2,1,0:T(8,128)(2,1)S(1)} %bitcast.32), channel_id=1, source_target_pairs={{0,64},{64,0},{1,65},{65,1},{2,66},{66,2},{3,67},{67,3},{4,68},{68... | collective-permute-start | bytes 3145736 | tf_op jit(solution)/shard_map/ppermute | solution.py:470
  165.0 7.8 %collective-permute-start.11 = (f32[3,16,4,128]{3,2,1,0:T(4,128)S(1)}, f32[3,16,4,128]{3,2,1,0:T(4,128)S(1)}, u32[]{:S(2)}, u32[]{:S(2)}) collective-permute-start(f32[3,16,4,128]{3,2,1,0:T(4,128)S(1)} %get-tuple-element.28), channel_id=1, source_target_pairs={{0,256},{128,384},{256,0},{384,128},{1,257},{129,385},{257,1},{385... | collective-permute-start | bytes 294920 | tf_op jit(solution)/shard_map/ppermute | solution.py:449
  167.5 6.0 %collective-permute-start.10 = (f32[3,16,4,128]{3,2,1,0:T(4,128)S(1)}, f32[3,16,4,128]{3,2,1,0:T(4,128)S(1)}, u32[]{:S(2)}, u32[]{:S(2)}) collective-permute-start(f32[3,16,4,128]{3,2,1,0:T(4,128)S(1)} %get-tuple-element.29), channel_id=1, source_target_pairs={{0,384},{128,0},{256,128},{384,256},{1,385},{129,1},{257,129},{385... | collective-permute-start | bytes 294920 | tf_op jit(solution)/shard_map/ppermute | solution.py:448
  170.7 6.9 %collective-permute-start.9 = (f32[3,16,4,128]{3,2,1,0:T(4,128)S(1)}, f32[3,16,4,128]{3,2,1,0:T(4,128)S(1)}, u32[]{:S(2)}, u32[]{:S(2)}) collective-permute-start(f32[3,16,4,128]{3,2,1,0:T(4,128)S(1)} %get-tuple-element.30), channel_id=1, source_target_pairs={{0,128},{128,256},{256,384},{384,0},{1,129},{129,257},{257,385},{3... | collective-permute-start | bytes 294920 | tf_op jit(solution)/shard_map/ppermute | solution.py:447

commit v10 on v9

--- a/solution.py
+++ b/solution.py
@@ -216,30 +216,23 @@
     out_ref[PLACES] = jnp.broadcast_to(jnp.max(peak, keepdims=True), out_ref.shape[1:])
 
 
-def forward_mine(mine, own, one, two, out_ref, weights_ref, held, sem):
-    copy = pltpu.make_async_copy(two, held, sem)
-    copy.start()
+def forward_mine(mine, own, one, two, out_ref, weights_ref):
     for y, block in enumerate(natural(mine)):
         weights_ref[y] = block
     core = lax.axis_index("core")
     out_ref[0] = forward_part(own, weights_ref, core)
     out_ref[1] = forward_part(one, weights_ref, core)
-    copy.wait()
-    out_ref[2] = forward_part(held, weights_ref, core)
-
-
-def near_grad(part_ref, theirs, payload, own, one, two, theirs_ref, mine_ref, weights_ref, held, sem):
-    copy = pltpu.make_async_copy(two, held, sem)
-    copy.start()
+    out_ref[2] = forward_part(two, weights_ref, core)
+
+
+def near_grad(part_ref, theirs, payload, own, one, two, theirs_ref, mine_ref, weights_ref):
     for y, block in enumerate(natural(theirs)):
         weights_ref[y] = block
     y_here, core = lax.axis_index("y"), lax.axis_index("core")
-    chunks = (own, one, held)
+    chunks = (own, one, two)
     steps = (0, 3 + 2 * core, 1 + 2 * core)
     locals_ = []
     for k, (step, chunk) in enumerate(zip(steps, chunks)):
-        if k == 2:
-            copy.wait()
         both = part_ref[k] + forward_part(chunk, weights_ref, 1 - core)
         locals_.append(local_part(both, payload, (y_here + step) % Y))
     wide = theirs_ref.shape[2]
@@ -353,13 +346,11 @@
 
     wide = PLACES * rows_shard
     weights_shape = jax.ShapeDtypeStruct((Y, wide, lanes), bf16)
-    held = [pltpu.VMEM(own.shape, bf16), pltpu.SemaphoreType.DMA(())]
     forward, w_mine = pl.pallas_call(
         forward_mine,
         out_shape=(jax.ShapeDtypeStruct((3, rows, lanes), f32), weights_shape),
-        in_specs=[VMEM] * 3 + [ANY],
+        in_specs=[VMEM] * 4,
         out_specs=(VMEM, VMEM),
-        scratch_shapes=held,
         compiler_params=grant(24),
         name="forward_mine",
     )(w_mine, own, near_one, near_two)
@@ -367,9 +358,8 @@
     begun_theirs, begun_mine, w_theirs = pl.pallas_call(
         near_grad,
         out_shape=(begun_shape, begun_shape, weights_shape),
-        in_specs=[VMEM] * 5 + [ANY],
+        in_specs=[VMEM] * 6,
         out_specs=(VMEM, VMEM, VMEM),
-        scratch_shapes=held,
         compiler_params=grant(24),
         name="near_grad",
     )(forward, w_theirs, payload, own, near_one, near_two)

time: 184 us -> 183 us (level)
  no operation moved by 1% of the time
where the time goes in v10:
time: 183 us; the launch traced here: 180 us
  starting transfers between devices  86.9 us (47%)
  blocking collectives  46.2 us (25%)
  waiting for transfers between devices  28.9 us (16%)
  Pallas kernels  14.2 us (8%)
    all_to_all x1, starting transfers between devices, shards(): landed = lax.all_to_all(picked, ('x', 'z'), 0, 0, tiled=True)  18.5 us
    all_to_all x1, blocking collectives, shards(): lax.all_to_all(picked.reshape(Z, X * Y * rows_shard, lanes), 'z', 0, 0, t...  17.8 us
    all_to_all x1, blocking collectives, shards(): lax.all_to_all(copies.reshape(Y * X, Y * Z * rows_shard, lanes), ('y', 'x...  16.2 us
    all_to_all x1, starting transfers between devices, shards(): lax.all_to_all(scaled.astype(jnp.float16), ('x', 'z'), 0, 0, tiled=True)  14.5 us
    all_to_all x1, blocking collectives, shards(): payload = lax.all_to_all(payload, 'y', 0, 0, tiled=True)  12.1 us
    all_to_all x1, waiting for transfers between devices, shards(): lax.all_to_all(scaled.astype(jnp.float16), ('x', 'z'), 0, 0, tiled=True)  11.8 us
    ppermute x1, starting transfers between devices, shards(): theirs = lax.ppermute(mine, 'core', SWAP)  10.3 us
    all_to_all x1, waiting for transfers between devices, shards(): landed = lax.all_to_all(picked, ('x', 'z'), 0, 0, tiled=True)  9.66 us
  transfers between devices with their start and end apart: 14, of which 6 were waited for; matrix products, arithmetic and copies ran while one was open for 0% of the time, Pallas kernels for 6%

profile of v10, /device:TPU:1, one launch (start us, length us, event | category | flops | bytes accessed | tf_op | source)
XLA Modules:
  0.0 179.9 jit_solution(1465194977472095397)
XLA Ops:
  0.6 5.6 %collective-permute-start = (bf16[256,2048]{1,0:T(8,128)(2,1)}, bf16[256,2048]{1,0:T(8,128)(2,1)S(1)}, u32[]{:S(2)}, u32[]{:S(2)}) collective-permute-start(bf16[256,2048]{1,0:T(8,128)(2,1)} %bitcast.34), channel_id=1, source_target_pairs={{0,128},{64,448},{128,256},{192,64},{256,384},{320,192},{384,0},{4... | collective-permute-start | bytes 3145736 | tf_op jit(solution)/shard_map/ppermute | solution.py:326
  6.2 1.9 %prepare.1 = bf16[4,192,128]{2,1,0:T(8,128)(2,1)} custom-call(s32[8,64]{1,0:T(8,128)} %counts.1, s32[4,64]{1,0:T(4,128)} %bitcast.44, bf16[256,256]{1,0:T(8,128)(2,1)} %bitcast.43, f32[16,4,512]{2,1,0:T(4,128)} %refs_0_.1), custom_call_target="tpu_custom_call" | custom-call | tf_op jit(solution)/shard_map/prepare/pallas_call | solution.py:318
  8.2 12.1 %all_to_all.25.payload = bf16[4,192,128]{2,1,0:T(8,128)(2,1)S(1)} all-to-all(bf16[4,192,128]{2,1,0:T(8,128)(2,1)} %prepare.1), channel_id=1, replica_groups=mesh['y'=4,'core'=2,'x'=4,'z'=16] {'y'}, dimensions={0} | all-to-all | bytes 393216 | tf_op jit(solution)/shard_map/all_to_all | solution.py:325
  21.0 1.3 pick_old.1
  22.3 18.5 %all-to-all-start.1 = ((bf16[64,16,128]{2,1,0:T(8,128)(2,1)}), bf16[64,16,128]{2,1,0:T(8,128)(2,1)}, u32[]{:S(2)}, u32[]{:S(2)}) async-start(bf16[64,16,128]{2,1,0:T(8,128)(2,1)} %pick_old.1), calls=%async_computation.1 | async-start | bytes 524288 | tf_op jit(solution)/shard_map/all_to_all | solution.py:341
  40.8 3.4 %collective-permute-start.1 = (bf16[256,2048]{1,0:T(8,128)(2,1)}, bf16[256,2048]{1,0:T(8,128)(2,1)}, u32[]{:S(2)}, u32[]{:S(2)}) collective-permute-start(bf16[256,2048]{1,0:T(8,128)(2,1)} %bitcast.35), channel_id=1, source_target_pairs={{128,0},{448,64},{256,128},{64,192},{384,256},{192,320},{0,384},{3... | collective-permute-start | bytes 3145736 | tf_op jit(solution)/shard_map/ppermute | solution.py:327
  44.2 3.6 %collective-permute-start.3 = (bf16[256,2048]{1,0:T(8,128)(2,1)S(1)}, bf16[256,2048]{1,0:T(8,128)(2,1)S(1)}, u32[]{:S(2)}, u32[]{:S(2)}) collective-permute-start(bf16[256,2048]{1,0:T(8,128)(2,1)S(1)} %collective-permute-done.one), channel_id=1, source_target_pairs={{0,128},{64,448},{128,256},{192,64},{256,384},{320,192},{384,0},{4... | collective-permute-start | bytes 3145736 | tf_op jit(solution)/shard_map/ppermute | solution.py:342
  47.8 9.7 %all-to-all-done.1.mine = bf16[64,16,128]{2,1,0:T(8,128)(2,1)} async-done(((bf16[64,16,128]{2,1,0:T(8,128)(2,1)}), bf16[64,16,128]{2,1,0:T(8,128)(2,1)}, u32[]{:S(2)}, u32[]{:S(2)}) %all-to-all-start.1) | async-done | bytes 262176 | tf_op jit(solution)/shard_map/all_to_all | solution.py:341
  57.5 6.9 %collective-permute-start.2 = (bf16[64,16,128]{2,1,0:T(8,128)(2,1)}, bf16[64,16,128]{2,1,0:T(8,128)(2,1)S(1)}, u32[]{:S(2)}, u32[]{:S(2)}) collective-permute-start(bf16[64,16,128]{2,1,0:T(8,128)(2,1)} %all-to-all-done.1.mine), channel_id=1, source_target_pairs={{0,64},{64,0},{1,65},{65,1},{2,66},{66,2},{3,67},{67,3},{4,68},{68... | collective-permute-start | bytes 786440 | tf_op jit(solution)/shard_map/ppermute | solution.py:345
  64.4 1.9 %forward_mine.1 = (f32[3,256,128]{2,1,0:T(8,128)S(1)}, bf16[4,256,128]{2,1,0:T(8,128)(2,1)S(1)}) custom-call(bf16[64,16,128]{2,1,0:T(8,128)(2,1)} %all-to-all-done.1.mine, bf16[256,2048]{1,0:T(8,128)(2,1)S(1)} %bitcast.36, bf16[256,2048]{1,0:T(8,128)(2,1)S(1)} %collective-permute-done.one, bf16[256,2048]{1,0:T(8,128)(2,1)} %collective-permute-done.1.two), custom_call_target="tpu_custom_call" | custom-call | tf_op jit(solution)/shard_map/forward_mine/pallas_call | solution.py:349
  66.3 2.5 %near_grad.1 = (f32[4,128,256]{2,1,0:T(8,128)S(1)}, f32[4,128,256]{2,1,0:T(8,128)S(1)}, bf16[4,256,128]{2,1,0:T(8,128)(2,1)S(1)}) custom-call(f32[3,256,128]{2,1,0:T(8,128)S(1)} %get-tuple-element.16.part_ref, bf16[64,16,128]{2,1,0:T(8,128)(2,1)S(1)} %collective-permute-done.2.theirs, bf16[4,192,128]{2,1,0:T(8,128)(2,1)S(1)} %all_to_all.25.payload, ...), custom_call_target="tpu_custom_call" | custom-call | tf_op jit(solution)/shard_map/near_grad/pallas_call | solution.py:358
  68.8 1.6 collective-permute-done.3.chunk
  70.4 1.0 grad_theirs.1
  71.4 7.7 %collective-permute-start.4 = (f32[65,16,128]{2,1,0:T(8,128)S(1)}, f32[65,16,128]{2,1,0:T(8,128)S(1)}, u32[]{:S(2)}, u32[]{:S(2)}) collective-permute-start(f32[65,16,128]{2,1,0:T(8,128)S(1)} %get-tuple-element.22), channel_id=1, source_target_pairs={{0,64},{64,0},{1,65},{65,1},{2,66},{66,2},{3,67},{67,3},{4,68},{68... | collective-permute-start | bytes 1597448 | tf_op jit(solution)/shard_map/ppermute | solution.py:375
  79.6 1.0 collective-permute-done.4.theirs
  81.1 0.9 convert_element_type.11
  82.1 14.5 %all-to-all-start.2 = ((f16[64,2,1152]{2,1,0:T(2,128)(2,1)}), f16[64,2,1152]{2,1,0:T(2,128)(2,1)S(1)}, u32[]{:S(2)}, u32[]{:S(2)}) async-start(f16[64,2,1152]{2,1,0:T(2,128)(2,1)} %convert_element_type.11), calls=%async_computation.2 | async-start | bytes 589824 | tf_op jit(solution)/shard_map/all_to_all | solution.py:411
  97.0 2.6 %collective-permute-start.7 = (f32[3,16,4,128]{3,2,1,0:T(4,128)S(1)}, f32[3,16,4,128]{3,2,1,0:T(4,128)S(1)}, u32[]{:S(2)}, u32[]{:S(2)}) collective-permute-start(f32[3,16,4,128]{3,2,1,0:T(4,128)S(1)} %get-tuple-element.32), channel_id=1, source_target_pairs={{0,256},{128,384},{256,0},{384,128},{1,257},{129,385},{257,1},{385... | collective-permute-start | bytes 294920 | tf_op jit(solution)/shard_map/ppermute | solution.py:408
  99.5 3.6 %collective-permute-start.6 = (f32[3,16,4,128]{3,2,1,0:T(4,128)S(1)}, f32[3,16,4,128]{3,2,1,0:T(4,128)S(1)}, u32[]{:S(2)}, u32[]{:S(2)}) collective-permute-start(f32[3,16,4,128]{3,2,1,0:T(4,128)S(1)} %get-tuple-element.33), channel_id=1, source_target_pairs={{0,384},{128,0},{256,128},{384,256},{1,385},{129,1},{257,129},{385... | collective-permute-start | bytes 294920 | tf_op jit(solution)/shard_map/ppermute | solution.py:407
  103.1 2.5 %collective-permute-start.5 = (f32[3,16,4,128]{3,2,1,0:T(4,128)S(1)}, f32[3,16,4,128]{3,2,1,0:T(4,128)S(1)}, u32[]{:S(2)}, u32[]{:S(2)}) collective-permute-start(f32[3,16,4,128]{3,2,1,0:T(4,128)S(1)} %get-tuple-element.34), channel_id=1, source_target_pairs={{0,128},{128,256},{256,384},{384,0},{1,129},{129,257},{257,385},{3... | collective-permute-start | bytes 294920 | tf_op jit(solution)/shard_map/ppermute | solution.py:406
  105.9 11.8 %all-to-all-done.2 = f16[64,2,1152]{2,1,0:T(2,128)(2,1)S(1)} async-done(((f16[64,2,1152]{2,1,0:T(2,128)(2,1)}), f16[64,2,1152]{2,1,0:T(2,128)(2,1)S(1)}, u32[]{:S(2)}, u32[]{:S(2)}) %all-to-all-start.2) | async-done | bytes 294944 | tf_op jit(solution)/shard_map/all_to_all | solution.py:411
  117.9 1.1 adam.1
  119.0 17.8 %all_to_all.26 = bf16[16,64,128]{2,1,0:T(8,128)(2,1)S(1)} all-to-all(bf16[16,64,128]{2,1,0:T(8,128)(2,1)S(1)} %bitcast.38), channel_id=1, replica_groups=mesh['y'=4,'core'=2,'x'=4,'z'=16] {'z'}, dimensions={0} | all-to-all | bytes 524288 | tf_op jit(solution)/shard_map/all_to_all | solution.py:433
  137.3 16.2 %all_to_all.27 = bf16[16,256,128]{2,1,0:T(8,128)(2,1)S(1)} all-to-all(bf16[16,256,128]{2,1,0:T(8,128)(2,1)S(1)} %bitcast.40), channel_id=1, replica_groups=mesh['y'=4,'core'=2,'x'=4,'z'=16] {'y','x'}, dimensions={0} | all-to-all | bytes 2097152 | tf_op jit(solution)/shard_map/all_to_all | solution.py:457
  153.5 10.3 %collective-permute-start.8 = (bf16[4,4,4,64,128]{4,3,2,1,0:T(8,128)(2,1)S(1)}, bf16[4,4,4,64,128]{4,3,2,1,0:T(8,128)(2,1)S(1)}, u32[]{:S(2)}, u32[]{:S(2)}) collective-permute-start(bf16[4,4,4,64,128]{4,3,2,1,0:T(8,128)(2,1)S(1)} %bitcast.32), channel_id=1, source_target_pairs={{0,64},{64,0},{1,65},{65,1},{2,66},{66,2},{3,67},{67,3},{4,68},{68... | collective-permute-start | bytes 3145736 | tf_op jit(solution)/shard_map/ppermute | solution.py:460
  163.9 2.5 %collective-permute-start.11 = (f32[3,16,4,128]{3,2,1,0:T(4,128)S(1)}, f32[3,16,4,128]{3,2,1,0:T(4,128)S(1)}, u32[]{:S(2)}, u32[]{:S(2)}) collective-permute-start(f32[3,16,4,128]{3,2,1,0:T(4,128)S(1)} %get-tuple-element.28), channel_id=1, source_target_pairs={{0,256},{128,384},{256,0},{384,128},{1,257},{129,385},{257,1},{385... | collective-permute-start | bytes 294920 | tf_op jit(solution)/shard_map/ppermute | solution.py:439
  166.4 3.2 %collective-permute-start.10 = (f32[3,16,4,128]{3,2,1,0:T(4,128)S(1)}, f32[3,16,4,128]{3,2,1,0:T(4,128)S(1)}, u32[]{:S(2)}, u32[]{:S(2)}) collective-permute-start(f32[3,16,4,128]{3,2,1,0:T(4,128)S(1)} %get-tuple-element.29), channel_id=1, source_target_pairs={{0,384},{128,0},{256,128},{384,256},{1,385},{129,1},{257,129},{385... | collective-permute-start | bytes 294920 | tf_op jit(solution)/shard_map/ppermute | solution.py:438
  169.7 2.0 %collective-permute-start.9 = (f32[3,16,4,128]{3,2,1,0:T(4,128)S(1)}, f32[3,16,4,128]{3,2,1,0:T(4,128)S(1)}, u32[]{:S(2)}, u32[]{:S(2)}) collective-permute-start(f32[3,16,4,128]{3,2,1,0:T(4,128)S(1)} %get-tuple-element.30), channel_id=1, source_target_pairs={{0,128},{128,256},{256,384},{384,0},{1,129},{129,257},{257,385},{3... | collective-permute-start | bytes 294920 | tf_op jit(solution)/shard_map/ppermute | solution.py:437
  172.4 4.2 %collective-permute-done.9.low = f32[3,16,4,128]{3,2,1,0:T(4,128)S(1)} collective-permute-done((f32[3,16,4,128]{3,2,1,0:T(4,128)S(1)}, f32[3,16,4,128]{3,2,1,0:T(4,128)S(1)}, u32[]{:S(2)}, u32[]{:S(2)}) %collective-permute-start.9) | collective-permute-done | bytes 98336 | tf_op jit(solution)/shard_map/ppermute | solution.py:437
  176.5 1.0 join_cols.1
  177.5 1.2 join_mine.1.begun
  178.7 1.2 join_theirs.1
  (36 shorter events, 3.5 us)
Async XLA Ops:
  0.6 63.8 %copy-start = (bf16[1,1,256,2048]{3,2,1,0:T(8,128)(2,1)S(1)}, bf16[1,1,256,2048]{3,2,1,0:T(8,128)(2,1)}, u32[]{:S(2)}) copy-start(bf16[1,1,256,2048]{3,2,1,0:T(8,128)(2,1)} %param.9) | copy-start | bytes 3145732
  0.6 43.6 %collective-permute-start = (bf16[256,2048]{1,0:T(8,128)(2,1)}, bf16[256,2048]{1,0:T(8,128)(2,1)S(1)}, u32[]{:S(2)}, u32[]{:S(2)}) collective-permute-start(bf16[256,2048]{1,0:T(8,128)(2,1)} %bitcast.34), channel_id=1, source_target_pairs={{0,128},{64,448},{128,256},{192,64},{256,384},{320,192},{384,0},{4... | collective-permute-start | bytes 3145736 | tf_op jit(solution)/shard_map/ppermute | solution.py:326
  20.3 0.7 copy-start.4
  22.3 35.2 %all-to-all-start.1 = ((bf16[64,16,128]{2,1,0:T(8,128)(2,1)}), bf16[64,16,128]{2,1,0:T(8,128)(2,1)}, u32[]{:S(2)}, u32[]{:S(2)}) async-start(bf16[64,16,128]{2,1,0:T(8,128)(2,1)} %pick_old.1), calls=%async_computation.1 | async-start | bytes 524288 | tf_op jit(solution)/shard_map/all_to_all | solution.py:341
  40.8 23.6 %collective-permute-start.1 = (bf16[256,2048]{1,0:T(8,128)(2,1)}, bf16[256,2048]{1,0:T(8,128)(2,1)}, u32[]{:S(2)}, u32[]{:S(2)}) collective-permute-start(bf16[256,2048]{1,0:T(8,128)(2,1)} %bitcast.35), channel_id=1, source_target_pairs={{128,0},{448,64},{256,128},{64,192},{384,256},{192,320},{0,384},{3... | collective-permute-start | bytes 3145736 | tf_op jit(solution)/shard_map/ppermute | solution.py:327
  44.2 26.2 %collective-permute-start.3 = (bf16[256,2048]{1,0:T(8,128)(2,1)S(1)}, bf16[256,2048]{1,0:T(8,128)(2,1)S(1)}, u32[]{:S(2)}, u32[]{:S(2)}) collective-permute-start(bf16[256,2048]{1,0:T(8,128)(2,1)S(1)} %collective-permute-done.one), channel_id=1, source_target_pairs={{0,128},{64,448},{128,256},{192,64},{256,384},{320,192},{384,0},{4... | collective-permute-start | bytes 3145736 | tf_op jit(solution)/shard_map/ppermute | solution.py:342
  57.5 8.9 %collective-permute-start.2 = (bf16[64,16,128]{2,1,0:T(8,128)(2,1)}, bf16[64,16,128]{2,1,0:T(8,128)(2,1)S(1)}, u32[]{:S(2)}, u32[]{:S(2)}) collective-permute-start(bf16[64,16,128]{2,1,0:T(8,128)(2,1)} %all-to-all-done.1.mine), channel_id=1, source_target_pairs={{0,64},{64,0},{1,65},{65,1},{2,66},{66,2},{3,67},{67,3},{4,68},{68... | collective-permute-start | bytes 786440 | tf_op jit(solution)/shard_map/ppermute | solution.py:345
  71.4 9.3 %collective-permute-start.4 = (f32[65,16,128]{2,1,0:T(8,128)S(1)}, f32[65,16,128]{2,1,0:T(8,128)S(1)}, u32[]{:S(2)}, u32[]{:S(2)}) collective-permute-start(f32[65,16,128]{2,1,0:T(8,128)S(1)} %get-tuple-element.22), channel_id=1, source_target_pairs={{0,64},{64,0},{1,65},{65,1},{2,66},{66,2},{3,67},{67,3},{4,68},{68... | collective-permute-start | bytes 1597448 | tf_op jit(solution)/shard_map/ppermute | solution.py:375
  79.6 17.1 %copy-start.1 = (f32[16,4,512]{2,1,0:T(4,128)S(1)}, f32[16,4,512]{2,1,0:T(4,128)}, u32[]{:S(2)}) copy-start(f32[16,4,512]{2,1,0:T(4,128)} %refs_0_.1) | copy-start | bytes 393220
  79.6 17.1 %copy-start.2 = (f32[16,4,512]{2,1,0:T(4,128)S(1)}, f32[16,4,512]{2,1,0:T(4,128)}, u32[]{:S(2)}) copy-start(f32[16,4,512]{2,1,0:T(4,128)} %refs_1_.1) | copy-start | bytes 393220
  79.6 17.1 %copy-start.3 = (f32[16,4,512]{2,1,0:T(4,128)S(1)}, f32[16,4,512]{2,1,0:T(4,128)}, u32[]{:S(2)}) copy-start(f32[16,4,512]{2,1,0:T(4,128)} %refs_2_.1) | copy-start | bytes 393220
  79.6 26.0 %copy-start.7 = (s32[8,64]{1,0:T(8,128)S(1)}, s32[8,64]{1,0:T(8,128)}, u32[]{:S(2)}) copy-start(s32[8,64]{1,0:T(8,128)} %counts.1) | copy-start | bytes 6148
  79.6 26.1 %copy-start.5 = (s32[64]{0:T(128)S(1)}, s32[64]{0:T(128)}, u32[]{:S(2)}) copy-start(s32[64]{0:T(128)} %old.1) | copy-start | bytes 772
  81.1 36.7 %copy-start.6 = (s32[64]{0:T(128)S(1)}, s32[64]{0:T(128)}, u32[]{:S(2)}) copy-start(s32[64]{0:T(128)} %new.1) | copy-start | bytes 772
  82.1 35.6 %all-to-all-start.2 = ((f16[64,2,1152]{2,1,0:T(2,128)(2,1)}), f16[64,2,1152]{2,1,0:T(2,128)(2,1)S(1)}, u32[]{:S(2)}, u32[]{:S(2)}) async-start(f16[64,2,1152]{2,1,0:T(2,128)(2,1)} %convert_element_type.11), calls=%async_computation.2 | async-start | bytes 589824 | tf_op jit(solution)/shard_map/all_to_all | solution.py:411
  97.0 20.9 %collective-permute-start.7 = (f32[3,16,4,128]{3,2,1,0:T(4,128)S(1)}, f32[3,16,4,128]{3,2,1,0:T(4,128)S(1)}, u32[]{:S(2)}, u32[]{:S(2)}) collective-permute-start(f32[3,16,4,128]{3,2,1,0:T(4,128)S(1)} %get-tuple-element.32), channel_id=1, source_target_pairs={{0,256},{128,384},{256,0},{384,128},{1,257},{129,385},{257,1},{385... | collective-permute-start | bytes 294920 | tf_op jit(solution)/shard_map/ppermute | solution.py:408
  99.5 18.3 %collective-permute-start.6 = (f32[3,16,4,128]{3,2,1,0:T(4,128)S(1)}, f32[3,16,4,128]{3,2,1,0:T(4,128)S(1)}, u32[]{:S(2)}, u32[]{:S(2)}) collective-permute-start(f32[3,16,4,128]{3,2,1,0:T(4,128)S(1)} %get-tuple-element.33), channel_id=1, source_target_pairs={{0,384},{128,0},{256,128},{384,256},{1,385},{129,1},{257,129},{385... | collective-permute-start | bytes 294920 | tf_op jit(solution)/shard_map/ppermute | solution.py:407
  103.1 14.7 %collective-permute-start.5 = (f32[3,16,4,128]{3,2,1,0:T(4,128)S(1)}, f32[3,16,4,128]{3,2,1,0:T(4,128)S(1)}, u32[]{:S(2)}, u32[]{:S(2)}) collective-permute-start(f32[3,16,4,128]{3,2,1,0:T(4,128)S(1)} %get-tuple-element.34), channel_id=1, source_target_pairs={{0,128},{128,256},{256,384},{384,0},{1,129},{129,257},{257,385},{3... | collective-permute-start | bytes 294920 | tf_op jit(solution)/shard_map/ppermute | solution.py:406
  153.5 25.2 %collective-permute-start.8 = (bf16[4,4,4,64,128]{4,3,2,1,0:T(8,128)(2,1)S(1)}, bf16[4,4,4,64,128]{4,3,2,1,0:T(8,128)(2,1)S(1)}, u32[]{:S(2)}, u32[]{:S(2)}) collective-permute-start(bf16[4,4,4,64,128]{4,3,2,1,0:T(8,128)(2,1)S(1)} %bitcast.32), channel_id=1, source_target_pairs={{0,64},{64,0},{1,65},{65,1},{2,66},{66,2},{3,67},{67,3},{4,68},{68... | collective-permute-start | bytes 3145736 | tf_op jit(solution)/shard_map/ppermute | solution.py:460
  163.9 7.8 %collective-permute-start.11 = (f32[3,16,4,128]{3,2,1,0:T(4,128)S(1)}, f32[3,16,4,128]{3,2,1,0:T(4,128)S(1)}, u32[]{:S(2)}, u32[]{:S(2)}) collective-permute-start(f32[3,16,4,128]{3,2,1,0:T(4,128)S(1)} %get-tuple-element.28), channel_id=1, source_target_pairs={{0,256},{128,384},{256,0},{384,128},{1,257},{129,385},{257,1},{385... | collective-permute-start | bytes 294920 | tf_op jit(solution)/shard_map/ppermute | solution.py:439
  166.4 6.0 %collective-permute-start.10 = (f32[3,16,4,128]{3,2,1,0:T(4,128)S(1)}, f32[3,16,4,128]{3,2,1,0:T(4,128)S(1)}, u32[]{:S(2)}, u32[]{:S(2)}) collective-permute-start(f32[3,16,4,128]{3,2,1,0:T(4,128)S(1)} %get-tuple-element.29), channel_id=1, source_target_pairs={{0,384},{128,0},{256,128},{384,256},{1,385},{129,1},{257,129},{385... | collective-permute-start | bytes 294920 | tf_op jit(solution)/shard_map/ppermute | solution.py:438
  169.7 6.9 %collective-permute-start.9 = (f32[3,16,4,128]{3,2,1,0:T(4,128)S(1)}, f32[3,16,4,128]{3,2,1,0:T(4,128)S(1)}, u32[]{:S(2)}, u32[]{:S(2)}) collective-permute-start(f32[3,16,4,128]{3,2,1,0:T(4,128)S(1)} %get-tuple-element.30), channel_id=1, source_target_pairs={{0,128},{128,256},{256,384},{384,0},{1,129},{129,257},{257,385},{3... | collective-permute-start | bytes 294920 | tf_op jit(solution)/shard_map/ppermute | solution.py:437

commit v11 on v10

--- a/solution.py
+++ b/solution.py
@@ -278,15 +278,15 @@
         for x in range(X):
             at = slice(x * rows, (x + 1) * rows)
             for pair in range(Y // 2):
-                a = source[2 * pair, x, y].astype(jnp.float32)
-                b = source[2 * pair + 1, x, y].astype(jnp.float32)
+                a = source[2 * pair, x, y]
+                b = source[2 * pair + 1, x, y]
                 first = lower_half(a)
                 blocks[y, at, pair * lanes : (pair + 1) * lanes] = jnp.where(
                     first, a, swapped(b)
-                ).astype(jnp.bfloat16)
+                )
                 blocks[y, at, half + pair * lanes : half + (pair + 1) * lanes] = jnp.where(
                     first, swapped(a), b
-                ).astype(jnp.bfloat16)
+                )
         copy = pltpu.make_async_copy(blocks.at[y], out.at[y, which], sems.at[y])
         copy.start()
         copies.append(copy)

time: 183 us -> 183 us (level)
  no operation moved by 1% of the time
where the time goes in v11:
time: 183 us; the launch traced here: 180 us
  starting transfers between devices  86.9 us (47%)
  blocking collectives  46.2 us (25%)
  waiting for transfers between devices  28.9 us (16%)
  Pallas kernels  14.1 us (8%)
    all_to_all x1, starting transfers between devices, shards(): landed = lax.all_to_all(picked, ('x', 'z'), 0, 0, tiled=True)  18.5 us
    all_to_all x1, blocking collectives, shards(): lax.all_to_all(picked.reshape(Z, X * Y * rows_shard, lanes), 'z', 0, 0, t...  17.8 us
    all_to_all x1, blocking collectives, shards(): lax.all_to_all(copies.reshape(Y * X, Y * Z * rows_shard, lanes), ('y', 'x...  16.2 us
    all_to_all x1, starting transfers between devices, shards(): lax.all_to_all(scaled.astype(jnp.float16), ('x', 'z'), 0, 0, tiled=True)  14.5 us
    all_to_all x1, blocking collectives, shards(): payload = lax.all_to_all(payload, 'y', 0, 0, tiled=True)  12.1 us
    all_to_all x1, waiting for transfers between devices, shards(): lax.all_to_all(scaled.astype(jnp.float16), ('x', 'z'), 0, 0, tiled=True)  11.8 us
    ppermute x1, starting transfers between devices, shards(): theirs = lax.ppermute(mine, 'core', SWAP)  10.3 us
    all_to_all x1, waiting for transfers between devices, shards(): landed = lax.all_to_all(picked, ('x', 'z'), 0, 0, tiled=True)  9.66 us
  transfers between devices with their start and end apart: 14, of which 6 were waited for; matrix products, arithmetic and copies ran while one was open for 0% of the time, Pallas kernels for 6%

profile of v11, /device:TPU:1, one launch (start us, length us, event | category | flops | bytes accessed | tf_op | source)
XLA Modules:
  0.0 179.8 jit_solution(14389652534120906857)
XLA Ops:
  0.6 5.6 %collective-permute-start = (bf16[256,2048]{1,0:T(8,128)(2,1)}, bf16[256,2048]{1,0:T(8,128)(2,1)S(1)}, u32[]{:S(2)}, u32[]{:S(2)}) collective-permute-start(bf16[256,2048]{1,0:T(8,128)(2,1)} %bitcast.34), channel_id=1, source_target_pairs={{0,128},{64,448},{128,256},{192,64},{256,384},{320,192},{384,0},{4... | collective-permute-start | bytes 3145736 | tf_op jit(solution)/shard_map/ppermute | solution.py:326
  6.2 1.9 %prepare.1 = bf16[4,192,128]{2,1,0:T(8,128)(2,1)} custom-call(s32[8,64]{1,0:T(8,128)} %counts.1, s32[4,64]{1,0:T(4,128)} %bitcast.44, bf16[256,256]{1,0:T(8,128)(2,1)} %bitcast.43, f32[16,4,512]{2,1,0:T(4,128)} %refs_0_.1), custom_call_target="tpu_custom_call" | custom-call | tf_op jit(solution)/shard_map/prepare/pallas_call | solution.py:318
  8.2 12.1 %all_to_all.25.payload = bf16[4,192,128]{2,1,0:T(8,128)(2,1)S(1)} all-to-all(bf16[4,192,128]{2,1,0:T(8,128)(2,1)} %prepare.1), channel_id=1, replica_groups=mesh['y'=4,'core'=2,'x'=4,'z'=16] {'y'}, dimensions={0} | all-to-all | bytes 393216 | tf_op jit(solution)/shard_map/all_to_all | solution.py:325
  21.0 1.3 pick_old.1
  22.3 18.5 %all-to-all-start.1 = ((bf16[64,16,128]{2,1,0:T(8,128)(2,1)}), bf16[64,16,128]{2,1,0:T(8,128)(2,1)}, u32[]{:S(2)}, u32[]{:S(2)}) async-start(bf16[64,16,128]{2,1,0:T(8,128)(2,1)} %pick_old.1), calls=%async_computation.1 | async-start | bytes 524288 | tf_op jit(solution)/shard_map/all_to_all | solution.py:341
  40.8 3.4 %collective-permute-start.1 = (bf16[256,2048]{1,0:T(8,128)(2,1)}, bf16[256,2048]{1,0:T(8,128)(2,1)}, u32[]{:S(2)}, u32[]{:S(2)}) collective-permute-start(bf16[256,2048]{1,0:T(8,128)(2,1)} %bitcast.35), channel_id=1, source_target_pairs={{128,0},{448,64},{256,128},{64,192},{384,256},{192,320},{0,384},{3... | collective-permute-start | bytes 3145736 | tf_op jit(solution)/shard_map/ppermute | solution.py:327
  44.2 3.6 %collective-permute-start.3 = (bf16[256,2048]{1,0:T(8,128)(2,1)S(1)}, bf16[256,2048]{1,0:T(8,128)(2,1)S(1)}, u32[]{:S(2)}, u32[]{:S(2)}) collective-permute-start(bf16[256,2048]{1,0:T(8,128)(2,1)S(1)} %collective-permute-done.one), channel_id=1, source_target_pairs={{0,128},{64,448},{128,256},{192,64},{256,384},{320,192},{384,0},{4... | collective-permute-start | bytes 3145736 | tf_op jit(solution)/shard_map/ppermute | solution.py:342
  47.8 9.7 %all-to-all-done.1.mine = bf16[64,16,128]{2,1,0:T(8,128)(2,1)} async-done(((bf16[64,16,128]{2,1,0:T(8,128)(2,1)}), bf16[64,16,128]{2,1,0:T(8,128)(2,1)}, u32[]{:S(2)}, u32[]{:S(2)}) %all-to-all-start.1) | async-done | bytes 262176 | tf_op jit(solution)/shard_map/all_to_all | solution.py:341
  57.5 6.9 %collective-permute-start.2 = (bf16[64,16,128]{2,1,0:T(8,128)(2,1)}, bf16[64,16,128]{2,1,0:T(8,128)(2,1)S(1)}, u32[]{:S(2)}, u32[]{:S(2)}) collective-permute-start(bf16[64,16,128]{2,1,0:T(8,128)(2,1)} %all-to-all-done.1.mine), channel_id=1, source_target_pairs={{0,64},{64,0},{1,65},{65,1},{2,66},{66,2},{3,67},{67,3},{4,68},{68... | collective-permute-start | bytes 786440 | tf_op jit(solution)/shard_map/ppermute | solution.py:345
  64.4 1.9 %forward_mine.1 = (f32[3,256,128]{2,1,0:T(8,128)S(1)}, bf16[4,256,128]{2,1,0:T(8,128)(2,1)S(1)}) custom-call(bf16[64,16,128]{2,1,0:T(8,128)(2,1)} %all-to-all-done.1.mine, bf16[256,2048]{1,0:T(8,128)(2,1)S(1)} %bitcast.36, bf16[256,2048]{1,0:T(8,128)(2,1)S(1)} %collective-permute-done.one, bf16[256,2048]{1,0:T(8,128)(2,1)} %collective-permute-done.1.two), custom_call_target="tpu_custom_call" | custom-call | tf_op jit(solution)/shard_map/forward_mine/pallas_call | solution.py:349
  66.3 2.5 %near_grad.1 = (f32[4,128,256]{2,1,0:T(8,128)S(1)}, f32[4,128,256]{2,1,0:T(8,128)S(1)}, bf16[4,256,128]{2,1,0:T(8,128)(2,1)S(1)}) custom-call(f32[3,256,128]{2,1,0:T(8,128)S(1)} %get-tuple-element.16.part_ref, bf16[64,16,128]{2,1,0:T(8,128)(2,1)S(1)} %collective-permute-done.2.theirs, bf16[4,192,128]{2,1,0:T(8,128)(2,1)S(1)} %all_to_all.25.payload, ...), custom_call_target="tpu_custom_call" | custom-call | tf_op jit(solution)/shard_map/near_grad/pallas_call | solution.py:358
  68.8 1.6 collective-permute-done.3.chunk
  70.4 1.0 grad_theirs.1
  71.4 7.7 %collective-permute-start.4 = (f32[65,16,128]{2,1,0:T(8,128)S(1)}, f32[65,16,128]{2,1,0:T(8,128)S(1)}, u32[]{:S(2)}, u32[]{:S(2)}) collective-permute-start(f32[65,16,128]{2,1,0:T(8,128)S(1)} %get-tuple-element.22), channel_id=1, source_target_pairs={{0,64},{64,0},{1,65},{65,1},{2,66},{66,2},{3,67},{67,3},{4,68},{68... | collective-permute-start | bytes 1597448 | tf_op jit(solution)/shard_map/ppermute | solution.py:375
  79.6 1.0 collective-permute-done.4.theirs
  81.1 0.9 convert_element_type.11
  82.1 14.5 %all-to-all-start.2 = ((f16[64,2,1152]{2,1,0:T(2,128)(2,1)}), f16[64,2,1152]{2,1,0:T(2,128)(2,1)S(1)}, u32[]{:S(2)}, u32[]{:S(2)}) async-start(f16[64,2,1152]{2,1,0:T(2,128)(2,1)} %convert_element_type.11), calls=%async_computation.2 | async-start | bytes 589824 | tf_op jit(solution)/shard_map/all_to_all | solution.py:411
  97.0 2.6 %collective-permute-start.7 = (f32[3,16,4,128]{3,2,1,0:T(4,128)S(1)}, f32[3,16,4,128]{3,2,1,0:T(4,128)S(1)}, u32[]{:S(2)}, u32[]{:S(2)}) collective-permute-start(f32[3,16,4,128]{3,2,1,0:T(4,128)S(1)} %get-tuple-element.32), channel_id=1, source_target_pairs={{0,256},{128,384},{256,0},{384,128},{1,257},{129,385},{257,1},{385... | collective-permute-start | bytes 294920 | tf_op jit(solution)/shard_map/ppermute | solution.py:408
  99.5 3.6 %collective-permute-start.6 = (f32[3,16,4,128]{3,2,1,0:T(4,128)S(1)}, f32[3,16,4,128]{3,2,1,0:T(4,128)S(1)}, u32[]{:S(2)}, u32[]{:S(2)}) collective-permute-start(f32[3,16,4,128]{3,2,1,0:T(4,128)S(1)} %get-tuple-element.33), channel_id=1, source_target_pairs={{0,384},{128,0},{256,128},{384,256},{1,385},{129,1},{257,129},{385... | collective-permute-start | bytes 294920 | tf_op jit(solution)/shard_map/ppermute | solution.py:407
  103.1 2.5 %collective-permute-start.5 = (f32[3,16,4,128]{3,2,1,0:T(4,128)S(1)}, f32[3,16,4,128]{3,2,1,0:T(4,128)S(1)}, u32[]{:S(2)}, u32[]{:S(2)}) collective-permute-start(f32[3,16,4,128]{3,2,1,0:T(4,128)S(1)} %get-tuple-element.34), channel_id=1, source_target_pairs={{0,128},{128,256},{256,384},{384,0},{1,129},{129,257},{257,385},{3... | collective-permute-start | bytes 294920 | tf_op jit(solution)/shard_map/ppermute | solution.py:406
  105.9 11.8 %all-to-all-done.2 = f16[64,2,1152]{2,1,0:T(2,128)(2,1)S(1)} async-done(((f16[64,2,1152]{2,1,0:T(2,128)(2,1)}), f16[64,2,1152]{2,1,0:T(2,128)(2,1)S(1)}, u32[]{:S(2)}, u32[]{:S(2)}) %all-to-all-start.2) | async-done | bytes 294944 | tf_op jit(solution)/shard_map/all_to_all | solution.py:411
  117.9 1.1 adam.1
  119.0 17.8 %all_to_all.26 = bf16[16,64,128]{2,1,0:T(8,128)(2,1)S(1)} all-to-all(bf16[16,64,128]{2,1,0:T(8,128)(2,1)S(1)} %bitcast.38), channel_id=1, replica_groups=mesh['y'=4,'core'=2,'x'=4,'z'=16] {'z'}, dimensions={0} | all-to-all | bytes 524288 | tf_op jit(solution)/shard_map/all_to_all | solution.py:433
  137.3 16.2 %all_to_all.27 = bf16[16,256,128]{2,1,0:T(8,128)(2,1)S(1)} all-to-all(bf16[16,256,128]{2,1,0:T(8,128)(2,1)S(1)} %bitcast.40), channel_id=1, replica_groups=mesh['y'=4,'core'=2,'x'=4,'z'=16] {'y','x'}, dimensions={0} | all-to-all | bytes 2097152 | tf_op jit(solution)/shard_map/all_to_all | solution.py:457
  153.5 10.3 %collective-permute-start.8 = (bf16[4,4,4,64,128]{4,3,2,1,0:T(8,128)(2,1)S(1)}, bf16[4,4,4,64,128]{4,3,2,1,0:T(8,128)(2,1)S(1)}, u32[]{:S(2)}, u32[]{:S(2)}) collective-permute-start(bf16[4,4,4,64,128]{4,3,2,1,0:T(8,128)(2,1)S(1)} %bitcast.32), channel_id=1, source_target_pairs={{0,64},{64,0},{1,65},{65,1},{2,66},{66,2},{3,67},{67,3},{4,68},{68... | collective-permute-start | bytes 3145736 | tf_op jit(solution)/shard_map/ppermute | solution.py:460
  163.9 2.5 %collective-permute-start.11 = (f32[3,16,4,128]{3,2,1,0:T(4,128)S(1)}, f32[3,16,4,128]{3,2,1,0:T(4,128)S(1)}, u32[]{:S(2)}, u32[]{:S(2)}) collective-permute-start(f32[3,16,4,128]{3,2,1,0:T(4,128)S(1)} %get-tuple-element.28), channel_id=1, source_target_pairs={{0,256},{128,384},{256,0},{384,128},{1,257},{129,385},{257,1},{385... | collective-permute-start | bytes 294920 | tf_op jit(solution)/shard_map/ppermute | solution.py:439
  166.4 3.2 %collective-permute-start.10 = (f32[3,16,4,128]{3,2,1,0:T(4,128)S(1)}, f32[3,16,4,128]{3,2,1,0:T(4,128)S(1)}, u32[]{:S(2)}, u32[]{:S(2)}) collective-permute-start(f32[3,16,4,128]{3,2,1,0:T(4,128)S(1)} %get-tuple-element.29), channel_id=1, source_target_pairs={{0,384},{128,0},{256,128},{384,256},{1,385},{129,1},{257,129},{385... | collective-permute-start | bytes 294920 | tf_op jit(solution)/shard_map/ppermute | solution.py:438
  169.7 2.0 %collective-permute-start.9 = (f32[3,16,4,128]{3,2,1,0:T(4,128)S(1)}, f32[3,16,4,128]{3,2,1,0:T(4,128)S(1)}, u32[]{:S(2)}, u32[]{:S(2)}) collective-permute-start(f32[3,16,4,128]{3,2,1,0:T(4,128)S(1)} %get-tuple-element.30), channel_id=1, source_target_pairs={{0,128},{128,256},{256,384},{384,0},{1,129},{129,257},{257,385},{3... | collective-permute-start | bytes 294920 | tf_op jit(solution)/shard_map/ppermute | solution.py:437
  172.4 4.2 %collective-permute-done.9.low = f32[3,16,4,128]{3,2,1,0:T(4,128)S(1)} collective-permute-done((f32[3,16,4,128]{3,2,1,0:T(4,128)S(1)}, f32[3,16,4,128]{3,2,1,0:T(4,128)S(1)}, u32[]{:S(2)}, u32[]{:S(2)}) %collective-permute-start.9) | collective-permute-done | bytes 98336 | tf_op jit(solution)/shard_map/ppermute | solution.py:437
  176.5 1.0 join_cols.1
  177.5 1.1 join_mine.1.begun
  178.6 1.1 join_theirs.1
  (36 shorter events, 3.5 us)
Async XLA Ops:
  0.6 63.8 %copy-start = (bf16[1,1,256,2048]{3,2,1,0:T(8,128)(2,1)S(1)}, bf16[1,1,256,2048]{3,2,1,0:T(8,128)(2,1)}, u32[]{:S(2)}) copy-start(bf16[1,1,256,2048]{3,2,1,0:T(8,128)(2,1)} %param.9) | copy-start | bytes 3145732
  0.6 43.6 %collective-permute-start = (bf16[256,2048]{1,0:T(8,128)(2,1)}, bf16[256,2048]{1,0:T(8,128)(2,1)S(1)}, u32[]{:S(2)}, u32[]{:S(2)}) collective-permute-start(bf16[256,2048]{1,0:T(8,128)(2,1)} %bitcast.34), channel_id=1, source_target_pairs={{0,128},{64,448},{128,256},{192,64},{256,384},{320,192},{384,0},{4... | collective-permute-start | bytes 3145736 | tf_op jit(solution)/shard_map/ppermute | solution.py:326
  20.3 0.7 copy-start.4
  22.3 35.2 %all-to-all-start.1 = ((bf16[64,16,128]{2,1,0:T(8,128)(2,1)}), bf16[64,16,128]{2,1,0:T(8,128)(2,1)}, u32[]{:S(2)}, u32[]{:S(2)}) async-start(bf16[64,16,128]{2,1,0:T(8,128)(2,1)} %pick_old.1), calls=%async_computation.1 | async-start | bytes 524288 | tf_op jit(solution)/shard_map/all_to_all | solution.py:341
  40.8 23.6 %collective-permute-start.1 = (bf16[256,2048]{1,0:T(8,128)(2,1)}, bf16[256,2048]{1,0:T(8,128)(2,1)}, u32[]{:S(2)}, u32[]{:S(2)}) collective-permute-start(bf16[256,2048]{1,0:T(8,128)(2,1)} %bitcast.35), channel_id=1, source_target_pairs={{128,0},{448,64},{256,128},{64,192},{384,256},{192,320},{0,384},{3... | collective-permute-start | bytes 3145736 | tf_op jit(solution)/shard_map/ppermute | solution.py:327
  44.2 26.2 %collective-permute-start.3 = (bf16[256,2048]{1,0:T(8,128)(2,1)S(1)}, bf16[256,2048]{1,0:T(8,128)(2,1)S(1)}, u32[]{:S(2)}, u32[]{:S(2)}) collective-permute-start(bf16[256,2048]{1,0:T(8,128)(2,1)S(1)} %collective-permute-done.one), channel_id=1, source_target_pairs={{0,128},{64,448},{128,256},{192,64},{256,384},{320,192},{384,0},{4... | collective-permute-start | bytes 3145736 | tf_op jit(solution)/shard_map/ppermute | solution.py:342
  57.5 8.9 %collective-permute-start.2 = (bf16[64,16,128]{2,1,0:T(8,128)(2,1)}, bf16[64,16,128]{2,1,0:T(8,128)(2,1)S(1)}, u32[]{:S(2)}, u32[]{:S(2)}) collective-permute-start(bf16[64,16,128]{2,1,0:T(8,128)(2,1)} %all-to-all-done.1.mine), channel_id=1, source_target_pairs={{0,64},{64,0},{1,65},{65,1},{2,66},{66,2},{3,67},{67,3},{4,68},{68... | collective-permute-start | bytes 786440 | tf_op jit(solution)/shard_map/ppermute | solution.py:345
  71.4 9.3 %collective-permute-start.4 = (f32[65,16,128]{2,1,0:T(8,128)S(1)}, f32[65,16,128]{2,1,0:T(8,128)S(1)}, u32[]{:S(2)}, u32[]{:S(2)}) collective-permute-start(f32[65,16,128]{2,1,0:T(8,128)S(1)} %get-tuple-element.22), channel_id=1, source_target_pairs={{0,64},{64,0},{1,65},{65,1},{2,66},{66,2},{3,67},{67,3},{4,68},{68... | collective-permute-start | bytes 1597448 | tf_op jit(solution)/shard_map/ppermute | solution.py:375
  79.6 17.1 %copy-start.1 = (f32[16,4,512]{2,1,0:T(4,128)S(1)}, f32[16,4,512]{2,1,0:T(4,128)}, u32[]{:S(2)}) copy-start(f32[16,4,512]{2,1,0:T(4,128)} %refs_0_.1) | copy-start | bytes 393220
  79.6 17.1 %copy-start.2 = (f32[16,4,512]{2,1,0:T(4,128)S(1)}, f32[16,4,512]{2,1,0:T(4,128)}, u32[]{:S(2)}) copy-start(f32[16,4,512]{2,1,0:T(4,128)} %refs_1_.1) | copy-start | bytes 393220
  79.6 17.1 %copy-start.3 = (f32[16,4,512]{2,1,0:T(4,128)S(1)}, f32[16,4,512]{2,1,0:T(4,128)}, u32[]{:S(2)}) copy-start(f32[16,4,512]{2,1,0:T(4,128)} %refs_2_.1) | copy-start | bytes 393220
  79.6 26.0 %copy-start.7 = (s32[8,64]{1,0:T(8,128)S(1)}, s32[8,64]{1,0:T(8,128)}, u32[]{:S(2)}) copy-start(s32[8,64]{1,0:T(8,128)} %counts.1) | copy-start | bytes 6148
  79.6 26.1 %copy-start.5 = (s32[64]{0:T(128)S(1)}, s32[64]{0:T(128)}, u32[]{:S(2)}) copy-start(s32[64]{0:T(128)} %old.1) | copy-start | bytes 772
  81.1 36.7 %copy-start.6 = (s32[64]{0:T(128)S(1)}, s32[64]{0:T(128)}, u32[]{:S(2)}) copy-start(s32[64]{0:T(128)} %new.1) | copy-start | bytes 772
  82.1 35.6 %all-to-all-start.2 = ((f16[64,2,1152]{2,1,0:T(2,128)(2,1)}), f16[64,2,1152]{2,1,0:T(2,128)(2,1)S(1)}, u32[]{:S(2)}, u32[]{:S(2)}) async-start(f16[64,2,1152]{2,1,0:T(2,128)(2,1)} %convert_element_type.11), calls=%async_computation.2 | async-start | bytes 589824 | tf_op jit(solution)/shard_map/all_to_all | solution.py:411
  97.0 20.9 %collective-permute-start.7 = (f32[3,16,4,128]{3,2,1,0:T(4,128)S(1)}, f32[3,16,4,128]{3,2,1,0:T(4,128)S(1)}, u32[]{:S(2)}, u32[]{:S(2)}) collective-permute-start(f32[3,16,4,128]{3,2,1,0:T(4,128)S(1)} %get-tuple-element.32), channel_id=1, source_target_pairs={{0,256},{128,384},{256,0},{384,128},{1,257},{129,385},{257,1},{385... | collective-permute-start | bytes 294920 | tf_op jit(solution)/shard_map/ppermute | solution.py:408
  99.5 18.3 %collective-permute-start.6 = (f32[3,16,4,128]{3,2,1,0:T(4,128)S(1)}, f32[3,16,4,128]{3,2,1,0:T(4,128)S(1)}, u32[]{:S(2)}, u32[]{:S(2)}) collective-permute-start(f32[3,16,4,128]{3,2,1,0:T(4,128)S(1)} %get-tuple-element.33), channel_id=1, source_target_pairs={{0,384},{128,0},{256,128},{384,256},{1,385},{129,1},{257,129},{385... | collective-permute-start | bytes 294920 | tf_op jit(solution)/shard_map/ppermute | solution.py:407
  103.1 14.7 %collective-permute-start.5 = (f32[3,16,4,128]{3,2,1,0:T(4,128)S(1)}, f32[3,16,4,128]{3,2,1,0:T(4,128)S(1)}, u32[]{:S(2)}, u32[]{:S(2)}) collective-permute-start(f32[3,16,4,128]{3,2,1,0:T(4,128)S(1)} %get-tuple-element.34), channel_id=1, source_target_pairs={{0,128},{128,256},{256,384},{384,0},{1,129},{129,257},{257,385},{3... | collective-permute-start | bytes 294920 | tf_op jit(solution)/shard_map/ppermute | solution.py:406
  153.5 25.1 %collective-permute-start.8 = (bf16[4,4,4,64,128]{4,3,2,1,0:T(8,128)(2,1)S(1)}, bf16[4,4,4,64,128]{4,3,2,1,0:T(8,128)(2,1)S(1)}, u32[]{:S(2)}, u32[]{:S(2)}) collective-permute-start(bf16[4,4,4,64,128]{4,3,2,1,0:T(8,128)(2,1)S(1)} %bitcast.32), channel_id=1, source_target_pairs={{0,64},{64,0},{1,65},{65,1},{2,66},{66,2},{3,67},{67,3},{4,68},{68... | collective-permute-start | bytes 3145736 | tf_op jit(solution)/shard_map/ppermute | solution.py:460
  163.9 7.8 %collective-permute-start.11 = (f32[3,16,4,128]{3,2,1,0:T(4,128)S(1)}, f32[3,16,4,128]{3,2,1,0:T(4,128)S(1)}, u32[]{:S(2)}, u32[]{:S(2)}) collective-permute-start(f32[3,16,4,128]{3,2,1,0:T(4,128)S(1)} %get-tuple-element.28), channel_id=1, source_target_pairs={{0,256},{128,384},{256,0},{384,128},{1,257},{129,385},{257,1},{385... | collective-permute-start | bytes 294920 | tf_op jit(solution)/shard_map/ppermute | solution.py:439
  166.4 6.0 %collective-permute-start.10 = (f32[3,16,4,128]{3,2,1,0:T(4,128)S(1)}, f32[3,16,4,128]{3,2,1,0:T(4,128)S(1)}, u32[]{:S(2)}, u32[]{:S(2)}) collective-permute-start(f32[3,16,4,128]{3,2,1,0:T(4,128)S(1)} %get-tuple-element.29), channel_id=1, source_target_pairs={{0,384},{128,0},{256,128},{384,256},{1,385},{129,1},{257,129},{385... | collective-permute-start | bytes 294920 | tf_op jit(solution)/shard_map/ppermute | solution.py:438
  169.7 6.9 %collective-permute-start.9 = (f32[3,16,4,128]{3,2,1,0:T(4,128)S(1)}, f32[3,16,4,128]{3,2,1,0:T(4,128)S(1)}, u32[]{:S(2)}, u32[]{:S(2)}) collective-permute-start(f32[3,16,4,128]{3,2,1,0:T(4,128)S(1)} %get-tuple-element.30), channel_id=1, source_target_pairs={{0,128},{128,256},{256,384},{384,0},{1,129},{129,257},{257,385},{3... | collective-permute-start | bytes 294920 | tf_op jit(solution)/shard_map/ppermute | solution.py:437

commit v12 on v10

--- a/solution.py
+++ b/solution.py
@@ -116,11 +116,16 @@
         table[e] = jnp.concatenate(
             [part[e * rows_shard : (e + 1) * rows_shard] for part in parts], axis=0
         ).astype(jnp.bfloat16)
-    for p in range(PLACES):
-        picked[p] = table[slots[p]]
-    copy = pltpu.make_async_copy(picked, out, sem)
-    copy.start()
-    copy.wait()
+    step = PLACES // 4
+    copies = []
+    for k in range(4):
+        for p in range(k * step, (k + 1) * step):
+            picked[p] = table[slots[p]]
+        part = pl.ds(k * step, step)
+        copies.append(pltpu.make_async_copy(picked.at[part], out.at[part], sem.at[k]))
+        copies[-1].start()
+    for copy in copies:
+        copy.wait()
 
 
 def adam(old, new, total, got, own, low, high, far, out, after, state, acc, table):
@@ -333,7 +338,7 @@
         scratch_shapes=[
             pltpu.VMEM((experts, Y * rows_shard, lanes), bf16),
             pltpu.VMEM((PLACES, Y * rows_shard, lanes), bf16),
-            pltpu.SemaphoreType.DMA(()),
+            pltpu.SemaphoreType.DMA((4,)),
         ],
         compiler_params=grant(4),
         name="pick_old",

time: 183 us -> 183 us (level)
  no operation moved by 1% of the time
where the time goes in v12:
time: 183 us; the launch traced here: 180 us
  starting transfers between devices  86.9 us (47%)
  blocking collectives  46.2 us (25%)
  waiting for transfers between devices  28.9 us (16%)
  Pallas kernels  14.2 us (8%)
    all_to_all x1, starting transfers between devices, shards(): landed = lax.all_to_all(picked, ('x', 'z'), 0, 0, tiled=True)  18.5 us
    all_to_all x1, blocking collectives, shards(): lax.all_to_all(picked.reshape(Z, X * Y * rows_shard, lanes), 'z', 0, 0, t...  17.8 us
    all_to_all x1, blocking collectives, shards(): lax.all_to_all(copies.reshape(Y * X, Y * Z * rows_shard, lanes), ('y', 'x...  16.2 us
    all_to_all x1, starting transfers between devices, shards(): lax.all_to_all(scaled.astype(jnp.float16), ('x', 'z'), 0, 0, tiled=True)  14.5 us
    all_to_all x1, blocking collectives, shards(): payload = lax.all_to_all(payload, 'y', 0, 0, tiled=True)  12.1 us
    all_to_all x1, waiting for transfers between devices, shards(): lax.all_to_all(scaled.astype(jnp.float16), ('x', 'z'), 0, 0, tiled=True)  11.8 us
    ppermute x1, starting transfers between devices, shards(): theirs = lax.ppermute(mine, 'core', SWAP)  10.3 us
    all_to_all x1, waiting for transfers between devices, shards(): landed = lax.all_to_all(picked, ('x', 'z'), 0, 0, tiled=True)  9.66 us
  transfers between devices with their start and end apart: 14, of which 6 were waited for; matrix products, arithmetic and copies ran while one was open for 0% of the time, Pallas kernels for 6%

profile of v12, /device:TPU:1, one launch (start us, length us, event | category | flops | bytes accessed | tf_op | source)
XLA Modules:
  0.0 179.9 jit_solution(12420018708132884704)
XLA Ops:
  0.6 5.6 %collective-permute-start = (bf16[256,2048]{1,0:T(8,128)(2,1)}, bf16[256,2048]{1,0:T(8,128)(2,1)S(1)}, u32[]{:S(2)}, u32[]{:S(2)}) collective-permute-start(bf16[256,2048]{1,0:T(8,128)(2,1)} %bitcast.34), channel_id=1, source_target_pairs={{0,128},{64,448},{128,256},{192,64},{256,384},{320,192},{384,0},{4... | collective-permute-start | bytes 3145736 | tf_op jit(solution)/shard_map/ppermute | solution.py:331
  6.2 1.9 %prepare.1 = bf16[4,192,128]{2,1,0:T(8,128)(2,1)} custom-call(s32[8,64]{1,0:T(8,128)} %counts.1, s32[4,64]{1,0:T(4,128)} %bitcast.44, bf16[256,256]{1,0:T(8,128)(2,1)} %bitcast.43, f32[16,4,512]{2,1,0:T(4,128)} %refs_0_.1), custom_call_target="tpu_custom_call" | custom-call | tf_op jit(solution)/shard_map/prepare/pallas_call | solution.py:323
  8.2 12.1 %all_to_all.25.payload = bf16[4,192,128]{2,1,0:T(8,128)(2,1)S(1)} all-to-all(bf16[4,192,128]{2,1,0:T(8,128)(2,1)} %prepare.1), channel_id=1, replica_groups=mesh['y'=4,'core'=2,'x'=4,'z'=16] {'y'}, dimensions={0} | all-to-all | bytes 393216 | tf_op jit(solution)/shard_map/all_to_all | solution.py:330
  21.0 1.3 pick_old.1
  22.3 18.5 %all-to-all-start.1 = ((bf16[64,16,128]{2,1,0:T(8,128)(2,1)}), bf16[64,16,128]{2,1,0:T(8,128)(2,1)}, u32[]{:S(2)}, u32[]{:S(2)}) async-start(bf16[64,16,128]{2,1,0:T(8,128)(2,1)} %pick_old.1), calls=%async_computation.1 | async-start | bytes 524288 | tf_op jit(solution)/shard_map/all_to_all | solution.py:346
  40.8 3.4 %collective-permute-start.1 = (bf16[256,2048]{1,0:T(8,128)(2,1)}, bf16[256,2048]{1,0:T(8,128)(2,1)}, u32[]{:S(2)}, u32[]{:S(2)}) collective-permute-start(bf16[256,2048]{1,0:T(8,128)(2,1)} %bitcast.35), channel_id=1, source_target_pairs={{128,0},{448,64},{256,128},{64,192},{384,256},{192,320},{0,384},{3... | collective-permute-start | bytes 3145736 | tf_op jit(solution)/shard_map/ppermute | solution.py:332
  44.2 3.6 %collective-permute-start.3 = (bf16[256,2048]{1,0:T(8,128)(2,1)S(1)}, bf16[256,2048]{1,0:T(8,128)(2,1)S(1)}, u32[]{:S(2)}, u32[]{:S(2)}) collective-permute-start(bf16[256,2048]{1,0:T(8,128)(2,1)S(1)} %collective-permute-done.one), channel_id=1, source_target_pairs={{0,128},{64,448},{128,256},{192,64},{256,384},{320,192},{384,0},{4... | collective-permute-start | bytes 3145736 | tf_op jit(solution)/shard_map/ppermute | solution.py:347
  47.8 9.7 %all-to-all-done.1.mine = bf16[64,16,128]{2,1,0:T(8,128)(2,1)} async-done(((bf16[64,16,128]{2,1,0:T(8,128)(2,1)}), bf16[64,16,128]{2,1,0:T(8,128)(2,1)}, u32[]{:S(2)}, u32[]{:S(2)}) %all-to-all-start.1) | async-done | bytes 262176 | tf_op jit(solution)/shard_map/all_to_all | solution.py:346
  57.4 6.9 %collective-permute-start.2 = (bf16[64,16,128]{2,1,0:T(8,128)(2,1)}, bf16[64,16,128]{2,1,0:T(8,128)(2,1)S(1)}, u32[]{:S(2)}, u32[]{:S(2)}) collective-permute-start(bf16[64,16,128]{2,1,0:T(8,128)(2,1)} %all-to-all-done.1.mine), channel_id=1, source_target_pairs={{0,64},{64,0},{1,65},{65,1},{2,66},{66,2},{3,67},{67,3},{4,68},{68... | collective-permute-start | bytes 786440 | tf_op jit(solution)/shard_map/ppermute | solution.py:350
  64.4 1.9 %forward_mine.1 = (f32[3,256,128]{2,1,0:T(8,128)S(1)}, bf16[4,256,128]{2,1,0:T(8,128)(2,1)S(1)}) custom-call(bf16[64,16,128]{2,1,0:T(8,128)(2,1)} %all-to-all-done.1.mine, bf16[256,2048]{1,0:T(8,128)(2,1)S(1)} %bitcast.36, bf16[256,2048]{1,0:T(8,128)(2,1)S(1)} %collective-permute-done.one, bf16[256,2048]{1,0:T(8,128)(2,1)} %collective-permute-done.1.two), custom_call_target="tpu_custom_call" | custom-call | tf_op jit(solution)/shard_map/forward_mine/pallas_call | solution.py:354
  66.3 2.5 %near_grad.1 = (f32[4,128,256]{2,1,0:T(8,128)S(1)}, f32[4,128,256]{2,1,0:T(8,128)S(1)}, bf16[4,256,128]{2,1,0:T(8,128)(2,1)S(1)}) custom-call(f32[3,256,128]{2,1,0:T(8,128)S(1)} %get-tuple-element.16.part_ref, bf16[64,16,128]{2,1,0:T(8,128)(2,1)S(1)} %collective-permute-done.2.theirs, bf16[4,192,128]{2,1,0:T(8,128)(2,1)S(1)} %all_to_all.25.payload, ...), custom_call_target="tpu_custom_call" | custom-call | tf_op jit(solution)/shard_map/near_grad/pallas_call | solution.py:363
  68.8 1.6 collective-permute-done.3.chunk
  70.4 1.0 grad_theirs.1
  71.4 7.7 %collective-permute-start.4 = (f32[65,16,128]{2,1,0:T(8,128)S(1)}, f32[65,16,128]{2,1,0:T(8,128)S(1)}, u32[]{:S(2)}, u32[]{:S(2)}) collective-permute-start(f32[65,16,128]{2,1,0:T(8,128)S(1)} %get-tuple-element.22), channel_id=1, source_target_pairs={{0,64},{64,0},{1,65},{65,1},{2,66},{66,2},{3,67},{67,3},{4,68},{68... | collective-permute-start | bytes 1597448 | tf_op jit(solution)/shard_map/ppermute | solution.py:380
  79.6 1.0 collective-permute-done.4.theirs
  81.1 0.9 convert_element_type.11
  82.0 14.5 %all-to-all-start.2 = ((f16[64,2,1152]{2,1,0:T(2,128)(2,1)}), f16[64,2,1152]{2,1,0:T(2,128)(2,1)S(1)}, u32[]{:S(2)}, u32[]{:S(2)}) async-start(f16[64,2,1152]{2,1,0:T(2,128)(2,1)} %convert_element_type.11), calls=%async_computation.2 | async-start | bytes 589824 | tf_op jit(solution)/shard_map/all_to_all | solution.py:416
  97.0 2.6 %collective-permute-start.7 = (f32[3,16,4,128]{3,2,1,0:T(4,128)S(1)}, f32[3,16,4,128]{3,2,1,0:T(4,128)S(1)}, u32[]{:S(2)}, u32[]{:S(2)}) collective-permute-start(f32[3,16,4,128]{3,2,1,0:T(4,128)S(1)} %get-tuple-element.32), channel_id=1, source_target_pairs={{0,256},{128,384},{256,0},{384,128},{1,257},{129,385},{257,1},{385... | collective-permute-start | bytes 294920 | tf_op jit(solution)/shard_map/ppermute | solution.py:413
  99.5 3.6 %collective-permute-start.6 = (f32[3,16,4,128]{3,2,1,0:T(4,128)S(1)}, f32[3,16,4,128]{3,2,1,0:T(4,128)S(1)}, u32[]{:S(2)}, u32[]{:S(2)}) collective-permute-start(f32[3,16,4,128]{3,2,1,0:T(4,128)S(1)} %get-tuple-element.33), channel_id=1, source_target_pairs={{0,384},{128,0},{256,128},{384,256},{1,385},{129,1},{257,129},{385... | collective-permute-start | bytes 294920 | tf_op jit(solution)/shard_map/ppermute | solution.py:412
  103.1 2.5 %collective-permute-start.5 = (f32[3,16,4,128]{3,2,1,0:T(4,128)S(1)}, f32[3,16,4,128]{3,2,1,0:T(4,128)S(1)}, u32[]{:S(2)}, u32[]{:S(2)}) collective-permute-start(f32[3,16,4,128]{3,2,1,0:T(4,128)S(1)} %get-tuple-element.34), channel_id=1, source_target_pairs={{0,128},{128,256},{256,384},{384,0},{1,129},{129,257},{257,385},{3... | collective-permute-start | bytes 294920 | tf_op jit(solution)/shard_map/ppermute | solution.py:411
  105.8 11.8 %all-to-all-done.2 = f16[64,2,1152]{2,1,0:T(2,128)(2,1)S(1)} async-done(((f16[64,2,1152]{2,1,0:T(2,128)(2,1)}), f16[64,2,1152]{2,1,0:T(2,128)(2,1)S(1)}, u32[]{:S(2)}, u32[]{:S(2)}) %all-to-all-start.2) | async-done | bytes 294944 | tf_op jit(solution)/shard_map/all_to_all | solution.py:416
  117.9 1.1 adam.1
  118.9 17.8 %all_to_all.26 = bf16[16,64,128]{2,1,0:T(8,128)(2,1)S(1)} all-to-all(bf16[16,64,128]{2,1,0:T(8,128)(2,1)S(1)} %bitcast.38), channel_id=1, replica_groups=mesh['y'=4,'core'=2,'x'=4,'z'=16] {'z'}, dimensions={0} | all-to-all | bytes 524288 | tf_op jit(solution)/shard_map/all_to_all | solution.py:438
  137.3 16.2 %all_to_all.27 = bf16[16,256,128]{2,1,0:T(8,128)(2,1)S(1)} all-to-all(bf16[16,256,128]{2,1,0:T(8,128)(2,1)S(1)} %bitcast.40), channel_id=1, replica_groups=mesh['y'=4,'core'=2,'x'=4,'z'=16] {'y','x'}, dimensions={0} | all-to-all | bytes 2097152 | tf_op jit(solution)/shard_map/all_to_all | solution.py:462
  153.5 10.3 %collective-permute-start.8 = (bf16[4,4,4,64,128]{4,3,2,1,0:T(8,128)(2,1)S(1)}, bf16[4,4,4,64,128]{4,3,2,1,0:T(8,128)(2,1)S(1)}, u32[]{:S(2)}, u32[]{:S(2)}) collective-permute-start(bf16[4,4,4,64,128]{4,3,2,1,0:T(8,128)(2,1)S(1)} %bitcast.32), channel_id=1, source_target_pairs={{0,64},{64,0},{1,65},{65,1},{2,66},{66,2},{3,67},{67,3},{4,68},{68... | collective-permute-start | bytes 3145736 | tf_op jit(solution)/shard_map/ppermute | solution.py:465
  163.9 2.5 %collective-permute-start.11 = (f32[3,16,4,128]{3,2,1,0:T(4,128)S(1)}, f32[3,16,4,128]{3,2,1,0:T(4,128)S(1)}, u32[]{:S(2)}, u32[]{:S(2)}) collective-permute-start(f32[3,16,4,128]{3,2,1,0:T(4,128)S(1)} %get-tuple-element.28), channel_id=1, source_target_pairs={{0,256},{128,384},{256,0},{384,128},{1,257},{129,385},{257,1},{385... | collective-permute-start | bytes 294920 | tf_op jit(solution)/shard_map/ppermute | solution.py:444
  166.4 3.2 %collective-permute-start.10 = (f32[3,16,4,128]{3,2,1,0:T(4,128)S(1)}, f32[3,16,4,128]{3,2,1,0:T(4,128)S(1)}, u32[]{:S(2)}, u32[]{:S(2)}) collective-permute-start(f32[3,16,4,128]{3,2,1,0:T(4,128)S(1)} %get-tuple-element.29), channel_id=1, source_target_pairs={{0,384},{128,0},{256,128},{384,256},{1,385},{129,1},{257,129},{385... | collective-permute-start | bytes 294920 | tf_op jit(solution)/shard_map/ppermute | solution.py:443
  169.6 2.0 %collective-permute-start.9 = (f32[3,16,4,128]{3,2,1,0:T(4,128)S(1)}, f32[3,16,4,128]{3,2,1,0:T(4,128)S(1)}, u32[]{:S(2)}, u32[]{:S(2)}) collective-permute-start(f32[3,16,4,128]{3,2,1,0:T(4,128)S(1)} %get-tuple-element.30), channel_id=1, source_target_pairs={{0,128},{128,256},{256,384},{384,0},{1,129},{129,257},{257,385},{3... | collective-permute-start | bytes 294920 | tf_op jit(solution)/shard_map/ppermute | solution.py:442
  172.3 4.2 %collective-permute-done.9.low = f32[3,16,4,128]{3,2,1,0:T(4,128)S(1)} collective-permute-done((f32[3,16,4,128]{3,2,1,0:T(4,128)S(1)}, f32[3,16,4,128]{3,2,1,0:T(4,128)S(1)}, u32[]{:S(2)}, u32[]{:S(2)}) %collective-permute-start.9) | collective-permute-done | bytes 98336 | tf_op jit(solution)/shard_map/ppermute | solution.py:442
  176.5 1.0 join_cols.1
  177.5 1.2 join_mine.1.begun
  178.7 1.2 join_theirs.1
  (36 shorter events, 3.5 us)
Async XLA Ops:
  0.6 63.8 %copy-start = (bf16[1,1,256,2048]{3,2,1,0:T(8,128)(2,1)S(1)}, bf16[1,1,256,2048]{3,2,1,0:T(8,128)(2,1)}, u32[]{:S(2)}) copy-start(bf16[1,1,256,2048]{3,2,1,0:T(8,128)(2,1)} %param.9) | copy-start | bytes 3145732
  0.6 43.6 %collective-permute-start = (bf16[256,2048]{1,0:T(8,128)(2,1)}, bf16[256,2048]{1,0:T(8,128)(2,1)S(1)}, u32[]{:S(2)}, u32[]{:S(2)}) collective-permute-start(bf16[256,2048]{1,0:T(8,128)(2,1)} %bitcast.34), channel_id=1, source_target_pairs={{0,128},{64,448},{128,256},{192,64},{256,384},{320,192},{384,0},{4... | collective-permute-start | bytes 3145736 | tf_op jit(solution)/shard_map/ppermute | solution.py:331
  20.3 0.7 copy-start.4
  22.3 35.2 %all-to-all-start.1 = ((bf16[64,16,128]{2,1,0:T(8,128)(2,1)}), bf16[64,16,128]{2,1,0:T(8,128)(2,1)}, u32[]{:S(2)}, u32[]{:S(2)}) async-start(bf16[64,16,128]{2,1,0:T(8,128)(2,1)} %pick_old.1), calls=%async_computation.1 | async-start | bytes 524288 | tf_op jit(solution)/shard_map/all_to_all | solution.py:346
  40.8 23.6 %collective-permute-start.1 = (bf16[256,2048]{1,0:T(8,128)(2,1)}, bf16[256,2048]{1,0:T(8,128)(2,1)}, u32[]{:S(2)}, u32[]{:S(2)}) collective-permute-start(bf16[256,2048]{1,0:T(8,128)(2,1)} %bitcast.35), channel_id=1, source_target_pairs={{128,0},{448,64},{256,128},{64,192},{384,256},{192,320},{0,384},{3... | collective-permute-start | bytes 3145736 | tf_op jit(solution)/shard_map/ppermute | solution.py:332
  44.2 26.2 %collective-permute-start.3 = (bf16[256,2048]{1,0:T(8,128)(2,1)S(1)}, bf16[256,2048]{1,0:T(8,128)(2,1)S(1)}, u32[]{:S(2)}, u32[]{:S(2)}) collective-permute-start(bf16[256,2048]{1,0:T(8,128)(2,1)S(1)} %collective-permute-done.one), channel_id=1, source_target_pairs={{0,128},{64,448},{128,256},{192,64},{256,384},{320,192},{384,0},{4... | collective-permute-start | bytes 3145736 | tf_op jit(solution)/shard_map/ppermute | solution.py:347
  57.4 8.9 %collective-permute-start.2 = (bf16[64,16,128]{2,1,0:T(8,128)(2,1)}, bf16[64,16,128]{2,1,0:T(8,128)(2,1)S(1)}, u32[]{:S(2)}, u32[]{:S(2)}) collective-permute-start(bf16[64,16,128]{2,1,0:T(8,128)(2,1)} %all-to-all-done.1.mine), channel_id=1, source_target_pairs={{0,64},{64,0},{1,65},{65,1},{2,66},{66,2},{3,67},{67,3},{4,68},{68... | collective-permute-start | bytes 786440 | tf_op jit(solution)/shard_map/ppermute | solution.py:350
  71.4 9.3 %collective-permute-start.4 = (f32[65,16,128]{2,1,0:T(8,128)S(1)}, f32[65,16,128]{2,1,0:T(8,128)S(1)}, u32[]{:S(2)}, u32[]{:S(2)}) collective-permute-start(f32[65,16,128]{2,1,0:T(8,128)S(1)} %get-tuple-element.22), channel_id=1, source_target_pairs={{0,64},{64,0},{1,65},{65,1},{2,66},{66,2},{3,67},{67,3},{4,68},{68... | collective-permute-start | bytes 1597448 | tf_op jit(solution)/shard_map/ppermute | solution.py:380
  79.5 17.1 %copy-start.1 = (f32[16,4,512]{2,1,0:T(4,128)S(1)}, f32[16,4,512]{2,1,0:T(4,128)}, u32[]{:S(2)}) copy-start(f32[16,4,512]{2,1,0:T(4,128)} %refs_0_.1) | copy-start | bytes 393220
  79.5 17.1 %copy-start.2 = (f32[16,4,512]{2,1,0:T(4,128)S(1)}, f32[16,4,512]{2,1,0:T(4,128)}, u32[]{:S(2)}) copy-start(f32[16,4,512]{2,1,0:T(4,128)} %refs_1_.1) | copy-start | bytes 393220
  79.6 17.1 %copy-start.3 = (f32[16,4,512]{2,1,0:T(4,128)S(1)}, f32[16,4,512]{2,1,0:T(4,128)}, u32[]{:S(2)}) copy-start(f32[16,4,512]{2,1,0:T(4,128)} %refs_2_.1) | copy-start | bytes 393220
  79.6 26.0 %copy-start.7 = (s32[8,64]{1,0:T(8,128)S(1)}, s32[8,64]{1,0:T(8,128)}, u32[]{:S(2)}) copy-start(s32[8,64]{1,0:T(8,128)} %counts.1) | copy-start | bytes 6148
  79.6 26.1 %copy-start.5 = (s32[64]{0:T(128)S(1)}, s32[64]{0:T(128)}, u32[]{:S(2)}) copy-start(s32[64]{0:T(128)} %old.1) | copy-start | bytes 772
  81.1 36.7 %copy-start.6 = (s32[64]{0:T(128)S(1)}, s32[64]{0:T(128)}, u32[]{:S(2)}) copy-start(s32[64]{0:T(128)} %new.1) | copy-start | bytes 772
  82.0 35.6 %all-to-all-start.2 = ((f16[64,2,1152]{2,1,0:T(2,128)(2,1)}), f16[64,2,1152]{2,1,0:T(2,128)(2,1)S(1)}, u32[]{:S(2)}, u32[]{:S(2)}) async-start(f16[64,2,1152]{2,1,0:T(2,128)(2,1)} %convert_element_type.11), calls=%async_computation.2 | async-start | bytes 589824 | tf_op jit(solution)/shard_map/all_to_all | solution.py:416
  97.0 20.9 %collective-permute-start.7 = (f32[3,16,4,128]{3,2,1,0:T(4,128)S(1)}, f32[3,16,4,128]{3,2,1,0:T(4,128)S(1)}, u32[]{:S(2)}, u32[]{:S(2)}) collective-permute-start(f32[3,16,4,128]{3,2,1,0:T(4,128)S(1)} %get-tuple-element.32), channel_id=1, source_target_pairs={{0,256},{128,384},{256,0},{384,128},{1,257},{129,385},{257,1},{385... | collective-permute-start | bytes 294920 | tf_op jit(solution)/shard_map/ppermute | solution.py:413
  99.5 18.3 %collective-permute-start.6 = (f32[3,16,4,128]{3,2,1,0:T(4,128)S(1)}, f32[3,16,4,128]{3,2,1,0:T(4,128)S(1)}, u32[]{:S(2)}, u32[]{:S(2)}) collective-permute-start(f32[3,16,4,128]{3,2,1,0:T(4,128)S(1)} %get-tuple-element.33), channel_id=1, source_target_pairs={{0,384},{128,0},{256,128},{384,256},{1,385},{129,1},{257,129},{385... | collective-permute-start | bytes 294920 | tf_op jit(solution)/shard_map/ppermute | solution.py:412
  103.1 14.7 %collective-permute-start.5 = (f32[3,16,4,128]{3,2,1,0:T(4,128)S(1)}, f32[3,16,4,128]{3,2,1,0:T(4,128)S(1)}, u32[]{:S(2)}, u32[]{:S(2)}) collective-permute-start(f32[3,16,4,128]{3,2,1,0:T(4,128)S(1)} %get-tuple-element.34), channel_id=1, source_target_pairs={{0,128},{128,256},{256,384},{384,0},{1,129},{129,257},{257,385},{3... | collective-permute-start | bytes 294920 | tf_op jit(solution)/shard_map/ppermute | solution.py:411
  153.5 25.2 %collective-permute-start.8 = (bf16[4,4,4,64,128]{4,3,2,1,0:T(8,128)(2,1)S(1)}, bf16[4,4,4,64,128]{4,3,2,1,0:T(8,128)(2,1)S(1)}, u32[]{:S(2)}, u32[]{:S(2)}) collective-permute-start(bf16[4,4,4,64,128]{4,3,2,1,0:T(8,128)(2,1)S(1)} %bitcast.32), channel_id=1, source_target_pairs={{0,64},{64,0},{1,65},{65,1},{2,66},{66,2},{3,67},{67,3},{4,68},{68... | collective-permute-start | bytes 3145736 | tf_op jit(solution)/shard_map/ppermute | solution.py:465
  163.9 7.8 %collective-permute-start.11 = (f32[3,16,4,128]{3,2,1,0:T(4,128)S(1)}, f32[3,16,4,128]{3,2,1,0:T(4,128)S(1)}, u32[]{:S(2)}, u32[]{:S(2)}) collective-permute-start(f32[3,16,4,128]{3,2,1,0:T(4,128)S(1)} %get-tuple-element.28), channel_id=1, source_target_pairs={{0,256},{128,384},{256,0},{384,128},{1,257},{129,385},{257,1},{385... | collective-permute-start | bytes 294920 | tf_op jit(solution)/shard_map/ppermute | solution.py:444
  166.4 6.0 %collective-permute-start.10 = (f32[3,16,4,128]{3,2,1,0:T(4,128)S(1)}, f32[3,16,4,128]{3,2,1,0:T(4,128)S(1)}, u32[]{:S(2)}, u32[]{:S(2)}) collective-permute-start(f32[3,16,4,128]{3,2,1,0:T(4,128)S(1)} %get-tuple-element.29), channel_id=1, source_target_pairs={{0,384},{128,0},{256,128},{384,256},{1,385},{129,1},{257,129},{385... | collective-permute-start | bytes 294920 | tf_op jit(solution)/shard_map/ppermute | solution.py:443
  169.6 6.9 %collective-permute-start.9 = (f32[3,16,4,128]{3,2,1,0:T(4,128)S(1)}, f32[3,16,4,128]{3,2,1,0:T(4,128)S(1)}, u32[]{:S(2)}, u32[]{:S(2)}) collective-permute-start(f32[3,16,4,128]{3,2,1,0:T(4,128)S(1)} %get-tuple-element.30), channel_id=1, source_target_pairs={{0,128},{128,256},{256,384},{384,0},{1,129},{129,257},{257,385},{3... | collective-permute-start | bytes 294920 | tf_op jit(solution)/shard_map/ppermute | solution.py:442
